TPU v7x, 32 devices: a whole 2x2x4 slice. The times are simulated.
32 devices in a mesh: rows: 16 (over z, y, x), panel: 2 (over core).
Axes of the slice: x: 2, y: 2, z: 4, core: 2. Of those that a mesh axis runs over, the one named last changes fastest.
Arguments:
- adj_tiles: bfloat16 [16, 2, 2, 16, 128, 128], P('rows', 'panel'), may hold values from -0.25 to 0.25
- row_counts: int32 [16, 2, 2], P('rows', 'panel'), may hold values from 1 to 16, as said below
- tile_cols: int32 [16, 2, 2, 16], P('rows', 'panel'), may hold values from 0 to 15, as said below
- start_basis: bfloat16 [64, 4096], P(None, ('rows', 'panel')), may hold values from -100 to 100
- start_resid: bfloat16 [64, 4096], P(None, ('rows', 'panel')), may hold values from -100 to 100
- start_search: bfloat16 [64, 4096], P(None, ('rows', 'panel')), may hold values from -100 to 100
- ritz_basis: float32 [3, 64, 192], replicated, may hold values from -1 to 1.5
- ritz_search: float32 [3, 64, 128], replicated, may hold values from -1 to 1.5
Outputs:
- eigvectors: float32 [64, 4096], P(None, ('rows', 'panel'))
- residual: float32 [64, 4096], P(None, ('rows', 'panel'))
- directions: float32 [64, 4096], P(None, ('rows', 'panel'))
- rayleigh: float32 [64, 64], replicated
Inputs may be any that keep to these rules, and one draw needn't show every extreme that they name: `row_counts`: each device's row blocks have 1 to 16 live slots, the live ones first; on one device every row block has 16. `tile_cols`: the live slots of one row block name distinct column blocks.
All inputs are finite; a program needn't handle non-finite values.
Results may differ from a plain program's by a relative error of at most 0.0053.
Values may be sent and summed in bfloat16 or wider, within the bound.
No kernel may reach another device: no remote copies, remote signals or barrier semaphores. Data moves between devices by JAX's collectives and lax.ppermute only.
A program may use at most 64 MiB of HBM per device.

v0:
```python
import jax
import jax.numpy as jnp
from jax import lax
from jax.sharding import PartitionSpec as P

epsilon = 1e-06
highest = lax.Precision.HIGHEST


def lower_solve(factor, values):
    return jax.scipy.linalg.solve_triangular(factor, values, lower=True)


def slot_product(gathered, tile_set, counts, columns):
    vec_rows = gathered.shape[0]
    tile_edge = tile_set.shape[2]
    blocks = gathered.reshape(vec_rows, gathered.shape[1] // tile_edge, tile_edge)
    slot_ids = jnp.arange(tile_set.shape[1], dtype=jnp.int32)
    in_use = slot_ids[None, :] < counts[:, None]
    chosen = jnp.take(blocks, columns.reshape(-1), axis=1)
    chosen = chosen.reshape(vec_rows, columns.shape[0], columns.shape[1], tile_edge)
    chosen = jnp.where(in_use[None, :, :, None], chosen, jnp.zeros((), chosen.dtype))
    summed = jnp.einsum("wbjk,bjik->wbi", chosen, tile_set, preferred_element_type=jnp.float32)
    return summed.reshape(vec_rows, -1)


def body(
    adj_tiles,
    row_counts,
    tile_cols,
    start_basis,
    start_resid,
    start_search,
    ritz_basis,
    ritz_search,
):
    tile_set = adj_tiles[0, 0]
    counts = row_counts[0, 0]
    columns = tile_cols[0, 0]
    vec_count = start_basis.shape[0]
    node_total = start_basis.shape[1] * lax.axis_size("rows") * lax.axis_size("panel")
    basis_b, resid_b, search_b = (start_basis, start_resid, start_search)
    for sweep in range(ritz_basis.shape[0]):
        stacked = jnp.concatenate([basis_b, resid_b, search_b], axis=0)
        stacked_all = lax.all_gather(stacked, "rows", axis=1, tiled=True)
        partial_value = slot_product(stacked_all, tile_set, counts, columns)
        product_rows = lax.psum_scatter(partial_value, "panel", scatter_dimension=1, tiled=True)
        stack_f32 = stacked.astype(jnp.float32)
        image_f32 = stack_f32 - product_rows
        mixing = ritz_basis[sweep]
        search_mix = ritz_search[sweep]
        rotated = jnp.dot(mixing, stack_f32, precision=highest)
        rotated_image = jnp.dot(mixing, image_f32, precision=highest)
        search_raw = jnp.dot(search_mix, stack_f32[vec_count:], precision=highest)
        gram_sum, curve_sum, search_sum = lax.psum(
            (
                jnp.dot(rotated, rotated.T, precision=highest),
                jnp.dot(rotated, rotated_image.T, precision=highest),
                jnp.sum(search_raw * search_raw, axis=1),
            ),
            ("rows", "panel"),
        )
        factor = jnp.linalg.cholesky(gram_sum / node_total)
        basis = lower_solve(factor, rotated)
        basis_image = lower_solve(factor, rotated_image)
        rayleigh = lower_solve(factor, lower_solve(factor, curve_sum / node_total).T).T
        resid_raw = basis_image - jnp.dot(rayleigh.T, basis, precision=highest)
        search_sq = search_sum / node_total
        resid_sq = lax.psum(jnp.sum(resid_raw * resid_raw, axis=1), ("rows", "panel")) / node_total
        resid = resid_raw / jnp.sqrt(resid_sq + epsilon)[:, None]
        search = search_raw / jnp.sqrt(search_sq + epsilon)[:, None]
        basis_b = basis.astype(jnp.bfloat16)
        resid_b = resid.astype(jnp.bfloat16)
        search_b = search.astype(jnp.bfloat16)
    return (basis, resid, search, rayleigh)


def solution(mesh):
    return jax.shard_map(
        body,
        mesh=mesh,
        in_specs=(
            P("rows", "panel", None, None, None, None),
            P("rows", "panel", None),
            P("rows", "panel", None, None),
            P(None, ("rows", "panel")),
            P(None, ("rows", "panel")),
            P(None, ("rows", "panel")),
            P(),
            P(),
        ),
        out_specs=(
            P(None, ("rows", "panel")),
            P(None, ("rows", "panel")),
            P(None, ("rows", "panel")),
            P(),
        ),
        check_vma=False,
    )
```

profile of v0, /device:TPU:0, one launch (start us, length us, event | category | flops | bytes accessed | tf_op | source)
XLA Modules:
  0.0 463.8 jit_solution(4816201861021060135)
XLA Ops:
  7.2 0.8 reshape_squeeze.2
  8.1 0.7 constant_dynamic-update-slice_fusion.2
  8.8 0.7 constant_dynamic-update-slice_fusion.1
  9.5 0.7 constant_dynamic-update-slice_fusion
  10.3 47.0 %all_gather.9 = bf16[192,2048]{1,0:T(8,128)(2,1)S(1)} all-gather(bf16[192,128]{1,0:T(8,128)(2,1)S(1)} %constant_dynamic-update-slice_fusion), channel_id=1, replica_groups=mesh['rows'=16,'panel'=2] {'rows'}, dimensions={1}, use_global_device_ids=true | all-gather | bytes 835584 | tf_op jit(solution)/shard_map/all_gather | solution.py:45
  57.6 0.8 gather_fusion
  58.4 0.2 broadcast_select_fusion.2
  58.7 0.6 fusion.9
  59.3 0.7 copy.75
  60.3 1.0 multiply_reduce_fusion.4
  61.5 2.1 reduce-scatter.4.cloned.1.call-done
  63.6 1.1 fusion.30
  64.9 41.0 %all-reduce.5 = (f32[64,64]{0,1:T(8,128)S(1)}, f32[64,64]{0,1:T(8,128)S(1)}) all-reduce(f32[64,64]{0,1:T(8,128)S(1)} %fusion.122, f32[64,64]{0,1:T(8,128)S(1)} %fusion.123), channel_id=1, replica_groups=mesh['rows'=16,'panel'=2] {'rows','panel'}, use_global_device_ids=true, to_apply=%region_0.1 | all-reduce | flops 8192 | bytes 65536 | tf_op jit(solution)/shard_map/psum | solution.py:55
  106.1 5.8 %cholesky.59 = f32[64,64]{1,0:T(8,128)S(1)} custom-call(f32[64,64]{1,0:T(8,128)S(1)} %fusion.95), custom_call_target="Cholesky" | custom-call | tf_op jit(solution)/shard_map/jit(cholesky)/cholesky | solution.py:63
  112.0 0.6 compare_reduce_fusion.2
  112.6 0.7 fusion.48
  113.3 4.9 %custom-call.18 = f32[1,64,64]{1,2,0:T(8,128)S(1)} custom-call(f32[1,64,64]{2,1,0:T(8,128)S(1)} %fusion.48), custom_call_target="InvertDiagBlocksLowerTriangular" | custom-call | tf_op jit(solution)/shard_map/jit(_solve_triangular)/triangular_solve | solution.py:11
  118.2 0.3 fusion.86
  118.4 0.2 fusion.120
  118.7 0.2 convolution_bitcast_fusion.2
  118.9 0.2 fusion.91
  119.1 0.3 multiply_reduce_fusion.5
  119.4 40.0 %all-reduce.4 = (f32[64]{0:T(128)S(1)}, f32[64]{0:T(128)S(1)}) all-reduce(f32[64]{0:T(128)S(1)} %get-tuple-element.32, f32[64]{0:T(128)S(1)} %get-tuple-element.34), channel_id=1, replica_groups=mesh['rows'=16,'panel'=2] {'rows','panel'}, use_global_device_ids=true, to_apply=%region_8.13 | all-reduce | flops 128 | bytes 1024 | tf_op jit(solution)/shard_map/psum | solution.py:55
  159.9 45.3 %all_gather.10 = bf16[192,2048]{1,0:T(8,128)(2,1)S(1)} all-gather(bf16[192,128]{1,0:T(8,128)(2,1)S(1)} %pad_maximum_fusion), channel_id=1, replica_groups=mesh['rows'=16,'panel'=2] {'rows'}, dimensions={1}, use_global_device_ids=true | all-gather | bytes 835584 | tf_op jit(solution)/shard_map/all_gather | solution.py:45
  205.3 0.9 gather_fusion.1
  206.2 0.2 broadcast_select_fusion.1
  206.4 0.6 fusion.12
  207.0 0.7 copy.74
  207.8 1.0 multiply_reduce_fusion.2
  209.0 2.3 reduce-scatter.6.cloned.1.call-done
  211.3 1.1 fusion.27
  212.7 41.0 %all-reduce.3 = (f32[64,64]{0,1:T(8,128)S(1)}, f32[64,64]{0,1:T(8,128)S(1)}) all-reduce(f32[64,64]{0,1:T(8,128)S(1)} %fusion.124, f32[64,64]{0,1:T(8,128)S(1)} %fusion.125), channel_id=1, replica_groups=mesh['rows'=16,'panel'=2] {'rows','panel'}, use_global_device_ids=true, to_apply=%region_9.14 | all-reduce | flops 8192 | bytes 65536 | tf_op jit(solution)/shard_map/psum | solution.py:55
  253.8 5.8 %cholesky.70 = f32[64,64]{1,0:T(8,128)S(1)} custom-call(f32[64,64]{1,0:T(8,128)S(1)} %fusion.84), custom_call_target="Cholesky" | custom-call | tf_op jit(solution)/shard_map/jit(cholesky)/cholesky | solution.py:63
  259.7 0.6 compare_reduce_fusion.1
  260.3 0.7 fusion.49
  261.0 4.9 %custom-call.22 = f32[1,64,64]{1,2,0:T(8,128)S(1)} custom-call(f32[1,64,64]{2,1,0:T(8,128)S(1)} %fusion.49), custom_call_target="InvertDiagBlocksLowerTriangular" | custom-call | tf_op jit(solution)/shard_map/jit(_solve_triangular)/triangular_solve | solution.py:11
  265.9 0.3 fusion.121
  266.2 0.2 fusion.75
  266.4 0.2 convolution_bitcast_fusion.1
  266.6 0.2 fusion.80
  266.9 0.3 multiply_reduce_fusion.3
  267.1 40.1 %all-reduce.2 = (f32[64]{0:T(128)S(1)}, f32[64]{0:T(128)S(1)}) all-reduce(f32[64]{0:T(128)S(1)} %get-tuple-element.36, f32[64]{0:T(128)S(1)} %get-tuple-element.40), channel_id=1, replica_groups=mesh['rows'=16,'panel'=2] {'rows','panel'}, use_global_device_ids=true, to_apply=%region_15.20 | all-reduce | flops 128 | bytes 1024 | tf_op jit(solution)/shard_map/psum | solution.py:55
  307.6 45.4 %all_gather.11 = bf16[192,2048]{1,0:T(8,128)(2,1)S(1)} all-gather(bf16[192,128]{1,0:T(8,128)(2,1)S(1)} %pad_maximum_fusion.1), channel_id=1, replica_groups=mesh['rows'=16,'panel'=2] {'rows'}, dimensions={1}, use_global_device_ids=true | all-gather | bytes 835584 | tf_op jit(solution)/shard_map/all_gather | solution.py:45
  353.3 0.9 gather_fusion.2
  354.1 0.2 broadcast_select_fusion
  354.3 0.6 fusion.15
  355.0 0.7 copy.73
  355.7 1.0 multiply_reduce_fusion
  356.9 2.4 reduce-scatter.8.cloned.1.call-done
  359.3 1.1 fusion.24
  360.6 41.0 %all-reduce.1 = (f32[64,64]{0,1:T(8,128)S(1)}, f32[64,64]{0,1:T(8,128)S(1)}) all-reduce(f32[64,64]{0,1:T(8,128)S(1)} %fusion.126, f32[64,64]{0,1:T(8,128)S(1)} %fusion.127), channel_id=1, replica_groups=mesh['rows'=16,'panel'=2] {'rows','panel'}, use_global_device_ids=true, to_apply=%region_16.21 | all-reduce | flops 8192 | bytes 65536 | tf_op jit(solution)/shard_map/psum | solution.py:55
  401.7 5.8 %cholesky.81 = f32[64,64]{1,0:T(8,128)S(1)} custom-call(f32[64,64]{1,0:T(8,128)S(1)} %fusion.73), custom_call_target="Cholesky" | custom-call | tf_op jit(solution)/shard_map/jit(cholesky)/cholesky | solution.py:63
  407.6 0.6 compare_reduce_fusion
  408.3 0.7 fusion.50
  408.9 4.9 %custom-call.26 = f32[1,64,64]{1,2,0:T(8,128)S(1)} custom-call(f32[1,64,64]{2,1,0:T(8,128)S(1)} %fusion.50), custom_call_target="InvertDiagBlocksLowerTriangular" | custom-call | tf_op jit(solution)/shard_map/jit(_solve_triangular)/triangular_solve | solution.py:11
  413.8 0.3 fusion.64
  414.1 0.2 fusion.66
  414.3 0.2 convolution_bitcast_fusion
  414.6 0.2 fusion.69
  414.8 0.3 multiply_reduce_fusion.1
  415.1 40.1 %all-reduce = (f32[64]{0:T(128)S(1)}, f32[64]{0:T(128)S(1)}) all-reduce(f32[64]{0:T(128)S(1)} %get-tuple-element.44, f32[64]{0:T(128)S(1)} %get-tuple-element.46), channel_id=1, replica_groups=mesh['rows'=16,'panel'=2] {'rows','panel'}, use_global_device_ids=true, to_apply=%region_20.25 | all-reduce | flops 128 | bytes 1024 | tf_op jit(solution)/shard_map/psum | solution.py:69
  455.2 0.7 copy.51
  455.9 0.7 divide_bitcast_fusion
  456.6 0.7 broadcast_divide_fusion
  (59 shorter events, 3.3 us)
Async XLA Ops:
  7.2 51.5 %copy-start = (bf16[1,1,2,16,128,128]{5,4,3,2,1,0:T(8,128)(2,1)S(1)}, bf16[1,1,2,16,128,128]{5,4,3,2,1,0:T(8,128)(2,1)}, u32[]{:S(2)}) copy-start(bf16[1,1,2,16,128,128]{5,4,3,2,1,0:T(8,128)(2,1)} %param.15) | copy-start | bytes 3145732
  7.2 50.3 %copy-start.6 = (s32[1,1,2]{2,1,0:T(1,128)S(1)}, s32[1,1,2]{2,1,0:T(1,128)}, u32[]{:S(2)}) copy-start(s32[1,1,2]{2,1,0:T(1,128)} %param.16) | copy-start | bytes 28
  7.2 56.4 %reduce-scatter.4.cloned.1.call-start = ((), (), s32[]{:S(2)}) async-start(), calls=%async_computation.3 | async-start | bytes 294912 | tf_op jit(solution)/shard_map/reduce_scatter | solution.py:47
  58.6 1.4 copy-start.1
  58.7 1.6 copy-start.4
  58.7 1.6 copy-start.5
  60.0 151.3 %reduce-scatter.6.cloned.1.call-start = ((), (), s32[]{:S(2)}) async-start(), calls=%async_computation.4 | async-start | bytes 294912 | tf_op jit(solution)/shard_map/reduce_scatter | solution.py:47
  206.4 4.9 %copy-start.2 = (f32[3,64,192]{2,1,0:T(8,128)S(1)}, f32[3,64,192]{2,1,0:T(8,128)}, u32[]{:S(2)}) copy-start(f32[3,64,192]{2,1,0:T(8,128)} %param.21) | copy-start | bytes 442372
  207.7 151.5 %reduce-scatter.8.cloned.1.call-start = ((), (), s32[]{:S(2)}) async-start(), calls=%async_computation.5 | async-start | bytes 294912 | tf_op jit(solution)/shard_map/reduce_scatter | solution.py:47
  414.3 43.0 %copy-start.3 = (f32[64,128]{1,0:T(8,128)}, f32[64,128]{1,0:T(8,128)S(1)}, u32[]{:S(2)}) copy-start(f32[64,128]{1,0:T(8,128)S(1)} %fusion.66) | copy-start | bytes 98308
Sparse Core Ops, SparseCore 0:
  60.1 3.4 reduce-scatter.3
  207.9 3.4 reduce-scatter.5
  355.8 3.4 reduce-scatter.7
where the time goes:
time: 465 us; the launch traced here: 464 us
  blocking collectives  381 us (82%)
  other arithmetic  38.8 us (8%)
  between operations  14.3 us (3%)
  matrix products  13.6 us (3%)
  local copies, waits for them, and re-layouts  9.17 us (2%)
  waiting for transfers between devices  6.79 us (1%)
    psum x5, blocking collectives, body(): lax.psum((jnp.dot(rotated, rotated.T, precision=highest), jnp.dot(rotated...  203 us
    all_gather x3, blocking collectives, body(): stacked_all = lax.all_gather(stacked, 'rows', axis=1, tiled=True)  138 us
    psum x1, blocking collectives, body(): lax.psum(jnp.sum(resid_raw * resid_raw, axis=1), ('rows', 'panel'))  40.1 us
    another operation x9, other arithmetic, body(): factor = jnp.linalg.cholesky(gram_sum / node_total)  19.6 us
    another operation x6, other arithmetic, lower_solve(): return jax.scipy.linalg.solve_triangular(factor, values, lower=True)  16.6 us
  transfers between devices with their start and end apart: 3, of which 3 were waited for; matrix products, arithmetic and copies ran while one was open for 1% of the time, Pallas kernels for 0%

commit v1 on v0

v1 whole, which is shorter than its diff:
```python
import functools

import jax
import jax.numpy as jnp
from jax import lax
from jax.experimental import pallas as pl
from jax.experimental.pallas import tpu as pltpu
from jax.sharding import PartitionSpec as P

epsilon = 1e-06
highest = lax.Precision.HIGHEST
f32 = jnp.float32
bf16 = jnp.bfloat16


def call(kernel, outs, args, smem=()):
    specs = [
        pl.BlockSpec(memory_space=pltpu.SMEM if i in smem else pltpu.VMEM) for i in range(len(args))
    ]
    return pl.pallas_call(
        kernel,
        out_shape=[jax.ShapeDtypeStruct(shape, kind) for shape, kind in outs],
        in_specs=specs,
        out_specs=[pl.BlockSpec(memory_space=pltpu.VMEM) for _ in outs],
        compiler_params=pltpu.CompilerParams(vmem_limit_bytes=40 << 20),
    )(*args)


def pieces(value):
    high = value.astype(bf16)
    rest = value - high.astype(f32)
    middle = rest.astype(bf16)
    low = (rest - middle.astype(f32)).astype(bf16)
    return jnp.concatenate([high, middle, low], axis=0)


def times_stack(weights, stack):
    rows = weights.shape[0]
    parts = jnp.dot(pieces(weights), stack, preferred_element_type=f32)
    return parts[:rows] + parts[rows : 2 * rows] + parts[2 * rows :]


def dot_nt(left, right):
    return lax.dot_general(
        left, right, (((1,), (1,)), ((), ())), precision=highest, preferred_element_type=f32
    )


def dot_tn(left, right):
    return lax.dot_general(
        left, right, (((0,), (0,)), ((), ())), precision=highest, preferred_element_type=f32
    )


def dot_nn(left, right):
    return jnp.dot(left, right, precision=highest, preferred_element_type=f32)


def product(slots_ref, place_ref, tiles_ref, mix_ref, stack_ref, mine_refs):
    blocks, slots, edge = tiles_ref.shape[:3]
    vec_rows = stack_ref.shape[0]
    sums = []
    for b in range(blocks):
        total = jnp.zeros((vec_rows, edge), f32)
        for j in range(0, slots, 2):
            chosen, tiles = [], []
            for s in (j, j + 1):
                start = pl.multiple_of(slots_ref[b, s] * edge, edge)
                chosen.append(stack_ref[:, pl.ds(start, edge)])
                tiles.append(tiles_ref[b, s])
            total = total + lax.dot_general(
                jnp.concatenate(chosen, axis=1),
                jnp.concatenate(tiles, axis=1),
                (((1,), (1,)), ((), ())),
                preferred_element_type=f32,
            )
        sums.append(total)
    mixed = dot_nn(mix_ref[...], jnp.concatenate(sums, axis=1))
    if len(mine_refs) == 2:
        first = place_ref[0] == 0
        low, high = mixed[:, :edge], mixed[:, edge:]
        mine_refs[0][...] = jnp.where(first, low, high)
        mine_refs[1][...] = jnp.where(first, high, low)
    else:
        for b in range(blocks):
            mine_refs[0][b] = mixed[:, b * edge : (b + 1) * edge]


def first_kernel(parts, slots_ref, place_ref, tiles_ref, mix_ref, *refs):
    part_refs, stack_ref, mine_refs = refs[:parts], refs[parts], refs[parts + 1 :]
    edge = tiles_ref.shape[2]
    vec_rows = stack_ref.shape[0]
    at = 0
    for ref in part_refs:
        for i in range(ref.shape[0]):
            stack_ref[:, at : at + edge] = ref[i]
            at += edge
    stack_ref[:, at : at + edge] = jnp.zeros((vec_rows, edge), bf16)
    product(slots_ref, place_ref, tiles_ref, mix_ref, stack_ref, mine_refs)


def next_kernel(nodes, many, slots_ref, place_ref, tiles_ref, mix_ref, basis_ref, raw_ref, sqs, dirs_ref, stack_ref, *mine_refs):
    edge = tiles_ref.shape[2]
    vecs = basis_ref.shape[0]
    wide = basis_ref.shape[1]
    square = sum(ref[...] for ref in sqs)[:, :1] / nodes
    scale = lax.rsqrt(square + epsilon)
    stack_ref[:vecs, :wide] = basis_ref[...].astype(bf16)
    stack_ref[vecs : 2 * vecs, :wide] = (raw_ref[...] * scale).astype(bf16)
    stack_ref[2 * vecs :, :wide] = dirs_ref[...]
    stack_ref[:, wide : wide + edge] = jnp.zeros((3 * vecs, edge), bf16)
    product(slots_ref, place_ref, tiles_ref, mix_ref, stack_ref, mine_refs)


def gram_kernel(stack_ref, mix_ref, search_ref, pack_ref, search_out):
    wide = search_out.shape[1]
    vecs = mix_ref.shape[0]
    rotated = times_stack(mix_ref[...], stack_ref[:, :wide])
    search = times_stack(search_ref[...], stack_ref[vecs:, :wide])
    search_out[...] = search
    square = jnp.sum(search * search, axis=1, keepdims=True)
    pack_ref[...] = jnp.concatenate(
        [dot_nt(rotated, rotated), jnp.broadcast_to(square, (vecs, vecs))], axis=1
    )


def factor_kernel(nodes, packs, stack_ref, mix_ref, search_ref, inverse_ref, basis_ref, dirs_ref, own_basis, own_dirs):
    vecs = mix_ref.shape[0]
    wide = search_ref.shape[1]
    edge = own_basis.shape[1]
    total = sum(ref[...] for ref in packs) / nodes
    scale = lax.rsqrt(total[:, vecs : vecs + 1] + epsilon)
    dirs = search_ref[...] * scale
    dirs_ref[...] = dirs.astype(bf16)
    own_dirs[...] = dirs[:, :edge]
    row_ids = lax.broadcasted_iota(jnp.int32, (vecs, 2 * vecs), 0)
    lane_ids = lax.broadcasted_iota(jnp.int32, (vecs, 2 * vecs), 1)
    left = lane_ids < vecs
    work = jnp.where(left, total, jnp.where(lane_ids == row_ids + vecs, 1.0, 0.0))
    for j in range(vecs - 1):
        pivot_row = work[j : j + 1, :]
        column = work[:, j : j + 1]
        ratio = jnp.where(row_ids[:, :1] > j, column / work[j : j + 1, j : j + 1], 0.0)
        work = work - ratio * pivot_row
    pivots = jnp.sum(jnp.where(lane_ids == row_ids, work, 0.0), axis=1, keepdims=True)
    inverse = (work * lax.rsqrt(pivots))[:, vecs:]
    inverse_ref[...] = inverse
    basis = times_stack(dot_nn(inverse, mix_ref[...]), stack_ref[:, :wide])
    basis_ref[...] = basis
    own_basis[...] = basis[:, :edge]


def cross_kernel(parts, *refs):
    part_refs, basis_ref, wide_ref, cross_ref = refs[:parts], refs[parts], refs[parts + 1], refs[parts + 2]
    vecs = basis_ref.shape[0]
    edge = part_refs[0].shape[1]
    at = 0
    for ref in part_refs:
        for i in range(ref.shape[0] // vecs):
            wide_ref[:, at : at + edge] = ref[i * vecs : (i + 1) * vecs, :]
            at += edge
    cross_ref[...] = dot_nt(basis_ref[...], wide_ref[...])


def residual_kernel(nodes, crosses, inverse_ref, basis_ref, wide_ref, raw_ref, square_ref, rayleigh_ref, own_raw):
    vecs = basis_ref.shape[0]
    inverse = inverse_ref[...]
    edge = own_raw.shape[1]
    q = dot_nt(sum(ref[...] for ref in crosses) / nodes, inverse)
    raw = dot_tn(q, basis_ref[...]) - dot_nn(inverse, wide_ref[...])
    raw_ref[...] = raw
    own_raw[...] = raw[:, :edge]
    square_ref[...] = jnp.broadcast_to(jnp.sum(raw * raw, axis=1, keepdims=True), square_ref.shape)
    row_ids = lax.broadcasted_iota(jnp.int32, (vecs, vecs), 0)
    lane_ids = lax.broadcasted_iota(jnp.int32, (vecs, vecs), 1)
    rayleigh_ref[...] = jnp.where(row_ids == lane_ids, 1.0, 0.0) - q


def swap(value, by, axis):
    size = lax.axis_size(axis)
    return lax.ppermute(value, axis, [(i, i ^ by) for i in range(size)])


def panel_terms(value):
    if lax.axis_size("panel") == 2:
        return [value, swap(value, 1, "panel")]
    return [lax.psum(value, "panel")]


def gather(value, near):
    far = lax.axis_size("rows") // near
    held = jnp.concatenate([value] + [swap(value, near * i, "rows") for i in range(1, far)], axis=0)
    return [held] + [swap(held, i, "rows") for i in range(1, near)]


def body(
    adj_tiles,
    row_counts,
    tile_cols,
    start_basis,
    start_resid,
    start_search,
    ritz_basis,
    ritz_search,
):
    tile_set = adj_tiles[0, 0]
    counts = row_counts[0, 0]
    columns = tile_cols[0, 0]
    blocks, slots, edge = tile_set.shape[:3]
    vecs = start_basis.shape[0]
    rows, panels = lax.axis_size("rows"), lax.axis_size("panel")
    nodes = start_basis.shape[1] * rows * panels
    wide = rows * edge
    near = 4
    away = columns ^ lax.axis_index("rows")
    position = (away % near) * (rows // near) + away // near
    in_use = jnp.arange(slots, dtype=jnp.int32)[None, :] < counts[:, None]
    slot_ids = jnp.where(in_use, position, rows).astype(jnp.int32)
    place = lax.axis_index("panel").astype(jnp.int32).reshape(1)

    if panels == 2:
        mine_outs = [((vecs, edge), f32)] * 2
    else:
        mine_outs = [((blocks, vecs, edge), f32)]
    stack_out = ((3 * vecs, wide + edge), bf16)

    start = jnp.concatenate([start_basis, start_resid, start_search], axis=0)[None]
    parts = gather(start, near)
    state = None
    sweeps = ritz_basis.shape[0]
    for sweep in range(sweeps):
        mixing = ritz_basis[sweep]
        if state is None:
            stack, *mine = call(
                functools.partial(first_kernel, near),
                [stack_out] + mine_outs,
                [slot_ids, place, tile_set, mixing] + parts,
                smem=(0, 1),
            )
        else:
            basis, raw, squares, dirs = state
            count = len(squares)

            def kernel(s, p, t, m, b, r, *refs):
                next_kernel(nodes, count, s, p, t, m, b, r, refs[:count], *refs[count:])

            stack, *mine = call(
                kernel,
                [stack_out] + mine_outs,
                [slot_ids, place, tile_set, mixing, basis, raw] + squares + [dirs],
                smem=(0, 1),
            )
        if panels == 2:
            rotated_adj = mine[0] + swap(mine[1], 1, "panel")
        else:
            rotated_adj = lax.psum_scatter(mine[0], "panel", scatter_dimension=0, tiled=True)[0]
        pack, search = call(
            gram_kernel,
            [((vecs, 2 * vecs), f32), ((vecs, wide), f32)],
            [stack, mixing, ritz_search[sweep]],
        )
        packs = panel_terms(pack)
        pack_count = len(packs)

        def kernel_factor(*refs):
            factor_kernel(nodes, refs[:pack_count], *refs[pack_count:])

        inverse, basis, dirs, own_basis, own_dirs = call(
            kernel_factor,
            [
                ((vecs, vecs), f32),
                ((vecs, wide), f32),
                ((vecs, wide), bf16),
                ((vecs, edge), f32),
                ((vecs, edge), f32),
            ],
            packs + [stack, mixing, search],
        )
        adj_parts = gather(rotated_adj, near)
        wide_adj, cross = call(
            functools.partial(cross_kernel, near),
            [((vecs, wide), f32), ((vecs, vecs), f32)],
            adj_parts + [basis],
        )
        crosses = panel_terms(cross)
        cross_count = len(crosses)

        def kernel_residual(*refs):
            residual_kernel(nodes, refs[:cross_count], *refs[cross_count:])

        raw, square, rayleigh, own_raw = call(
            kernel_residual,
            [((vecs, wide), f32), ((vecs, edge), f32), ((vecs, vecs), f32), ((vecs, edge), f32)],
            crosses + [inverse, basis, wide_adj],
        )
        squares = panel_terms(square)
        state = (basis, raw, squares, dirs)
    resid = own_raw / jnp.sqrt(sum(squares) / nodes + epsilon)
    return (own_basis, resid, own_dirs, rayleigh)


def solution(mesh):
    return jax.shard_map(
        body,
        mesh=mesh,
        in_specs=(
            P("rows", "panel", None, None, None, None),
            P("rows", "panel", None),
            P("rows", "panel", None, None),
            P(None, ("rows", "panel")),
            P(None, ("rows", "panel")),
            P(None, ("rows", "panel")),
            P(),
            P(),
        ),
        out_specs=(
            P(None, ("rows", "panel")),
            P(None, ("rows", "panel")),
            P(None, ("rows", "panel")),
            P(),
        ),
        check_vma=False,
    )
```

time: 465 us -> 106 us (0.23)
  blocking collectives: 381 us -> 0 us
  other arithmetic: 38.8 us -> 1.53 us
  starting transfers between devices: 0.12 us -> 35 us
  Pallas kernels: 0 us -> 34.2 us
  waiting for transfers between devices: 6.79 us -> 31.9 us
  matrix products: 13.6 us -> 0 us
  between operations: 14.3 us -> 0.84 us
  local copies, waits for them, and re-layouts: 9.17 us -> 2.17 us
    psum x6 -> x0, blocking collectives: 243 us -> none  [the longest x5 203 us: body(): lax.psum((jnp.dot(rotated, rotated.T, precision=highest), jnp.dot(rotated...]
    all_gather x3 -> x0, blocking collectives: 138 us -> none  [body(): stacked_all = lax.all_gather(stacked, 'rows', axis=1, tiled=True)]
    another operation x15 -> x0, other arithmetic: 36.2 us -> none  [the longest x9 19.6 us: body(): factor = jnp.linalg.cholesky(gram_sum / node_total)]
    ppermute x0 -> x36, starting transfers between devices: none -> 35 us  [swap(): return lax.ppermute(value, axis, [(i, i ^ by) for i in range(size)])]
    pallas_call x0 -> x15, Pallas kernels: none -> 34.2 us  [call(): pl.pallas_call(kernel, out_shape=[jax.ShapeDtypeStruct(shape, kind) for s...]
    ppermute x0 -> x36, waiting for transfers between devices: none -> 31.9 us  [swap(): return lax.ppermute(value, axis, [(i, i ^ by) for i in range(size)])]
    dot_general x21 -> x0, matrix products: 10.8 us -> none  [the longest x3 3.36 us: body(): rotated_image = jnp.dot(mixing, image_f32, precision=highest)]
    reduce_scatter x3 -> x0, waiting for transfers between devices: 6.74 us -> none  [body(): lax.psum_scatter(partial_value, 'panel', scatter_dimension=1, tiled=True)]
  transfers between devices with their start and end apart: 3 -> 36, of which waited for: 3 -> 24; matrix products, arithmetic and copies ran while one was open for 1% -> 1% of each run, Pallas kernels for 0% -> 22%
where the time goes in v1:
time: 106 us
  starting transfers between devices  35 us (33%)
  Pallas kernels  34.2 us (32%)
  waiting for transfers between devices  31.9 us (30%)
  local copies, waits for them, and re-layouts  2.17 us (2%)
  other arithmetic  1.53 us (1%)
    ppermute x36, starting transfers between devices, swap(): return lax.ppermute(value, axis, [(i, i ^ by) for i in range(size)])  35 us
    pallas_call x15, Pallas kernels, call(): pl.pallas_call(kernel, out_shape=[jax.ShapeDtypeStruct(shape, kind) for s...  34.2 us
    ppermute x36, waiting for transfers between devices, swap(): return lax.ppermute(value, axis, [(i, i ^ by) for i in range(size)])  31.9 us
  transfers between devices with their start and end apart: 36, of which 24 were waited for; matrix products, arithmetic and copies ran while one was open for 1% of the time, Pallas kernels for 22%

profile of v1, /device:TPU:0, one launch (start us, length us, event | category | flops | bytes accessed | tf_op | source)
XLA Modules:
  0.0 105.7 jit_solution(5808798360584710767)
XLA Ops:
  0.6 0.8 maximum_bitcast_fusion
  1.4 5.0 %collective-permute-start.2 = (bf16[1,192,128]{2,1,0:T(8,128)(2,1)S(1)}, bf16[1,192,128]{2,1,0:T(8,128)(2,1)S(1)}, u32[]{:S(2)}, u32[]{:S(2)}) collective-permute-start(bf16[1,192,128]{2,1,0:T(8,128)(2,1)S(1)} %maximum_bitcast_fusion), channel_id=1, source_target_pairs={{0,24},{2,26},{4,28},{6,30},{8,16},{10,18},{12,20},{14,22},{16,8},... | collective-permute-start | bytes 147464 | tf_op jit(solution)/shard_map/ppermute | solution.py:181
  6.4 0.6 collective-permute-start
  7.0 0.9 slice_bitcast_fusion
  8.0 0.7 collective-permute-done.2
  8.7 2.8 %collective-permute-done.1 = bf16[1,192,128]{2,1,0:T(8,128)(2,1)S(1)} collective-permute-done((bf16[1,192,128]{2,1,0:T(8,128)(2,1)S(1)}, bf16[1,192,128]{2,1,0:T(8,128)(2,1)S(1)}, u32[]{:S(2)}, u32[]{:S(2)}) %collective-permute-start.1) | collective-permute-done | bytes 49184 | tf_op jit(solution)/shard_map/ppermute | solution.py:181
  11.5 1.6 %collective-permute-start.3 = (bf16[4,192,128]{2,1,0:T(8,128)(2,1)S(1)}, bf16[4,192,128]{2,1,0:T(8,128)(2,1)S(1)}, u32[]{:S(2)}, u32[]{:S(2)}) collective-permute-start(bf16[4,192,128]{2,1,0:T(8,128)(2,1)S(1)} %pad_maximum_fusion.refs_0_), channel_id=1, source_target_pairs={{0,2},{2,0},{4,6},{6,4},{8,10},{10,8},{12,14},{14,12},{16,18},{18,... | collective-permute-start | bytes 589832 | tf_op jit(solution)/shard_map/ppermute | solution.py:181
  13.0 1.5 %collective-permute-start.4 = (bf16[4,192,128]{2,1,0:T(8,128)(2,1)S(1)}, bf16[4,192,128]{2,1,0:T(8,128)(2,1)S(1)}, u32[]{:S(2)}, u32[]{:S(2)}) collective-permute-start(bf16[4,192,128]{2,1,0:T(8,128)(2,1)S(1)} %pad_maximum_fusion.refs_0_), channel_id=1, source_target_pairs={{0,4},{2,6},{4,0},{6,2},{8,12},{10,14},{12,8},{14,10},{16,20},{18,... | collective-permute-start | bytes 589832 | tf_op jit(solution)/shard_map/ppermute | solution.py:181
  14.6 0.5 collective-permute-start.5
  15.1 4.0 %collective-permute-done.3.refs_1_ = bf16[4,192,128]{2,1,0:T(8,128)(2,1)S(1)} collective-permute-done((bf16[4,192,128]{2,1,0:T(8,128)(2,1)S(1)}, bf16[4,192,128]{2,1,0:T(8,128)(2,1)S(1)}, u32[]{:S(2)}, u32[]{:S(2)}) %collective-permute-start.3) | collective-permute-done | bytes 196640 | tf_op jit(solution)/shard_map/ppermute | solution.py:181
  19.1 3.7 %collective-permute-done.4.refs_2_ = bf16[4,192,128]{2,1,0:T(8,128)(2,1)S(1)} collective-permute-done((bf16[4,192,128]{2,1,0:T(8,128)(2,1)S(1)}, bf16[4,192,128]{2,1,0:T(8,128)(2,1)S(1)}, u32[]{:S(2)}, u32[]{:S(2)}) %collective-permute-start.4) | collective-permute-done | bytes 196640 | tf_op jit(solution)/shard_map/ppermute | solution.py:181
  22.9 1.2 %copy-done = bf16[1,1,2,16,128,128]{5,4,3,2,1,0:T(8,128)(2,1)S(1)} copy-done((bf16[1,1,2,16,128,128]{5,4,3,2,1,0:T(8,128)(2,1)S(1)}, bf16[1,1,2,16,128,128]{5,4,3,2,1,0:T(8,128)(2,1)}, u32[]{:S(2)}) %copy-start) | copy-done | bytes 1048600
  24.1 1.5 %shard_map.111 = (bf16[192,2176]{1,0:T(8,128)(2,1)S(1)}, f32[64,128]{1,0:T(8,128)S(1)}, f32[64,128]{1,0:T(8,128)S(1)}) custom-call(s32[2,16]{1,0:T(2,128)S(1)} %compare_select_fusion.slots_ref.s, s32[1]{0:T(128)} %bitcast.2.place_ref.p, bf16[2,16,128,128]{3,2,1,0:T(8,128)(2,1)S(1)} %bitcast.25, f32[64,192]{1,0:T(8,128)S(1)} %get-tuple-element.80.mix_ref.refs_3_, ...), custom_call_target="tpu_custom_call" | custom-call | tf_op jit(solution)/shard_map/pallas_call | solution.py:20
  25.7 1.2 %collective-permute-done.7 = f32[64,128]{1,0:T(8,128)S(1)} collective-permute-done((f32[64,128]{1,0:T(8,128)S(1)}, f32[64,128]{1,0:T(8,128)S(1)}, u32[]{:S(2)}, u32[]{:S(2)}) %collective-permute-start.7) | collective-permute-done | bytes 32800 | tf_op jit(solution)/shard_map/ppermute | solution.py:181
  26.9 1.8 %collective-permute-start.10 = (f32[64,128]{1,0:T(8,128)S(1)}, f32[64,128]{1,0:T(8,128)S(1)}, u32[]{:S(2)}, u32[]{:S(2)}) collective-permute-start(f32[64,128]{1,0:T(8,128)S(1)} %add.30), channel_id=1, source_target_pairs={{0,24},{2,26},{4,28},{6,30},{8,16},{10,18},{12,20},{14,22},{16,8},... | collective-permute-start | bytes 98312 | tf_op jit(solution)/shard_map/ppermute | solution.py:181
  28.7 0.4 collective-permute-start.9
  29.1 2.3 %collective-permute-start.8 = (f32[64,128]{1,0:T(8,128)S(1)}, f32[64,128]{1,0:T(8,128)S(1)}, u32[]{:S(2)}, u32[]{:S(2)}) collective-permute-start(f32[64,128]{1,0:T(8,128)S(1)} %add.30), channel_id=1, source_target_pairs={{0,8},{2,10},{4,12},{6,14},{8,0},{10,2},{12,4},{14,6},{16,24},{18,... | collective-permute-start | bytes 98312 | tf_op jit(solution)/shard_map/ppermute | solution.py:181
  31.3 1.3 %collective-permute-done.10 = f32[64,128]{1,0:T(8,128)S(1)} collective-permute-done((f32[64,128]{1,0:T(8,128)S(1)}, f32[64,128]{1,0:T(8,128)S(1)}, u32[]{:S(2)}, u32[]{:S(2)}) %collective-permute-start.10) | collective-permute-done | bytes 32800 | tf_op jit(solution)/shard_map/ppermute | solution.py:181
  32.7 0.9 collective-permute-done.9
  33.6 1.3 %collective-permute-start.11 = (f32[256,128]{1,0:T(8,128)S(1)}, f32[256,128]{1,0:T(8,128)S(1)}, u32[]{:S(2)}, u32[]{:S(2)}) collective-permute-start(f32[256,128]{1,0:T(8,128)S(1)} %pad_maximum_fusion.1.refs_0_), channel_id=1, source_target_pairs={{0,2},{2,0},{4,6},{6,4},{8,10},{10,8},{12,14},{14,12},{16,18},{18,... | collective-permute-start | bytes 393224 | tf_op jit(solution)/shard_map/ppermute | solution.py:181
  35.0 0.8 collective-permute-start.12
  35.8 1.4 %collective-permute-start.13 = (f32[256,128]{1,0:T(8,128)S(1)}, f32[256,128]{1,0:T(8,128)S(1)}, u32[]{:S(2)}, u32[]{:S(2)}) collective-permute-start(f32[256,128]{1,0:T(8,128)S(1)} %pad_maximum_fusion.1.refs_0_), channel_id=1, source_target_pairs={{0,6},{2,4},{4,2},{6,0},{8,14},{10,12},{12,10},{14,8},{16,22},{18,... | collective-permute-start | bytes 393224 | tf_op jit(solution)/shard_map/ppermute | solution.py:181
  37.2 1.1 %shard_map.112 = (f32[64,128]{1,0:T(8,128)S(1)}, f32[64,2048]{1,0:T(8,128)S(1)}) custom-call(bf16[192,2176]{1,0:T(8,128)(2,1)S(1)} %get-tuple-element.42.stack_ref.refs_2_, f32[64,192]{1,0:T(8,128)S(1)} %get-tuple-element.80.mix_ref.refs_3_, f32[64,128]{1,0:T(8,128)S(1)} %get-tuple-element.84.search_ref), custom_call_target="tpu_custom_call" | custom-call | tf_op jit(solution)/shard_map/pallas_call | solution.py:20
  38.4 1.2 %collective-permute-done.6.refs_1_ = f32[64,128]{1,0:T(8,128)S(1)} collective-permute-done((f32[64,128]{1,0:T(8,128)S(1)}, f32[64,128]{1,0:T(8,128)S(1)}, u32[]{:S(2)}, u32[]{:S(2)}) %collective-permute-start.6) | collective-permute-done | bytes 32800 | tf_op jit(solution)/shard_map/ppermute | solution.py:181
  39.6 6.5 %shard_map.113 = (f32[64,64]{1,0:T(8,128)S(1)}, f32[64,2048]{1,0:T(8,128)S(1)}, bf16[64,2048]{1,0:T(8,128)(2,1)S(1)}, f32[64,128]{1,0:T(8,128)}, f32[64,128]{1,0:T(8,128)}) custom-call(f32[64,128]{1,0:T(8,128)S(1)} %get-tuple-element.43.refs_0_, f32[64,128]{1,0:T(8,128)S(1)} %collective-permute-done.6.refs_1_, ...), custom_call_target="tpu_custom_call" | custom-call | tf_op jit(solution)/shard_map/pallas_call | solution.py:20
  46.1 0.6 shard_map.114
  46.9 1.0 collective-permute-done.14.refs_1_
  47.9 1.5 %shard_map.115 = (f32[64,2048]{1,0:T(8,128)S(1)}, f32[64,128]{1,0:T(8,128)S(1)}, f32[64,64]{1,0:T(8,128)}, f32[64,128]{1,0:T(8,128)}) custom-call(f32[64,64]{1,0:T(8,128)S(1)} %get-tuple-element.48.refs_0_, f32[64,64]{1,0:T(8,128)S(1)} %collective-permute-done.14.refs_1_, f32[64,64]{1,0:T(8,128)S(1)} %get-tuple-element.49.refs_2_, ...), custom_call_target="tpu_custom_call" | custom-call | tf_op jit(solution)/shard_map/pallas_call | solution.py:20
  49.6 1.0 collective-permute-done.15.refs_1_
  50.7 1.5 %shard_map.116 = (bf16[192,2176]{1,0:T(8,128)(2,1)S(1)}, f32[64,128]{1,0:T(8,128)S(1)}, f32[64,128]{1,0:T(8,128)S(1)}) custom-call(s32[2,16]{1,0:T(2,128)S(1)} %compare_select_fusion.slots_ref.s, s32[1]{0:T(128)} %bitcast.2.place_ref.p, bf16[2,16,128,128]{3,2,1,0:T(8,128)(2,1)S(1)} %bitcast.26, f32[64,192]{1,0:T(8,128)S(1)} %get-tuple-element.82.m.mix_ref.refs_3_, ...), custom_call_target="tpu_custom_call" | custom-call | tf_op jit(solution)/shard_map/pallas_call | solution.py:20
  52.4 1.0 collective-permute-done.17
  53.5 2.2 %collective-permute-start.20 = (f32[64,128]{1,0:T(8,128)S(1)}, f32[64,128]{1,0:T(8,128)S(1)}, u32[]{:S(2)}, u32[]{:S(2)}) collective-permute-start(f32[64,128]{1,0:T(8,128)S(1)} %add.31), channel_id=1, source_target_pairs={{0,24},{2,26},{4,28},{6,30},{8,16},{10,18},{12,20},{14,22},{16,8},... | collective-permute-start | bytes 98312 | tf_op jit(solution)/shard_map/ppermute | solution.py:181
  55.7 0.9 collective-permute-start.19
  56.6 1.3 %collective-permute-start.18 = (f32[64,128]{1,0:T(8,128)S(1)}, f32[64,128]{1,0:T(8,128)S(1)}, u32[]{:S(2)}, u32[]{:S(2)}) collective-permute-start(f32[64,128]{1,0:T(8,128)S(1)} %add.31), channel_id=1, source_target_pairs={{0,8},{2,10},{4,12},{6,14},{8,0},{10,2},{12,4},{14,6},{16,24},{18,... | collective-permute-start | bytes 98312 | tf_op jit(solution)/shard_map/ppermute | solution.py:181
  57.9 1.7 %collective-permute-done.20 = f32[64,128]{1,0:T(8,128)S(1)} collective-permute-done((f32[64,128]{1,0:T(8,128)S(1)}, f32[64,128]{1,0:T(8,128)S(1)}, u32[]{:S(2)}, u32[]{:S(2)}) %collective-permute-start.20) | collective-permute-done | bytes 32800 | tf_op jit(solution)/shard_map/ppermute | solution.py:181
  59.5 1.2 %collective-permute-done.19 = f32[64,128]{1,0:T(8,128)S(1)} collective-permute-done((f32[64,128]{1,0:T(8,128)S(1)}, f32[64,128]{1,0:T(8,128)S(1)}, u32[]{:S(2)}, u32[]{:S(2)}) %collective-permute-start.19) | collective-permute-done | bytes 32800 | tf_op jit(solution)/shard_map/ppermute | solution.py:181
  60.9 1.3 %collective-permute-start.21 = (f32[256,128]{1,0:T(8,128)S(1)}, f32[256,128]{1,0:T(8,128)S(1)}, u32[]{:S(2)}, u32[]{:S(2)}) collective-permute-start(f32[256,128]{1,0:T(8,128)S(1)} %pad_maximum_fusion.2.refs_0_), channel_id=1, source_target_pairs={{0,2},{2,0},{4,6},{6,4},{8,10},{10,8},{12,14},{14,12},{16,18},{18,... | collective-permute-start | bytes 393224 | tf_op jit(solution)/shard_map/ppermute | solution.py:181
  62.1 0.8 collective-permute-start.22
  63.0 1.5 %collective-permute-start.23 = (f32[256,128]{1,0:T(8,128)S(1)}, f32[256,128]{1,0:T(8,128)S(1)}, u32[]{:S(2)}, u32[]{:S(2)}) collective-permute-start(f32[256,128]{1,0:T(8,128)S(1)} %pad_maximum_fusion.2.refs_0_), channel_id=1, source_target_pairs={{0,6},{2,4},{4,2},{6,0},{8,14},{10,12},{12,10},{14,8},{16,22},{18,... | collective-permute-start | bytes 393224 | tf_op jit(solution)/shard_map/ppermute | solution.py:181
  64.4 1.1 %shard_map.117 = (f32[64,128]{1,0:T(8,128)S(1)}, f32[64,2048]{1,0:T(8,128)S(1)}) custom-call(bf16[192,2176]{1,0:T(8,128)(2,1)S(1)} %get-tuple-element.54.stack_ref.refs_2_, f32[64,192]{1,0:T(8,128)S(1)} %get-tuple-element.82.m.mix_ref.refs_3_, f32[64,128]{1,0:T(8,128)S(1)} %get-tuple-element.85.search_ref), custom_call_target="tpu_custom_call" | custom-call | tf_op jit(solution)/shard_map/pallas_call | solution.py:20
  65.6 1.2 %collective-permute-done.16.refs_1_ = f32[64,128]{1,0:T(8,128)S(1)} collective-permute-done((f32[64,128]{1,0:T(8,128)S(1)}, f32[64,128]{1,0:T(8,128)S(1)}, u32[]{:S(2)}, u32[]{:S(2)}) %collective-permute-start.16) | collective-permute-done | bytes 32800 | tf_op jit(solution)/shard_map/ppermute | solution.py:181
  66.8 6.5 %shard_map.118 = (f32[64,64]{1,0:T(8,128)S(1)}, f32[64,2048]{1,0:T(8,128)S(1)}, bf16[64,2048]{1,0:T(8,128)(2,1)S(1)}, f32[64,128]{1,0:T(8,128)}, f32[64,128]{1,0:T(8,128)}) custom-call(f32[64,128]{1,0:T(8,128)S(1)} %get-tuple-element.55.refs_0_, f32[64,128]{1,0:T(8,128)S(1)} %collective-permute-done.16.refs_1_, ...), custom_call_target="tpu_custom_call" | custom-call | tf_op jit(solution)/shard_map/pallas_call | solution.py:20
  73.3 0.6 shard_map.119
  74.1 1.0 collective-permute-done.24.refs_1_
  75.2 1.5 %shard_map.120 = (f32[64,2048]{1,0:T(8,128)S(1)}, f32[64,128]{1,0:T(8,128)S(1)}, f32[64,64]{1,0:T(8,128)}, f32[64,128]{1,0:T(8,128)}) custom-call(f32[64,64]{1,0:T(8,128)S(1)} %get-tuple-element.60.refs_0_, f32[64,64]{1,0:T(8,128)S(1)} %collective-permute-done.24.refs_1_, f32[64,64]{1,0:T(8,128)S(1)} %get-tuple-element.61.refs_2_, ...), custom_call_target="tpu_custom_call" | custom-call | tf_op jit(solution)/shard_map/pallas_call | solution.py:20
  76.8 1.0 collective-permute-done.25.refs_1_
  77.9 1.5 %shard_map.121 = (bf16[192,2176]{1,0:T(8,128)(2,1)S(1)}, f32[64,128]{1,0:T(8,128)S(1)}, f32[64,128]{1,0:T(8,128)S(1)}) custom-call(s32[2,16]{1,0:T(2,128)S(1)} %compare_select_fusion.slots_ref.s, s32[1]{0:T(128)} %bitcast.2.place_ref.p, bf16[2,16,128,128]{3,2,1,0:T(8,128)(2,1)S(1)} %bitcast.27, f32[64,192]{1,0:T(8,128)S(1)} %get-tuple-element.81.m.mix_ref.refs_3_, ...), custom_call_target="tpu_custom_call" | custom-call | tf_op jit(solution)/shard_map/pallas_call | solution.py:20
  79.6 1.0 collective-permute-done.27
  80.7 1.6 %collective-permute-start.30 = (f32[64,128]{1,0:T(8,128)S(1)}, f32[64,128]{1,0:T(8,128)S(1)}, u32[]{:S(2)}, u32[]{:S(2)}) collective-permute-start(f32[64,128]{1,0:T(8,128)S(1)} %add.32), channel_id=1, source_target_pairs={{0,24},{2,26},{4,28},{6,30},{8,16},{10,18},{12,20},{14,22},{16,8},... | collective-permute-start | bytes 98312 | tf_op jit(solution)/shard_map/ppermute | solution.py:181
  82.3 0.8 collective-permute-start.29
  83.1 2.0 %collective-permute-start.28 = (f32[64,128]{1,0:T(8,128)S(1)}, f32[64,128]{1,0:T(8,128)S(1)}, u32[]{:S(2)}, u32[]{:S(2)}) collective-permute-start(f32[64,128]{1,0:T(8,128)S(1)} %add.32), channel_id=1, source_target_pairs={{0,8},{2,10},{4,12},{6,14},{8,0},{10,2},{12,4},{14,6},{16,24},{18,... | collective-permute-start | bytes 98312 | tf_op jit(solution)/shard_map/ppermute | solution.py:181
  85.1 1.5 %collective-permute-done.30 = f32[64,128]{1,0:T(8,128)S(1)} collective-permute-done((f32[64,128]{1,0:T(8,128)S(1)}, f32[64,128]{1,0:T(8,128)S(1)}, u32[]{:S(2)}, u32[]{:S(2)}) %collective-permute-start.30) | collective-permute-done | bytes 32800 | tf_op jit(solution)/shard_map/ppermute | solution.py:181
  86.6 0.8 collective-permute-done.29
  87.4 1.4 %collective-permute-start.31 = (f32[256,128]{1,0:T(8,128)S(1)}, f32[256,128]{1,0:T(8,128)S(1)}, u32[]{:S(2)}, u32[]{:S(2)}) collective-permute-start(f32[256,128]{1,0:T(8,128)S(1)} %pad_maximum_fusion.3.refs_0_), channel_id=1, source_target_pairs={{0,2},{2,0},{4,6},{6,4},{8,10},{10,8},{12,14},{14,12},{16,18},{18,... | collective-permute-start | bytes 393224 | tf_op jit(solution)/shard_map/ppermute | solution.py:181
  88.8 0.8 collective-permute-start.32
  89.7 1.3 %collective-permute-start.33 = (f32[256,128]{1,0:T(8,128)S(1)}, f32[256,128]{1,0:T(8,128)S(1)}, u32[]{:S(2)}, u32[]{:S(2)}) collective-permute-start(f32[256,128]{1,0:T(8,128)S(1)} %pad_maximum_fusion.3.refs_0_), channel_id=1, source_target_pairs={{0,6},{2,4},{4,2},{6,0},{8,14},{10,12},{12,10},{14,8},{16,22},{18,... | collective-permute-start | bytes 393224 | tf_op jit(solution)/shard_map/ppermute | solution.py:181
  91.0 1.1 %shard_map.122 = (f32[64,128]{1,0:T(8,128)S(1)}, f32[64,2048]{1,0:T(8,128)S(1)}) custom-call(bf16[192,2176]{1,0:T(8,128)(2,1)S(1)} %get-tuple-element.66.stack_ref.refs_2_, f32[64,192]{1,0:T(8,128)S(1)} %get-tuple-element.81.m.mix_ref.refs_3_, f32[64,128]{1,0:T(8,128)S(1)} %get-tuple-element.83.search_ref), custom_call_target="tpu_custom_call" | custom-call | tf_op jit(solution)/shard_map/pallas_call | solution.py:20
  92.2 1.2 %collective-permute-done.26.refs_1_ = f32[64,128]{1,0:T(8,128)S(1)} collective-permute-done((f32[64,128]{1,0:T(8,128)S(1)}, f32[64,128]{1,0:T(8,128)S(1)}, u32[]{:S(2)}, u32[]{:S(2)}) %collective-permute-start.26) | collective-permute-done | bytes 32800 | tf_op jit(solution)/shard_map/ppermute | solution.py:181
  93.4 6.6 %shard_map.123 = (f32[64,64]{1,0:T(8,128)S(1)}, f32[64,2048]{1,0:T(8,128)S(1)}, bf16[64,2048]{1,0:T(8,128)(2,1)}, f32[64,128]{1,0:T(8,128)}, f32[64,128]{1,0:T(8,128)}) custom-call(f32[64,128]{1,0:T(8,128)S(1)} %get-tuple-element.67.refs_0_, f32[64,128]{1,0:T(8,128)S(1)} %collective-permute-done.26.refs_1_, ...), custom_call_target="tpu_custom_call" | custom-call | tf_op jit(solution)/shard_map/pallas_call | solution.py:20
  100.0 0.6 shard_map.124
  100.8 1.1 collective-permute-done.34.refs_1_
  101.8 2.0 %shard_map.125 = (f32[64,2048]{1,0:T(8,128)}, f32[64,128]{1,0:T(8,128)S(1)}, f32[64,64]{1,0:T(8,128)}, f32[64,128]{1,0:T(8,128)S(1)}) custom-call(f32[64,64]{1,0:T(8,128)S(1)} %get-tuple-element.73.refs_0_, f32[64,64]{1,0:T(8,128)S(1)} %collective-permute-done.34.refs_1_, f32[64,64]{1,0:T(8,128)S(1)} %get-tuple-element.74.refs_2_, ...), custom_call_target="tpu_custom_call" | custom-call | tf_op jit(solution)/shard_map/pallas_call | solution.py:20
  104.0 1.0 collective-permute-done.35
  105.0 0.6 rsqrt_multiply_fusion
  (45 shorter events, 2.3 us)
Async XLA Ops:
  1.4 7.3 %collective-permute-start.2 = (bf16[1,192,128]{2,1,0:T(8,128)(2,1)S(1)}, bf16[1,192,128]{2,1,0:T(8,128)(2,1)S(1)}, u32[]{:S(2)}, u32[]{:S(2)}) collective-permute-start(bf16[1,192,128]{2,1,0:T(8,128)(2,1)S(1)} %maximum_bitcast_fusion), channel_id=1, source_target_pairs={{0,24},{2,26},{4,28},{6,30},{8,16},{10,18},{12,20},{14,22},{16,8},... | collective-permute-start | bytes 147464 | tf_op jit(solution)/shard_map/ppermute | solution.py:181
  6.4 5.0 %collective-permute-start.1 = (bf16[1,192,128]{2,1,0:T(8,128)(2,1)S(1)}, bf16[1,192,128]{2,1,0:T(8,128)(2,1)S(1)}, u32[]{:S(2)}, u32[]{:S(2)}) collective-permute-start(bf16[1,192,128]{2,1,0:T(8,128)(2,1)S(1)} %maximum_bitcast_fusion), channel_id=1, source_target_pairs={{0,16},{2,18},{4,20},{6,22},{8,24},{10,26},{12,28},{14,30},{16,0},... | collective-permute-start | bytes 147464 | tf_op jit(solution)/shard_map/ppermute | solution.py:181
  6.4 5.0 %collective-permute-start = (bf16[1,192,128]{2,1,0:T(8,128)(2,1)S(1)}, bf16[1,192,128]{2,1,0:T(8,128)(2,1)S(1)}, u32[]{:S(2)}, u32[]{:S(2)}) collective-permute-start(bf16[1,192,128]{2,1,0:T(8,128)(2,1)S(1)} %maximum_bitcast_fusion), channel_id=1, source_target_pairs={{0,8},{2,10},{4,12},{6,14},{8,0},{10,2},{12,4},{14,6},{16,24},{18,... | collective-permute-start | bytes 147464 | tf_op jit(solution)/shard_map/ppermute | solution.py:181
  11.5 3.6 %copy-start.3 = (s32[1,1,2,16]{3,2,1,0:T(2,128)S(1)}, s32[1,1,2,16]{3,2,1,0:T(2,128)}, u32[]{:S(2)}) copy-start(s32[1,1,2,16]{3,2,1,0:T(2,128)} %param.10) | copy-start | bytes 388
  11.5 3.6 %copy-start.4 = (s32[1,1,2]{2,1,0:T(1,128)S(1)}, s32[1,1,2]{2,1,0:T(1,128)}, u32[]{:S(2)}) copy-start(s32[1,1,2]{2,1,0:T(1,128)} %param.9) | copy-start | bytes 28
  11.5 7.6 %collective-permute-start.3 = (bf16[4,192,128]{2,1,0:T(8,128)(2,1)S(1)}, bf16[4,192,128]{2,1,0:T(8,128)(2,1)S(1)}, u32[]{:S(2)}, u32[]{:S(2)}) collective-permute-start(bf16[4,192,128]{2,1,0:T(8,128)(2,1)S(1)} %pad_maximum_fusion.refs_0_), channel_id=1, source_target_pairs={{0,2},{2,0},{4,6},{6,4},{8,10},{10,8},{12,14},{14,12},{16,18},{18,... | collective-permute-start | bytes 589832 | tf_op jit(solution)/shard_map/ppermute | solution.py:181
  13.0 9.8 %collective-permute-start.4 = (bf16[4,192,128]{2,1,0:T(8,128)(2,1)S(1)}, bf16[4,192,128]{2,1,0:T(8,128)(2,1)S(1)}, u32[]{:S(2)}, u32[]{:S(2)}) collective-permute-start(bf16[4,192,128]{2,1,0:T(8,128)(2,1)S(1)} %pad_maximum_fusion.refs_0_), channel_id=1, source_target_pairs={{0,4},{2,6},{4,0},{6,2},{8,12},{10,14},{12,8},{14,10},{16,20},{18,... | collective-permute-start | bytes 589832 | tf_op jit(solution)/shard_map/ppermute | solution.py:181
  14.6 8.3 %collective-permute-start.5 = (bf16[4,192,128]{2,1,0:T(8,128)(2,1)S(1)}, bf16[4,192,128]{2,1,0:T(8,128)(2,1)S(1)}, u32[]{:S(2)}, u32[]{:S(2)}) collective-permute-start(bf16[4,192,128]{2,1,0:T(8,128)(2,1)S(1)} %pad_maximum_fusion.refs_0_), channel_id=1, source_target_pairs={{0,6},{2,4},{4,2},{6,0},{8,14},{10,12},{12,10},{14,8},{16,22},{18,... | collective-permute-start | bytes 589832 | tf_op jit(solution)/shard_map/ppermute | solution.py:181
  22.8 1.2 %copy-start = (bf16[1,1,2,16,128,128]{5,4,3,2,1,0:T(8,128)(2,1)S(1)}, bf16[1,1,2,16,128,128]{5,4,3,2,1,0:T(8,128)(2,1)}, u32[]{:S(2)}) copy-start(bf16[1,1,2,16,128,128]{5,4,3,2,1,0:T(8,128)(2,1)} %param.8) | copy-start | bytes 3145732
  25.6 1.3 %collective-permute-start.7 = (f32[64,128]{1,0:T(8,128)S(1)}, f32[64,128]{1,0:T(8,128)S(1)}, u32[]{:S(2)}, u32[]{:S(2)}) collective-permute-start(f32[64,128]{1,0:T(8,128)S(1)} %get-tuple-element.47), channel_id=1, source_target_pairs={{0,1},{1,0},{2,3},{3,2},{4,5},{5,4},{6,7},{7,6},{8,9},{9,8},{10,11... | collective-permute-start | bytes 98312 | tf_op jit(solution)/shard_map/ppermute | solution.py:181
  26.9 10.3 %copy-start.2 = (f32[3,64,128]{2,1,0:T(8,128)S(1)}, f32[3,64,128]{2,1,0:T(8,128)}, u32[]{:S(2)}) copy-start(f32[3,64,128]{2,1,0:T(8,128)} %param.15) | copy-start | bytes 294916
  26.9 5.8 %collective-permute-start.10 = (f32[64,128]{1,0:T(8,128)S(1)}, f32[64,128]{1,0:T(8,128)S(1)}, u32[]{:S(2)}, u32[]{:S(2)}) collective-permute-start(f32[64,128]{1,0:T(8,128)S(1)} %add.30), channel_id=1, source_target_pairs={{0,24},{2,26},{4,28},{6,30},{8,16},{10,18},{12,20},{14,22},{16,8},... | collective-permute-start | bytes 98312 | tf_op jit(solution)/shard_map/ppermute | solution.py:181
  28.7 4.9 %collective-permute-start.9 = (f32[64,128]{1,0:T(8,128)S(1)}, f32[64,128]{1,0:T(8,128)S(1)}, u32[]{:S(2)}, u32[]{:S(2)}) collective-permute-start(f32[64,128]{1,0:T(8,128)S(1)} %add.30), channel_id=1, source_target_pairs={{0,16},{2,18},{4,20},{6,22},{8,24},{10,26},{12,28},{14,30},{16,0},... | collective-permute-start | bytes 98312 | tf_op jit(solution)/shard_map/ppermute | solution.py:181
  29.1 4.5 %collective-permute-start.8 = (f32[64,128]{1,0:T(8,128)S(1)}, f32[64,128]{1,0:T(8,128)S(1)}, u32[]{:S(2)}, u32[]{:S(2)}) collective-permute-start(f32[64,128]{1,0:T(8,128)S(1)} %add.30), channel_id=1, source_target_pairs={{0,8},{2,10},{4,12},{6,14},{8,0},{10,2},{12,4},{14,6},{16,24},{18,... | collective-permute-start | bytes 98312 | tf_op jit(solution)/shard_map/ppermute | solution.py:181
  33.6 12.4 %collective-permute-start.11 = (f32[256,128]{1,0:T(8,128)S(1)}, f32[256,128]{1,0:T(8,128)S(1)}, u32[]{:S(2)}, u32[]{:S(2)}) collective-permute-start(f32[256,128]{1,0:T(8,128)S(1)} %pad_maximum_fusion.1.refs_0_), channel_id=1, source_target_pairs={{0,2},{2,0},{4,6},{6,4},{8,10},{10,8},{12,14},{14,12},{16,18},{18,... | collective-permute-start | bytes 393224 | tf_op jit(solution)/shard_map/ppermute | solution.py:181
  35.0 11.1 %collective-permute-start.12 = (f32[256,128]{1,0:T(8,128)S(1)}, f32[256,128]{1,0:T(8,128)S(1)}, u32[]{:S(2)}, u32[]{:S(2)}) collective-permute-start(f32[256,128]{1,0:T(8,128)S(1)} %pad_maximum_fusion.1.refs_0_), channel_id=1, source_target_pairs={{0,4},{2,6},{4,0},{6,2},{8,12},{10,14},{12,8},{14,10},{16,20},{18,... | collective-permute-start | bytes 393224 | tf_op jit(solution)/shard_map/ppermute | solution.py:181
  35.8 10.3 %collective-permute-start.13 = (f32[256,128]{1,0:T(8,128)S(1)}, f32[256,128]{1,0:T(8,128)S(1)}, u32[]{:S(2)}, u32[]{:S(2)}) collective-permute-start(f32[256,128]{1,0:T(8,128)S(1)} %pad_maximum_fusion.1.refs_0_), channel_id=1, source_target_pairs={{0,6},{2,4},{4,2},{6,0},{8,14},{10,12},{12,10},{14,8},{16,22},{18,... | collective-permute-start | bytes 393224 | tf_op jit(solution)/shard_map/ppermute | solution.py:181
  38.3 1.3 %collective-permute-start.6 = (f32[64,128]{1,0:T(8,128)S(1)}, f32[64,128]{1,0:T(8,128)S(1)}, u32[]{:S(2)}, u32[]{:S(2)}) collective-permute-start(f32[64,128]{1,0:T(8,128)S(1)} %get-tuple-element.43.refs_0_), channel_id=1, source_target_pairs={{0,1},{1,0},{2,3},{3,2},{4,5},{5,4},{6,7},{7,6},{8,9},{9,8},{10,11... | collective-permute-start | bytes 98312 | tf_op jit(solution)/shard_map/ppermute | solution.py:181
  46.1 4.6 %copy-start.1 = (bf16[1,1,2,16,128,128]{5,4,3,2,1,0:T(8,128)(2,1)S(1)}, bf16[1,1,2,16,128,128]{5,4,3,2,1,0:T(8,128)(2,1)}, u32[]{:S(2)}) copy-start(bf16[1,1,2,16,128,128]{5,4,3,2,1,0:T(8,128)(2,1)} %param.8) | copy-start | bytes 3145732
  46.7 1.3 %collective-permute-start.14 = (f32[64,64]{1,0:T(8,128)S(1)}, f32[64,64]{1,0:T(8,128)S(1)}, u32[]{:S(2)}, u32[]{:S(2)}) collective-permute-start(f32[64,64]{1,0:T(8,128)S(1)} %get-tuple-element.48.refs_0_), channel_id=1, source_target_pairs={{0,1},{1,0},{2,3},{3,2},{4,5},{5,4},{6,7},{7,6},{8,9},{9,8},{10,11... | collective-permute-start | bytes 49160 | tf_op jit(solution)/shard_map/ppermute | solution.py:181
  49.5 1.2 %collective-permute-start.15 = (f32[64,128]{1,0:T(8,128)S(1)}, f32[64,128]{1,0:T(8,128)S(1)}, u32[]{:S(2)}, u32[]{:S(2)}) collective-permute-start(f32[64,128]{1,0:T(8,128)S(1)} %get-tuple-element.52.refs_0_), channel_id=1, source_target_pairs={{0,1},{1,0},{2,3},{3,2},{4,5},{5,4},{6,7},{7,6},{8,9},{9,8},{10,11... | collective-permute-start | bytes 98312 | tf_op jit(solution)/shard_map/ppermute | solution.py:181
  52.2 1.3 %collective-permute-start.17 = (f32[64,128]{1,0:T(8,128)S(1)}, f32[64,128]{1,0:T(8,128)S(1)}, u32[]{:S(2)}, u32[]{:S(2)}) collective-permute-start(f32[64,128]{1,0:T(8,128)S(1)} %get-tuple-element.59), channel_id=1, source_target_pairs={{0,1},{1,0},{2,3},{3,2},{4,5},{5,4},{6,7},{7,6},{8,9},{9,8},{10,11... | collective-permute-start | bytes 98312 | tf_op jit(solution)/shard_map/ppermute | solution.py:181
  53.5 6.0 %collective-permute-start.20 = (f32[64,128]{1,0:T(8,128)S(1)}, f32[64,128]{1,0:T(8,128)S(1)}, u32[]{:S(2)}, u32[]{:S(2)}) collective-permute-start(f32[64,128]{1,0:T(8,128)S(1)} %add.31), channel_id=1, source_target_pairs={{0,24},{2,26},{4,28},{6,30},{8,16},{10,18},{12,20},{14,22},{16,8},... | collective-permute-start | bytes 98312 | tf_op jit(solution)/shard_map/ppermute | solution.py:181
  55.7 5.0 %collective-permute-start.19 = (f32[64,128]{1,0:T(8,128)S(1)}, f32[64,128]{1,0:T(8,128)S(1)}, u32[]{:S(2)}, u32[]{:S(2)}) collective-permute-start(f32[64,128]{1,0:T(8,128)S(1)} %add.31), channel_id=1, source_target_pairs={{0,16},{2,18},{4,20},{6,22},{8,24},{10,26},{12,28},{14,30},{16,0},... | collective-permute-start | bytes 98312 | tf_op jit(solution)/shard_map/ppermute | solution.py:181
  56.6 4.3 %collective-permute-start.18 = (f32[64,128]{1,0:T(8,128)S(1)}, f32[64,128]{1,0:T(8,128)S(1)}, u32[]{:S(2)}, u32[]{:S(2)}) collective-permute-start(f32[64,128]{1,0:T(8,128)S(1)} %add.31), channel_id=1, source_target_pairs={{0,8},{2,10},{4,12},{6,14},{8,0},{10,2},{12,4},{14,6},{16,24},{18,... | collective-permute-start | bytes 98312 | tf_op jit(solution)/shard_map/ppermute | solution.py:181
  60.9 12.4 %collective-permute-start.21 = (f32[256,128]{1,0:T(8,128)S(1)}, f32[256,128]{1,0:T(8,128)S(1)}, u32[]{:S(2)}, u32[]{:S(2)}) collective-permute-start(f32[256,128]{1,0:T(8,128)S(1)} %pad_maximum_fusion.2.refs_0_), channel_id=1, source_target_pairs={{0,2},{2,0},{4,6},{6,4},{8,10},{10,8},{12,14},{14,12},{16,18},{18,... | collective-permute-start | bytes 393224 | tf_op jit(solution)/shard_map/ppermute | solution.py:181
  62.1 11.2 %collective-permute-start.22 = (f32[256,128]{1,0:T(8,128)S(1)}, f32[256,128]{1,0:T(8,128)S(1)}, u32[]{:S(2)}, u32[]{:S(2)}) collective-permute-start(f32[256,128]{1,0:T(8,128)S(1)} %pad_maximum_fusion.2.refs_0_), channel_id=1, source_target_pairs={{0,4},{2,6},{4,0},{6,2},{8,12},{10,14},{12,8},{14,10},{16,20},{18,... | collective-permute-start | bytes 393224 | tf_op jit(solution)/shard_map/ppermute | solution.py:181
  63.0 10.3 %collective-permute-start.23 = (f32[256,128]{1,0:T(8,128)S(1)}, f32[256,128]{1,0:T(8,128)S(1)}, u32[]{:S(2)}, u32[]{:S(2)}) collective-permute-start(f32[256,128]{1,0:T(8,128)S(1)} %pad_maximum_fusion.2.refs_0_), channel_id=1, source_target_pairs={{0,6},{2,4},{4,2},{6,0},{8,14},{10,12},{12,10},{14,8},{16,22},{18,... | collective-permute-start | bytes 393224 | tf_op jit(solution)/shard_map/ppermute | solution.py:181
  65.6 1.3 %collective-permute-start.16 = (f32[64,128]{1,0:T(8,128)S(1)}, f32[64,128]{1,0:T(8,128)S(1)}, u32[]{:S(2)}, u32[]{:S(2)}) collective-permute-start(f32[64,128]{1,0:T(8,128)S(1)} %get-tuple-element.55.refs_0_), channel_id=1, source_target_pairs={{0,1},{1,0},{2,3},{3,2},{4,5},{5,4},{6,7},{7,6},{8,9},{9,8},{10,11... | collective-permute-start | bytes 98312 | tf_op jit(solution)/shard_map/ppermute | solution.py:181
  73.9 1.3 %collective-permute-start.24 = (f32[64,64]{1,0:T(8,128)S(1)}, f32[64,64]{1,0:T(8,128)S(1)}, u32[]{:S(2)}, u32[]{:S(2)}) collective-permute-start(f32[64,64]{1,0:T(8,128)S(1)} %get-tuple-element.60.refs_0_), channel_id=1, source_target_pairs={{0,1},{1,0},{2,3},{3,2},{4,5},{5,4},{6,7},{7,6},{8,9},{9,8},{10,11... | collective-permute-start | bytes 49160 | tf_op jit(solution)/shard_map/ppermute | solution.py:181
  76.7 1.2 %collective-permute-start.25 = (f32[64,128]{1,0:T(8,128)S(1)}, f32[64,128]{1,0:T(8,128)S(1)}, u32[]{:S(2)}, u32[]{:S(2)}) collective-permute-start(f32[64,128]{1,0:T(8,128)S(1)} %get-tuple-element.64.refs_0_), channel_id=1, source_target_pairs={{0,1},{1,0},{2,3},{3,2},{4,5},{5,4},{6,7},{7,6},{8,9},{9,8},{10,11... | collective-permute-start | bytes 98312 | tf_op jit(solution)/shard_map/ppermute | solution.py:181
  79.4 1.3 %collective-permute-start.27 = (f32[64,128]{1,0:T(8,128)S(1)}, f32[64,128]{1,0:T(8,128)S(1)}, u32[]{:S(2)}, u32[]{:S(2)}) collective-permute-start(f32[64,128]{1,0:T(8,128)S(1)} %get-tuple-element.71), channel_id=1, source_target_pairs={{0,1},{1,0},{2,3},{3,2},{4,5},{5,4},{6,7},{7,6},{8,9},{9,8},{10,11... | collective-permute-start | bytes 98312 | tf_op jit(solution)/shard_map/ppermute | solution.py:181
  80.7 5.9 %collective-permute-start.30 = (f32[64,128]{1,0:T(8,128)S(1)}, f32[64,128]{1,0:T(8,128)S(1)}, u32[]{:S(2)}, u32[]{:S(2)}) collective-permute-start(f32[64,128]{1,0:T(8,128)S(1)} %add.32), channel_id=1, source_target_pairs={{0,24},{2,26},{4,28},{6,30},{8,16},{10,18},{12,20},{14,22},{16,8},... | collective-permute-start | bytes 98312 | tf_op jit(solution)/shard_map/ppermute | solution.py:181
  82.3 5.1 %collective-permute-start.29 = (f32[64,128]{1,0:T(8,128)S(1)}, f32[64,128]{1,0:T(8,128)S(1)}, u32[]{:S(2)}, u32[]{:S(2)}) collective-permute-start(f32[64,128]{1,0:T(8,128)S(1)} %add.32), channel_id=1, source_target_pairs={{0,16},{2,18},{4,20},{6,22},{8,24},{10,26},{12,28},{14,30},{16,0},... | collective-permute-start | bytes 98312 | tf_op jit(solution)/shard_map/ppermute | solution.py:181
  83.1 4.3 %collective-permute-start.28 = (f32[64,128]{1,0:T(8,128)S(1)}, f32[64,128]{1,0:T(8,128)S(1)}, u32[]{:S(2)}, u32[]{:S(2)}) collective-permute-start(f32[64,128]{1,0:T(8,128)S(1)} %add.32), channel_id=1, source_target_pairs={{0,8},{2,10},{4,12},{6,14},{8,0},{10,2},{12,4},{14,6},{16,24},{18,... | collective-permute-start | bytes 98312 | tf_op jit(solution)/shard_map/ppermute | solution.py:181
  87.4 12.5 %collective-permute-start.31 = (f32[256,128]{1,0:T(8,128)S(1)}, f32[256,128]{1,0:T(8,128)S(1)}, u32[]{:S(2)}, u32[]{:S(2)}) collective-permute-start(f32[256,128]{1,0:T(8,128)S(1)} %pad_maximum_fusion.3.refs_0_), channel_id=1, source_target_pairs={{0,2},{2,0},{4,6},{6,4},{8,10},{10,8},{12,14},{14,12},{16,18},{18,... | collective-permute-start | bytes 393224 | tf_op jit(solution)/shard_map/ppermute | solution.py:181
  88.8 11.1 %collective-permute-start.32 = (f32[256,128]{1,0:T(8,128)S(1)}, f32[256,128]{1,0:T(8,128)S(1)}, u32[]{:S(2)}, u32[]{:S(2)}) collective-permute-start(f32[256,128]{1,0:T(8,128)S(1)} %pad_maximum_fusion.3.refs_0_), channel_id=1, source_target_pairs={{0,4},{2,6},{4,0},{6,2},{8,12},{10,14},{12,8},{14,10},{16,20},{18,... | collective-permute-start | bytes 393224 | tf_op jit(solution)/shard_map/ppermute | solution.py:181
  89.7 10.3 %collective-permute-start.33 = (f32[256,128]{1,0:T(8,128)S(1)}, f32[256,128]{1,0:T(8,128)S(1)}, u32[]{:S(2)}, u32[]{:S(2)}) collective-permute-start(f32[256,128]{1,0:T(8,128)S(1)} %pad_maximum_fusion.3.refs_0_), channel_id=1, source_target_pairs={{0,6},{2,4},{4,2},{6,0},{8,14},{10,12},{12,10},{14,8},{16,22},{18,... | collective-permute-start | bytes 393224 | tf_op jit(solution)/shard_map/ppermute | solution.py:181
  92.1 1.3 %collective-permute-start.26 = (f32[64,128]{1,0:T(8,128)S(1)}, f32[64,128]{1,0:T(8,128)S(1)}, u32[]{:S(2)}, u32[]{:S(2)}) collective-permute-start(f32[64,128]{1,0:T(8,128)S(1)} %get-tuple-element.67.refs_0_), channel_id=1, source_target_pairs={{0,1},{1,0},{2,3},{3,2},{4,5},{5,4},{6,7},{7,6},{8,9},{9,8},{10,11... | collective-permute-start | bytes 98312 | tf_op jit(solution)/shard_map/ppermute | solution.py:181
  100.5 1.3 %collective-permute-start.34 = (f32[64,64]{1,0:T(8,128)S(1)}, f32[64,64]{1,0:T(8,128)S(1)}, u32[]{:S(2)}, u32[]{:S(2)}) collective-permute-start(f32[64,64]{1,0:T(8,128)S(1)} %get-tuple-element.73.refs_0_), channel_id=1, source_target_pairs={{0,1},{1,0},{2,3},{3,2},{4,5},{5,4},{6,7},{7,6},{8,9},{9,8},{10,11... | collective-permute-start | bytes 49160 | tf_op jit(solution)/shard_map/ppermute | solution.py:181
  103.8 1.2 %collective-permute-start.35 = (f32[64,128]{1,0:T(8,128)S(1)}, f32[64,128]{1,0:T(8,128)S(1)}, u32[]{:S(2)}, u32[]{:S(2)}) collective-permute-start(f32[64,128]{1,0:T(8,128)S(1)} %get-tuple-element.77), channel_id=1, source_target_pairs={{0,1},{1,0},{2,3},{3,2},{4,5},{5,4},{6,7},{7,6},{8,9},{9,8},{10,11... | collective-permute-start | bytes 98312 | tf_op jit(solution)/shard_map/ppermute | solution.py:181

commit v2 on v1

--- a/solution.py
+++ b/solution.py
@@ -124,28 +124,57 @@
     )
 
 
-def factor_kernel(nodes, packs, stack_ref, mix_ref, search_ref, inverse_ref, basis_ref, dirs_ref, own_basis, own_dirs):
-    vecs = mix_ref.shape[0]
+def factor_kernel(nodes, packs, inverse_ref, scale_ref):
+    vecs = inverse_ref.shape[0]
+    total = sum(ref[...] for ref in packs) / nodes
+    scale_ref[...] = jnp.broadcast_to(lax.rsqrt(total[:, vecs : vecs + 1] + epsilon), scale_ref.shape)
+    row_ids = lax.broadcasted_iota(jnp.int32, (vecs, 2 * vecs), 0)
+    lane_ids = lax.broadcasted_iota(jnp.int32, (vecs, 2 * vecs), 1)
+    diagonal = jnp.where(lane_ids == row_ids, total, 0.0)
+    down = lax.rsqrt(jnp.sum(diagonal, axis=1, keepdims=True))
+    across = lax.rsqrt(jnp.sum(diagonal, axis=0, keepdims=True))
+    work = jnp.where(lane_ids < vecs, total * down * across, jnp.where(lane_ids == row_ids + vecs, down, 0.0))
+    height = 8
+    tiles = [work[t : t + height] for t in range(0, vecs, height)]
+    shape = tiles[0].shape
+    ids = lax.broadcasted_iota(jnp.int32, shape, 0)
+    for j in range(0, vecs, 2):
+        t, s = divmod(j, height)
+        top, under = tiles[t][s : s + 1], tiles[t][s + 1 : s + 2]
+        columns = [
+            [jnp.broadcast_to(tile[:, k : k + 1], shape) for k in (j, j + 1)] for tile in tiles[t:]
+        ]
+        a = columns[0][0][s : s + 1]
+        b = columns[0][0][s + 1 : s + 2]
+        c = columns[0][1][s + 1 : s + 2]
+        determinant = 1.0 / (a * c - b * b)
+        a, b, c = a * determinant, b * determinant, c * determinant
+        for u in range(t, len(tiles)):
+            if u == t and s == height - 2:
+                continue
+            x, y = columns[u - t]
+            one, two = x * c - y * b, y * a - x * b
+            if u == t:
+                one, two = jnp.where(ids > s + 1, one, 0.0), jnp.where(ids > s + 1, two, 0.0)
+            tiles[u] = tiles[u] - one * top - two * under
+    work = jnp.concatenate(tiles, axis=0)
+    above = jnp.concatenate([work[:1], work[:-1]], axis=0)
+    odd = row_ids % 2 == 1
+    pivots = jnp.sum(jnp.where(lane_ids == row_ids, work, 0.0), axis=1, keepdims=True)
+    beside = jnp.sum(jnp.where(lane_ids == row_ids - 1, work, 0.0), axis=1, keepdims=True)
+    firsts = jnp.concatenate([pivots[:1], pivots[:-1]], axis=0)
+    ratio = jnp.where(odd[:, :1], beside / firsts, 0.0)
+    inverse = (work - ratio * above) * lax.rsqrt(pivots - ratio * beside)
+    inverse_ref[...] = inverse[:, vecs:]
+
+
+def basis_kernel(inverse_ref, scale_ref, stack_ref, mix_ref, search_ref, basis_ref, dirs_ref, own_basis, own_dirs):
     wide = search_ref.shape[1]
     edge = own_basis.shape[1]
-    total = sum(ref[...] for ref in packs) / nodes
-    scale = lax.rsqrt(total[:, vecs : vecs + 1] + epsilon)
-    dirs = search_ref[...] * scale
+    dirs = search_ref[...] * scale_ref[:, :1]
     dirs_ref[...] = dirs.astype(bf16)
     own_dirs[...] = dirs[:, :edge]
-    row_ids = lax.broadcasted_iota(jnp.int32, (vecs, 2 * vecs), 0)
-    lane_ids = lax.broadcasted_iota(jnp.int32, (vecs, 2 * vecs), 1)
-    left = lane_ids < vecs
-    work = jnp.where(left, total, jnp.where(lane_ids == row_ids + vecs, 1.0, 0.0))
-    for j in range(vecs - 1):
-        pivot_row = work[j : j + 1, :]
-        column = work[:, j : j + 1]
-        ratio = jnp.where(row_ids[:, :1] > j, column / work[j : j + 1, j : j + 1], 0.0)
-        work = work - ratio * pivot_row
-    pivots = jnp.sum(jnp.where(lane_ids == row_ids, work, 0.0), axis=1, keepdims=True)
-    inverse = (work * lax.rsqrt(pivots))[:, vecs:]
-    inverse_ref[...] = inverse
-    basis = times_stack(dot_nn(inverse, mix_ref[...]), stack_ref[:, :wide])
+    basis = times_stack(dot_nn(inverse_ref[...], mix_ref[...]), stack_ref[:, :wide])
     basis_ref[...] = basis
     own_basis[...] = basis[:, :edge]
 
@@ -187,10 +216,13 @@
     return [lax.psum(value, "panel")]
 
 
-def gather(value, near):
+def gather(value, near, beside=None):
     far = lax.axis_size("rows") // near
-    held = jnp.concatenate([value] + [swap(value, near * i, "rows") for i in range(1, far)], axis=0)
-    return [held] + [swap(held, i, "rows") for i in range(1, near)]
+    first = [value] + [swap(value, near * i, "rows") for i in range(1, far)]
+    if beside is not None:
+        first, beside = lax.optimization_barrier((first, beside))
+    held = jnp.concatenate(first, axis=0)
+    return [held] + [swap(held, i, "rows") for i in range(1, near)], beside
 
 
 def body(
@@ -225,7 +257,7 @@
     stack_out = ((3 * vecs, wide + edge), bf16)
 
     start = jnp.concatenate([start_basis, start_resid, start_search], axis=0)[None]
-    parts = gather(start, near)
+    parts, _ = gather(start, near)
     state = None
     sweeps = ritz_basis.shape[0]
     for sweep in range(sweeps):
@@ -250,33 +282,37 @@
                 [slot_ids, place, tile_set, mixing, basis, raw] + squares + [dirs],
                 smem=(0, 1),
             )
-        if panels == 2:
-            rotated_adj = mine[0] + swap(mine[1], 1, "panel")
-        else:
-            rotated_adj = lax.psum_scatter(mine[0], "panel", scatter_dimension=0, tiled=True)[0]
         pack, search = call(
             gram_kernel,
             [((vecs, 2 * vecs), f32), ((vecs, wide), f32)],
             [stack, mixing, ritz_search[sweep]],
         )
+        if panels == 2:
+            other = swap(mine[1], 1, "panel")
+            other, pack = lax.optimization_barrier((other, pack))
+            rotated_adj = mine[0] + other
+        else:
+            rotated_adj = lax.psum_scatter(mine[0], "panel", scatter_dimension=0, tiled=True)[0]
         packs = panel_terms(pack)
         pack_count = len(packs)
 
         def kernel_factor(*refs):
             factor_kernel(nodes, refs[:pack_count], *refs[pack_count:])
 
-        inverse, basis, dirs, own_basis, own_dirs = call(
-            kernel_factor,
+        inverse, scale = call(
+            kernel_factor, [((vecs, vecs), f32), ((vecs, 2 * vecs), f32)], packs
+        )
+        adj_parts, inverse = gather(rotated_adj, near, inverse)
+        basis, dirs, own_basis, own_dirs = call(
+            basis_kernel,
             [
-                ((vecs, vecs), f32),
                 ((vecs, wide), f32),
                 ((vecs, wide), bf16),
                 ((vecs, edge), f32),
                 ((vecs, edge), f32),
             ],
-            packs + [stack, mixing, search],
-        )
-        adj_parts = gather(rotated_adj, near)
+            [inverse, scale, stack, mixing, search],
+        )
         wide_adj, cross = call(
             functools.partial(cross_kernel, near),
             [((vecs, wide), f32), ((vecs, vecs), f32)],

time: 106 us -> 98.2 us (0.926)
  Pallas kernels: 34.2 us -> 28.6 us
  waiting for transfers between devices: 31.9 us -> 29 us
    pallas_call x15 -> x18, Pallas kernels: 34.2 us -> 28.6 us  [call(): pl.pallas_call(kernel, out_shape=[jax.ShapeDtypeStruct(shape, kind) for s...]
    ppermute x36, waiting for transfers between devices: 31.9 us -> 29 us  [swap(): return lax.ppermute(value, axis, [(i, i ^ by) for i in range(size)])]
  transfers between devices with their start and end apart: 36 -> 36, of which waited for: 24 -> 18; matrix products, arithmetic and copies ran while one was open for 1% -> 1% of each run, Pallas kernels for 22% -> 18%
where the time goes in v2:
time: 98.2 us; the launch traced here: 97.9 us
  starting transfers between devices  35.6 us (36%)
  waiting for transfers between devices  29 us (30%)
  Pallas kernels  28.6 us (29%)
  local copies, waits for them, and re-layouts  2.23 us (2%)
  other arithmetic  1.5 us (2%)
    ppermute x36, starting transfers between devices, swap(): return lax.ppermute(value, axis, [(i, i ^ by) for i in range(size)])  35.6 us
    ppermute x36, waiting for transfers between devices, swap(): return lax.ppermute(value, axis, [(i, i ^ by) for i in range(size)])  29 us
    pallas_call x18, Pallas kernels, call(): pl.pallas_call(kernel, out_shape=[jax.ShapeDtypeStruct(shape, kind) for s...  28.6 us
  transfers between devices with their start and end apart: 36, of which 18 were waited for; matrix products, arithmetic and copies ran while one was open for 1% of the time, Pallas kernels for 18%

profile of v2, /device:TPU:0, one launch (start us, length us, event | category | flops | bytes accessed | tf_op | source)
XLA Modules:
  0.0 97.9 jit_solution(5855829990659412719)
XLA Ops:
  0.6 0.8 maximum_bitcast_fusion
  1.4 5.0 %collective-permute-start.2 = (bf16[1,192,128]{2,1,0:T(8,128)(2,1)S(1)}, bf16[1,192,128]{2,1,0:T(8,128)(2,1)S(1)}, u32[]{:S(2)}, u32[]{:S(2)}) collective-permute-start(bf16[1,192,128]{2,1,0:T(8,128)(2,1)S(1)} %maximum_bitcast_fusion), channel_id=1, source_target_pairs={{0,24},{2,26},{4,28},{6,30},{8,16},{10,18},{12,20},{14,22},{16,8},... | collective-permute-start | bytes 147464 | tf_op jit(solution)/shard_map/ppermute | solution.py:210
  6.4 0.6 collective-permute-start
  7.0 0.9 slice_bitcast_fusion
  8.0 0.7 collective-permute-done.2
  8.7 2.8 %collective-permute-done.1 = bf16[1,192,128]{2,1,0:T(8,128)(2,1)S(1)} collective-permute-done((bf16[1,192,128]{2,1,0:T(8,128)(2,1)S(1)}, bf16[1,192,128]{2,1,0:T(8,128)(2,1)S(1)}, u32[]{:S(2)}, u32[]{:S(2)}) %collective-permute-start.1) | collective-permute-done | bytes 49184 | tf_op jit(solution)/shard_map/ppermute | solution.py:210
  11.5 2.5 %collective-permute-start.5 = (bf16[4,192,128]{2,1,0:T(8,128)(2,1)S(1)}, bf16[4,192,128]{2,1,0:T(8,128)(2,1)S(1)}, u32[]{:S(2)}, u32[]{:S(2)}) collective-permute-start(bf16[4,192,128]{2,1,0:T(8,128)(2,1)S(1)} %pad_maximum_fusion.refs_0_), channel_id=1, source_target_pairs={{0,6},{2,4},{4,2},{6,0},{8,14},{10,12},{12,10},{14,8},{16,22},{18,... | collective-permute-start | bytes 589832 | tf_op jit(solution)/shard_map/ppermute | solution.py:210
  14.0 0.5 collective-permute-start.4
  14.5 0.5 collective-permute-start.3
  15.1 4.8 %collective-permute-done.5.refs_3_ = bf16[4,192,128]{2,1,0:T(8,128)(2,1)S(1)} collective-permute-done((bf16[4,192,128]{2,1,0:T(8,128)(2,1)S(1)}, bf16[4,192,128]{2,1,0:T(8,128)(2,1)S(1)}, u32[]{:S(2)}, u32[]{:S(2)}) %collective-permute-start.5) | collective-permute-done | bytes 196640 | tf_op jit(solution)/shard_map/ppermute | solution.py:210
  20.0 2.5 %collective-permute-done.4.refs_2_ = bf16[4,192,128]{2,1,0:T(8,128)(2,1)S(1)} collective-permute-done((bf16[4,192,128]{2,1,0:T(8,128)(2,1)S(1)}, bf16[4,192,128]{2,1,0:T(8,128)(2,1)S(1)}, u32[]{:S(2)}, u32[]{:S(2)}) %collective-permute-start.4) | collective-permute-done | bytes 196640 | tf_op jit(solution)/shard_map/ppermute | solution.py:210
  22.5 1.2 %copy-done = bf16[1,1,2,16,128,128]{5,4,3,2,1,0:T(8,128)(2,1)S(1)} copy-done((bf16[1,1,2,16,128,128]{5,4,3,2,1,0:T(8,128)(2,1)S(1)}, bf16[1,1,2,16,128,128]{5,4,3,2,1,0:T(8,128)(2,1)}, u32[]{:S(2)}) %copy-start) | copy-done | bytes 1048600
  23.7 1.5 %shard_map.111 = (bf16[192,2176]{1,0:T(8,128)(2,1)S(1)}, f32[64,128]{1,0:T(8,128)S(1)}, f32[64,128]{1,0:T(8,128)S(1)}) custom-call(s32[2,16]{1,0:T(2,128)S(1)} %compare_select_fusion.slots_ref.s, s32[1]{0:T(128)} %bitcast.2.place_ref.p, bf16[2,16,128,128]{3,2,1,0:T(8,128)(2,1)S(1)} %bitcast.25, f32[64,192]{1,0:T(8,128)S(1)} %get-tuple-element.128.mix_ref, ...), custom_call_target="tpu_custom_call" | custom-call | tf_op jit(solution)/shard_map/pallas_call | solution.py:20
  25.4 1.1 %shard_map.112 = (f32[64,128]{1,0:T(8,128)S(1)}, f32[64,2048]{1,0:T(8,128)S(1)}) custom-call(bf16[192,2176]{1,0:T(8,128)(2,1)S(1)} %get-tuple-element.68.stack_ref, f32[64,192]{1,0:T(8,128)S(1)} %get-tuple-element.128.mix_ref, f32[64,128]{1,0:T(8,128)S(1)} %get-tuple-element.132.search_ref), custom_call_target="tpu_custom_call" | custom-call | tf_op jit(solution)/shard_map/pallas_call | solution.py:20
  26.6 0.5 collective-permute-start.10
  27.1 1.6 %collective-permute-start.9 = (f32[64,128]{1,0:T(8,128)S(1)}, f32[64,128]{1,0:T(8,128)S(1)}, u32[]{:S(2)}, u32[]{:S(2)}) collective-permute-start(f32[64,128]{1,0:T(8,128)S(1)} %add.30), channel_id=1, source_target_pairs={{0,24},{2,26},{4,28},{6,30},{8,16},{10,18},{12,20},{14,22},{16,8},... | collective-permute-start | bytes 98312 | tf_op jit(solution)/shard_map/ppermute | solution.py:210
  28.7 0.6 collective-permute-start.8
  29.2 2.2 %collective-permute-start.7 = (f32[64,128]{1,0:T(8,128)S(1)}, f32[64,128]{1,0:T(8,128)S(1)}, u32[]{:S(2)}, u32[]{:S(2)}) collective-permute-start(f32[64,128]{1,0:T(8,128)S(1)} %add.30), channel_id=1, source_target_pairs={{0,8},{2,10},{4,12},{6,14},{8,0},{10,2},{12,4},{14,6},{16,24},{18,... | collective-permute-start | bytes 98312 | tf_op jit(solution)/shard_map/ppermute | solution.py:210
  31.5 3.4 %shard_map.113 = (f32[64,64]{1,0:T(8,128)S(1)}, f32[64,128]{1,0:T(8,128)S(1)}) custom-call(f32[64,128]{1,0:T(8,128)S(1)} %get-tuple-element.71.refs_0_, f32[64,128]{1,0:T(8,128)S(1)} %collective-permute-done.10.refs_1_), custom_call_target="tpu_custom_call" | custom-call | tf_op jit(solution)/shard_map/pallas_call | solution.py:20
  34.9 1.7 %collective-permute-start.13 = (f32[256,128]{1,0:T(8,128)S(1)}, f32[256,128]{1,0:T(8,128)S(1)}, u32[]{:S(2)}, u32[]{:S(2)}) collective-permute-start(f32[256,128]{1,0:T(8,128)S(1)} %constant_dynamic-update-slice_fusion.refs_0_), channel_id=1, source_target_pairs={{0,6},{2,4},{4,2},{6,0},{8,14},{10,12},{12,10},{14,8},{16,22},{18,... | collective-permute-start | bytes 393224 | tf_op jit(solution)/shard_map/ppermute | solution.py:210
  36.6 1.3 %collective-permute-start.12 = (f32[256,128]{1,0:T(8,128)S(1)}, f32[256,128]{1,0:T(8,128)S(1)}, u32[]{:S(2)}, u32[]{:S(2)}) collective-permute-start(f32[256,128]{1,0:T(8,128)S(1)} %constant_dynamic-update-slice_fusion.refs_0_), channel_id=1, source_target_pairs={{0,4},{2,6},{4,0},{6,2},{8,12},{10,14},{12,8},{14,10},{16,20},{18,... | collective-permute-start | bytes 393224 | tf_op jit(solution)/shard_map/ppermute | solution.py:210
  38.0 0.5 collective-permute-start.11
  38.5 1.1 %shard_map.114 = (f32[64,2048]{1,0:T(8,128)S(1)}, bf16[64,2048]{1,0:T(8,128)(2,1)S(1)}, f32[64,128]{1,0:T(8,128)}, f32[64,128]{1,0:T(8,128)}) custom-call(f32[64,64]{1,0:T(8,128)S(1)} %get-tuple-element.73.inverse_ref.refs_2_, f32[64,128]{1,0:T(8,128)S(1)} %get-tuple-element.74.scale_ref, bf16[192,2176]{1,0:T(8,128)(2,1)S(1)} %get-tuple-element.68.stack_ref, ...), custom_call_target="tpu_custom_call" | custom-call | tf_op jit(solution)/shard_map/pallas_call | solution.py:20
  39.6 2.6 %collective-permute-done.13.refs_3_ = f32[256,128]{1,0:T(8,128)S(1)} collective-permute-done((f32[256,128]{1,0:T(8,128)S(1)}, f32[256,128]{1,0:T(8,128)S(1)}, u32[]{:S(2)}, u32[]{:S(2)}) %collective-permute-start.13) | collective-permute-done | bytes 131104 | tf_op jit(solution)/shard_map/ppermute | solution.py:210
  42.2 1.2 %collective-permute-done.12.refs_2_ = f32[256,128]{1,0:T(8,128)S(1)} collective-permute-done((f32[256,128]{1,0:T(8,128)S(1)}, f32[256,128]{1,0:T(8,128)S(1)}, u32[]{:S(2)}, u32[]{:S(2)}) %collective-permute-start.12) | collective-permute-done | bytes 131104 | tf_op jit(solution)/shard_map/ppermute | solution.py:210
  43.5 0.6 shard_map.115
  44.1 1.2 %collective-permute-done.14.refs_1_ = f32[64,64]{1,0:T(8,128)S(1)} collective-permute-done((f32[64,64]{1,0:T(8,128)S(1)}, f32[64,64]{1,0:T(8,128)S(1)}, u32[]{:S(2)}, u32[]{:S(2)}) %collective-permute-start.14) | collective-permute-done | bytes 16416 | tf_op jit(solution)/shard_map/ppermute | solution.py:210
  45.3 1.5 %shard_map.116 = (f32[64,2048]{1,0:T(8,128)S(1)}, f32[64,128]{1,0:T(8,128)S(1)}, f32[64,64]{1,0:T(8,128)}, f32[64,128]{1,0:T(8,128)}) custom-call(f32[64,64]{1,0:T(8,128)S(1)} %get-tuple-element.81.refs_0_, f32[64,64]{1,0:T(8,128)S(1)} %collective-permute-done.14.refs_1_, f32[64,64]{1,0:T(8,128)S(1)} %get-tuple-element.73.inverse_ref.refs_2_, ...), custom_call_target="tpu_custom_call" | custom-call | tf_op jit(solution)/shard_map/pallas_call | solution.py:20
  47.0 1.0 %collective-permute-done.15.refs_1_ = f32[64,128]{1,0:T(8,128)S(1)} collective-permute-done((f32[64,128]{1,0:T(8,128)S(1)}, f32[64,128]{1,0:T(8,128)S(1)}, u32[]{:S(2)}, u32[]{:S(2)}) %collective-permute-start.15) | collective-permute-done | bytes 32800 | tf_op jit(solution)/shard_map/ppermute | solution.py:210
  48.0 1.5 %shard_map.117 = (bf16[192,2176]{1,0:T(8,128)(2,1)S(1)}, f32[64,128]{1,0:T(8,128)S(1)}, f32[64,128]{1,0:T(8,128)S(1)}) custom-call(s32[2,16]{1,0:T(2,128)S(1)} %compare_select_fusion.slots_ref.s, s32[1]{0:T(128)} %bitcast.2.place_ref.p, bf16[2,16,128,128]{3,2,1,0:T(8,128)(2,1)S(1)} %bitcast.26, f32[64,192]{1,0:T(8,128)S(1)} %get-tuple-element.130.m.mix_ref, ...), custom_call_target="tpu_custom_call" | custom-call | tf_op jit(solution)/shard_map/pallas_call | solution.py:20
  49.5 0.2 collective-permute-start.16
  49.8 1.1 %shard_map.118 = (f32[64,128]{1,0:T(8,128)S(1)}, f32[64,2048]{1,0:T(8,128)S(1)}) custom-call(bf16[192,2176]{1,0:T(8,128)(2,1)S(1)} %get-tuple-element.88.stack_ref, f32[64,192]{1,0:T(8,128)S(1)} %get-tuple-element.130.m.mix_ref, f32[64,128]{1,0:T(8,128)S(1)} %get-tuple-element.133.search_ref), custom_call_target="tpu_custom_call" | custom-call | tf_op jit(solution)/shard_map/pallas_call | solution.py:20
  50.9 0.4 collective-permute-start.20
  51.3 1.6 %collective-permute-start.19 = (f32[64,128]{1,0:T(8,128)S(1)}, f32[64,128]{1,0:T(8,128)S(1)}, u32[]{:S(2)}, u32[]{:S(2)}) collective-permute-start(f32[64,128]{1,0:T(8,128)S(1)} %add.31), channel_id=1, source_target_pairs={{0,24},{2,26},{4,28},{6,30},{8,16},{10,18},{12,20},{14,22},{16,8},... | collective-permute-start | bytes 98312 | tf_op jit(solution)/shard_map/ppermute | solution.py:210
  53.1 2.6 %collective-permute-start.17 = (f32[64,128]{1,0:T(8,128)S(1)}, f32[64,128]{1,0:T(8,128)S(1)}, u32[]{:S(2)}, u32[]{:S(2)}) collective-permute-start(f32[64,128]{1,0:T(8,128)S(1)} %add.31), channel_id=1, source_target_pairs={{0,8},{2,10},{4,12},{6,14},{8,0},{10,2},{12,4},{14,6},{16,24},{18,... | collective-permute-start | bytes 98312 | tf_op jit(solution)/shard_map/ppermute | solution.py:210
  55.7 3.4 %shard_map.119 = (f32[64,64]{1,0:T(8,128)S(1)}, f32[64,128]{1,0:T(8,128)S(1)}) custom-call(f32[64,128]{1,0:T(8,128)S(1)} %get-tuple-element.91.refs_0_, f32[64,128]{1,0:T(8,128)S(1)} %collective-permute-done.20.refs_1_), custom_call_target="tpu_custom_call" | custom-call | tf_op jit(solution)/shard_map/pallas_call | solution.py:20
  59.2 1.6 %collective-permute-start.23 = (f32[256,128]{1,0:T(8,128)S(1)}, f32[256,128]{1,0:T(8,128)S(1)}, u32[]{:S(2)}, u32[]{:S(2)}) collective-permute-start(f32[256,128]{1,0:T(8,128)S(1)} %constant_dynamic-update-slice_fusion.4.refs_0_), channel_id=1, source_target_pairs={{0,6},{2,4},{4,2},{6,0},{8,14},{10,12},{12,10},{14,8},{16,22},{18,... | collective-permute-start | bytes 393224 | tf_op jit(solution)/shard_map/ppermute | solution.py:210
  60.8 1.3 %collective-permute-start.22 = (f32[256,128]{1,0:T(8,128)S(1)}, f32[256,128]{1,0:T(8,128)S(1)}, u32[]{:S(2)}, u32[]{:S(2)}) collective-permute-start(f32[256,128]{1,0:T(8,128)S(1)} %constant_dynamic-update-slice_fusion.4.refs_0_), channel_id=1, source_target_pairs={{0,4},{2,6},{4,0},{6,2},{8,12},{10,14},{12,8},{14,10},{16,20},{18,... | collective-permute-start | bytes 393224 | tf_op jit(solution)/shard_map/ppermute | solution.py:210
  62.1 0.6 collective-permute-start.21
  62.7 1.2 %shard_map.120 = (f32[64,2048]{1,0:T(8,128)S(1)}, bf16[64,2048]{1,0:T(8,128)(2,1)S(1)}, f32[64,128]{1,0:T(8,128)}, f32[64,128]{1,0:T(8,128)}) custom-call(f32[64,64]{1,0:T(8,128)S(1)} %get-tuple-element.93.inverse_ref.refs_2_, f32[64,128]{1,0:T(8,128)S(1)} %get-tuple-element.94.scale_ref, bf16[192,2176]{1,0:T(8,128)(2,1)S(1)} %get-tuple-element.88.stack_ref, ...), custom_call_target="tpu_custom_call" | custom-call | tf_op jit(solution)/shard_map/pallas_call | solution.py:20
  63.9 2.6 %collective-permute-done.23.refs_3_ = f32[256,128]{1,0:T(8,128)S(1)} collective-permute-done((f32[256,128]{1,0:T(8,128)S(1)}, f32[256,128]{1,0:T(8,128)S(1)}, u32[]{:S(2)}, u32[]{:S(2)}) %collective-permute-start.23) | collective-permute-done | bytes 131104 | tf_op jit(solution)/shard_map/ppermute | solution.py:210
  66.5 1.2 %collective-permute-done.22.refs_2_ = f32[256,128]{1,0:T(8,128)S(1)} collective-permute-done((f32[256,128]{1,0:T(8,128)S(1)}, f32[256,128]{1,0:T(8,128)S(1)}, u32[]{:S(2)}, u32[]{:S(2)}) %collective-permute-start.22) | collective-permute-done | bytes 131104 | tf_op jit(solution)/shard_map/ppermute | solution.py:210
  67.7 0.6 shard_map.121
  68.4 1.2 %collective-permute-done.24.refs_1_ = f32[64,64]{1,0:T(8,128)S(1)} collective-permute-done((f32[64,64]{1,0:T(8,128)S(1)}, f32[64,64]{1,0:T(8,128)S(1)}, u32[]{:S(2)}, u32[]{:S(2)}) %collective-permute-start.24) | collective-permute-done | bytes 16416 | tf_op jit(solution)/shard_map/ppermute | solution.py:210
  69.6 1.5 %shard_map.122 = (f32[64,2048]{1,0:T(8,128)S(1)}, f32[64,128]{1,0:T(8,128)S(1)}, f32[64,64]{1,0:T(8,128)}, f32[64,128]{1,0:T(8,128)}) custom-call(f32[64,64]{1,0:T(8,128)S(1)} %get-tuple-element.101.refs_0_, f32[64,64]{1,0:T(8,128)S(1)} %collective-permute-done.24.refs_1_, f32[64,64]{1,0:T(8,128)S(1)} %get-tuple-element.93.inverse_ref.refs_2_, ...), custom_call_target="tpu_custom_call" | custom-call | tf_op jit(solution)/shard_map/pallas_call | solution.py:20
  71.2 1.0 %collective-permute-done.25.refs_1_ = f32[64,128]{1,0:T(8,128)S(1)} collective-permute-done((f32[64,128]{1,0:T(8,128)S(1)}, f32[64,128]{1,0:T(8,128)S(1)}, u32[]{:S(2)}, u32[]{:S(2)}) %collective-permute-start.25) | collective-permute-done | bytes 32800 | tf_op jit(solution)/shard_map/ppermute | solution.py:210
  72.3 1.5 %shard_map.123 = (bf16[192,2176]{1,0:T(8,128)(2,1)S(1)}, f32[64,128]{1,0:T(8,128)S(1)}, f32[64,128]{1,0:T(8,128)S(1)}) custom-call(s32[2,16]{1,0:T(2,128)S(1)} %compare_select_fusion.slots_ref.s, s32[1]{0:T(128)} %bitcast.2.place_ref.p, bf16[2,16,128,128]{3,2,1,0:T(8,128)(2,1)S(1)} %bitcast.27, f32[64,192]{1,0:T(8,128)S(1)} %get-tuple-element.129.m.mix_ref, ...), custom_call_target="tpu_custom_call" | custom-call | tf_op jit(solution)/shard_map/pallas_call | solution.py:20
  73.8 0.2 collective-permute-start.26
  74.0 1.3 %shard_map.124 = (f32[64,128]{1,0:T(8,128)S(1)}, f32[64,2048]{1,0:T(8,128)S(1)}) custom-call(bf16[192,2176]{1,0:T(8,128)(2,1)S(1)} %get-tuple-element.108.stack_ref, f32[64,192]{1,0:T(8,128)S(1)} %get-tuple-element.129.m.mix_ref, f32[64,128]{1,0:T(8,128)S(1)} %get-tuple-element.131.search_ref), custom_call_target="tpu_custom_call" | custom-call | tf_op jit(solution)/shard_map/pallas_call | solution.py:20
  75.4 0.4 collective-permute-start.30
  75.8 1.6 %collective-permute-start.29 = (f32[64,128]{1,0:T(8,128)S(1)}, f32[64,128]{1,0:T(8,128)S(1)}, u32[]{:S(2)}, u32[]{:S(2)}) collective-permute-start(f32[64,128]{1,0:T(8,128)S(1)} %add.32), channel_id=1, source_target_pairs={{0,24},{2,26},{4,28},{6,30},{8,16},{10,18},{12,20},{14,22},{16,8},... | collective-permute-start | bytes 98312 | tf_op jit(solution)/shard_map/ppermute | solution.py:210
  77.5 2.6 %collective-permute-start.27 = (f32[64,128]{1,0:T(8,128)S(1)}, f32[64,128]{1,0:T(8,128)S(1)}, u32[]{:S(2)}, u32[]{:S(2)}) collective-permute-start(f32[64,128]{1,0:T(8,128)S(1)} %add.32), channel_id=1, source_target_pairs={{0,8},{2,10},{4,12},{6,14},{8,0},{10,2},{12,4},{14,6},{16,24},{18,... | collective-permute-start | bytes 98312 | tf_op jit(solution)/shard_map/ppermute | solution.py:210
  80.2 3.4 %shard_map.125 = (f32[64,64]{1,0:T(8,128)S(1)}, f32[64,128]{1,0:T(8,128)S(1)}) custom-call(f32[64,128]{1,0:T(8,128)S(1)} %get-tuple-element.111.refs_0_, f32[64,128]{1,0:T(8,128)S(1)} %collective-permute-done.30.refs_1_), custom_call_target="tpu_custom_call" | custom-call | tf_op jit(solution)/shard_map/pallas_call | solution.py:20
  83.6 1.6 %collective-permute-start.33 = (f32[256,128]{1,0:T(8,128)S(1)}, f32[256,128]{1,0:T(8,128)S(1)}, u32[]{:S(2)}, u32[]{:S(2)}) collective-permute-start(f32[256,128]{1,0:T(8,128)S(1)} %constant_dynamic-update-slice_fusion.8.refs_0_), channel_id=1, source_target_pairs={{0,6},{2,4},{4,2},{6,0},{8,14},{10,12},{12,10},{14,8},{16,22},{18,... | collective-permute-start | bytes 393224 | tf_op jit(solution)/shard_map/ppermute | solution.py:210
  85.3 1.3 %collective-permute-start.32 = (f32[256,128]{1,0:T(8,128)S(1)}, f32[256,128]{1,0:T(8,128)S(1)}, u32[]{:S(2)}, u32[]{:S(2)}) collective-permute-start(f32[256,128]{1,0:T(8,128)S(1)} %constant_dynamic-update-slice_fusion.8.refs_0_), channel_id=1, source_target_pairs={{0,4},{2,6},{4,0},{6,2},{8,12},{10,14},{12,8},{14,10},{16,20},{18,... | collective-permute-start | bytes 393224 | tf_op jit(solution)/shard_map/ppermute | solution.py:210
  86.6 0.6 collective-permute-start.31
  87.2 1.2 %shard_map.126 = (f32[64,2048]{1,0:T(8,128)S(1)}, bf16[64,2048]{1,0:T(8,128)(2,1)}, f32[64,128]{1,0:T(8,128)}, f32[64,128]{1,0:T(8,128)}) custom-call(f32[64,64]{1,0:T(8,128)S(1)} %get-tuple-element.113.inverse_ref.refs_2_, f32[64,128]{1,0:T(8,128)S(1)} %get-tuple-element.114.scale_ref, bf16[192,2176]{1,0:T(8,128)(2,1)S(1)} %get-tuple-element.108.stack_ref, ...), custom_call_target="tpu_custom_call" | custom-call | tf_op jit(solution)/shard_map/pallas_call | solution.py:20
  88.4 2.5 %collective-permute-done.33.refs_3_ = f32[256,128]{1,0:T(8,128)S(1)} collective-permute-done((f32[256,128]{1,0:T(8,128)S(1)}, f32[256,128]{1,0:T(8,128)S(1)}, u32[]{:S(2)}, u32[]{:S(2)}) %collective-permute-start.33) | collective-permute-done | bytes 131104 | tf_op jit(solution)/shard_map/ppermute | solution.py:210
  90.9 1.3 %collective-permute-done.32.refs_2_ = f32[256,128]{1,0:T(8,128)S(1)} collective-permute-done((f32[256,128]{1,0:T(8,128)S(1)}, f32[256,128]{1,0:T(8,128)S(1)}, u32[]{:S(2)}, u32[]{:S(2)}) %collective-permute-start.32) | collective-permute-done | bytes 131104 | tf_op jit(solution)/shard_map/ppermute | solution.py:210
  92.2 0.6 shard_map.127
  92.8 1.2 %collective-permute-done.34.refs_1_ = f32[64,64]{1,0:T(8,128)S(1)} collective-permute-done((f32[64,64]{1,0:T(8,128)S(1)}, f32[64,64]{1,0:T(8,128)S(1)}, u32[]{:S(2)}, u32[]{:S(2)}) %collective-permute-start.34) | collective-permute-done | bytes 16416 | tf_op jit(solution)/shard_map/ppermute | solution.py:210
  94.0 2.0 %shard_map.128 = (f32[64,2048]{1,0:T(8,128)}, f32[64,128]{1,0:T(8,128)S(1)}, f32[64,64]{1,0:T(8,128)}, f32[64,128]{1,0:T(8,128)S(1)}) custom-call(f32[64,64]{1,0:T(8,128)S(1)} %get-tuple-element.122.refs_0_, f32[64,64]{1,0:T(8,128)S(1)} %collective-permute-done.34.refs_1_, f32[64,64]{1,0:T(8,128)S(1)} %get-tuple-element.113.inverse_ref.refs_2_, ...), custom_call_target="tpu_custom_call" | custom-call | tf_op jit(solution)/shard_map/pallas_call | solution.py:20
  96.2 1.0 %collective-permute-done.35 = f32[64,128]{1,0:T(8,128)S(1)} collective-permute-done((f32[64,128]{1,0:T(8,128)S(1)}, f32[64,128]{1,0:T(8,128)S(1)}, u32[]{:S(2)}, u32[]{:S(2)}) %collective-permute-start.35) | collective-permute-done | bytes 32800 | tf_op jit(solution)/shard_map/ppermute | solution.py:210
  97.2 0.6 rsqrt_multiply_fusion
  (57 shorter events, 1.6 us)
Async XLA Ops:
  1.4 7.3 %collective-permute-start.2 = (bf16[1,192,128]{2,1,0:T(8,128)(2,1)S(1)}, bf16[1,192,128]{2,1,0:T(8,128)(2,1)S(1)}, u32[]{:S(2)}, u32[]{:S(2)}) collective-permute-start(bf16[1,192,128]{2,1,0:T(8,128)(2,1)S(1)} %maximum_bitcast_fusion), channel_id=1, source_target_pairs={{0,24},{2,26},{4,28},{6,30},{8,16},{10,18},{12,20},{14,22},{16,8},... | collective-permute-start | bytes 147464 | tf_op jit(solution)/shard_map/ppermute | solution.py:210
  6.4 5.0 %collective-permute-start.1 = (bf16[1,192,128]{2,1,0:T(8,128)(2,1)S(1)}, bf16[1,192,128]{2,1,0:T(8,128)(2,1)S(1)}, u32[]{:S(2)}, u32[]{:S(2)}) collective-permute-start(bf16[1,192,128]{2,1,0:T(8,128)(2,1)S(1)} %maximum_bitcast_fusion), channel_id=1, source_target_pairs={{0,16},{2,18},{4,20},{6,22},{8,24},{10,26},{12,28},{14,30},{16,0},... | collective-permute-start | bytes 147464 | tf_op jit(solution)/shard_map/ppermute | solution.py:210
  6.4 5.0 %collective-permute-start = (bf16[1,192,128]{2,1,0:T(8,128)(2,1)S(1)}, bf16[1,192,128]{2,1,0:T(8,128)(2,1)S(1)}, u32[]{:S(2)}, u32[]{:S(2)}) collective-permute-start(bf16[1,192,128]{2,1,0:T(8,128)(2,1)S(1)} %maximum_bitcast_fusion), channel_id=1, source_target_pairs={{0,8},{2,10},{4,12},{6,14},{8,0},{10,2},{12,4},{14,6},{16,24},{18,... | collective-permute-start | bytes 147464 | tf_op jit(solution)/shard_map/ppermute | solution.py:210
  11.5 3.6 %copy-start.3 = (s32[1,1,2,16]{3,2,1,0:T(2,128)S(1)}, s32[1,1,2,16]{3,2,1,0:T(2,128)}, u32[]{:S(2)}) copy-start(s32[1,1,2,16]{3,2,1,0:T(2,128)} %param.10) | copy-start | bytes 388
  11.5 3.6 %copy-start.4 = (s32[1,1,2]{2,1,0:T(1,128)S(1)}, s32[1,1,2]{2,1,0:T(1,128)}, u32[]{:S(2)}) copy-start(s32[1,1,2]{2,1,0:T(1,128)} %param.9) | copy-start | bytes 28
  11.5 8.5 %collective-permute-start.5 = (bf16[4,192,128]{2,1,0:T(8,128)(2,1)S(1)}, bf16[4,192,128]{2,1,0:T(8,128)(2,1)S(1)}, u32[]{:S(2)}, u32[]{:S(2)}) collective-permute-start(bf16[4,192,128]{2,1,0:T(8,128)(2,1)S(1)} %pad_maximum_fusion.refs_0_), channel_id=1, source_target_pairs={{0,6},{2,4},{4,2},{6,0},{8,14},{10,12},{12,10},{14,8},{16,22},{18,... | collective-permute-start | bytes 589832 | tf_op jit(solution)/shard_map/ppermute | solution.py:210
  14.0 8.4 %collective-permute-start.4 = (bf16[4,192,128]{2,1,0:T(8,128)(2,1)S(1)}, bf16[4,192,128]{2,1,0:T(8,128)(2,1)S(1)}, u32[]{:S(2)}, u32[]{:S(2)}) collective-permute-start(bf16[4,192,128]{2,1,0:T(8,128)(2,1)S(1)} %pad_maximum_fusion.refs_0_), channel_id=1, source_target_pairs={{0,4},{2,6},{4,0},{6,2},{8,12},{10,14},{12,8},{14,10},{16,20},{18,... | collective-permute-start | bytes 589832 | tf_op jit(solution)/shard_map/ppermute | solution.py:210
  14.5 8.0 %collective-permute-start.3 = (bf16[4,192,128]{2,1,0:T(8,128)(2,1)S(1)}, bf16[4,192,128]{2,1,0:T(8,128)(2,1)S(1)}, u32[]{:S(2)}, u32[]{:S(2)}) collective-permute-start(bf16[4,192,128]{2,1,0:T(8,128)(2,1)S(1)} %pad_maximum_fusion.refs_0_), channel_id=1, source_target_pairs={{0,2},{2,0},{4,6},{6,4},{8,10},{10,8},{12,14},{14,12},{16,18},{18,... | collective-permute-start | bytes 589832 | tf_op jit(solution)/shard_map/ppermute | solution.py:210
  22.5 1.2 %copy-start = (bf16[1,1,2,16,128,128]{5,4,3,2,1,0:T(8,128)(2,1)S(1)}, bf16[1,1,2,16,128,128]{5,4,3,2,1,0:T(8,128)(2,1)}, u32[]{:S(2)}) copy-start(bf16[1,1,2,16,128,128]{5,4,3,2,1,0:T(8,128)(2,1)} %param.8) | copy-start | bytes 3145732
  23.7 1.6 %copy-start.2 = (f32[3,64,128]{2,1,0:T(8,128)S(1)}, f32[3,64,128]{2,1,0:T(8,128)}, u32[]{:S(2)}) copy-start(f32[3,64,128]{2,1,0:T(8,128)} %param.15) | copy-start | bytes 294916
  25.3 1.3 %collective-permute-start.6 = (f32[64,128]{1,0:T(8,128)S(1)}, f32[64,128]{1,0:T(8,128)S(1)}, u32[]{:S(2)}, u32[]{:S(2)}) collective-permute-start(f32[64,128]{1,0:T(8,128)S(1)} %get-tuple-element.67), channel_id=1, source_target_pairs={{0,1},{1,0},{2,3},{3,2},{4,5},{5,4},{6,7},{7,6},{8,9},{9,8},{10,11... | collective-permute-start | bytes 98312 | tf_op jit(solution)/shard_map/ppermute | solution.py:210
  26.6 4.9 %collective-permute-start.10 = (f32[64,128]{1,0:T(8,128)S(1)}, f32[64,128]{1,0:T(8,128)S(1)}, u32[]{:S(2)}, u32[]{:S(2)}) collective-permute-start(f32[64,128]{1,0:T(8,128)S(1)} %get-tuple-element.71.refs_0_), channel_id=1, source_target_pairs={{0,1},{1,0},{2,3},{3,2},{4,5},{5,4},{6,7},{7,6},{8,9},{9,8},{10,11... | collective-permute-start | bytes 98312 | tf_op jit(solution)/shard_map/ppermute | solution.py:210
  27.1 7.8 %collective-permute-start.9 = (f32[64,128]{1,0:T(8,128)S(1)}, f32[64,128]{1,0:T(8,128)S(1)}, u32[]{:S(2)}, u32[]{:S(2)}) collective-permute-start(f32[64,128]{1,0:T(8,128)S(1)} %add.30), channel_id=1, source_target_pairs={{0,24},{2,26},{4,28},{6,30},{8,16},{10,18},{12,20},{14,22},{16,8},... | collective-permute-start | bytes 98312 | tf_op jit(solution)/shard_map/ppermute | solution.py:210
  28.7 6.2 %collective-permute-start.8 = (f32[64,128]{1,0:T(8,128)S(1)}, f32[64,128]{1,0:T(8,128)S(1)}, u32[]{:S(2)}, u32[]{:S(2)}) collective-permute-start(f32[64,128]{1,0:T(8,128)S(1)} %add.30), channel_id=1, source_target_pairs={{0,16},{2,18},{4,20},{6,22},{8,24},{10,26},{12,28},{14,30},{16,0},... | collective-permute-start | bytes 98312 | tf_op jit(solution)/shard_map/ppermute | solution.py:210
  29.2 5.6 %collective-permute-start.7 = (f32[64,128]{1,0:T(8,128)S(1)}, f32[64,128]{1,0:T(8,128)S(1)}, u32[]{:S(2)}, u32[]{:S(2)}) collective-permute-start(f32[64,128]{1,0:T(8,128)S(1)} %add.30), channel_id=1, source_target_pairs={{0,8},{2,10},{4,12},{6,14},{8,0},{10,2},{12,4},{14,6},{16,24},{18,... | collective-permute-start | bytes 98312 | tf_op jit(solution)/shard_map/ppermute | solution.py:210
  34.9 7.3 %collective-permute-start.13 = (f32[256,128]{1,0:T(8,128)S(1)}, f32[256,128]{1,0:T(8,128)S(1)}, u32[]{:S(2)}, u32[]{:S(2)}) collective-permute-start(f32[256,128]{1,0:T(8,128)S(1)} %constant_dynamic-update-slice_fusion.refs_0_), channel_id=1, source_target_pairs={{0,6},{2,4},{4,2},{6,0},{8,14},{10,12},{12,10},{14,8},{16,22},{18,... | collective-permute-start | bytes 393224 | tf_op jit(solution)/shard_map/ppermute | solution.py:210
  36.6 6.7 %collective-permute-start.12 = (f32[256,128]{1,0:T(8,128)S(1)}, f32[256,128]{1,0:T(8,128)S(1)}, u32[]{:S(2)}, u32[]{:S(2)}) collective-permute-start(f32[256,128]{1,0:T(8,128)S(1)} %constant_dynamic-update-slice_fusion.refs_0_), channel_id=1, source_target_pairs={{0,4},{2,6},{4,0},{6,2},{8,12},{10,14},{12,8},{14,10},{16,20},{18,... | collective-permute-start | bytes 393224 | tf_op jit(solution)/shard_map/ppermute | solution.py:210
  38.0 5.5 %collective-permute-start.11 = (f32[256,128]{1,0:T(8,128)S(1)}, f32[256,128]{1,0:T(8,128)S(1)}, u32[]{:S(2)}, u32[]{:S(2)}) collective-permute-start(f32[256,128]{1,0:T(8,128)S(1)} %constant_dynamic-update-slice_fusion.refs_0_), channel_id=1, source_target_pairs={{0,2},{2,0},{4,6},{6,4},{8,10},{10,8},{12,14},{14,12},{16,18},{18,... | collective-permute-start | bytes 393224 | tf_op jit(solution)/shard_map/ppermute | solution.py:210
  43.5 4.6 %copy-start.1 = (bf16[1,1,2,16,128,128]{5,4,3,2,1,0:T(8,128)(2,1)S(1)}, bf16[1,1,2,16,128,128]{5,4,3,2,1,0:T(8,128)(2,1)}, u32[]{:S(2)}) copy-start(bf16[1,1,2,16,128,128]{5,4,3,2,1,0:T(8,128)(2,1)} %param.8) | copy-start | bytes 3145732
  44.0 1.3 %collective-permute-start.14 = (f32[64,64]{1,0:T(8,128)S(1)}, f32[64,64]{1,0:T(8,128)S(1)}, u32[]{:S(2)}, u32[]{:S(2)}) collective-permute-start(f32[64,64]{1,0:T(8,128)S(1)} %get-tuple-element.81.refs_0_), channel_id=1, source_target_pairs={{0,1},{1,0},{2,3},{3,2},{4,5},{5,4},{6,7},{7,6},{8,9},{9,8},{10,11... | collective-permute-start | bytes 49160 | tf_op jit(solution)/shard_map/ppermute | solution.py:210
  46.8 1.2 %collective-permute-start.15 = (f32[64,128]{1,0:T(8,128)S(1)}, f32[64,128]{1,0:T(8,128)S(1)}, u32[]{:S(2)}, u32[]{:S(2)}) collective-permute-start(f32[64,128]{1,0:T(8,128)S(1)} %get-tuple-element.84.refs_0_), channel_id=1, source_target_pairs={{0,1},{1,0},{2,3},{3,2},{4,5},{5,4},{6,7},{7,6},{8,9},{9,8},{10,11... | collective-permute-start | bytes 98312 | tf_op jit(solution)/shard_map/ppermute | solution.py:210
  49.5 1.4 %collective-permute-start.16 = (f32[64,128]{1,0:T(8,128)S(1)}, f32[64,128]{1,0:T(8,128)S(1)}, u32[]{:S(2)}, u32[]{:S(2)}) collective-permute-start(f32[64,128]{1,0:T(8,128)S(1)} %get-tuple-element.87), channel_id=1, source_target_pairs={{0,1},{1,0},{2,3},{3,2},{4,5},{5,4},{6,7},{7,6},{8,9},{9,8},{10,11... | collective-permute-start | bytes 98312 | tf_op jit(solution)/shard_map/ppermute | solution.py:210
  50.9 4.8 %collective-permute-start.20 = (f32[64,128]{1,0:T(8,128)S(1)}, f32[64,128]{1,0:T(8,128)S(1)}, u32[]{:S(2)}, u32[]{:S(2)}) collective-permute-start(f32[64,128]{1,0:T(8,128)S(1)} %get-tuple-element.91.refs_0_), channel_id=1, source_target_pairs={{0,1},{1,0},{2,3},{3,2},{4,5},{5,4},{6,7},{7,6},{8,9},{9,8},{10,11... | collective-permute-start | bytes 98312 | tf_op jit(solution)/shard_map/ppermute | solution.py:210
  51.3 7.8 %collective-permute-start.19 = (f32[64,128]{1,0:T(8,128)S(1)}, f32[64,128]{1,0:T(8,128)S(1)}, u32[]{:S(2)}, u32[]{:S(2)}) collective-permute-start(f32[64,128]{1,0:T(8,128)S(1)} %add.31), channel_id=1, source_target_pairs={{0,24},{2,26},{4,28},{6,30},{8,16},{10,18},{12,20},{14,22},{16,8},... | collective-permute-start | bytes 98312 | tf_op jit(solution)/shard_map/ppermute | solution.py:210
  52.9 6.2 %collective-permute-start.18 = (f32[64,128]{1,0:T(8,128)S(1)}, f32[64,128]{1,0:T(8,128)S(1)}, u32[]{:S(2)}, u32[]{:S(2)}) collective-permute-start(f32[64,128]{1,0:T(8,128)S(1)} %add.31), channel_id=1, source_target_pairs={{0,16},{2,18},{4,20},{6,22},{8,24},{10,26},{12,28},{14,30},{16,0},... | collective-permute-start | bytes 98312 | tf_op jit(solution)/shard_map/ppermute | solution.py:210
  53.1 6.0 %collective-permute-start.17 = (f32[64,128]{1,0:T(8,128)S(1)}, f32[64,128]{1,0:T(8,128)S(1)}, u32[]{:S(2)}, u32[]{:S(2)}) collective-permute-start(f32[64,128]{1,0:T(8,128)S(1)} %add.31), channel_id=1, source_target_pairs={{0,8},{2,10},{4,12},{6,14},{8,0},{10,2},{12,4},{14,6},{16,24},{18,... | collective-permute-start | bytes 98312 | tf_op jit(solution)/shard_map/ppermute | solution.py:210
  59.2 7.3 %collective-permute-start.23 = (f32[256,128]{1,0:T(8,128)S(1)}, f32[256,128]{1,0:T(8,128)S(1)}, u32[]{:S(2)}, u32[]{:S(2)}) collective-permute-start(f32[256,128]{1,0:T(8,128)S(1)} %constant_dynamic-update-slice_fusion.4.refs_0_), channel_id=1, source_target_pairs={{0,6},{2,4},{4,2},{6,0},{8,14},{10,12},{12,10},{14,8},{16,22},{18,... | collective-permute-start | bytes 393224 | tf_op jit(solution)/shard_map/ppermute | solution.py:210
  60.8 6.9 %collective-permute-start.22 = (f32[256,128]{1,0:T(8,128)S(1)}, f32[256,128]{1,0:T(8,128)S(1)}, u32[]{:S(2)}, u32[]{:S(2)}) collective-permute-start(f32[256,128]{1,0:T(8,128)S(1)} %constant_dynamic-update-slice_fusion.4.refs_0_), channel_id=1, source_target_pairs={{0,4},{2,6},{4,0},{6,2},{8,12},{10,14},{12,8},{14,10},{16,20},{18,... | collective-permute-start | bytes 393224 | tf_op jit(solution)/shard_map/ppermute | solution.py:210
  62.1 5.6 %collective-permute-start.21 = (f32[256,128]{1,0:T(8,128)S(1)}, f32[256,128]{1,0:T(8,128)S(1)}, u32[]{:S(2)}, u32[]{:S(2)}) collective-permute-start(f32[256,128]{1,0:T(8,128)S(1)} %constant_dynamic-update-slice_fusion.4.refs_0_), channel_id=1, source_target_pairs={{0,2},{2,0},{4,6},{6,4},{8,10},{10,8},{12,14},{14,12},{16,18},{18,... | collective-permute-start | bytes 393224 | tf_op jit(solution)/shard_map/ppermute | solution.py:210
  68.3 1.3 %collective-permute-start.24 = (f32[64,64]{1,0:T(8,128)S(1)}, f32[64,64]{1,0:T(8,128)S(1)}, u32[]{:S(2)}, u32[]{:S(2)}) collective-permute-start(f32[64,64]{1,0:T(8,128)S(1)} %get-tuple-element.101.refs_0_), channel_id=1, source_target_pairs={{0,1},{1,0},{2,3},{3,2},{4,5},{5,4},{6,7},{7,6},{8,9},{9,8},{10,11... | collective-permute-start | bytes 49160 | tf_op jit(solution)/shard_map/ppermute | solution.py:210
  71.1 1.2 %collective-permute-start.25 = (f32[64,128]{1,0:T(8,128)S(1)}, f32[64,128]{1,0:T(8,128)S(1)}, u32[]{:S(2)}, u32[]{:S(2)}) collective-permute-start(f32[64,128]{1,0:T(8,128)S(1)} %get-tuple-element.104.refs_0_), channel_id=1, source_target_pairs={{0,1},{1,0},{2,3},{3,2},{4,5},{5,4},{6,7},{7,6},{8,9},{9,8},{10,11... | collective-permute-start | bytes 98312 | tf_op jit(solution)/shard_map/ppermute | solution.py:210
  73.8 1.6 %collective-permute-start.26 = (f32[64,128]{1,0:T(8,128)S(1)}, f32[64,128]{1,0:T(8,128)S(1)}, u32[]{:S(2)}, u32[]{:S(2)}) collective-permute-start(f32[64,128]{1,0:T(8,128)S(1)} %get-tuple-element.107), channel_id=1, source_target_pairs={{0,1},{1,0},{2,3},{3,2},{4,5},{5,4},{6,7},{7,6},{8,9},{9,8},{10,11... | collective-permute-start | bytes 98312 | tf_op jit(solution)/shard_map/ppermute | solution.py:210
  75.4 4.8 %collective-permute-start.30 = (f32[64,128]{1,0:T(8,128)S(1)}, f32[64,128]{1,0:T(8,128)S(1)}, u32[]{:S(2)}, u32[]{:S(2)}) collective-permute-start(f32[64,128]{1,0:T(8,128)S(1)} %get-tuple-element.111.refs_0_), channel_id=1, source_target_pairs={{0,1},{1,0},{2,3},{3,2},{4,5},{5,4},{6,7},{7,6},{8,9},{9,8},{10,11... | collective-permute-start | bytes 98312 | tf_op jit(solution)/shard_map/ppermute | solution.py:210
  75.8 7.8 %collective-permute-start.29 = (f32[64,128]{1,0:T(8,128)S(1)}, f32[64,128]{1,0:T(8,128)S(1)}, u32[]{:S(2)}, u32[]{:S(2)}) collective-permute-start(f32[64,128]{1,0:T(8,128)S(1)} %add.32), channel_id=1, source_target_pairs={{0,24},{2,26},{4,28},{6,30},{8,16},{10,18},{12,20},{14,22},{16,8},... | collective-permute-start | bytes 98312 | tf_op jit(solution)/shard_map/ppermute | solution.py:210
  77.4 6.2 %collective-permute-start.28 = (f32[64,128]{1,0:T(8,128)S(1)}, f32[64,128]{1,0:T(8,128)S(1)}, u32[]{:S(2)}, u32[]{:S(2)}) collective-permute-start(f32[64,128]{1,0:T(8,128)S(1)} %add.32), channel_id=1, source_target_pairs={{0,16},{2,18},{4,20},{6,22},{8,24},{10,26},{12,28},{14,30},{16,0},... | collective-permute-start | bytes 98312 | tf_op jit(solution)/shard_map/ppermute | solution.py:210
  77.5 6.0 %collective-permute-start.27 = (f32[64,128]{1,0:T(8,128)S(1)}, f32[64,128]{1,0:T(8,128)S(1)}, u32[]{:S(2)}, u32[]{:S(2)}) collective-permute-start(f32[64,128]{1,0:T(8,128)S(1)} %add.32), channel_id=1, source_target_pairs={{0,8},{2,10},{4,12},{6,14},{8,0},{10,2},{12,4},{14,6},{16,24},{18,... | collective-permute-start | bytes 98312 | tf_op jit(solution)/shard_map/ppermute | solution.py:210
  83.6 7.3 %collective-permute-start.33 = (f32[256,128]{1,0:T(8,128)S(1)}, f32[256,128]{1,0:T(8,128)S(1)}, u32[]{:S(2)}, u32[]{:S(2)}) collective-permute-start(f32[256,128]{1,0:T(8,128)S(1)} %constant_dynamic-update-slice_fusion.8.refs_0_), channel_id=1, source_target_pairs={{0,6},{2,4},{4,2},{6,0},{8,14},{10,12},{12,10},{14,8},{16,22},{18,... | collective-permute-start | bytes 393224 | tf_op jit(solution)/shard_map/ppermute | solution.py:210
  85.3 6.9 %collective-permute-start.32 = (f32[256,128]{1,0:T(8,128)S(1)}, f32[256,128]{1,0:T(8,128)S(1)}, u32[]{:S(2)}, u32[]{:S(2)}) collective-permute-start(f32[256,128]{1,0:T(8,128)S(1)} %constant_dynamic-update-slice_fusion.8.refs_0_), channel_id=1, source_target_pairs={{0,4},{2,6},{4,0},{6,2},{8,12},{10,14},{12,8},{14,10},{16,20},{18,... | collective-permute-start | bytes 393224 | tf_op jit(solution)/shard_map/ppermute | solution.py:210
  86.6 5.6 %collective-permute-start.31 = (f32[256,128]{1,0:T(8,128)S(1)}, f32[256,128]{1,0:T(8,128)S(1)}, u32[]{:S(2)}, u32[]{:S(2)}) collective-permute-start(f32[256,128]{1,0:T(8,128)S(1)} %constant_dynamic-update-slice_fusion.8.refs_0_), channel_id=1, source_target_pairs={{0,2},{2,0},{4,6},{6,4},{8,10},{10,8},{12,14},{14,12},{16,18},{18,... | collective-permute-start | bytes 393224 | tf_op jit(solution)/shard_map/ppermute | solution.py:210
  92.7 1.3 %collective-permute-start.34 = (f32[64,64]{1,0:T(8,128)S(1)}, f32[64,64]{1,0:T(8,128)S(1)}, u32[]{:S(2)}, u32[]{:S(2)}) collective-permute-start(f32[64,64]{1,0:T(8,128)S(1)} %get-tuple-element.122.refs_0_), channel_id=1, source_target_pairs={{0,1},{1,0},{2,3},{3,2},{4,5},{5,4},{6,7},{7,6},{8,9},{9,8},{10,11... | collective-permute-start | bytes 49160 | tf_op jit(solution)/shard_map/ppermute | solution.py:210
  96.0 1.2 %collective-permute-start.35 = (f32[64,128]{1,0:T(8,128)S(1)}, f32[64,128]{1,0:T(8,128)S(1)}, u32[]{:S(2)}, u32[]{:S(2)}) collective-permute-start(f32[64,128]{1,0:T(8,128)S(1)} %get-tuple-element.125), channel_id=1, source_target_pairs={{0,1},{1,0},{2,3},{3,2},{4,5},{5,4},{6,7},{7,6},{8,9},{9,8},{10,11... | collective-permute-start | bytes 98312 | tf_op jit(solution)/shard_map/ppermute | solution.py:210

commit v3 on v2

--- a/solution.py
+++ b/solution.py
@@ -101,11 +101,10 @@
 
 def next_kernel(nodes, many, slots_ref, place_ref, tiles_ref, mix_ref, basis_ref, raw_ref, sqs, dirs_ref, stack_ref, *mine_refs):
     edge = tiles_ref.shape[2]
-    vecs = basis_ref.shape[0]
-    wide = basis_ref.shape[1]
+    vecs, wide = raw_ref.shape
     square = sum(ref[...] for ref in sqs)[:, :1] / nodes
     scale = lax.rsqrt(square + epsilon)
-    stack_ref[:vecs, :wide] = basis_ref[...].astype(bf16)
+    stack_ref[:vecs, :wide] = basis_ref[:vecs]
     stack_ref[vecs : 2 * vecs, :wide] = (raw_ref[...] * scale).astype(bf16)
     stack_ref[2 * vecs :, :wide] = dirs_ref[...]
     stack_ref[:, wide : wide + edge] = jnp.zeros((3 * vecs, edge), bf16)
@@ -175,30 +174,46 @@
     dirs_ref[...] = dirs.astype(bf16)
     own_dirs[...] = dirs[:, :edge]
     basis = times_stack(dot_nn(inverse_ref[...], mix_ref[...]), stack_ref[:, :wide])
-    basis_ref[...] = basis
+    basis_ref[...] = pieces(basis)
     own_basis[...] = basis[:, :edge]
 
 
-def cross_kernel(parts, *refs):
+def solve_kernel(parts, *refs):
+    part_refs, inverse_ref, blocks_ref, own_ref = refs[:parts], refs[parts], refs[parts + 1], refs[parts + 2]
+    vecs, edge = own_ref.shape
+    solved = dot_nn(inverse_ref[...], jnp.concatenate([ref[...] for ref in part_refs], axis=1))
+    own_ref[...] = solved[:, :edge]
+    for i in range(parts):
+        blocks_ref[i * vecs : (i + 1) * vecs, :] = solved[:, i * edge : (i + 1) * edge].astype(bf16)
+
+
+def cross_kernel(nodes, parts, *refs):
     part_refs, basis_ref, wide_ref, cross_ref = refs[:parts], refs[parts], refs[parts + 1], refs[parts + 2]
-    vecs = basis_ref.shape[0]
+    vecs = wide_ref.shape[0]
     edge = part_refs[0].shape[1]
     at = 0
     for ref in part_refs:
         for i in range(ref.shape[0] // vecs):
             wide_ref[:, at : at + edge] = ref[i * vecs : (i + 1) * vecs, :]
             at += edge
-    cross_ref[...] = dot_nt(basis_ref[...], wide_ref[...])
-
-
-def residual_kernel(nodes, crosses, inverse_ref, basis_ref, wide_ref, raw_ref, square_ref, rayleigh_ref, own_raw):
-    vecs = basis_ref.shape[0]
-    inverse = inverse_ref[...]
+    cross = lax.dot_general(
+        basis_ref[...], wide_ref[...], (((1,), (1,)), ((), ())), preferred_element_type=f32
+    )
+    cross_ref[...] = (cross[:vecs] + cross[vecs : 2 * vecs] + cross[2 * vecs :]) / nodes
+
+
+def residual_kernel(crosses, basis_ref, wide_ref, own_ref, raw_ref, square_ref, rayleigh_ref, own_raw):
+    vecs = wide_ref.shape[0]
     edge = own_raw.shape[1]
-    q = dot_nt(sum(ref[...] for ref in crosses) / nodes, inverse)
-    raw = dot_tn(q, basis_ref[...]) - dot_nn(inverse, wide_ref[...])
+    q = sum(ref[...] for ref in crosses)
+    high = q.astype(bf16)
+    low = (q - high.astype(f32)).astype(bf16)
+    terms = jnp.concatenate([high, high, low], axis=0)
+    basis = jnp.concatenate([basis_ref[: 2 * vecs], basis_ref[:vecs]], axis=0)
+    part = lax.dot_general(terms, basis, (((0,), (0,)), ((), ())), preferred_element_type=f32)
+    raw = part - wide_ref[...].astype(f32)
     raw_ref[...] = raw
-    own_raw[...] = raw[:, :edge]
+    own_raw[...] = part[:, :edge] - own_ref[...]
     square_ref[...] = jnp.broadcast_to(jnp.sum(raw * raw, axis=1, keepdims=True), square_ref.shape)
     row_ids = lax.broadcasted_iota(jnp.int32, (vecs, vecs), 0)
     lane_ids = lax.broadcasted_iota(jnp.int32, (vecs, vecs), 1)
@@ -216,13 +231,13 @@
     return [lax.psum(value, "panel")]
 
 
-def gather(value, near, beside=None):
+def far_values(value, near):
     far = lax.axis_size("rows") // near
-    first = [value] + [swap(value, near * i, "rows") for i in range(1, far)]
-    if beside is not None:
-        first, beside = lax.optimization_barrier((first, beside))
-    held = jnp.concatenate(first, axis=0)
-    return [held] + [swap(held, i, "rows") for i in range(1, near)], beside
+    return [value] + [swap(value, near * i, "rows") for i in range(1, far)]
+
+
+def near_values(held, near):
+    return [held] + [swap(held, i, "rows") for i in range(1, near)]
 
 
 def body(
@@ -257,7 +272,7 @@
     stack_out = ((3 * vecs, wide + edge), bf16)
 
     start = jnp.concatenate([start_basis, start_resid, start_search], axis=0)[None]
-    parts, _ = gather(start, near)
+    parts = near_values(jnp.concatenate(far_values(start, near), axis=0), near)
     state = None
     sweeps = ritz_basis.shape[0]
     for sweep in range(sweeps):
@@ -302,11 +317,18 @@
         inverse, scale = call(
             kernel_factor, [((vecs, vecs), f32), ((vecs, 2 * vecs), f32)], packs
         )
-        adj_parts, inverse = gather(rotated_adj, near, inverse)
+        far_parts = far_values(rotated_adj, near)
+        far_parts, inverse = lax.optimization_barrier((far_parts, inverse))
+        held, own_adj = call(
+            functools.partial(solve_kernel, len(far_parts)),
+            [((len(far_parts) * vecs, edge), bf16), ((vecs, edge), f32)],
+            far_parts + [inverse],
+        )
+        adj_parts = near_values(held, near)
         basis, dirs, own_basis, own_dirs = call(
             basis_kernel,
             [
-                ((vecs, wide), f32),
+                ((3 * vecs, wide), bf16),
                 ((vecs, wide), bf16),
                 ((vecs, edge), f32),
                 ((vecs, edge), f32),
@@ -314,20 +336,20 @@
             [inverse, scale, stack, mixing, search],
         )
         wide_adj, cross = call(
-            functools.partial(cross_kernel, near),
-            [((vecs, wide), f32), ((vecs, vecs), f32)],
+            functools.partial(cross_kernel, nodes, near),
+            [((vecs, wide), bf16), ((vecs, vecs), f32)],
             adj_parts + [basis],
         )
         crosses = panel_terms(cross)
         cross_count = len(crosses)
 
         def kernel_residual(*refs):
-            residual_kernel(nodes, refs[:cross_count], *refs[cross_count:])
+            residual_kernel(refs[:cross_count], *refs[cross_count:])
 
         raw, square, rayleigh, own_raw = call(
             kernel_residual,
             [((vecs, wide), f32), ((vecs, edge), f32), ((vecs, vecs), f32), ((vecs, edge), f32)],
-            crosses + [inverse, basis, wide_adj],
+            crosses + [basis, wide_adj, own_adj],
         )
         squares = panel_terms(square)
         state = (basis, raw, squares, dirs)

time: 98.2 us -> 91.3 us (0.930)
  waiting for transfers between devices: 29 us -> 24.2 us
  Pallas kernels: 28.6 us -> 26.6 us
    ppermute x36, waiting for transfers between devices: 29 us -> 24.2 us  [swap(): return lax.ppermute(value, axis, [(i, i ^ by) for i in range(size)])]
    pallas_call x18 -> x21, Pallas kernels: 28.6 us -> 26.6 us  [call(): pl.pallas_call(kernel, out_shape=[jax.ShapeDtypeStruct(shape, kind) for s...]
  transfers between devices with their start and end apart: 36 -> 36, of which waited for: 18 -> 20; matrix products, arithmetic and copies ran while one was open for 1% -> 1% of each run, Pallas kernels for 18% -> 19%
where the time goes in v3:
time: 91.3 us; the launch traced here: 90.9 us
  starting transfers between devices  35.6 us (39%)
  Pallas kernels  26.6 us (29%)
  waiting for transfers between devices  24.2 us (27%)
  local copies, waits for them, and re-layouts  2.17 us (2%)
  other arithmetic  1.5 us (2%)
    ppermute x36, starting transfers between devices, swap(): return lax.ppermute(value, axis, [(i, i ^ by) for i in range(size)])  35.6 us
    pallas_call x21, Pallas kernels, call(): pl.pallas_call(kernel, out_shape=[jax.ShapeDtypeStruct(shape, kind) for s...  26.6 us
    ppermute x36, waiting for transfers between devices, swap(): return lax.ppermute(value, axis, [(i, i ^ by) for i in range(size)])  24.2 us
  transfers between devices with their start and end apart: 36, of which 20 were waited for; matrix products, arithmetic and copies ran while one was open for 1% of the time, Pallas kernels for 19%

profile of v3, /device:TPU:0, one launch (start us, length us, event | category | flops | bytes accessed | tf_op | source)
XLA Modules:
  0.0 90.9 jit_solution(12567069576396001027)
XLA Ops:
  0.6 0.8 maximum_bitcast_fusion
  1.4 5.0 %collective-permute-start.2 = (bf16[1,192,128]{2,1,0:T(8,128)(2,1)S(1)}, bf16[1,192,128]{2,1,0:T(8,128)(2,1)S(1)}, u32[]{:S(2)}, u32[]{:S(2)}) collective-permute-start(bf16[1,192,128]{2,1,0:T(8,128)(2,1)S(1)} %maximum_bitcast_fusion), channel_id=1, source_target_pairs={{0,24},{2,26},{4,28},{6,30},{8,16},{10,18},{12,20},{14,22},{16,8},... | collective-permute-start | bytes 147464 | tf_op jit(solution)/shard_map/ppermute | solution.py:225
  6.4 0.6 collective-permute-start
  7.0 0.9 %slice_bitcast_fusion = (f32[64,192]{1,0:T(8,128)S(1)}, f32[64,192]{1,0:T(8,128)S(1)}, f32[64,192]{1,0:T(8,128)S(1)}) fusion(f32[3,64,192]{2,1,0:T(8,128)} %param.14), kind=kLoop, calls=%fused_computation.1 | loop fusion | bytes 294912 | tf_op jit(solution)/shard_map/squeeze | solution.py:279
  8.0 0.7 collective-permute-done.2
  8.7 2.8 %collective-permute-done.1 = bf16[1,192,128]{2,1,0:T(8,128)(2,1)S(1)} collective-permute-done((bf16[1,192,128]{2,1,0:T(8,128)(2,1)S(1)}, bf16[1,192,128]{2,1,0:T(8,128)(2,1)S(1)}, u32[]{:S(2)}, u32[]{:S(2)}) %collective-permute-start.1) | collective-permute-done | bytes 49184 | tf_op jit(solution)/shard_map/ppermute | solution.py:225
  11.5 2.5 %collective-permute-start.5 = (bf16[4,192,128]{2,1,0:T(8,128)(2,1)S(1)}, bf16[4,192,128]{2,1,0:T(8,128)(2,1)S(1)}, u32[]{:S(2)}, u32[]{:S(2)}) collective-permute-start(bf16[4,192,128]{2,1,0:T(8,128)(2,1)S(1)} %pad_maximum_fusion.refs_0_), channel_id=1, source_target_pairs={{0,6},{2,4},{4,2},{6,0},{8,14},{10,12},{12,10},{14,8},{16,22},{18,... | collective-permute-start | bytes 589832 | tf_op jit(solution)/shard_map/ppermute | solution.py:225
  14.0 0.5 collective-permute-start.4
  14.5 0.5 collective-permute-start.3
  15.1 4.8 %collective-permute-done.5.refs_3_ = bf16[4,192,128]{2,1,0:T(8,128)(2,1)S(1)} collective-permute-done((bf16[4,192,128]{2,1,0:T(8,128)(2,1)S(1)}, bf16[4,192,128]{2,1,0:T(8,128)(2,1)S(1)}, u32[]{:S(2)}, u32[]{:S(2)}) %collective-permute-start.5) | collective-permute-done | bytes 196640 | tf_op jit(solution)/shard_map/ppermute | solution.py:225
  20.0 2.5 %collective-permute-done.4.refs_2_ = bf16[4,192,128]{2,1,0:T(8,128)(2,1)S(1)} collective-permute-done((bf16[4,192,128]{2,1,0:T(8,128)(2,1)S(1)}, bf16[4,192,128]{2,1,0:T(8,128)(2,1)S(1)}, u32[]{:S(2)}, u32[]{:S(2)}) %collective-permute-start.4) | collective-permute-done | bytes 196640 | tf_op jit(solution)/shard_map/ppermute | solution.py:225
  22.5 1.2 %copy-done = bf16[1,1,2,16,128,128]{5,4,3,2,1,0:T(8,128)(2,1)S(1)} copy-done((bf16[1,1,2,16,128,128]{5,4,3,2,1,0:T(8,128)(2,1)S(1)}, bf16[1,1,2,16,128,128]{5,4,3,2,1,0:T(8,128)(2,1)}, u32[]{:S(2)}) %copy-start) | copy-done | bytes 1048600
  23.7 1.5 %shard_map.111 = (bf16[192,2176]{1,0:T(8,128)(2,1)S(1)}, f32[64,128]{1,0:T(8,128)S(1)}, f32[64,128]{1,0:T(8,128)S(1)}) custom-call(s32[2,16]{1,0:T(2,128)S(1)} %compare_select_fusion.slots_ref.s, s32[1]{0:T(128)} %bitcast.2.place_ref.p, bf16[2,16,128,128]{3,2,1,0:T(8,128)(2,1)S(1)} %bitcast.25, f32[64,192]{1,0:T(8,128)S(1)} %get-tuple-element.140.mix_ref, ...), custom_call_target="tpu_custom_call" | custom-call | tf_op jit(solution)/shard_map/pallas_call | solution.py:20
  25.4 1.1 %shard_map.112 = (f32[64,128]{1,0:T(8,128)S(1)}, f32[64,2048]{1,0:T(8,128)S(1)}) custom-call(bf16[192,2176]{1,0:T(8,128)(2,1)S(1)} %get-tuple-element.74.stack_ref, f32[64,192]{1,0:T(8,128)S(1)} %get-tuple-element.140.mix_ref, f32[64,128]{1,0:T(8,128)S(1)} %get-tuple-element.144.search_ref), custom_call_target="tpu_custom_call" | custom-call | tf_op jit(solution)/shard_map/pallas_call | solution.py:20
  26.6 0.5 collective-permute-start.10
  27.1 1.6 %collective-permute-start.9 = (f32[64,128]{1,0:T(8,128)S(1)}, f32[64,128]{1,0:T(8,128)S(1)}, u32[]{:S(2)}, u32[]{:S(2)}) collective-permute-start(f32[64,128]{1,0:T(8,128)S(1)} %add.30.refs_0_), channel_id=1, source_target_pairs={{0,24},{2,26},{4,28},{6,30},{8,16},{10,18},{12,20},{14,22},{16,8},... | collective-permute-start | bytes 98312 | tf_op jit(solution)/shard_map/ppermute | solution.py:225
  28.7 0.6 collective-permute-start.8
  29.3 2.2 %collective-permute-start.7 = (f32[64,128]{1,0:T(8,128)S(1)}, f32[64,128]{1,0:T(8,128)S(1)}, u32[]{:S(2)}, u32[]{:S(2)}) collective-permute-start(f32[64,128]{1,0:T(8,128)S(1)} %add.30.refs_0_), channel_id=1, source_target_pairs={{0,8},{2,10},{4,12},{6,14},{8,0},{10,2},{12,4},{14,6},{16,24},{18,... | collective-permute-start | bytes 98312 | tf_op jit(solution)/shard_map/ppermute | solution.py:225
  31.5 3.4 %shard_map.113 = (f32[64,64]{1,0:T(8,128)S(1)}, f32[64,128]{1,0:T(8,128)S(1)}) custom-call(f32[64,128]{1,0:T(8,128)S(1)} %get-tuple-element.77.refs_0_, f32[64,128]{1,0:T(8,128)S(1)} %collective-permute-done.10.refs_1_), custom_call_target="tpu_custom_call" | custom-call | tf_op jit(solution)/shard_map/pallas_call | solution.py:20
  35.1 1.7 %collective-permute-start.13 = (bf16[256,128]{1,0:T(8,128)(2,1)S(1)}, bf16[256,128]{1,0:T(8,128)(2,1)S(1)}, u32[]{:S(2)}, u32[]{:S(2)}) collective-permute-start(bf16[256,128]{1,0:T(8,128)(2,1)S(1)} %get-tuple-element.87.refs_0_), channel_id=1, source_target_pairs={{0,6},{2,4},{4,2},{6,0},{8,14},{10,12},{12,10},{14,8},{16,22},{18,... | collective-permute-start | bytes 196616 | tf_op jit(solution)/shard_map/ppermute | solution.py:225
  36.9 1.3 %collective-permute-start.12 = (bf16[256,128]{1,0:T(8,128)(2,1)S(1)}, bf16[256,128]{1,0:T(8,128)(2,1)S(1)}, u32[]{:S(2)}, u32[]{:S(2)}) collective-permute-start(bf16[256,128]{1,0:T(8,128)(2,1)S(1)} %get-tuple-element.87.refs_0_), channel_id=1, source_target_pairs={{0,4},{2,6},{4,0},{6,2},{8,12},{10,14},{12,8},{14,10},{16,20},{18,... | collective-permute-start | bytes 196616 | tf_op jit(solution)/shard_map/ppermute | solution.py:225
  38.2 0.5 collective-permute-start.11
  38.7 1.2 %shard_map.114 = (bf16[192,2048]{1,0:T(8,128)(2,1)S(1)}, bf16[64,2048]{1,0:T(8,128)(2,1)S(1)}, f32[64,128]{1,0:T(8,128)}, f32[64,128]{1,0:T(8,128)}) custom-call(f32[64,64]{1,0:T(8,128)S(1)} %get-tuple-element.79.inverse_ref.refs_4_, f32[64,128]{1,0:T(8,128)S(1)} %get-tuple-element.80.scale_ref, bf16[192,2176]{1,0:T(8,128)(2,1)S(1)} %get-tuple-element.74.stack_ref, ...), custom_call_target="tpu_custom_call" | custom-call | tf_op jit(solution)/shard_map/pallas_call | solution.py:20
  39.9 1.2 %collective-permute-done.13.refs_3_ = bf16[256,128]{1,0:T(8,128)(2,1)S(1)} collective-permute-done((bf16[256,128]{1,0:T(8,128)(2,1)S(1)}, bf16[256,128]{1,0:T(8,128)(2,1)S(1)}, u32[]{:S(2)}, u32[]{:S(2)}) %collective-permute-start.13) | collective-permute-done | bytes 65568 | tf_op jit(solution)/shard_map/ppermute | solution.py:225
  41.5 1.0 %collective-permute-done.11.refs_1_ = bf16[256,128]{1,0:T(8,128)(2,1)S(1)} collective-permute-done((bf16[256,128]{1,0:T(8,128)(2,1)S(1)}, bf16[256,128]{1,0:T(8,128)(2,1)S(1)}, u32[]{:S(2)}, u32[]{:S(2)}) %collective-permute-start.11) | collective-permute-done | bytes 65568 | tf_op jit(solution)/shard_map/ppermute | solution.py:225
  42.4 0.4 shard_map.116
  42.9 1.2 %collective-permute-done.14.refs_1_ = f32[64,64]{1,0:T(8,128)S(1)} collective-permute-done((f32[64,64]{1,0:T(8,128)S(1)}, f32[64,64]{1,0:T(8,128)S(1)}, u32[]{:S(2)}, u32[]{:S(2)}) %collective-permute-start.14) | collective-permute-done | bytes 16416 | tf_op jit(solution)/shard_map/ppermute | solution.py:225
  44.1 0.9 %shard_map.117 = (f32[64,2048]{1,0:T(8,128)S(1)}, f32[64,128]{1,0:T(8,128)S(1)}, f32[64,64]{1,0:T(8,128)}, f32[64,128]{1,0:T(8,128)}) custom-call(f32[64,64]{1,0:T(8,128)S(1)} %get-tuple-element.88.refs_0_, f32[64,64]{1,0:T(8,128)S(1)} %collective-permute-done.14.refs_1_, bf16[192,2048]{1,0:T(8,128)(2,1)S(1)} %get-tuple-element.82.refs_4_.refs_2_.b, ...), custom_call_target="tpu_custom_call" | custom-call | tf_op jit(solution)/shard_map/pallas_call | solution.py:20
  45.2 1.0 %collective-permute-done.15.refs_1_ = f32[64,128]{1,0:T(8,128)S(1)} collective-permute-done((f32[64,128]{1,0:T(8,128)S(1)}, f32[64,128]{1,0:T(8,128)S(1)}, u32[]{:S(2)}, u32[]{:S(2)}) %collective-permute-start.15) | collective-permute-done | bytes 32800 | tf_op jit(solution)/shard_map/ppermute | solution.py:225
  46.2 1.5 %shard_map.118 = (bf16[192,2176]{1,0:T(8,128)(2,1)S(1)}, f32[64,128]{1,0:T(8,128)S(1)}, f32[64,128]{1,0:T(8,128)S(1)}) custom-call(s32[2,16]{1,0:T(2,128)S(1)} %compare_select_fusion.slots_ref.s, s32[1]{0:T(128)} %bitcast.2.place_ref.p, bf16[2,16,128,128]{3,2,1,0:T(8,128)(2,1)S(1)} %bitcast.26, f32[64,192]{1,0:T(8,128)S(1)} %get-tuple-element.142.m.mix_ref, ...), custom_call_target="tpu_custom_call" | custom-call | tf_op jit(solution)/shard_map/pallas_call | solution.py:20
  47.9 1.1 %shard_map.119 = (f32[64,128]{1,0:T(8,128)S(1)}, f32[64,2048]{1,0:T(8,128)S(1)}) custom-call(bf16[192,2176]{1,0:T(8,128)(2,1)S(1)} %get-tuple-element.96.stack_ref, f32[64,192]{1,0:T(8,128)S(1)} %get-tuple-element.142.m.mix_ref, f32[64,128]{1,0:T(8,128)S(1)} %get-tuple-element.145.search_ref), custom_call_target="tpu_custom_call" | custom-call | tf_op jit(solution)/shard_map/pallas_call | solution.py:20
  49.1 0.4 collective-permute-start.20
  49.5 1.6 %collective-permute-start.19 = (f32[64,128]{1,0:T(8,128)S(1)}, f32[64,128]{1,0:T(8,128)S(1)}, u32[]{:S(2)}, u32[]{:S(2)}) collective-permute-start(f32[64,128]{1,0:T(8,128)S(1)} %add.31.refs_0_), channel_id=1, source_target_pairs={{0,24},{2,26},{4,28},{6,30},{8,16},{10,18},{12,20},{14,22},{16,8},... | collective-permute-start | bytes 98312 | tf_op jit(solution)/shard_map/ppermute | solution.py:225
  51.1 0.4 collective-permute-start.18
  51.5 2.4 %collective-permute-start.17 = (f32[64,128]{1,0:T(8,128)S(1)}, f32[64,128]{1,0:T(8,128)S(1)}, u32[]{:S(2)}, u32[]{:S(2)}) collective-permute-start(f32[64,128]{1,0:T(8,128)S(1)} %add.31.refs_0_), channel_id=1, source_target_pairs={{0,8},{2,10},{4,12},{6,14},{8,0},{10,2},{12,4},{14,6},{16,24},{18,... | collective-permute-start | bytes 98312 | tf_op jit(solution)/shard_map/ppermute | solution.py:225
  53.9 3.4 %shard_map.120 = (f32[64,64]{1,0:T(8,128)S(1)}, f32[64,128]{1,0:T(8,128)S(1)}) custom-call(f32[64,128]{1,0:T(8,128)S(1)} %get-tuple-element.99.refs_0_, f32[64,128]{1,0:T(8,128)S(1)} %collective-permute-done.20.refs_1_), custom_call_target="tpu_custom_call" | custom-call | tf_op jit(solution)/shard_map/pallas_call | solution.py:20
  57.6 1.5 %collective-permute-start.23 = (bf16[256,128]{1,0:T(8,128)(2,1)S(1)}, bf16[256,128]{1,0:T(8,128)(2,1)S(1)}, u32[]{:S(2)}, u32[]{:S(2)}) collective-permute-start(bf16[256,128]{1,0:T(8,128)(2,1)S(1)} %get-tuple-element.109.refs_0_), channel_id=1, source_target_pairs={{0,6},{2,4},{4,2},{6,0},{8,14},{10,12},{12,10},{14,8},{16,22},{18,... | collective-permute-start | bytes 196616 | tf_op jit(solution)/shard_map/ppermute | solution.py:225
  59.0 0.6 collective-permute-start.22
  59.7 1.5 %collective-permute-start.21 = (bf16[256,128]{1,0:T(8,128)(2,1)S(1)}, bf16[256,128]{1,0:T(8,128)(2,1)S(1)}, u32[]{:S(2)}, u32[]{:S(2)}) collective-permute-start(bf16[256,128]{1,0:T(8,128)(2,1)S(1)} %get-tuple-element.109.refs_0_), channel_id=1, source_target_pairs={{0,2},{2,0},{4,6},{6,4},{8,10},{10,8},{12,14},{14,12},{16,18},{18,... | collective-permute-start | bytes 196616 | tf_op jit(solution)/shard_map/ppermute | solution.py:225
  61.1 1.2 %shard_map.121 = (bf16[192,2048]{1,0:T(8,128)(2,1)S(1)}, bf16[64,2048]{1,0:T(8,128)(2,1)S(1)}, f32[64,128]{1,0:T(8,128)}, f32[64,128]{1,0:T(8,128)}) custom-call(f32[64,64]{1,0:T(8,128)S(1)} %get-tuple-element.101.inverse_ref.refs_4_, f32[64,128]{1,0:T(8,128)S(1)} %get-tuple-element.102.scale_ref, bf16[192,2176]{1,0:T(8,128)(2,1)S(1)} %get-tuple-element.96.stack_ref, ...), custom_call_target="tpu_custom_call" | custom-call | tf_op jit(solution)/shard_map/pallas_call | solution.py:20
  62.3 1.0 %collective-permute-done.23.refs_3_ = bf16[256,128]{1,0:T(8,128)(2,1)S(1)} collective-permute-done((bf16[256,128]{1,0:T(8,128)(2,1)S(1)}, bf16[256,128]{1,0:T(8,128)(2,1)S(1)}, u32[]{:S(2)}, u32[]{:S(2)}) %collective-permute-start.23) | collective-permute-done | bytes 65568 | tf_op jit(solution)/shard_map/ppermute | solution.py:225
  63.4 0.4 collective-permute-done.22.refs_2_
  63.9 0.4 shard_map.123
  64.4 1.2 %collective-permute-done.24.refs_1_ = f32[64,64]{1,0:T(8,128)S(1)} collective-permute-done((f32[64,64]{1,0:T(8,128)S(1)}, f32[64,64]{1,0:T(8,128)S(1)}, u32[]{:S(2)}, u32[]{:S(2)}) %collective-permute-start.24) | collective-permute-done | bytes 16416 | tf_op jit(solution)/shard_map/ppermute | solution.py:225
  65.6 0.9 %shard_map.124 = (f32[64,2048]{1,0:T(8,128)S(1)}, f32[64,128]{1,0:T(8,128)S(1)}, f32[64,64]{1,0:T(8,128)}, f32[64,128]{1,0:T(8,128)}) custom-call(f32[64,64]{1,0:T(8,128)S(1)} %get-tuple-element.110.refs_0_, f32[64,64]{1,0:T(8,128)S(1)} %collective-permute-done.24.refs_1_, bf16[192,2048]{1,0:T(8,128)(2,1)S(1)} %get-tuple-element.104.refs_4_.refs_2_.b, ...), custom_call_target="tpu_custom_call" | custom-call | tf_op jit(solution)/shard_map/pallas_call | solution.py:20
  66.6 1.0 %collective-permute-done.25.refs_1_ = f32[64,128]{1,0:T(8,128)S(1)} collective-permute-done((f32[64,128]{1,0:T(8,128)S(1)}, f32[64,128]{1,0:T(8,128)S(1)}, u32[]{:S(2)}, u32[]{:S(2)}) %collective-permute-start.25) | collective-permute-done | bytes 32800 | tf_op jit(solution)/shard_map/ppermute | solution.py:225
  67.7 1.5 %shard_map.125 = (bf16[192,2176]{1,0:T(8,128)(2,1)S(1)}, f32[64,128]{1,0:T(8,128)S(1)}, f32[64,128]{1,0:T(8,128)S(1)}) custom-call(s32[2,16]{1,0:T(2,128)S(1)} %compare_select_fusion.slots_ref.s, s32[1]{0:T(128)} %bitcast.2.place_ref.p, bf16[2,16,128,128]{3,2,1,0:T(8,128)(2,1)S(1)} %bitcast.27, f32[64,192]{1,0:T(8,128)S(1)} %get-tuple-element.141.m.mix_ref, ...), custom_call_target="tpu_custom_call" | custom-call | tf_op jit(solution)/shard_map/pallas_call | solution.py:20
  69.4 1.1 %shard_map.126 = (f32[64,128]{1,0:T(8,128)S(1)}, f32[64,2048]{1,0:T(8,128)S(1)}) custom-call(bf16[192,2176]{1,0:T(8,128)(2,1)S(1)} %get-tuple-element.118.stack_ref, f32[64,192]{1,0:T(8,128)S(1)} %get-tuple-element.141.m.mix_ref, f32[64,128]{1,0:T(8,128)S(1)} %get-tuple-element.143.search_ref), custom_call_target="tpu_custom_call" | custom-call | tf_op jit(solution)/shard_map/pallas_call | solution.py:20
  70.6 0.4 collective-permute-start.30
  71.0 1.6 %collective-permute-start.29 = (f32[64,128]{1,0:T(8,128)S(1)}, f32[64,128]{1,0:T(8,128)S(1)}, u32[]{:S(2)}, u32[]{:S(2)}) collective-permute-start(f32[64,128]{1,0:T(8,128)S(1)} %add.32.refs_0_), channel_id=1, source_target_pairs={{0,24},{2,26},{4,28},{6,30},{8,16},{10,18},{12,20},{14,22},{16,8},... | collective-permute-start | bytes 98312 | tf_op jit(solution)/shard_map/ppermute | solution.py:225
  72.6 0.4 collective-permute-start.28
  73.0 2.4 %collective-permute-start.27 = (f32[64,128]{1,0:T(8,128)S(1)}, f32[64,128]{1,0:T(8,128)S(1)}, u32[]{:S(2)}, u32[]{:S(2)}) collective-permute-start(f32[64,128]{1,0:T(8,128)S(1)} %add.32.refs_0_), channel_id=1, source_target_pairs={{0,8},{2,10},{4,12},{6,14},{8,0},{10,2},{12,4},{14,6},{16,24},{18,... | collective-permute-start | bytes 98312 | tf_op jit(solution)/shard_map/ppermute | solution.py:225
  75.4 3.4 %shard_map.127 = (f32[64,64]{1,0:T(8,128)S(1)}, f32[64,128]{1,0:T(8,128)S(1)}) custom-call(f32[64,128]{1,0:T(8,128)S(1)} %get-tuple-element.121.refs_0_, f32[64,128]{1,0:T(8,128)S(1)} %collective-permute-done.30.refs_1_), custom_call_target="tpu_custom_call" | custom-call | tf_op jit(solution)/shard_map/pallas_call | solution.py:20
  79.1 1.7 %collective-permute-start.33 = (bf16[256,128]{1,0:T(8,128)(2,1)S(1)}, bf16[256,128]{1,0:T(8,128)(2,1)S(1)}, u32[]{:S(2)}, u32[]{:S(2)}) collective-permute-start(bf16[256,128]{1,0:T(8,128)(2,1)S(1)} %get-tuple-element.131.refs_0_), channel_id=1, source_target_pairs={{0,6},{2,4},{4,2},{6,0},{8,14},{10,12},{12,10},{14,8},{16,22},{18,... | collective-permute-start | bytes 196616 | tf_op jit(solution)/shard_map/ppermute | solution.py:225
  80.8 1.3 %collective-permute-start.32 = (bf16[256,128]{1,0:T(8,128)(2,1)S(1)}, bf16[256,128]{1,0:T(8,128)(2,1)S(1)}, u32[]{:S(2)}, u32[]{:S(2)}) collective-permute-start(bf16[256,128]{1,0:T(8,128)(2,1)S(1)} %get-tuple-element.131.refs_0_), channel_id=1, source_target_pairs={{0,4},{2,6},{4,0},{6,2},{8,12},{10,14},{12,8},{14,10},{16,20},{18,... | collective-permute-start | bytes 196616 | tf_op jit(solution)/shard_map/ppermute | solution.py:225
  82.1 0.5 collective-permute-start.31
  82.6 1.3 %shard_map.128 = (bf16[192,2048]{1,0:T(8,128)(2,1)S(1)}, bf16[64,2048]{1,0:T(8,128)(2,1)}, f32[64,128]{1,0:T(8,128)}, f32[64,128]{1,0:T(8,128)}) custom-call(f32[64,64]{1,0:T(8,128)S(1)} %get-tuple-element.123.inverse_ref.refs_4_, f32[64,128]{1,0:T(8,128)S(1)} %get-tuple-element.124.scale_ref, bf16[192,2176]{1,0:T(8,128)(2,1)S(1)} %get-tuple-element.118.stack_ref, ...), custom_call_target="tpu_custom_call" | custom-call | tf_op jit(solution)/shard_map/pallas_call | solution.py:20
  83.9 1.1 %collective-permute-done.33.refs_3_ = bf16[256,128]{1,0:T(8,128)(2,1)S(1)} collective-permute-done((bf16[256,128]{1,0:T(8,128)(2,1)S(1)}, bf16[256,128]{1,0:T(8,128)(2,1)S(1)}, u32[]{:S(2)}, u32[]{:S(2)}) %collective-permute-start.33) | collective-permute-done | bytes 65568 | tf_op jit(solution)/shard_map/ppermute | solution.py:225
  85.0 0.4 collective-permute-done.32.refs_2_
  85.4 1.0 %collective-permute-done.31.refs_1_ = bf16[256,128]{1,0:T(8,128)(2,1)S(1)} collective-permute-done((bf16[256,128]{1,0:T(8,128)(2,1)S(1)}, bf16[256,128]{1,0:T(8,128)(2,1)S(1)}, u32[]{:S(2)}, u32[]{:S(2)}) %collective-permute-start.31) | collective-permute-done | bytes 65568 | tf_op jit(solution)/shard_map/ppermute | solution.py:225
  86.8 1.2 %collective-permute-done.34.refs_1_ = f32[64,64]{1,0:T(8,128)S(1)} collective-permute-done((f32[64,64]{1,0:T(8,128)S(1)}, f32[64,64]{1,0:T(8,128)S(1)}, u32[]{:S(2)}, u32[]{:S(2)}) %collective-permute-start.34) | collective-permute-done | bytes 16416 | tf_op jit(solution)/shard_map/ppermute | solution.py:225
  88.0 1.1 %shard_map.131 = (f32[64,2048]{1,0:T(8,128)}, f32[64,128]{1,0:T(8,128)S(1)}, f32[64,64]{1,0:T(8,128)}, f32[64,128]{1,0:T(8,128)S(1)}) custom-call(f32[64,64]{1,0:T(8,128)S(1)} %get-tuple-element.133.refs_0_, f32[64,64]{1,0:T(8,128)S(1)} %collective-permute-done.34.refs_1_, bf16[192,2048]{1,0:T(8,128)(2,1)S(1)} %get-tuple-element.132.refs_4_.refs_2_, ...), custom_call_target="tpu_custom_call" | custom-call | tf_op jit(solution)/shard_map/pallas_call | solution.py:20
  89.3 1.0 %collective-permute-done.35 = f32[64,128]{1,0:T(8,128)S(1)} collective-permute-done((f32[64,128]{1,0:T(8,128)S(1)}, f32[64,128]{1,0:T(8,128)S(1)}, u32[]{:S(2)}, u32[]{:S(2)}) %collective-permute-start.35) | collective-permute-done | bytes 32800 | tf_op jit(solution)/shard_map/ppermute | solution.py:225
  90.3 0.6 rsqrt_multiply_fusion
  (48 shorter events, 3.2 us)
Async XLA Ops:
  1.4 7.3 %collective-permute-start.2 = (bf16[1,192,128]{2,1,0:T(8,128)(2,1)S(1)}, bf16[1,192,128]{2,1,0:T(8,128)(2,1)S(1)}, u32[]{:S(2)}, u32[]{:S(2)}) collective-permute-start(bf16[1,192,128]{2,1,0:T(8,128)(2,1)S(1)} %maximum_bitcast_fusion), channel_id=1, source_target_pairs={{0,24},{2,26},{4,28},{6,30},{8,16},{10,18},{12,20},{14,22},{16,8},... | collective-permute-start | bytes 147464 | tf_op jit(solution)/shard_map/ppermute | solution.py:225
  6.4 5.0 %collective-permute-start.1 = (bf16[1,192,128]{2,1,0:T(8,128)(2,1)S(1)}, bf16[1,192,128]{2,1,0:T(8,128)(2,1)S(1)}, u32[]{:S(2)}, u32[]{:S(2)}) collective-permute-start(bf16[1,192,128]{2,1,0:T(8,128)(2,1)S(1)} %maximum_bitcast_fusion), channel_id=1, source_target_pairs={{0,16},{2,18},{4,20},{6,22},{8,24},{10,26},{12,28},{14,30},{16,0},... | collective-permute-start | bytes 147464 | tf_op jit(solution)/shard_map/ppermute | solution.py:225
  6.4 5.0 %collective-permute-start = (bf16[1,192,128]{2,1,0:T(8,128)(2,1)S(1)}, bf16[1,192,128]{2,1,0:T(8,128)(2,1)S(1)}, u32[]{:S(2)}, u32[]{:S(2)}) collective-permute-start(bf16[1,192,128]{2,1,0:T(8,128)(2,1)S(1)} %maximum_bitcast_fusion), channel_id=1, source_target_pairs={{0,8},{2,10},{4,12},{6,14},{8,0},{10,2},{12,4},{14,6},{16,24},{18,... | collective-permute-start | bytes 147464 | tf_op jit(solution)/shard_map/ppermute | solution.py:225
  11.5 3.6 %copy-start.3 = (s32[1,1,2,16]{3,2,1,0:T(2,128)S(1)}, s32[1,1,2,16]{3,2,1,0:T(2,128)}, u32[]{:S(2)}) copy-start(s32[1,1,2,16]{3,2,1,0:T(2,128)} %param.10) | copy-start | bytes 388
  11.5 3.6 %copy-start.4 = (s32[1,1,2]{2,1,0:T(1,128)S(1)}, s32[1,1,2]{2,1,0:T(1,128)}, u32[]{:S(2)}) copy-start(s32[1,1,2]{2,1,0:T(1,128)} %param.9) | copy-start | bytes 28
  11.5 8.5 %collective-permute-start.5 = (bf16[4,192,128]{2,1,0:T(8,128)(2,1)S(1)}, bf16[4,192,128]{2,1,0:T(8,128)(2,1)S(1)}, u32[]{:S(2)}, u32[]{:S(2)}) collective-permute-start(bf16[4,192,128]{2,1,0:T(8,128)(2,1)S(1)} %pad_maximum_fusion.refs_0_), channel_id=1, source_target_pairs={{0,6},{2,4},{4,2},{6,0},{8,14},{10,12},{12,10},{14,8},{16,22},{18,... | collective-permute-start | bytes 589832 | tf_op jit(solution)/shard_map/ppermute | solution.py:225
  14.0 8.4 %collective-permute-start.4 = (bf16[4,192,128]{2,1,0:T(8,128)(2,1)S(1)}, bf16[4,192,128]{2,1,0:T(8,128)(2,1)S(1)}, u32[]{:S(2)}, u32[]{:S(2)}) collective-permute-start(bf16[4,192,128]{2,1,0:T(8,128)(2,1)S(1)} %pad_maximum_fusion.refs_0_), channel_id=1, source_target_pairs={{0,4},{2,6},{4,0},{6,2},{8,12},{10,14},{12,8},{14,10},{16,20},{18,... | collective-permute-start | bytes 589832 | tf_op jit(solution)/shard_map/ppermute | solution.py:225
  14.5 8.0 %collective-permute-start.3 = (bf16[4,192,128]{2,1,0:T(8,128)(2,1)S(1)}, bf16[4,192,128]{2,1,0:T(8,128)(2,1)S(1)}, u32[]{:S(2)}, u32[]{:S(2)}) collective-permute-start(bf16[4,192,128]{2,1,0:T(8,128)(2,1)S(1)} %pad_maximum_fusion.refs_0_), channel_id=1, source_target_pairs={{0,2},{2,0},{4,6},{6,4},{8,10},{10,8},{12,14},{14,12},{16,18},{18,... | collective-permute-start | bytes 589832 | tf_op jit(solution)/shard_map/ppermute | solution.py:225
  22.5 1.2 %copy-start = (bf16[1,1,2,16,128,128]{5,4,3,2,1,0:T(8,128)(2,1)S(1)}, bf16[1,1,2,16,128,128]{5,4,3,2,1,0:T(8,128)(2,1)}, u32[]{:S(2)}) copy-start(bf16[1,1,2,16,128,128]{5,4,3,2,1,0:T(8,128)(2,1)} %param.8) | copy-start | bytes 3145732
  23.7 1.6 %copy-start.2 = (f32[3,64,128]{2,1,0:T(8,128)S(1)}, f32[3,64,128]{2,1,0:T(8,128)}, u32[]{:S(2)}) copy-start(f32[3,64,128]{2,1,0:T(8,128)} %param.15) | copy-start | bytes 294916
  25.3 1.3 %collective-permute-start.6 = (f32[64,128]{1,0:T(8,128)S(1)}, f32[64,128]{1,0:T(8,128)S(1)}, u32[]{:S(2)}, u32[]{:S(2)}) collective-permute-start(f32[64,128]{1,0:T(8,128)S(1)} %get-tuple-element.73), channel_id=1, source_target_pairs={{0,1},{1,0},{2,3},{3,2},{4,5},{5,4},{6,7},{7,6},{8,9},{9,8},{10,11... | collective-permute-start | bytes 98312 | tf_op jit(solution)/shard_map/ppermute | solution.py:225
  26.6 4.9 %collective-permute-start.10 = (f32[64,128]{1,0:T(8,128)S(1)}, f32[64,128]{1,0:T(8,128)S(1)}, u32[]{:S(2)}, u32[]{:S(2)}) collective-permute-start(f32[64,128]{1,0:T(8,128)S(1)} %get-tuple-element.77.refs_0_), channel_id=1, source_target_pairs={{0,1},{1,0},{2,3},{3,2},{4,5},{5,4},{6,7},{7,6},{8,9},{9,8},{10,11... | collective-permute-start | bytes 98312 | tf_op jit(solution)/shard_map/ppermute | solution.py:225
  27.1 7.8 %collective-permute-start.9 = (f32[64,128]{1,0:T(8,128)S(1)}, f32[64,128]{1,0:T(8,128)S(1)}, u32[]{:S(2)}, u32[]{:S(2)}) collective-permute-start(f32[64,128]{1,0:T(8,128)S(1)} %add.30.refs_0_), channel_id=1, source_target_pairs={{0,24},{2,26},{4,28},{6,30},{8,16},{10,18},{12,20},{14,22},{16,8},... | collective-permute-start | bytes 98312 | tf_op jit(solution)/shard_map/ppermute | solution.py:225
  28.7 6.2 %collective-permute-start.8 = (f32[64,128]{1,0:T(8,128)S(1)}, f32[64,128]{1,0:T(8,128)S(1)}, u32[]{:S(2)}, u32[]{:S(2)}) collective-permute-start(f32[64,128]{1,0:T(8,128)S(1)} %add.30.refs_0_), channel_id=1, source_target_pairs={{0,16},{2,18},{4,20},{6,22},{8,24},{10,26},{12,28},{14,30},{16,0},... | collective-permute-start | bytes 98312 | tf_op jit(solution)/shard_map/ppermute | solution.py:225
  29.3 5.6 %collective-permute-start.7 = (f32[64,128]{1,0:T(8,128)S(1)}, f32[64,128]{1,0:T(8,128)S(1)}, u32[]{:S(2)}, u32[]{:S(2)}) collective-permute-start(f32[64,128]{1,0:T(8,128)S(1)} %add.30.refs_0_), channel_id=1, source_target_pairs={{0,8},{2,10},{4,12},{6,14},{8,0},{10,2},{12,4},{14,6},{16,24},{18,... | collective-permute-start | bytes 98312 | tf_op jit(solution)/shard_map/ppermute | solution.py:225
  35.1 6.0 %collective-permute-start.13 = (bf16[256,128]{1,0:T(8,128)(2,1)S(1)}, bf16[256,128]{1,0:T(8,128)(2,1)S(1)}, u32[]{:S(2)}, u32[]{:S(2)}) collective-permute-start(bf16[256,128]{1,0:T(8,128)(2,1)S(1)} %get-tuple-element.87.refs_0_), channel_id=1, source_target_pairs={{0,6},{2,4},{4,2},{6,0},{8,14},{10,12},{12,10},{14,8},{16,22},{18,... | collective-permute-start | bytes 196616 | tf_op jit(solution)/shard_map/ppermute | solution.py:225
  36.9 4.6 %collective-permute-start.12 = (bf16[256,128]{1,0:T(8,128)(2,1)S(1)}, bf16[256,128]{1,0:T(8,128)(2,1)S(1)}, u32[]{:S(2)}, u32[]{:S(2)}) collective-permute-start(bf16[256,128]{1,0:T(8,128)(2,1)S(1)} %get-tuple-element.87.refs_0_), channel_id=1, source_target_pairs={{0,4},{2,6},{4,0},{6,2},{8,12},{10,14},{12,8},{14,10},{16,20},{18,... | collective-permute-start | bytes 196616 | tf_op jit(solution)/shard_map/ppermute | solution.py:225
  38.2 4.3 %collective-permute-start.11 = (bf16[256,128]{1,0:T(8,128)(2,1)S(1)}, bf16[256,128]{1,0:T(8,128)(2,1)S(1)}, u32[]{:S(2)}, u32[]{:S(2)}) collective-permute-start(bf16[256,128]{1,0:T(8,128)(2,1)S(1)} %get-tuple-element.87.refs_0_), channel_id=1, source_target_pairs={{0,2},{2,0},{4,6},{6,4},{8,10},{10,8},{12,14},{14,12},{16,18},{18,... | collective-permute-start | bytes 196616 | tf_op jit(solution)/shard_map/ppermute | solution.py:225
  42.4 3.8 %copy-start.1 = (bf16[1,1,2,16,128,128]{5,4,3,2,1,0:T(8,128)(2,1)S(1)}, bf16[1,1,2,16,128,128]{5,4,3,2,1,0:T(8,128)(2,1)}, u32[]{:S(2)}) copy-start(bf16[1,1,2,16,128,128]{5,4,3,2,1,0:T(8,128)(2,1)} %param.8) | copy-start | bytes 3145732
  42.8 1.3 %collective-permute-start.14 = (f32[64,64]{1,0:T(8,128)S(1)}, f32[64,64]{1,0:T(8,128)S(1)}, u32[]{:S(2)}, u32[]{:S(2)}) collective-permute-start(f32[64,64]{1,0:T(8,128)S(1)} %get-tuple-element.88.refs_0_), channel_id=1, source_target_pairs={{0,1},{1,0},{2,3},{3,2},{4,5},{5,4},{6,7},{7,6},{8,9},{9,8},{10,11... | collective-permute-start | bytes 49160 | tf_op jit(solution)/shard_map/ppermute | solution.py:225
  45.0 1.2 %collective-permute-start.15 = (f32[64,128]{1,0:T(8,128)S(1)}, f32[64,128]{1,0:T(8,128)S(1)}, u32[]{:S(2)}, u32[]{:S(2)}) collective-permute-start(f32[64,128]{1,0:T(8,128)S(1)} %get-tuple-element.92.refs_0_), channel_id=1, source_target_pairs={{0,1},{1,0},{2,3},{3,2},{4,5},{5,4},{6,7},{7,6},{8,9},{9,8},{10,11... | collective-permute-start | bytes 98312 | tf_op jit(solution)/shard_map/ppermute | solution.py:225
  47.7 1.4 %collective-permute-start.16 = (f32[64,128]{1,0:T(8,128)S(1)}, f32[64,128]{1,0:T(8,128)S(1)}, u32[]{:S(2)}, u32[]{:S(2)}) collective-permute-start(f32[64,128]{1,0:T(8,128)S(1)} %get-tuple-element.95), channel_id=1, source_target_pairs={{0,1},{1,0},{2,3},{3,2},{4,5},{5,4},{6,7},{7,6},{8,9},{9,8},{10,11... | collective-permute-start | bytes 98312 | tf_op jit(solution)/shard_map/ppermute | solution.py:225
  49.1 4.8 %collective-permute-start.20 = (f32[64,128]{1,0:T(8,128)S(1)}, f32[64,128]{1,0:T(8,128)S(1)}, u32[]{:S(2)}, u32[]{:S(2)}) collective-permute-start(f32[64,128]{1,0:T(8,128)S(1)} %get-tuple-element.99.refs_0_), channel_id=1, source_target_pairs={{0,1},{1,0},{2,3},{3,2},{4,5},{5,4},{6,7},{7,6},{8,9},{9,8},{10,11... | collective-permute-start | bytes 98312 | tf_op jit(solution)/shard_map/ppermute | solution.py:225
  49.5 7.8 %collective-permute-start.19 = (f32[64,128]{1,0:T(8,128)S(1)}, f32[64,128]{1,0:T(8,128)S(1)}, u32[]{:S(2)}, u32[]{:S(2)}) collective-permute-start(f32[64,128]{1,0:T(8,128)S(1)} %add.31.refs_0_), channel_id=1, source_target_pairs={{0,24},{2,26},{4,28},{6,30},{8,16},{10,18},{12,20},{14,22},{16,8},... | collective-permute-start | bytes 98312 | tf_op jit(solution)/shard_map/ppermute | solution.py:225
  51.1 6.2 %collective-permute-start.18 = (f32[64,128]{1,0:T(8,128)S(1)}, f32[64,128]{1,0:T(8,128)S(1)}, u32[]{:S(2)}, u32[]{:S(2)}) collective-permute-start(f32[64,128]{1,0:T(8,128)S(1)} %add.31.refs_0_), channel_id=1, source_target_pairs={{0,16},{2,18},{4,20},{6,22},{8,24},{10,26},{12,28},{14,30},{16,0},... | collective-permute-start | bytes 98312 | tf_op jit(solution)/shard_map/ppermute | solution.py:225
  51.5 5.8 %collective-permute-start.17 = (f32[64,128]{1,0:T(8,128)S(1)}, f32[64,128]{1,0:T(8,128)S(1)}, u32[]{:S(2)}, u32[]{:S(2)}) collective-permute-start(f32[64,128]{1,0:T(8,128)S(1)} %add.31.refs_0_), channel_id=1, source_target_pairs={{0,8},{2,10},{4,12},{6,14},{8,0},{10,2},{12,4},{14,6},{16,24},{18,... | collective-permute-start | bytes 98312 | tf_op jit(solution)/shard_map/ppermute | solution.py:225
  57.6 5.8 %collective-permute-start.23 = (bf16[256,128]{1,0:T(8,128)(2,1)S(1)}, bf16[256,128]{1,0:T(8,128)(2,1)S(1)}, u32[]{:S(2)}, u32[]{:S(2)}) collective-permute-start(bf16[256,128]{1,0:T(8,128)(2,1)S(1)} %get-tuple-element.109.refs_0_), channel_id=1, source_target_pairs={{0,6},{2,4},{4,2},{6,0},{8,14},{10,12},{12,10},{14,8},{16,22},{18,... | collective-permute-start | bytes 196616 | tf_op jit(solution)/shard_map/ppermute | solution.py:225
  59.0 4.7 %collective-permute-start.22 = (bf16[256,128]{1,0:T(8,128)(2,1)S(1)}, bf16[256,128]{1,0:T(8,128)(2,1)S(1)}, u32[]{:S(2)}, u32[]{:S(2)}) collective-permute-start(bf16[256,128]{1,0:T(8,128)(2,1)S(1)} %get-tuple-element.109.refs_0_), channel_id=1, source_target_pairs={{0,4},{2,6},{4,0},{6,2},{8,12},{10,14},{12,8},{14,10},{16,20},{18,... | collective-permute-start | bytes 196616 | tf_op jit(solution)/shard_map/ppermute | solution.py:225
  59.7 4.3 %collective-permute-start.21 = (bf16[256,128]{1,0:T(8,128)(2,1)S(1)}, bf16[256,128]{1,0:T(8,128)(2,1)S(1)}, u32[]{:S(2)}, u32[]{:S(2)}) collective-permute-start(bf16[256,128]{1,0:T(8,128)(2,1)S(1)} %get-tuple-element.109.refs_0_), channel_id=1, source_target_pairs={{0,2},{2,0},{4,6},{6,4},{8,10},{10,8},{12,14},{14,12},{16,18},{18,... | collective-permute-start | bytes 196616 | tf_op jit(solution)/shard_map/ppermute | solution.py:225
  64.3 1.3 %collective-permute-start.24 = (f32[64,64]{1,0:T(8,128)S(1)}, f32[64,64]{1,0:T(8,128)S(1)}, u32[]{:S(2)}, u32[]{:S(2)}) collective-permute-start(f32[64,64]{1,0:T(8,128)S(1)} %get-tuple-element.110.refs_0_), channel_id=1, source_target_pairs={{0,1},{1,0},{2,3},{3,2},{4,5},{5,4},{6,7},{7,6},{8,9},{9,8},{10,11... | collective-permute-start | bytes 49160 | tf_op jit(solution)/shard_map/ppermute | solution.py:225
  66.5 1.2 %collective-permute-start.25 = (f32[64,128]{1,0:T(8,128)S(1)}, f32[64,128]{1,0:T(8,128)S(1)}, u32[]{:S(2)}, u32[]{:S(2)}) collective-permute-start(f32[64,128]{1,0:T(8,128)S(1)} %get-tuple-element.114.refs_0_), channel_id=1, source_target_pairs={{0,1},{1,0},{2,3},{3,2},{4,5},{5,4},{6,7},{7,6},{8,9},{9,8},{10,11... | collective-permute-start | bytes 98312 | tf_op jit(solution)/shard_map/ppermute | solution.py:225
  69.2 1.4 %collective-permute-start.26 = (f32[64,128]{1,0:T(8,128)S(1)}, f32[64,128]{1,0:T(8,128)S(1)}, u32[]{:S(2)}, u32[]{:S(2)}) collective-permute-start(f32[64,128]{1,0:T(8,128)S(1)} %get-tuple-element.117), channel_id=1, source_target_pairs={{0,1},{1,0},{2,3},{3,2},{4,5},{5,4},{6,7},{7,6},{8,9},{9,8},{10,11... | collective-permute-start | bytes 98312 | tf_op jit(solution)/shard_map/ppermute | solution.py:225
  70.6 4.8 %collective-permute-start.30 = (f32[64,128]{1,0:T(8,128)S(1)}, f32[64,128]{1,0:T(8,128)S(1)}, u32[]{:S(2)}, u32[]{:S(2)}) collective-permute-start(f32[64,128]{1,0:T(8,128)S(1)} %get-tuple-element.121.refs_0_), channel_id=1, source_target_pairs={{0,1},{1,0},{2,3},{3,2},{4,5},{5,4},{6,7},{7,6},{8,9},{9,8},{10,11... | collective-permute-start | bytes 98312 | tf_op jit(solution)/shard_map/ppermute | solution.py:225
  71.0 7.8 %collective-permute-start.29 = (f32[64,128]{1,0:T(8,128)S(1)}, f32[64,128]{1,0:T(8,128)S(1)}, u32[]{:S(2)}, u32[]{:S(2)}) collective-permute-start(f32[64,128]{1,0:T(8,128)S(1)} %add.32.refs_0_), channel_id=1, source_target_pairs={{0,24},{2,26},{4,28},{6,30},{8,16},{10,18},{12,20},{14,22},{16,8},... | collective-permute-start | bytes 98312 | tf_op jit(solution)/shard_map/ppermute | solution.py:225
  72.6 6.2 %collective-permute-start.28 = (f32[64,128]{1,0:T(8,128)S(1)}, f32[64,128]{1,0:T(8,128)S(1)}, u32[]{:S(2)}, u32[]{:S(2)}) collective-permute-start(f32[64,128]{1,0:T(8,128)S(1)} %add.32.refs_0_), channel_id=1, source_target_pairs={{0,16},{2,18},{4,20},{6,22},{8,24},{10,26},{12,28},{14,30},{16,0},... | collective-permute-start | bytes 98312 | tf_op jit(solution)/shard_map/ppermute | solution.py:225
  73.0 5.8 %collective-permute-start.27 = (f32[64,128]{1,0:T(8,128)S(1)}, f32[64,128]{1,0:T(8,128)S(1)}, u32[]{:S(2)}, u32[]{:S(2)}) collective-permute-start(f32[64,128]{1,0:T(8,128)S(1)} %add.32.refs_0_), channel_id=1, source_target_pairs={{0,8},{2,10},{4,12},{6,14},{8,0},{10,2},{12,4},{14,6},{16,24},{18,... | collective-permute-start | bytes 98312 | tf_op jit(solution)/shard_map/ppermute | solution.py:225
  79.1 5.9 %collective-permute-start.33 = (bf16[256,128]{1,0:T(8,128)(2,1)S(1)}, bf16[256,128]{1,0:T(8,128)(2,1)S(1)}, u32[]{:S(2)}, u32[]{:S(2)}) collective-permute-start(bf16[256,128]{1,0:T(8,128)(2,1)S(1)} %get-tuple-element.131.refs_0_), channel_id=1, source_target_pairs={{0,6},{2,4},{4,2},{6,0},{8,14},{10,12},{12,10},{14,8},{16,22},{18,... | collective-permute-start | bytes 196616 | tf_op jit(solution)/shard_map/ppermute | solution.py:225
  80.8 4.6 %collective-permute-start.32 = (bf16[256,128]{1,0:T(8,128)(2,1)S(1)}, bf16[256,128]{1,0:T(8,128)(2,1)S(1)}, u32[]{:S(2)}, u32[]{:S(2)}) collective-permute-start(bf16[256,128]{1,0:T(8,128)(2,1)S(1)} %get-tuple-element.131.refs_0_), channel_id=1, source_target_pairs={{0,4},{2,6},{4,0},{6,2},{8,12},{10,14},{12,8},{14,10},{16,20},{18,... | collective-permute-start | bytes 196616 | tf_op jit(solution)/shard_map/ppermute | solution.py:225
  82.1 4.3 %collective-permute-start.31 = (bf16[256,128]{1,0:T(8,128)(2,1)S(1)}, bf16[256,128]{1,0:T(8,128)(2,1)S(1)}, u32[]{:S(2)}, u32[]{:S(2)}) collective-permute-start(bf16[256,128]{1,0:T(8,128)(2,1)S(1)} %get-tuple-element.131.refs_0_), channel_id=1, source_target_pairs={{0,2},{2,0},{4,6},{6,4},{8,10},{10,8},{12,14},{14,12},{16,18},{18,... | collective-permute-start | bytes 196616 | tf_op jit(solution)/shard_map/ppermute | solution.py:225
  86.7 1.3 %collective-permute-start.34 = (f32[64,64]{1,0:T(8,128)S(1)}, f32[64,64]{1,0:T(8,128)S(1)}, u32[]{:S(2)}, u32[]{:S(2)}) collective-permute-start(f32[64,64]{1,0:T(8,128)S(1)} %get-tuple-element.133.refs_0_), channel_id=1, source_target_pairs={{0,1},{1,0},{2,3},{3,2},{4,5},{5,4},{6,7},{7,6},{8,9},{9,8},{10,11... | collective-permute-start | bytes 49160 | tf_op jit(solution)/shard_map/ppermute | solution.py:225
  89.1 1.2 %collective-permute-start.35 = (f32[64,128]{1,0:T(8,128)S(1)}, f32[64,128]{1,0:T(8,128)S(1)}, u32[]{:S(2)}, u32[]{:S(2)}) collective-permute-start(f32[64,128]{1,0:T(8,128)S(1)} %get-tuple-element.137), channel_id=1, source_target_pairs={{0,1},{1,0},{2,3},{3,2},{4,5},{5,4},{6,7},{7,6},{8,9},{9,8},{10,11... | collective-permute-start | bytes 98312 | tf_op jit(solution)/shard_map/ppermute | solution.py:225

commit v4 on v3

--- a/solution.py
+++ b/solution.py
@@ -13,7 +13,7 @@
 bf16 = jnp.bfloat16
 
 
-def call(kernel, outs, args, smem=()):
+def call(kernel, outs, args, smem=(), limit=16):
     specs = [
         pl.BlockSpec(memory_space=pltpu.SMEM if i in smem else pltpu.VMEM) for i in range(len(args))
     ]
@@ -22,7 +22,7 @@
         out_shape=[jax.ShapeDtypeStruct(shape, kind) for shape, kind in outs],
         in_specs=specs,
         out_specs=[pl.BlockSpec(memory_space=pltpu.VMEM) for _ in outs],
-        compiler_params=pltpu.CompilerParams(vmem_limit_bytes=40 << 20),
+        compiler_params=pltpu.CompilerParams(vmem_limit_bytes=limit << 20),
     )(*args)
 
 
@@ -56,66 +56,58 @@
     return jnp.dot(left, right, precision=highest, preferred_element_type=f32)
 
 
-def product(slots_ref, place_ref, tiles_ref, mix_ref, stack_ref, mine_refs):
+def layout_kernel(slots_ref, tiles_ref, dense_ref):
     blocks, slots, edge = tiles_ref.shape[:3]
-    vec_rows = stack_ref.shape[0]
-    sums = []
+    many = dense_ref.shape[0] // edge
+    dense_ref[...] = jnp.zeros_like(dense_ref)
     for b in range(blocks):
-        total = jnp.zeros((vec_rows, edge), f32)
-        for j in range(0, slots, 2):
-            chosen, tiles = [], []
-            for s in (j, j + 1):
+        for s in range(slots):
+
+            @pl.when(slots_ref[b, s] < many)
+            def _():
                 start = pl.multiple_of(slots_ref[b, s] * edge, edge)
-                chosen.append(stack_ref[:, pl.ds(start, edge)])
-                tiles.append(tiles_ref[b, s])
-            total = total + lax.dot_general(
-                jnp.concatenate(chosen, axis=1),
-                jnp.concatenate(tiles, axis=1),
-                (((1,), (1,)), ((), ())),
-                preferred_element_type=f32,
-            )
-        sums.append(total)
-    mixed = dot_nn(mix_ref[...], jnp.concatenate(sums, axis=1))
+                dense_ref[pl.ds(start, edge), b * edge : (b + 1) * edge] = tiles_ref[b, s].T
+
+
+def product(place_ref, dense_ref, mix_ref, stack, mine_refs):
+    edge = mine_refs[0].shape[-1]
+    mixed = dot_nn(mix_ref[...], jnp.dot(stack, dense_ref[...], preferred_element_type=f32))
     if len(mine_refs) == 2:
         first = place_ref[0] == 0
         low, high = mixed[:, :edge], mixed[:, edge:]
         mine_refs[0][...] = jnp.where(first, low, high)
         mine_refs[1][...] = jnp.where(first, high, low)
     else:
-        for b in range(blocks):
+        for b in range(mine_refs[0].shape[0]):
             mine_refs[0][b] = mixed[:, b * edge : (b + 1) * edge]
 
 
-def first_kernel(parts, slots_ref, place_ref, tiles_ref, mix_ref, *refs):
+def first_kernel(parts, place_ref, dense_ref, mix_ref, *refs):
     part_refs, stack_ref, mine_refs = refs[:parts], refs[parts], refs[parts + 1 :]
-    edge = tiles_ref.shape[2]
-    vec_rows = stack_ref.shape[0]
+    edge = mine_refs[0].shape[-1]
     at = 0
     for ref in part_refs:
         for i in range(ref.shape[0]):
             stack_ref[:, at : at + edge] = ref[i]
             at += edge
-    stack_ref[:, at : at + edge] = jnp.zeros((vec_rows, edge), bf16)
-    product(slots_ref, place_ref, tiles_ref, mix_ref, stack_ref, mine_refs)
-
-
-def next_kernel(nodes, many, slots_ref, place_ref, tiles_ref, mix_ref, basis_ref, raw_ref, sqs, dirs_ref, stack_ref, *mine_refs):
-    edge = tiles_ref.shape[2]
-    vecs, wide = raw_ref.shape
+    product(place_ref, dense_ref, mix_ref, stack_ref[...], mine_refs)
+
+
+def next_kernel(nodes, place_ref, dense_ref, mix_ref, basis_ref, raw_ref, sqs, dirs_ref, stack_ref, *mine_refs):
+    vecs = raw_ref.shape[0]
     square = sum(ref[...] for ref in sqs)[:, :1] / nodes
     scale = lax.rsqrt(square + epsilon)
-    stack_ref[:vecs, :wide] = basis_ref[:vecs]
-    stack_ref[vecs : 2 * vecs, :wide] = (raw_ref[...] * scale).astype(bf16)
-    stack_ref[2 * vecs :, :wide] = dirs_ref[...]
-    stack_ref[:, wide : wide + edge] = jnp.zeros((3 * vecs, edge), bf16)
-    product(slots_ref, place_ref, tiles_ref, mix_ref, stack_ref, mine_refs)
+    stack_ref[:vecs] = basis_ref[:vecs]
+    stack_ref[vecs : 2 * vecs] = (raw_ref[...] * scale).astype(bf16)
+    stack_ref[2 * vecs :] = dirs_ref[...]
+    product(place_ref, dense_ref, mix_ref, stack_ref[...], mine_refs)
 
 
 def gram_kernel(stack_ref, mix_ref, search_ref, pack_ref, search_out):
     wide = search_out.shape[1]
     vecs = mix_ref.shape[0]
-    rotated = times_stack(mix_ref[...], stack_ref[:, :wide])
-    search = times_stack(search_ref[...], stack_ref[vecs:, :wide])
+    rotated = times_stack(mix_ref[...], stack_ref[...])
+    search = times_stack(search_ref[...], stack_ref[vecs:])
     search_out[...] = search
     square = jnp.sum(search * search, axis=1, keepdims=True)
     pack_ref[...] = jnp.concatenate(
@@ -173,7 +165,7 @@
     dirs = search_ref[...] * scale_ref[:, :1]
     dirs_ref[...] = dirs.astype(bf16)
     own_dirs[...] = dirs[:, :edge]
-    basis = times_stack(dot_nn(inverse_ref[...], mix_ref[...]), stack_ref[:, :wide])
+    basis = times_stack(dot_nn(inverse_ref[...], mix_ref[...]), stack_ref[...])
     basis_ref[...] = pieces(basis)
     own_basis[...] = basis[:, :edge]
 
@@ -269,10 +261,15 @@
         mine_outs = [((vecs, edge), f32)] * 2
     else:
         mine_outs = [((blocks, vecs, edge), f32)]
-    stack_out = ((3 * vecs, wide + edge), bf16)
+    stack_out = ((3 * vecs, wide), bf16)
+    limit = 16 if wide <= 4096 else 56
+    dense, = call(
+        layout_kernel, [((wide, blocks * edge), bf16)], [slot_ids, tile_set], smem=(0,), limit=limit
+    )
 
     start = jnp.concatenate([start_basis, start_resid, start_search], axis=0)[None]
     parts = near_values(jnp.concatenate(far_values(start, near), axis=0), near)
+    parts, dense = lax.optimization_barrier((parts, dense))
     state = None
     sweeps = ritz_basis.shape[0]
     for sweep in range(sweeps):
@@ -281,26 +278,29 @@
             stack, *mine = call(
                 functools.partial(first_kernel, near),
                 [stack_out] + mine_outs,
-                [slot_ids, place, tile_set, mixing] + parts,
-                smem=(0, 1),
+                [place, dense, mixing] + parts,
+                smem=(0,),
+                limit=limit,
             )
         else:
             basis, raw, squares, dirs = state
             count = len(squares)
 
-            def kernel(s, p, t, m, b, r, *refs):
-                next_kernel(nodes, count, s, p, t, m, b, r, refs[:count], *refs[count:])
+            def kernel(p, t, m, b, r, *refs):
+                next_kernel(nodes, p, t, m, b, r, refs[:count], *refs[count:])
 
             stack, *mine = call(
                 kernel,
                 [stack_out] + mine_outs,
-                [slot_ids, place, tile_set, mixing, basis, raw] + squares + [dirs],
-                smem=(0, 1),
+                [place, dense, mixing, basis, raw] + squares + [dirs],
+                smem=(0,),
+                limit=limit,
             )
         pack, search = call(
             gram_kernel,
             [((vecs, 2 * vecs), f32), ((vecs, wide), f32)],
             [stack, mixing, ritz_search[sweep]],
+            limit=limit,
         )
         if panels == 2:
             other = swap(mine[1], 1, "panel")
@@ -323,6 +323,7 @@
             functools.partial(solve_kernel, len(far_parts)),
             [((len(far_parts) * vecs, edge), bf16), ((vecs, edge), f32)],
             far_parts + [inverse],
+            limit=limit,
         )
         adj_parts = near_values(held, near)
         basis, dirs, own_basis, own_dirs = call(
@@ -334,11 +335,13 @@
                 ((vecs, edge), f32),
             ],
             [inverse, scale, stack, mixing, search],
+            limit=limit,
         )
         wide_adj, cross = call(
             functools.partial(cross_kernel, nodes, near),
             [((vecs, wide), bf16), ((vecs, vecs), f32)],
             adj_parts + [basis],
+            limit=limit,
         )
         crosses = panel_terms(cross)
         cross_count = len(crosses)
@@ -350,6 +353,7 @@
             kernel_residual,
             [((vecs, wide), f32), ((vecs, edge), f32), ((vecs, vecs), f32), ((vecs, edge), f32)],
             crosses + [basis, wide_adj, own_adj],
+            limit=limit,
         )
         squares = panel_terms(square)
         state = (basis, raw, squares, dirs)

time: 91.3 us -> 88 us (0.964)
  waiting for transfers between devices: 24.2 us -> 22 us
  Pallas kernels: 26.6 us -> 25.5 us
    ppermute x36, waiting for transfers between devices: 24.2 us -> 22 us  [swap(): return lax.ppermute(value, axis, [(i, i ^ by) for i in range(size)])]
    pallas_call x21 -> x22, Pallas kernels: 26.6 us -> 25.5 us  [call(): pl.pallas_call(kernel, out_shape=[jax.ShapeDtypeStruct(shape, kind) for s...]
  transfers between devices with their start and end apart: 36 -> 36, of which waited for: 20 -> 20; matrix products, arithmetic and copies ran while one was open for 1% -> 0% of each run, Pallas kernels for 19% -> 21%
where the time goes in v4:
time: 88 us; the launch traced here: 87.7 us
  starting transfers between devices  35.9 us (41%)
  Pallas kernels  25.5 us (29%)
  waiting for transfers between devices  22 us (25%)
  local copies, waits for them, and re-layouts  1.98 us (2%)
  other arithmetic  1.5 us (2%)
  between operations  0.88 us (1%)
    ppermute x36, starting transfers between devices, swap(): return lax.ppermute(value, axis, [(i, i ^ by) for i in range(size)])  35.9 us
    pallas_call x22, Pallas kernels, call(): pl.pallas_call(kernel, out_shape=[jax.ShapeDtypeStruct(shape, kind) for s...  25.5 us
    ppermute x36, waiting for transfers between devices, swap(): return lax.ppermute(value, axis, [(i, i ^ by) for i in range(size)])  22 us
    unnamed x10, local copies, waits for them, and re-layouts  1.96 us
  transfers between devices with their start and end apart: 36, of which 20 were waited for; matrix products, arithmetic and copies ran while one was open for 0% of the time, Pallas kernels for 21%

profile of v4, /device:TPU:0, one launch (start us, length us, event | category | flops | bytes accessed | tf_op | source)
XLA Modules:
  0.0 87.7 jit_solution(8328832302039445622)
XLA Ops:
  0.6 0.8 maximum_bitcast_fusion
  1.4 5.0 %collective-permute-start.2 = (bf16[1,192,128]{2,1,0:T(8,128)(2,1)S(1)}, bf16[1,192,128]{2,1,0:T(8,128)(2,1)S(1)}, u32[]{:S(2)}, u32[]{:S(2)}) collective-permute-start(bf16[1,192,128]{2,1,0:T(8,128)(2,1)S(1)} %maximum_bitcast_fusion), channel_id=1, source_target_pairs={{0,24},{2,26},{4,28},{6,30},{8,16},{10,18},{12,20},{14,22},{16,8},... | collective-permute-start | bytes 147464 | tf_op jit(solution)/shard_map/ppermute | solution.py:217
  6.4 0.6 collective-permute-start
  7.1 0.7 copy-done.3
  7.8 1.2 %copy-done = bf16[1,1,2,16,128,128]{5,4,3,2,1,0:T(8,128)(2,1)S(1)} copy-done((bf16[1,1,2,16,128,128]{5,4,3,2,1,0:T(8,128)(2,1)S(1)}, bf16[1,1,2,16,128,128]{5,4,3,2,1,0:T(8,128)(2,1)}, u32[]{:S(2)}) %copy-start) | copy-done | bytes 1048600
  9.0 1.1 %shard_map.111.dense_ref.t = bf16[2048,256]{1,0:T(8,128)(2,1)S(1)} custom-call(s32[2,16]{1,0:T(2,128)S(1)} %compare_select_fusion.slots_ref, bf16[2,16,128,128]{3,2,1,0:T(8,128)(2,1)S(1)} %bitcast.25), custom_call_target="tpu_custom_call" | custom-call | tf_op jit(solution)/shard_map/pallas_call | solution.py:20
  10.2 1.2 %collective-permute-done.1 = bf16[1,192,128]{2,1,0:T(8,128)(2,1)S(1)} collective-permute-done((bf16[1,192,128]{2,1,0:T(8,128)(2,1)S(1)}, bf16[1,192,128]{2,1,0:T(8,128)(2,1)S(1)}, u32[]{:S(2)}, u32[]{:S(2)}) %collective-permute-start.1) | collective-permute-done | bytes 49184 | tf_op jit(solution)/shard_map/ppermute | solution.py:217
  11.5 2.5 %collective-permute-start.5 = (bf16[4,192,128]{2,1,0:T(8,128)(2,1)S(1)}, bf16[4,192,128]{2,1,0:T(8,128)(2,1)S(1)}, u32[]{:S(2)}, u32[]{:S(2)}) collective-permute-start(bf16[4,192,128]{2,1,0:T(8,128)(2,1)S(1)} %pad_maximum_fusion.refs_0_), channel_id=1, source_target_pairs={{0,6},{2,4},{4,2},{6,0},{8,14},{10,12},{12,10},{14,8},{16,22},{18,... | collective-permute-start | bytes 589832 | tf_op jit(solution)/shard_map/ppermute | solution.py:217
  14.0 0.5 collective-permute-start.4
  14.5 0.5 collective-permute-start.3
  15.0 4.8 %collective-permute-done.5.refs_3_ = bf16[4,192,128]{2,1,0:T(8,128)(2,1)S(1)} collective-permute-done((bf16[4,192,128]{2,1,0:T(8,128)(2,1)S(1)}, bf16[4,192,128]{2,1,0:T(8,128)(2,1)S(1)}, u32[]{:S(2)}, u32[]{:S(2)}) %collective-permute-start.5) | collective-permute-done | bytes 196640 | tf_op jit(solution)/shard_map/ppermute | solution.py:217
  19.8 2.6 %collective-permute-done.4.refs_2_ = bf16[4,192,128]{2,1,0:T(8,128)(2,1)S(1)} collective-permute-done((bf16[4,192,128]{2,1,0:T(8,128)(2,1)S(1)}, bf16[4,192,128]{2,1,0:T(8,128)(2,1)S(1)}, u32[]{:S(2)}, u32[]{:S(2)}) %collective-permute-start.4) | collective-permute-done | bytes 196640 | tf_op jit(solution)/shard_map/ppermute | solution.py:217
  22.5 0.8 shard_map.112
  23.4 1.1 %shard_map.113 = (f32[64,128]{1,0:T(8,128)S(1)}, f32[64,2048]{1,0:T(8,128)S(1)}) custom-call(bf16[192,2048]{1,0:T(8,128)(2,1)S(1)} %get-tuple-element.84.stack_ref, f32[64,192]{1,0:T(8,128)S(1)} %get-tuple-element.150.mix_ref, f32[64,128]{1,0:T(8,128)S(1)} %get-tuple-element.154.search_ref), custom_call_target="tpu_custom_call" | custom-call | tf_op jit(solution)/shard_map/pallas_call | solution.py:20
  24.5 0.5 collective-permute-start.10
  25.1 4.0 %collective-permute-start.9 = (f32[64,128]{1,0:T(8,128)S(1)}, f32[64,128]{1,0:T(8,128)S(1)}, u32[]{:S(2)}, u32[]{:S(2)}) collective-permute-start(f32[64,128]{1,0:T(8,128)S(1)} %add.30.refs_0_), channel_id=1, source_target_pairs={{0,24},{2,26},{4,28},{6,30},{8,16},{10,18},{12,20},{14,22},{16,8},... | collective-permute-start | bytes 98312 | tf_op jit(solution)/shard_map/ppermute | solution.py:217
  29.1 0.6 collective-permute-start.7
  29.8 3.4 %shard_map.114 = (f32[64,64]{1,0:T(8,128)S(1)}, f32[64,128]{1,0:T(8,128)S(1)}) custom-call(f32[64,128]{1,0:T(8,128)S(1)} %get-tuple-element.87.refs_0_, f32[64,128]{1,0:T(8,128)S(1)} %collective-permute-done.10.refs_1_), custom_call_target="tpu_custom_call" | custom-call | tf_op jit(solution)/shard_map/pallas_call | solution.py:20
  33.1 0.8 collective-permute-done.8.refs_2_
  34.2 1.4 %collective-permute-start.13 = (bf16[256,128]{1,0:T(8,128)(2,1)S(1)}, bf16[256,128]{1,0:T(8,128)(2,1)S(1)}, u32[]{:S(2)}, u32[]{:S(2)}) collective-permute-start(bf16[256,128]{1,0:T(8,128)(2,1)S(1)} %get-tuple-element.97.refs_0_), channel_id=1, source_target_pairs={{0,6},{2,4},{4,2},{6,0},{8,14},{10,12},{12,10},{14,8},{16,22},{18,... | collective-permute-start | bytes 196616 | tf_op jit(solution)/shard_map/ppermute | solution.py:217
  35.6 0.8 collective-permute-start.12
  36.4 1.4 %collective-permute-start.11 = (bf16[256,128]{1,0:T(8,128)(2,1)S(1)}, bf16[256,128]{1,0:T(8,128)(2,1)S(1)}, u32[]{:S(2)}, u32[]{:S(2)}) collective-permute-start(bf16[256,128]{1,0:T(8,128)(2,1)S(1)} %get-tuple-element.97.refs_0_), channel_id=1, source_target_pairs={{0,2},{2,0},{4,6},{6,4},{8,10},{10,8},{12,14},{14,12},{16,18},{18,... | collective-permute-start | bytes 196616 | tf_op jit(solution)/shard_map/ppermute | solution.py:217
  37.7 1.2 %shard_map.115 = (bf16[192,2048]{1,0:T(8,128)(2,1)S(1)}, bf16[64,2048]{1,0:T(8,128)(2,1)S(1)}, f32[64,128]{1,0:T(8,128)}, f32[64,128]{1,0:T(8,128)}) custom-call(f32[64,64]{1,0:T(8,128)S(1)} %get-tuple-element.89.inverse_ref.refs_4_, f32[64,128]{1,0:T(8,128)S(1)} %get-tuple-element.90.scale_ref, bf16[192,2048]{1,0:T(8,128)(2,1)S(1)} %get-tuple-element.84.stack_ref, ...), custom_call_target="tpu_custom_call" | custom-call | tf_op jit(solution)/shard_map/pallas_call | solution.py:20
  38.9 0.7 collective-permute-done.13.refs_3_
  39.6 0.7 collective-permute-done.12.refs_2_
  40.3 0.3 collective-permute-done.11.refs_1_
  40.6 0.4 shard_map.117
  41.1 1.2 %collective-permute-done.14.refs_1_ = f32[64,64]{1,0:T(8,128)S(1)} collective-permute-done((f32[64,64]{1,0:T(8,128)S(1)}, f32[64,64]{1,0:T(8,128)S(1)}, u32[]{:S(2)}, u32[]{:S(2)}) %collective-permute-start.14) | collective-permute-done | bytes 16416 | tf_op jit(solution)/shard_map/ppermute | solution.py:217
  42.3 0.9 %shard_map.118 = (f32[64,2048]{1,0:T(8,128)S(1)}, f32[64,128]{1,0:T(8,128)S(1)}, f32[64,64]{1,0:T(8,128)}, f32[64,128]{1,0:T(8,128)}) custom-call(f32[64,64]{1,0:T(8,128)S(1)} %get-tuple-element.98.refs_0_, f32[64,64]{1,0:T(8,128)S(1)} %collective-permute-done.14.refs_1_, bf16[192,2048]{1,0:T(8,128)(2,1)S(1)} %get-tuple-element.92.refs_4_.refs_2_.b, ...), custom_call_target="tpu_custom_call" | custom-call | tf_op jit(solution)/shard_map/pallas_call | solution.py:20
  43.4 1.0 %collective-permute-done.15.refs_1_ = f32[64,128]{1,0:T(8,128)S(1)} collective-permute-done((f32[64,128]{1,0:T(8,128)S(1)}, f32[64,128]{1,0:T(8,128)S(1)}, u32[]{:S(2)}, u32[]{:S(2)}) %collective-permute-start.15) | collective-permute-done | bytes 32800 | tf_op jit(solution)/shard_map/ppermute | solution.py:217
  44.4 0.8 shard_map.119
  45.4 1.1 %shard_map.120 = (f32[64,128]{1,0:T(8,128)S(1)}, f32[64,2048]{1,0:T(8,128)S(1)}) custom-call(bf16[192,2048]{1,0:T(8,128)(2,1)S(1)} %get-tuple-element.106.stack_ref, f32[64,192]{1,0:T(8,128)S(1)} %get-tuple-element.152.m.mix_ref, f32[64,128]{1,0:T(8,128)S(1)} %get-tuple-element.155.search_ref), custom_call_target="tpu_custom_call" | custom-call | tf_op jit(solution)/shard_map/pallas_call | solution.py:20
  46.6 0.4 collective-permute-start.20
  47.0 2.8 %collective-permute-start.19 = (f32[64,128]{1,0:T(8,128)S(1)}, f32[64,128]{1,0:T(8,128)S(1)}, u32[]{:S(2)}, u32[]{:S(2)}) collective-permute-start(f32[64,128]{1,0:T(8,128)S(1)} %add.31.refs_0_), channel_id=1, source_target_pairs={{0,24},{2,26},{4,28},{6,30},{8,16},{10,18},{12,20},{14,22},{16,8},... | collective-permute-start | bytes 98312 | tf_op jit(solution)/shard_map/ppermute | solution.py:217
  49.8 1.6 %collective-permute-start.17 = (f32[64,128]{1,0:T(8,128)S(1)}, f32[64,128]{1,0:T(8,128)S(1)}, u32[]{:S(2)}, u32[]{:S(2)}) collective-permute-start(f32[64,128]{1,0:T(8,128)S(1)} %add.31.refs_0_), channel_id=1, source_target_pairs={{0,8},{2,10},{4,12},{6,14},{8,0},{10,2},{12,4},{14,6},{16,24},{18,... | collective-permute-start | bytes 98312 | tf_op jit(solution)/shard_map/ppermute | solution.py:217
  51.4 3.4 %shard_map.121 = (f32[64,64]{1,0:T(8,128)S(1)}, f32[64,128]{1,0:T(8,128)S(1)}) custom-call(f32[64,128]{1,0:T(8,128)S(1)} %get-tuple-element.109.refs_0_, f32[64,128]{1,0:T(8,128)S(1)} %collective-permute-done.20.refs_1_), custom_call_target="tpu_custom_call" | custom-call | tf_op jit(solution)/shard_map/pallas_call | solution.py:20
  55.1 1.5 %collective-permute-start.23 = (bf16[256,128]{1,0:T(8,128)(2,1)S(1)}, bf16[256,128]{1,0:T(8,128)(2,1)S(1)}, u32[]{:S(2)}, u32[]{:S(2)}) collective-permute-start(bf16[256,128]{1,0:T(8,128)(2,1)S(1)} %get-tuple-element.119.refs_0_), channel_id=1, source_target_pairs={{0,6},{2,4},{4,2},{6,0},{8,14},{10,12},{12,10},{14,8},{16,22},{18,... | collective-permute-start | bytes 196616 | tf_op jit(solution)/shard_map/ppermute | solution.py:217
  56.5 1.4 %collective-permute-start.22 = (bf16[256,128]{1,0:T(8,128)(2,1)S(1)}, bf16[256,128]{1,0:T(8,128)(2,1)S(1)}, u32[]{:S(2)}, u32[]{:S(2)}) collective-permute-start(bf16[256,128]{1,0:T(8,128)(2,1)S(1)} %get-tuple-element.119.refs_0_), channel_id=1, source_target_pairs={{0,4},{2,6},{4,0},{6,2},{8,12},{10,14},{12,8},{14,10},{16,20},{18,... | collective-permute-start | bytes 196616 | tf_op jit(solution)/shard_map/ppermute | solution.py:217
  58.0 0.6 collective-permute-start.21
  58.6 1.2 %shard_map.122 = (bf16[192,2048]{1,0:T(8,128)(2,1)S(1)}, bf16[64,2048]{1,0:T(8,128)(2,1)S(1)}, f32[64,128]{1,0:T(8,128)}, f32[64,128]{1,0:T(8,128)}) custom-call(f32[64,64]{1,0:T(8,128)S(1)} %get-tuple-element.111.inverse_ref.refs_4_, f32[64,128]{1,0:T(8,128)S(1)} %get-tuple-element.112.scale_ref, bf16[192,2048]{1,0:T(8,128)(2,1)S(1)} %get-tuple-element.106.stack_ref, ...), custom_call_target="tpu_custom_call" | custom-call | tf_op jit(solution)/shard_map/pallas_call | solution.py:20
  59.8 1.1 %collective-permute-done.23.refs_3_ = bf16[256,128]{1,0:T(8,128)(2,1)S(1)} collective-permute-done((bf16[256,128]{1,0:T(8,128)(2,1)S(1)}, bf16[256,128]{1,0:T(8,128)(2,1)S(1)}, u32[]{:S(2)}, u32[]{:S(2)}) %collective-permute-start.23) | collective-permute-done | bytes 65568 | tf_op jit(solution)/shard_map/ppermute | solution.py:217
  60.9 0.4 collective-permute-done.22.refs_2_
  61.2 1.0 %collective-permute-done.21.refs_1_ = bf16[256,128]{1,0:T(8,128)(2,1)S(1)} collective-permute-done((bf16[256,128]{1,0:T(8,128)(2,1)S(1)}, bf16[256,128]{1,0:T(8,128)(2,1)S(1)}, u32[]{:S(2)}, u32[]{:S(2)}) %collective-permute-start.21) | collective-permute-done | bytes 65568 | tf_op jit(solution)/shard_map/ppermute | solution.py:217
  62.2 0.4 shard_map.124
  62.7 1.2 %collective-permute-done.24.refs_1_ = f32[64,64]{1,0:T(8,128)S(1)} collective-permute-done((f32[64,64]{1,0:T(8,128)S(1)}, f32[64,64]{1,0:T(8,128)S(1)}, u32[]{:S(2)}, u32[]{:S(2)}) %collective-permute-start.24) | collective-permute-done | bytes 16416 | tf_op jit(solution)/shard_map/ppermute | solution.py:217
  63.9 0.9 %shard_map.125 = (f32[64,2048]{1,0:T(8,128)S(1)}, f32[64,128]{1,0:T(8,128)S(1)}, f32[64,64]{1,0:T(8,128)}, f32[64,128]{1,0:T(8,128)}) custom-call(f32[64,64]{1,0:T(8,128)S(1)} %get-tuple-element.120.refs_0_, f32[64,64]{1,0:T(8,128)S(1)} %collective-permute-done.24.refs_1_, bf16[192,2048]{1,0:T(8,128)(2,1)S(1)} %get-tuple-element.114.refs_4_.refs_2_.b, ...), custom_call_target="tpu_custom_call" | custom-call | tf_op jit(solution)/shard_map/pallas_call | solution.py:20
  65.0 1.0 %collective-permute-done.25.refs_1_ = f32[64,128]{1,0:T(8,128)S(1)} collective-permute-done((f32[64,128]{1,0:T(8,128)S(1)}, f32[64,128]{1,0:T(8,128)S(1)}, u32[]{:S(2)}, u32[]{:S(2)}) %collective-permute-start.25) | collective-permute-done | bytes 32800 | tf_op jit(solution)/shard_map/ppermute | solution.py:217
  66.0 0.8 shard_map.126
  67.0 1.1 %shard_map.127 = (f32[64,128]{1,0:T(8,128)S(1)}, f32[64,2048]{1,0:T(8,128)S(1)}) custom-call(bf16[192,2048]{1,0:T(8,128)(2,1)S(1)} %get-tuple-element.128.stack_ref, f32[64,192]{1,0:T(8,128)S(1)} %get-tuple-element.151.m.mix_ref, f32[64,128]{1,0:T(8,128)S(1)} %get-tuple-element.153.search_ref), custom_call_target="tpu_custom_call" | custom-call | tf_op jit(solution)/shard_map/pallas_call | solution.py:20
  68.2 0.4 collective-permute-start.30
  68.6 3.0 %collective-permute-start.29 = (f32[64,128]{1,0:T(8,128)S(1)}, f32[64,128]{1,0:T(8,128)S(1)}, u32[]{:S(2)}, u32[]{:S(2)}) collective-permute-start(f32[64,128]{1,0:T(8,128)S(1)} %add.32.refs_0_), channel_id=1, source_target_pairs={{0,24},{2,26},{4,28},{6,30},{8,16},{10,18},{12,20},{14,22},{16,8},... | collective-permute-start | bytes 98312 | tf_op jit(solution)/shard_map/ppermute | solution.py:217
  71.6 1.4 %collective-permute-start.27 = (f32[64,128]{1,0:T(8,128)S(1)}, f32[64,128]{1,0:T(8,128)S(1)}, u32[]{:S(2)}, u32[]{:S(2)}) collective-permute-start(f32[64,128]{1,0:T(8,128)S(1)} %add.32.refs_0_), channel_id=1, source_target_pairs={{0,8},{2,10},{4,12},{6,14},{8,0},{10,2},{12,4},{14,6},{16,24},{18,... | collective-permute-start | bytes 98312 | tf_op jit(solution)/shard_map/ppermute | solution.py:217
  73.0 3.4 %shard_map.128 = (f32[64,64]{1,0:T(8,128)S(1)}, f32[64,128]{1,0:T(8,128)S(1)}) custom-call(f32[64,128]{1,0:T(8,128)S(1)} %get-tuple-element.131.refs_0_, f32[64,128]{1,0:T(8,128)S(1)} %collective-permute-done.30.refs_1_), custom_call_target="tpu_custom_call" | custom-call | tf_op jit(solution)/shard_map/pallas_call | solution.py:20
  76.7 1.4 %collective-permute-start.33 = (bf16[256,128]{1,0:T(8,128)(2,1)S(1)}, bf16[256,128]{1,0:T(8,128)(2,1)S(1)}, u32[]{:S(2)}, u32[]{:S(2)}) collective-permute-start(bf16[256,128]{1,0:T(8,128)(2,1)S(1)} %get-tuple-element.141.refs_0_), channel_id=1, source_target_pairs={{0,6},{2,4},{4,2},{6,0},{8,14},{10,12},{12,10},{14,8},{16,22},{18,... | collective-permute-start | bytes 196616 | tf_op jit(solution)/shard_map/ppermute | solution.py:217
  78.1 0.8 collective-permute-start.32
  78.8 1.4 %collective-permute-start.31 = (bf16[256,128]{1,0:T(8,128)(2,1)S(1)}, bf16[256,128]{1,0:T(8,128)(2,1)S(1)}, u32[]{:S(2)}, u32[]{:S(2)}) collective-permute-start(bf16[256,128]{1,0:T(8,128)(2,1)S(1)} %get-tuple-element.141.refs_0_), channel_id=1, source_target_pairs={{0,2},{2,0},{4,6},{6,4},{8,10},{10,8},{12,14},{14,12},{16,18},{18,... | collective-permute-start | bytes 196616 | tf_op jit(solution)/shard_map/ppermute | solution.py:217
  80.2 1.3 %shard_map.129 = (bf16[192,2048]{1,0:T(8,128)(2,1)S(1)}, bf16[64,2048]{1,0:T(8,128)(2,1)}, f32[64,128]{1,0:T(8,128)}, f32[64,128]{1,0:T(8,128)}) custom-call(f32[64,64]{1,0:T(8,128)S(1)} %get-tuple-element.133.inverse_ref.refs_4_, f32[64,128]{1,0:T(8,128)S(1)} %get-tuple-element.134.scale_ref, bf16[192,2048]{1,0:T(8,128)(2,1)S(1)} %get-tuple-element.128.stack_ref, ...), custom_call_target="tpu_custom_call" | custom-call | tf_op jit(solution)/shard_map/pallas_call | solution.py:20
  81.5 0.9 collective-permute-done.33.refs_3_
  82.4 0.4 collective-permute-done.32.refs_2_
  83.1 0.4 shard_map.131
  83.5 1.2 %collective-permute-done.34.refs_1_ = f32[64,64]{1,0:T(8,128)S(1)} collective-permute-done((f32[64,64]{1,0:T(8,128)S(1)}, f32[64,64]{1,0:T(8,128)S(1)}, u32[]{:S(2)}, u32[]{:S(2)}) %collective-permute-start.34) | collective-permute-done | bytes 16416 | tf_op jit(solution)/shard_map/ppermute | solution.py:217
  84.7 1.1 %shard_map.132 = (f32[64,2048]{1,0:T(8,128)}, f32[64,128]{1,0:T(8,128)S(1)}, f32[64,64]{1,0:T(8,128)}, f32[64,128]{1,0:T(8,128)S(1)}) custom-call(f32[64,64]{1,0:T(8,128)S(1)} %get-tuple-element.143.refs_0_, f32[64,64]{1,0:T(8,128)S(1)} %collective-permute-done.34.refs_1_, bf16[192,2048]{1,0:T(8,128)(2,1)S(1)} %get-tuple-element.142.refs_4_.refs_2_, ...), custom_call_target="tpu_custom_call" | custom-call | tf_op jit(solution)/shard_map/pallas_call | solution.py:20
  86.0 1.0 %collective-permute-done.35 = f32[64,128]{1,0:T(8,128)S(1)} collective-permute-done((f32[64,128]{1,0:T(8,128)S(1)}, f32[64,128]{1,0:T(8,128)S(1)}, u32[]{:S(2)}, u32[]{:S(2)}) %collective-permute-start.35) | collective-permute-done | bytes 32800 | tf_op jit(solution)/shard_map/ppermute | solution.py:217
  87.1 0.6 rsqrt_multiply_fusion
  (49 shorter events, 2.6 us)
Async XLA Ops:
  1.4 8.8 %collective-permute-start.2 = (bf16[1,192,128]{2,1,0:T(8,128)(2,1)S(1)}, bf16[1,192,128]{2,1,0:T(8,128)(2,1)S(1)}, u32[]{:S(2)}, u32[]{:S(2)}) collective-permute-start(bf16[1,192,128]{2,1,0:T(8,128)(2,1)S(1)} %maximum_bitcast_fusion), channel_id=1, source_target_pairs={{0,24},{2,26},{4,28},{6,30},{8,16},{10,18},{12,20},{14,22},{16,8},... | collective-permute-start | bytes 147464 | tf_op jit(solution)/shard_map/ppermute | solution.py:217
  6.4 5.0 %collective-permute-start.1 = (bf16[1,192,128]{2,1,0:T(8,128)(2,1)S(1)}, bf16[1,192,128]{2,1,0:T(8,128)(2,1)S(1)}, u32[]{:S(2)}, u32[]{:S(2)}) collective-permute-start(bf16[1,192,128]{2,1,0:T(8,128)(2,1)S(1)} %maximum_bitcast_fusion), channel_id=1, source_target_pairs={{0,16},{2,18},{4,20},{6,22},{8,24},{10,26},{12,28},{14,30},{16,0},... | collective-permute-start | bytes 147464 | tf_op jit(solution)/shard_map/ppermute | solution.py:217
  6.4 5.0 %collective-permute-start = (bf16[1,192,128]{2,1,0:T(8,128)(2,1)S(1)}, bf16[1,192,128]{2,1,0:T(8,128)(2,1)S(1)}, u32[]{:S(2)}, u32[]{:S(2)}) collective-permute-start(bf16[1,192,128]{2,1,0:T(8,128)(2,1)S(1)} %maximum_bitcast_fusion), channel_id=1, source_target_pairs={{0,8},{2,10},{4,12},{6,14},{8,0},{10,2},{12,4},{14,6},{16,24},{18,... | collective-permute-start | bytes 147464 | tf_op jit(solution)/shard_map/ppermute | solution.py:217
  7.0 0.7 copy-start.3
  7.1 0.7 copy-start.4
  7.8 1.2 %copy-start = (bf16[1,1,2,16,128,128]{5,4,3,2,1,0:T(8,128)(2,1)S(1)}, bf16[1,1,2,16,128,128]{5,4,3,2,1,0:T(8,128)(2,1)}, u32[]{:S(2)}) copy-start(bf16[1,1,2,16,128,128]{5,4,3,2,1,0:T(8,128)(2,1)} %param.8) | copy-start | bytes 3145732
  10.2 4.9 %copy-start.1 = (f32[3,64,192]{2,1,0:T(8,128)S(1)}, f32[3,64,192]{2,1,0:T(8,128)}, u32[]{:S(2)}) copy-start(f32[3,64,192]{2,1,0:T(8,128)} %param.14) | copy-start | bytes 442372
  11.5 8.4 %collective-permute-start.5 = (bf16[4,192,128]{2,1,0:T(8,128)(2,1)S(1)}, bf16[4,192,128]{2,1,0:T(8,128)(2,1)S(1)}, u32[]{:S(2)}, u32[]{:S(2)}) collective-permute-start(bf16[4,192,128]{2,1,0:T(8,128)(2,1)S(1)} %pad_maximum_fusion.refs_0_), channel_id=1, source_target_pairs={{0,6},{2,4},{4,2},{6,0},{8,14},{10,12},{12,10},{14,8},{16,22},{18,... | collective-permute-start | bytes 589832 | tf_op jit(solution)/shard_map/ppermute | solution.py:217
  14.0 8.4 %collective-permute-start.4 = (bf16[4,192,128]{2,1,0:T(8,128)(2,1)S(1)}, bf16[4,192,128]{2,1,0:T(8,128)(2,1)S(1)}, u32[]{:S(2)}, u32[]{:S(2)}) collective-permute-start(bf16[4,192,128]{2,1,0:T(8,128)(2,1)S(1)} %pad_maximum_fusion.refs_0_), channel_id=1, source_target_pairs={{0,4},{2,6},{4,0},{6,2},{8,12},{10,14},{12,8},{14,10},{16,20},{18,... | collective-permute-start | bytes 589832 | tf_op jit(solution)/shard_map/ppermute | solution.py:217
  14.5 8.0 %collective-permute-start.3 = (bf16[4,192,128]{2,1,0:T(8,128)(2,1)S(1)}, bf16[4,192,128]{2,1,0:T(8,128)(2,1)S(1)}, u32[]{:S(2)}, u32[]{:S(2)}) collective-permute-start(bf16[4,192,128]{2,1,0:T(8,128)(2,1)S(1)} %pad_maximum_fusion.refs_0_), channel_id=1, source_target_pairs={{0,2},{2,0},{4,6},{6,4},{8,10},{10,8},{12,14},{14,12},{16,18},{18,... | collective-permute-start | bytes 589832 | tf_op jit(solution)/shard_map/ppermute | solution.py:217
  22.5 0.9 %copy-start.2 = (f32[3,64,128]{2,1,0:T(8,128)S(1)}, f32[3,64,128]{2,1,0:T(8,128)}, u32[]{:S(2)}) copy-start(f32[3,64,128]{2,1,0:T(8,128)} %param.15) | copy-start | bytes 294916
  23.3 1.3 %collective-permute-start.6 = (f32[64,128]{1,0:T(8,128)S(1)}, f32[64,128]{1,0:T(8,128)S(1)}, u32[]{:S(2)}, u32[]{:S(2)}) collective-permute-start(f32[64,128]{1,0:T(8,128)S(1)} %get-tuple-element.83), channel_id=1, source_target_pairs={{0,1},{1,0},{2,3},{3,2},{4,5},{5,4},{6,7},{7,6},{8,9},{9,8},{10,11... | collective-permute-start | bytes 98312 | tf_op jit(solution)/shard_map/ppermute | solution.py:217
  24.5 5.2 %collective-permute-start.10 = (f32[64,128]{1,0:T(8,128)S(1)}, f32[64,128]{1,0:T(8,128)S(1)}, u32[]{:S(2)}, u32[]{:S(2)}) collective-permute-start(f32[64,128]{1,0:T(8,128)S(1)} %get-tuple-element.87.refs_0_), channel_id=1, source_target_pairs={{0,1},{1,0},{2,3},{3,2},{4,5},{5,4},{6,7},{7,6},{8,9},{9,8},{10,11... | collective-permute-start | bytes 98312 | tf_op jit(solution)/shard_map/ppermute | solution.py:217
  25.1 8.1 %collective-permute-start.9 = (f32[64,128]{1,0:T(8,128)S(1)}, f32[64,128]{1,0:T(8,128)S(1)}, u32[]{:S(2)}, u32[]{:S(2)}) collective-permute-start(f32[64,128]{1,0:T(8,128)S(1)} %add.30.refs_0_), channel_id=1, source_target_pairs={{0,24},{2,26},{4,28},{6,30},{8,16},{10,18},{12,20},{14,22},{16,8},... | collective-permute-start | bytes 98312 | tf_op jit(solution)/shard_map/ppermute | solution.py:217
  29.1 4.8 %collective-permute-start.8 = (f32[64,128]{1,0:T(8,128)S(1)}, f32[64,128]{1,0:T(8,128)S(1)}, u32[]{:S(2)}, u32[]{:S(2)}) collective-permute-start(f32[64,128]{1,0:T(8,128)S(1)} %add.30.refs_0_), channel_id=1, source_target_pairs={{0,16},{2,18},{4,20},{6,22},{8,24},{10,26},{12,28},{14,30},{16,0},... | collective-permute-start | bytes 98312 | tf_op jit(solution)/shard_map/ppermute | solution.py:217
  29.1 4.8 %collective-permute-start.7 = (f32[64,128]{1,0:T(8,128)S(1)}, f32[64,128]{1,0:T(8,128)S(1)}, u32[]{:S(2)}, u32[]{:S(2)}) collective-permute-start(f32[64,128]{1,0:T(8,128)S(1)} %add.30.refs_0_), channel_id=1, source_target_pairs={{0,8},{2,10},{4,12},{6,14},{8,0},{10,2},{12,4},{14,6},{16,24},{18,... | collective-permute-start | bytes 98312 | tf_op jit(solution)/shard_map/ppermute | solution.py:217
  34.2 5.5 %collective-permute-start.13 = (bf16[256,128]{1,0:T(8,128)(2,1)S(1)}, bf16[256,128]{1,0:T(8,128)(2,1)S(1)}, u32[]{:S(2)}, u32[]{:S(2)}) collective-permute-start(bf16[256,128]{1,0:T(8,128)(2,1)S(1)} %get-tuple-element.97.refs_0_), channel_id=1, source_target_pairs={{0,6},{2,4},{4,2},{6,0},{8,14},{10,12},{12,10},{14,8},{16,22},{18,... | collective-permute-start | bytes 196616 | tf_op jit(solution)/shard_map/ppermute | solution.py:217
  35.6 4.7 %collective-permute-start.12 = (bf16[256,128]{1,0:T(8,128)(2,1)S(1)}, bf16[256,128]{1,0:T(8,128)(2,1)S(1)}, u32[]{:S(2)}, u32[]{:S(2)}) collective-permute-start(bf16[256,128]{1,0:T(8,128)(2,1)S(1)} %get-tuple-element.97.refs_0_), channel_id=1, source_target_pairs={{0,4},{2,6},{4,0},{6,2},{8,12},{10,14},{12,8},{14,10},{16,20},{18,... | collective-permute-start | bytes 196616 | tf_op jit(solution)/shard_map/ppermute | solution.py:217
  36.4 4.3 %collective-permute-start.11 = (bf16[256,128]{1,0:T(8,128)(2,1)S(1)}, bf16[256,128]{1,0:T(8,128)(2,1)S(1)}, u32[]{:S(2)}, u32[]{:S(2)}) collective-permute-start(bf16[256,128]{1,0:T(8,128)(2,1)S(1)} %get-tuple-element.97.refs_0_), channel_id=1, source_target_pairs={{0,2},{2,0},{4,6},{6,4},{8,10},{10,8},{12,14},{14,12},{16,18},{18,... | collective-permute-start | bytes 196616 | tf_op jit(solution)/shard_map/ppermute | solution.py:217
  41.0 1.3 %collective-permute-start.14 = (f32[64,64]{1,0:T(8,128)S(1)}, f32[64,64]{1,0:T(8,128)S(1)}, u32[]{:S(2)}, u32[]{:S(2)}) collective-permute-start(f32[64,64]{1,0:T(8,128)S(1)} %get-tuple-element.98.refs_0_), channel_id=1, source_target_pairs={{0,1},{1,0},{2,3},{3,2},{4,5},{5,4},{6,7},{7,6},{8,9},{9,8},{10,11... | collective-permute-start | bytes 49160 | tf_op jit(solution)/shard_map/ppermute | solution.py:217
  43.2 1.2 %collective-permute-start.15 = (f32[64,128]{1,0:T(8,128)S(1)}, f32[64,128]{1,0:T(8,128)S(1)}, u32[]{:S(2)}, u32[]{:S(2)}) collective-permute-start(f32[64,128]{1,0:T(8,128)S(1)} %get-tuple-element.102.refs_0_), channel_id=1, source_target_pairs={{0,1},{1,0},{2,3},{3,2},{4,5},{5,4},{6,7},{7,6},{8,9},{9,8},{10,11... | collective-permute-start | bytes 98312 | tf_op jit(solution)/shard_map/ppermute | solution.py:217
  45.2 1.4 %collective-permute-start.16 = (f32[64,128]{1,0:T(8,128)S(1)}, f32[64,128]{1,0:T(8,128)S(1)}, u32[]{:S(2)}, u32[]{:S(2)}) collective-permute-start(f32[64,128]{1,0:T(8,128)S(1)} %get-tuple-element.105), channel_id=1, source_target_pairs={{0,1},{1,0},{2,3},{3,2},{4,5},{5,4},{6,7},{7,6},{8,9},{9,8},{10,11... | collective-permute-start | bytes 98312 | tf_op jit(solution)/shard_map/ppermute | solution.py:217
  46.6 4.8 %collective-permute-start.20 = (f32[64,128]{1,0:T(8,128)S(1)}, f32[64,128]{1,0:T(8,128)S(1)}, u32[]{:S(2)}, u32[]{:S(2)}) collective-permute-start(f32[64,128]{1,0:T(8,128)S(1)} %get-tuple-element.109.refs_0_), channel_id=1, source_target_pairs={{0,1},{1,0},{2,3},{3,2},{4,5},{5,4},{6,7},{7,6},{8,9},{9,8},{10,11... | collective-permute-start | bytes 98312 | tf_op jit(solution)/shard_map/ppermute | solution.py:217
  47.0 7.8 %collective-permute-start.19 = (f32[64,128]{1,0:T(8,128)S(1)}, f32[64,128]{1,0:T(8,128)S(1)}, u32[]{:S(2)}, u32[]{:S(2)}) collective-permute-start(f32[64,128]{1,0:T(8,128)S(1)} %add.31.refs_0_), channel_id=1, source_target_pairs={{0,24},{2,26},{4,28},{6,30},{8,16},{10,18},{12,20},{14,22},{16,8},... | collective-permute-start | bytes 98312 | tf_op jit(solution)/shard_map/ppermute | solution.py:217
  49.8 5.0 %collective-permute-start.18 = (f32[64,128]{1,0:T(8,128)S(1)}, f32[64,128]{1,0:T(8,128)S(1)}, u32[]{:S(2)}, u32[]{:S(2)}) collective-permute-start(f32[64,128]{1,0:T(8,128)S(1)} %add.31.refs_0_), channel_id=1, source_target_pairs={{0,16},{2,18},{4,20},{6,22},{8,24},{10,26},{12,28},{14,30},{16,0},... | collective-permute-start | bytes 98312 | tf_op jit(solution)/shard_map/ppermute | solution.py:217
  49.8 5.0 %collective-permute-start.17 = (f32[64,128]{1,0:T(8,128)S(1)}, f32[64,128]{1,0:T(8,128)S(1)}, u32[]{:S(2)}, u32[]{:S(2)}) collective-permute-start(f32[64,128]{1,0:T(8,128)S(1)} %add.31.refs_0_), channel_id=1, source_target_pairs={{0,8},{2,10},{4,12},{6,14},{8,0},{10,2},{12,4},{14,6},{16,24},{18,... | collective-permute-start | bytes 98312 | tf_op jit(solution)/shard_map/ppermute | solution.py:217
  55.1 5.8 %collective-permute-start.23 = (bf16[256,128]{1,0:T(8,128)(2,1)S(1)}, bf16[256,128]{1,0:T(8,128)(2,1)S(1)}, u32[]{:S(2)}, u32[]{:S(2)}) collective-permute-start(bf16[256,128]{1,0:T(8,128)(2,1)S(1)} %get-tuple-element.119.refs_0_), channel_id=1, source_target_pairs={{0,6},{2,4},{4,2},{6,0},{8,14},{10,12},{12,10},{14,8},{16,22},{18,... | collective-permute-start | bytes 196616 | tf_op jit(solution)/shard_map/ppermute | solution.py:217
  56.5 4.7 %collective-permute-start.22 = (bf16[256,128]{1,0:T(8,128)(2,1)S(1)}, bf16[256,128]{1,0:T(8,128)(2,1)S(1)}, u32[]{:S(2)}, u32[]{:S(2)}) collective-permute-start(bf16[256,128]{1,0:T(8,128)(2,1)S(1)} %get-tuple-element.119.refs_0_), channel_id=1, source_target_pairs={{0,4},{2,6},{4,0},{6,2},{8,12},{10,14},{12,8},{14,10},{16,20},{18,... | collective-permute-start | bytes 196616 | tf_op jit(solution)/shard_map/ppermute | solution.py:217
  58.0 4.3 %collective-permute-start.21 = (bf16[256,128]{1,0:T(8,128)(2,1)S(1)}, bf16[256,128]{1,0:T(8,128)(2,1)S(1)}, u32[]{:S(2)}, u32[]{:S(2)}) collective-permute-start(bf16[256,128]{1,0:T(8,128)(2,1)S(1)} %get-tuple-element.119.refs_0_), channel_id=1, source_target_pairs={{0,2},{2,0},{4,6},{6,4},{8,10},{10,8},{12,14},{14,12},{16,18},{18,... | collective-permute-start | bytes 196616 | tf_op jit(solution)/shard_map/ppermute | solution.py:217
  62.6 1.3 %collective-permute-start.24 = (f32[64,64]{1,0:T(8,128)S(1)}, f32[64,64]{1,0:T(8,128)S(1)}, u32[]{:S(2)}, u32[]{:S(2)}) collective-permute-start(f32[64,64]{1,0:T(8,128)S(1)} %get-tuple-element.120.refs_0_), channel_id=1, source_target_pairs={{0,1},{1,0},{2,3},{3,2},{4,5},{5,4},{6,7},{7,6},{8,9},{9,8},{10,11... | collective-permute-start | bytes 49160 | tf_op jit(solution)/shard_map/ppermute | solution.py:217
  64.8 1.2 %collective-permute-start.25 = (f32[64,128]{1,0:T(8,128)S(1)}, f32[64,128]{1,0:T(8,128)S(1)}, u32[]{:S(2)}, u32[]{:S(2)}) collective-permute-start(f32[64,128]{1,0:T(8,128)S(1)} %get-tuple-element.124.refs_0_), channel_id=1, source_target_pairs={{0,1},{1,0},{2,3},{3,2},{4,5},{5,4},{6,7},{7,6},{8,9},{9,8},{10,11... | collective-permute-start | bytes 98312 | tf_op jit(solution)/shard_map/ppermute | solution.py:217
  66.8 1.4 %collective-permute-start.26 = (f32[64,128]{1,0:T(8,128)S(1)}, f32[64,128]{1,0:T(8,128)S(1)}, u32[]{:S(2)}, u32[]{:S(2)}) collective-permute-start(f32[64,128]{1,0:T(8,128)S(1)} %get-tuple-element.127), channel_id=1, source_target_pairs={{0,1},{1,0},{2,3},{3,2},{4,5},{5,4},{6,7},{7,6},{8,9},{9,8},{10,11... | collective-permute-start | bytes 98312 | tf_op jit(solution)/shard_map/ppermute | solution.py:217
  68.2 4.8 %collective-permute-start.30 = (f32[64,128]{1,0:T(8,128)S(1)}, f32[64,128]{1,0:T(8,128)S(1)}, u32[]{:S(2)}, u32[]{:S(2)}) collective-permute-start(f32[64,128]{1,0:T(8,128)S(1)} %get-tuple-element.131.refs_0_), channel_id=1, source_target_pairs={{0,1},{1,0},{2,3},{3,2},{4,5},{5,4},{6,7},{7,6},{8,9},{9,8},{10,11... | collective-permute-start | bytes 98312 | tf_op jit(solution)/shard_map/ppermute | solution.py:217
  68.6 7.8 %collective-permute-start.29 = (f32[64,128]{1,0:T(8,128)S(1)}, f32[64,128]{1,0:T(8,128)S(1)}, u32[]{:S(2)}, u32[]{:S(2)}) collective-permute-start(f32[64,128]{1,0:T(8,128)S(1)} %add.32.refs_0_), channel_id=1, source_target_pairs={{0,24},{2,26},{4,28},{6,30},{8,16},{10,18},{12,20},{14,22},{16,8},... | collective-permute-start | bytes 98312 | tf_op jit(solution)/shard_map/ppermute | solution.py:217
  71.6 4.8 %collective-permute-start.28 = (f32[64,128]{1,0:T(8,128)S(1)}, f32[64,128]{1,0:T(8,128)S(1)}, u32[]{:S(2)}, u32[]{:S(2)}) collective-permute-start(f32[64,128]{1,0:T(8,128)S(1)} %add.32.refs_0_), channel_id=1, source_target_pairs={{0,16},{2,18},{4,20},{6,22},{8,24},{10,26},{12,28},{14,30},{16,0},... | collective-permute-start | bytes 98312 | tf_op jit(solution)/shard_map/ppermute | solution.py:217
  71.6 4.8 %collective-permute-start.27 = (f32[64,128]{1,0:T(8,128)S(1)}, f32[64,128]{1,0:T(8,128)S(1)}, u32[]{:S(2)}, u32[]{:S(2)}) collective-permute-start(f32[64,128]{1,0:T(8,128)S(1)} %add.32.refs_0_), channel_id=1, source_target_pairs={{0,8},{2,10},{4,12},{6,14},{8,0},{10,2},{12,4},{14,6},{16,24},{18,... | collective-permute-start | bytes 98312 | tf_op jit(solution)/shard_map/ppermute | solution.py:217
  76.7 5.7 %collective-permute-start.33 = (bf16[256,128]{1,0:T(8,128)(2,1)S(1)}, bf16[256,128]{1,0:T(8,128)(2,1)S(1)}, u32[]{:S(2)}, u32[]{:S(2)}) collective-permute-start(bf16[256,128]{1,0:T(8,128)(2,1)S(1)} %get-tuple-element.141.refs_0_), channel_id=1, source_target_pairs={{0,6},{2,4},{4,2},{6,0},{8,14},{10,12},{12,10},{14,8},{16,22},{18,... | collective-permute-start | bytes 196616 | tf_op jit(solution)/shard_map/ppermute | solution.py:217
  78.1 4.7 %collective-permute-start.32 = (bf16[256,128]{1,0:T(8,128)(2,1)S(1)}, bf16[256,128]{1,0:T(8,128)(2,1)S(1)}, u32[]{:S(2)}, u32[]{:S(2)}) collective-permute-start(bf16[256,128]{1,0:T(8,128)(2,1)S(1)} %get-tuple-element.141.refs_0_), channel_id=1, source_target_pairs={{0,4},{2,6},{4,0},{6,2},{8,12},{10,14},{12,8},{14,10},{16,20},{18,... | collective-permute-start | bytes 196616 | tf_op jit(solution)/shard_map/ppermute | solution.py:217
  78.8 4.3 %collective-permute-start.31 = (bf16[256,128]{1,0:T(8,128)(2,1)S(1)}, bf16[256,128]{1,0:T(8,128)(2,1)S(1)}, u32[]{:S(2)}, u32[]{:S(2)}) collective-permute-start(bf16[256,128]{1,0:T(8,128)(2,1)S(1)} %get-tuple-element.141.refs_0_), channel_id=1, source_target_pairs={{0,2},{2,0},{4,6},{6,4},{8,10},{10,8},{12,14},{14,12},{16,18},{18,... | collective-permute-start | bytes 196616 | tf_op jit(solution)/shard_map/ppermute | solution.py:217
  83.5 1.3 %collective-permute-start.34 = (f32[64,64]{1,0:T(8,128)S(1)}, f32[64,64]{1,0:T(8,128)S(1)}, u32[]{:S(2)}, u32[]{:S(2)}) collective-permute-start(f32[64,64]{1,0:T(8,128)S(1)} %get-tuple-element.143.refs_0_), channel_id=1, source_target_pairs={{0,1},{1,0},{2,3},{3,2},{4,5},{5,4},{6,7},{7,6},{8,9},{9,8},{10,11... | collective-permute-start | bytes 49160 | tf_op jit(solution)/shard_map/ppermute | solution.py:217
  85.9 1.2 %collective-permute-start.35 = (f32[64,128]{1,0:T(8,128)S(1)}, f32[64,128]{1,0:T(8,128)S(1)}, u32[]{:S(2)}, u32[]{:S(2)}) collective-permute-start(f32[64,128]{1,0:T(8,128)S(1)} %get-tuple-element.147), channel_id=1, source_target_pairs={{0,1},{1,0},{2,3},{3,2},{4,5},{5,4},{6,7},{7,6},{8,9},{9,8},{10,11... | collective-permute-start | bytes 98312 | tf_op jit(solution)/shard_map/ppermute | solution.py:217

commit v5 on v4

--- a/solution.py
+++ b/solution.py
@@ -13,7 +13,7 @@
 bf16 = jnp.bfloat16
 
 
-def call(kernel, outs, args, smem=(), limit=16):
+def call(kernel, outs, args, smem=(), limit=16, scratch=()):
     specs = [
         pl.BlockSpec(memory_space=pltpu.SMEM if i in smem else pltpu.VMEM) for i in range(len(args))
     ]
@@ -22,6 +22,7 @@
         out_shape=[jax.ShapeDtypeStruct(shape, kind) for shape, kind in outs],
         in_specs=specs,
         out_specs=[pl.BlockSpec(memory_space=pltpu.VMEM) for _ in outs],
+        scratch_shapes=[pltpu.VMEM(shape, kind) for shape, kind in scratch],
         compiler_params=pltpu.CompilerParams(vmem_limit_bytes=limit << 20),
     )(*args)
 
@@ -93,14 +94,36 @@
     product(place_ref, dense_ref, mix_ref, stack_ref[...], mine_refs)
 
 
-def next_kernel(nodes, place_ref, dense_ref, mix_ref, basis_ref, raw_ref, sqs, dirs_ref, stack_ref, *mine_refs):
-    vecs = raw_ref.shape[0]
-    square = sum(ref[...] for ref in sqs)[:, :1] / nodes
-    scale = lax.rsqrt(square + epsilon)
+def residual_terms(crosses, gram_ref):
+    both = sum(ref[...] for ref in crosses)
+    vecs = both.shape[0]
+    q = both[:, :vecs]
+    taken = q * (2.0 * q - dot_nn(gram_ref[...], q))
+    square = both[:, vecs : vecs + 1] - jnp.sum(taken.T, axis=1, keepdims=True)
+    return q, lax.rsqrt(jnp.maximum(square, 0.0) + epsilon)
+
+
+def next_kernel(place_ref, dense_ref, mix_ref, crosses, gram_ref, basis_ref, wide_ref, dirs_ref, stack_ref, *mine_refs):
+    vecs = wide_ref.shape[0]
+    q, scale = residual_terms(crosses, gram_ref)
+    high = q.astype(bf16)
+    low = (q - high.astype(f32)).astype(bf16)
+    terms = jnp.concatenate([high, high, low], axis=0)
+    basis = jnp.concatenate([basis_ref[: 2 * vecs], basis_ref[:vecs]], axis=0)
+    part = lax.dot_general(terms, basis, (((0,), (0,)), ((), ())), preferred_element_type=f32)
     stack_ref[:vecs] = basis_ref[:vecs]
-    stack_ref[vecs : 2 * vecs] = (raw_ref[...] * scale).astype(bf16)
+    stack_ref[vecs : 2 * vecs] = ((part - wide_ref[...].astype(f32)) * scale).astype(bf16)
     stack_ref[2 * vecs :] = dirs_ref[...]
     product(place_ref, dense_ref, mix_ref, stack_ref[...], mine_refs)
+
+
+def last_kernel(crosses, gram_ref, basis_ref, own_ref, resid_ref, rayleigh_ref):
+    vecs = own_ref.shape[0]
+    q, scale = residual_terms(crosses, gram_ref)
+    resid_ref[...] = (dot_tn(q, basis_ref[...]) - own_ref[...]) * scale
+    row_ids = lax.broadcasted_iota(jnp.int32, (vecs, vecs), 0)
+    lane_ids = lax.broadcasted_iota(jnp.int32, (vecs, vecs), 1)
+    rayleigh_ref[...] = jnp.where(row_ids == lane_ids, 1.0, 0.0) - q
 
 
 def gram_kernel(stack_ref, mix_ref, search_ref, pack_ref, search_out):
@@ -159,28 +182,31 @@
     inverse_ref[...] = inverse[:, vecs:]
 
 
-def basis_kernel(inverse_ref, scale_ref, stack_ref, mix_ref, search_ref, basis_ref, dirs_ref, own_basis, own_dirs):
-    wide = search_ref.shape[1]
-    edge = own_basis.shape[1]
-    dirs = search_ref[...] * scale_ref[:, :1]
-    dirs_ref[...] = dirs.astype(bf16)
-    own_dirs[...] = dirs[:, :edge]
-    basis = times_stack(dot_nn(inverse_ref[...], mix_ref[...]), stack_ref[...])
+def basis_kernel(nodes, packs, inverse_ref, scale_ref, stack_ref, mix_ref, search_ref, basis_ref, gram_ref, dirs_ref, *own_basis):
+    vecs = mix_ref.shape[0]
+    inverse = inverse_ref[...]
+    total = sum(ref[...] for ref in packs)[:, :vecs] / nodes
+    gram_ref[...] = dot_nt(dot_nn(inverse, total), inverse)
+    edge = dirs_ref.shape[1]
+    dirs_ref[...] = (search_ref[:, :edge] * scale_ref[:, :1]).astype(dirs_ref.dtype)
+    basis = times_stack(dot_nn(inverse, mix_ref[...]), stack_ref[...])
     basis_ref[...] = pieces(basis)
-    own_basis[...] = basis[:, :edge]
+    if own_basis:
+        own_basis[0][...] = basis[:, :edge]
 
 
 def solve_kernel(parts, *refs):
-    part_refs, inverse_ref, blocks_ref, own_ref = refs[:parts], refs[parts], refs[parts + 1], refs[parts + 2]
-    vecs, edge = own_ref.shape
+    part_refs, inverse_ref, blocks_ref, own_ref = refs[:parts], refs[parts], refs[parts + 1], refs[parts + 2 :]
+    vecs, edge = part_refs[0].shape
     solved = dot_nn(inverse_ref[...], jnp.concatenate([ref[...] for ref in part_refs], axis=1))
-    own_ref[...] = solved[:, :edge]
+    if own_ref:
+        own_ref[0][...] = solved[:, :edge]
     for i in range(parts):
         blocks_ref[i * vecs : (i + 1) * vecs, :] = solved[:, i * edge : (i + 1) * edge].astype(bf16)
 
 
 def cross_kernel(nodes, parts, *refs):
-    part_refs, basis_ref, wide_ref, cross_ref = refs[:parts], refs[parts], refs[parts + 1], refs[parts + 2]
+    part_refs, basis_ref, cross_ref, wide_ref = refs[:parts], refs[parts], refs[parts + 1], refs[parts + 2]
     vecs = wide_ref.shape[0]
     edge = part_refs[0].shape[1]
     at = 0
@@ -191,25 +217,10 @@
     cross = lax.dot_general(
         basis_ref[...], wide_ref[...], (((1,), (1,)), ((), ())), preferred_element_type=f32
     )
-    cross_ref[...] = (cross[:vecs] + cross[vecs : 2 * vecs] + cross[2 * vecs :]) / nodes
-
-
-def residual_kernel(crosses, basis_ref, wide_ref, own_ref, raw_ref, square_ref, rayleigh_ref, own_raw):
-    vecs = wide_ref.shape[0]
-    edge = own_raw.shape[1]
-    q = sum(ref[...] for ref in crosses)
-    high = q.astype(bf16)
-    low = (q - high.astype(f32)).astype(bf16)
-    terms = jnp.concatenate([high, high, low], axis=0)
-    basis = jnp.concatenate([basis_ref[: 2 * vecs], basis_ref[:vecs]], axis=0)
-    part = lax.dot_general(terms, basis, (((0,), (0,)), ((), ())), preferred_element_type=f32)
-    raw = part - wide_ref[...].astype(f32)
-    raw_ref[...] = raw
-    own_raw[...] = part[:, :edge] - own_ref[...]
-    square_ref[...] = jnp.broadcast_to(jnp.sum(raw * raw, axis=1, keepdims=True), square_ref.shape)
-    row_ids = lax.broadcasted_iota(jnp.int32, (vecs, vecs), 0)
-    lane_ids = lax.broadcasted_iota(jnp.int32, (vecs, vecs), 1)
-    rayleigh_ref[...] = jnp.where(row_ids == lane_ids, 1.0, 0.0) - q
+    cross = cross[:vecs] + cross[vecs : 2 * vecs] + cross[2 * vecs :]
+    values = wide_ref[...].astype(f32)
+    square = jnp.sum(values * values, axis=1, keepdims=True)
+    cross_ref[...] = jnp.concatenate([cross, jnp.broadcast_to(square, cross.shape)], axis=1) / nodes
 
 
 def swap(value, by, axis):
@@ -273,6 +284,7 @@
     state = None
     sweeps = ritz_basis.shape[0]
     for sweep in range(sweeps):
+        last = sweep == sweeps - 1
         mixing = ritz_basis[sweep]
         if state is None:
             stack, *mine = call(
@@ -283,16 +295,16 @@
                 limit=limit,
             )
         else:
-            basis, raw, squares, dirs = state
-            count = len(squares)
-
-            def kernel(p, t, m, b, r, *refs):
-                next_kernel(nodes, p, t, m, b, r, refs[:count], *refs[count:])
+            crosses, gram, basis, wide_adj, dirs = state
+            count = len(crosses)
+
+            def kernel(p, t, m, *refs):
+                next_kernel(p, t, m, refs[:count], *refs[count:])
 
             stack, *mine = call(
                 kernel,
                 [stack_out] + mine_outs,
-                [place, dense, mixing, basis, raw] + squares + [dirs],
+                [place, dense, mixing] + crosses + [gram, basis] + wide_adj + [dirs],
                 smem=(0,),
                 limit=limit,
             )
@@ -319,46 +331,49 @@
         )
         far_parts = far_values(rotated_adj, near)
         far_parts, inverse = lax.optimization_barrier((far_parts, inverse))
-        held, own_adj = call(
+        held, *own_adj = call(
             functools.partial(solve_kernel, len(far_parts)),
-            [((len(far_parts) * vecs, edge), bf16), ((vecs, edge), f32)],
+            [((len(far_parts) * vecs, edge), bf16)] + [((vecs, edge), f32)] * last,
             far_parts + [inverse],
             limit=limit,
         )
         adj_parts = near_values(held, near)
-        basis, dirs, own_basis, own_dirs = call(
-            basis_kernel,
+
+        def kernel_basis(*refs):
+            basis_kernel(nodes, refs[:pack_count], *refs[pack_count:])
+
+        basis, gram, dirs, *own_basis = call(
+            kernel_basis,
             [
                 ((3 * vecs, wide), bf16),
-                ((vecs, wide), bf16),
-                ((vecs, edge), f32),
-                ((vecs, edge), f32),
-            ],
-            [inverse, scale, stack, mixing, search],
+                ((vecs, vecs), f32),
+                ((vecs, edge), f32) if last else ((vecs, wide), bf16),
+            ]
+            + [((vecs, edge), f32)] * last,
+            packs + [inverse, scale, stack, mixing, search],
             limit=limit,
         )
-        wide_adj, cross = call(
+        wide_out = [((vecs, wide), bf16)]
+        cross, *wide_adj = call(
             functools.partial(cross_kernel, nodes, near),
-            [((vecs, wide), bf16), ((vecs, vecs), f32)],
+            [((vecs, 2 * vecs), f32)] + ([] if last else wide_out),
             adj_parts + [basis],
             limit=limit,
+            scratch=wide_out if last else [],
         )
         crosses = panel_terms(cross)
-        cross_count = len(crosses)
-
-        def kernel_residual(*refs):
-            residual_kernel(refs[:cross_count], *refs[cross_count:])
-
-        raw, square, rayleigh, own_raw = call(
-            kernel_residual,
-            [((vecs, wide), f32), ((vecs, edge), f32), ((vecs, vecs), f32), ((vecs, edge), f32)],
-            crosses + [basis, wide_adj, own_adj],
-            limit=limit,
-        )
-        squares = panel_terms(square)
-        state = (basis, raw, squares, dirs)
-    resid = own_raw / jnp.sqrt(sum(squares) / nodes + epsilon)
-    return (own_basis, resid, own_dirs, rayleigh)
+        state = (crosses, gram, basis, wide_adj, dirs)
+    count = len(crosses)
+
+    def kernel_last(*refs):
+        last_kernel(refs[:count], *refs[count:])
+
+    resid, rayleigh = call(
+        kernel_last,
+        [((vecs, edge), f32), ((vecs, vecs), f32)],
+        crosses + [gram] + own_basis + own_adj,
+    )
+    return (own_basis[0], resid, dirs, rayleigh)
 
 
 def solution(mesh):

time: 88 us -> 82.5 us (0.938)
  Pallas kernels: 25.5 us -> 23.3 us
  waiting for transfers between devices: 22 us -> 20 us
    pallas_call x22 -> x20, Pallas kernels: 25.5 us -> 23.3 us  [call(): pl.pallas_call(kernel, out_shape=[jax.ShapeDtypeStruct(shape, kind) for s...]
    ppermute x36 -> x33, waiting for transfers between devices: 22 us -> 20 us  [swap(): return lax.ppermute(value, axis, [(i, i ^ by) for i in range(size)])]
    ppermute x36 -> x33, starting transfers between devices: 35.9 us -> 35.1 us  [swap(): return lax.ppermute(value, axis, [(i, i ^ by) for i in range(size)])]
    unnamed x10 -> x12, local copies, waits for them, and re-layouts: 1.96 us -> 1.98 us
  transfers between devices with their start and end apart: 36 -> 33, of which waited for: 20 -> 17; matrix products, arithmetic and copies ran while one was open for 0% -> 0% of each run, Pallas kernels for 21% -> 21%
where the time goes in v5:
time: 82.5 us; the launch traced here: 82.1 us
  starting transfers between devices  35.1 us (43%)
  Pallas kernels  23.3 us (28%)
  waiting for transfers between devices  20 us (24%)
  local copies, waits for them, and re-layouts  2 us (2%)
  between operations  0.88 us (1%)
  other arithmetic  0.87 us (1%)
    ppermute x33, starting transfers between devices, swap(): return lax.ppermute(value, axis, [(i, i ^ by) for i in range(size)])  35.1 us
    pallas_call x20, Pallas kernels, call(): pl.pallas_call(kernel, out_shape=[jax.ShapeDtypeStruct(shape, kind) for s...  23.3 us
    ppermute x33, waiting for transfers between devices, swap(): return lax.ppermute(value, axis, [(i, i ^ by) for i in range(size)])  20 us
    unnamed x12, local copies, waits for them, and re-layouts  1.98 us
  transfers between devices with their start and end apart: 33, of which 17 were waited for; matrix products, arithmetic and copies ran while one was open for 0% of the time, Pallas kernels for 21%

profile of v5, /device:TPU:0, one launch (start us, length us, event | category | flops | bytes accessed | tf_op | source)
XLA Modules:
  0.0 82.1 jit_solution(9772405396088109384)
XLA Ops:
  0.6 0.8 maximum_bitcast_fusion
  1.4 5.0 %collective-permute-start.2 = (bf16[1,192,128]{2,1,0:T(8,128)(2,1)S(1)}, bf16[1,192,128]{2,1,0:T(8,128)(2,1)S(1)}, u32[]{:S(2)}, u32[]{:S(2)}) collective-permute-start(bf16[1,192,128]{2,1,0:T(8,128)(2,1)S(1)} %maximum_bitcast_fusion), channel_id=1, source_target_pairs={{0,24},{2,26},{4,28},{6,30},{8,16},{10,18},{12,20},{14,22},{16,8},... | collective-permute-start | bytes 147464 | tf_op jit(solution)/shard_map/ppermute | solution.py:228
  6.4 0.6 collective-permute-start
  7.1 0.7 copy-done.4
  7.8 1.2 %copy-done = bf16[1,1,2,16,128,128]{5,4,3,2,1,0:T(8,128)(2,1)S(1)} copy-done((bf16[1,1,2,16,128,128]{5,4,3,2,1,0:T(8,128)(2,1)S(1)}, bf16[1,1,2,16,128,128]{5,4,3,2,1,0:T(8,128)(2,1)}, u32[]{:S(2)}) %copy-start) | copy-done | bytes 1048600
  9.0 1.4 %shard_map.111.dense_ref.t = bf16[2048,256]{1,0:T(8,128)(2,1)S(1)} custom-call(s32[2,16]{1,0:T(2,128)S(1)} %compare_select_fusion.slots_ref, bf16[2,16,128,128]{3,2,1,0:T(8,128)(2,1)S(1)} %bitcast.25), custom_call_target="tpu_custom_call" | custom-call | tf_op jit(solution)/shard_map/pallas_call | solution.py:20
  10.4 1.0 %collective-permute-done.1 = bf16[1,192,128]{2,1,0:T(8,128)(2,1)S(1)} collective-permute-done((bf16[1,192,128]{2,1,0:T(8,128)(2,1)S(1)}, bf16[1,192,128]{2,1,0:T(8,128)(2,1)S(1)}, u32[]{:S(2)}, u32[]{:S(2)}) %collective-permute-start.1) | collective-permute-done | bytes 49184 | tf_op jit(solution)/shard_map/ppermute | solution.py:228
  11.5 2.5 %collective-permute-start.5 = (bf16[4,192,128]{2,1,0:T(8,128)(2,1)S(1)}, bf16[4,192,128]{2,1,0:T(8,128)(2,1)S(1)}, u32[]{:S(2)}, u32[]{:S(2)}) collective-permute-start(bf16[4,192,128]{2,1,0:T(8,128)(2,1)S(1)} %pad_maximum_fusion.refs_0_), channel_id=1, source_target_pairs={{0,6},{2,4},{4,2},{6,0},{8,14},{10,12},{12,10},{14,8},{16,22},{18,... | collective-permute-start | bytes 589832 | tf_op jit(solution)/shard_map/ppermute | solution.py:228
  14.0 0.5 collective-permute-start.4
  14.5 0.5 collective-permute-start.3
  15.0 4.9 %collective-permute-done.5.refs_3_ = bf16[4,192,128]{2,1,0:T(8,128)(2,1)S(1)} collective-permute-done((bf16[4,192,128]{2,1,0:T(8,128)(2,1)S(1)}, bf16[4,192,128]{2,1,0:T(8,128)(2,1)S(1)}, u32[]{:S(2)}, u32[]{:S(2)}) %collective-permute-start.5) | collective-permute-done | bytes 196640 | tf_op jit(solution)/shard_map/ppermute | solution.py:228
  19.9 2.5 %collective-permute-done.4.refs_2_ = bf16[4,192,128]{2,1,0:T(8,128)(2,1)S(1)} collective-permute-done((bf16[4,192,128]{2,1,0:T(8,128)(2,1)S(1)}, bf16[4,192,128]{2,1,0:T(8,128)(2,1)S(1)}, u32[]{:S(2)}, u32[]{:S(2)}) %collective-permute-start.4) | collective-permute-done | bytes 196640 | tf_op jit(solution)/shard_map/ppermute | solution.py:228
  22.5 0.7 shard_map.112
  23.4 1.1 %shard_map.113 = (f32[64,128]{1,0:T(8,128)S(1)}, f32[64,2048]{1,0:T(8,128)S(1)}) custom-call(bf16[192,2048]{1,0:T(8,128)(2,1)S(1)} %get-tuple-element.76.stack_ref.refs_4_, f32[64,192]{1,0:T(8,128)S(1)} %get-tuple-element.134.mix_ref.refs_5_, f32[64,128]{1,0:T(8,128)S(1)} %get-tuple-element.138.search_ref), custom_call_target="tpu_custom_call" | custom-call | tf_op jit(solution)/shard_map/pallas_call | solution.py:20
  24.5 0.5 collective-permute-start.10
  25.1 3.8 %collective-permute-start.9 = (f32[64,128]{1,0:T(8,128)S(1)}, f32[64,128]{1,0:T(8,128)S(1)}, u32[]{:S(2)}, u32[]{:S(2)}) collective-permute-start(f32[64,128]{1,0:T(8,128)S(1)} %add.21.refs_0_), channel_id=1, source_target_pairs={{0,24},{2,26},{4,28},{6,30},{8,16},{10,18},{12,20},{14,22},{16,8},... | collective-permute-start | bytes 98312 | tf_op jit(solution)/shard_map/ppermute | solution.py:228
  28.8 0.6 collective-permute-start.7
  29.5 3.4 %shard_map.114 = (f32[64,64]{1,0:T(8,128)S(1)}, f32[64,128]{1,0:T(8,128)S(1)}) custom-call(f32[64,128]{1,0:T(8,128)S(1)} %get-tuple-element.79.refs_0_, f32[64,128]{1,0:T(8,128)S(1)} %collective-permute-done.10.refs_1_), custom_call_target="tpu_custom_call" | custom-call | tf_op jit(solution)/shard_map/pallas_call | solution.py:20
  32.9 0.8 collective-permute-done.8.refs_2_
  33.7 0.3 shard_map.115.refs_0_
  33.9 1.5 %collective-permute-start.13 = (bf16[256,128]{1,0:T(8,128)(2,1)S(1)}, bf16[256,128]{1,0:T(8,128)(2,1)S(1)}, u32[]{:S(2)}, u32[]{:S(2)}) collective-permute-start(bf16[256,128]{1,0:T(8,128)(2,1)S(1)} %shard_map.115.refs_0_), channel_id=1, source_target_pairs={{0,6},{2,4},{4,2},{6,0},{8,14},{10,12},{12,10},{14,8},{16,22},{18,... | collective-permute-start | bytes 196616 | tf_op jit(solution)/shard_map/ppermute | solution.py:228
  35.4 0.9 %collective-permute-start.12 = (bf16[256,128]{1,0:T(8,128)(2,1)S(1)}, bf16[256,128]{1,0:T(8,128)(2,1)S(1)}, u32[]{:S(2)}, u32[]{:S(2)}) collective-permute-start(bf16[256,128]{1,0:T(8,128)(2,1)S(1)} %shard_map.115.refs_0_), channel_id=1, source_target_pairs={{0,4},{2,6},{4,0},{6,2},{8,12},{10,14},{12,8},{14,10},{16,20},{18,... | collective-permute-start | bytes 196616 | tf_op jit(solution)/shard_map/ppermute | solution.py:228
  36.3 1.2 %collective-permute-start.11 = (bf16[256,128]{1,0:T(8,128)(2,1)S(1)}, bf16[256,128]{1,0:T(8,128)(2,1)S(1)}, u32[]{:S(2)}, u32[]{:S(2)}) collective-permute-start(bf16[256,128]{1,0:T(8,128)(2,1)S(1)} %shard_map.115.refs_0_), channel_id=1, source_target_pairs={{0,2},{2,0},{4,6},{6,4},{8,10},{10,8},{12,14},{14,12},{16,18},{18,... | collective-permute-start | bytes 196616 | tf_op jit(solution)/shard_map/ppermute | solution.py:228
  37.5 0.6 shard_map.116
  38.1 1.0 %collective-permute-done.13.refs_3_ = bf16[256,128]{1,0:T(8,128)(2,1)S(1)} collective-permute-done((bf16[256,128]{1,0:T(8,128)(2,1)S(1)}, bf16[256,128]{1,0:T(8,128)(2,1)S(1)}, u32[]{:S(2)}, u32[]{:S(2)}) %collective-permute-start.13) | collective-permute-done | bytes 65568 | tf_op jit(solution)/shard_map/ppermute | solution.py:228
  39.2 0.7 collective-permute-done.12.refs_2_
  39.9 0.7 collective-permute-done.11.refs_1_
  40.5 0.4 shard_map.117
  41.0 1.2 %collective-permute-done.14.refs_1_ = f32[64,128]{1,0:T(8,128)S(1)} collective-permute-done((f32[64,128]{1,0:T(8,128)S(1)}, f32[64,128]{1,0:T(8,128)S(1)}, u32[]{:S(2)}, u32[]{:S(2)}) %collective-permute-start.14) | collective-permute-done | bytes 32800 | tf_op jit(solution)/shard_map/ppermute | solution.py:228
  42.2 1.1 %shard_map.118 = (bf16[192,2048]{1,0:T(8,128)(2,1)S(1)}, f32[64,128]{1,0:T(8,128)S(1)}, f32[64,128]{1,0:T(8,128)S(1)}) custom-call(s32[1]{0:T(128)} %bitcast.place_ref.p, bf16[2048,256]{1,0:T(8,128)(2,1)S(1)} %shard_map.111.dense_ref.t, f32[64,192]{1,0:T(8,128)S(1)} %get-tuple-element.136.m.mix_ref.refs_5_, f32[64,128]{1,0:T(8,128)S(1)} %get-tuple-element.89.refs_0_, ...), custom_call_target="tpu_custom_call" | custom-call | tf_op jit(solution)/shard_map/pallas_call | solution.py:20
  43.3 0.2 collective-permute-start.15
  43.6 1.1 %shard_map.119 = (f32[64,128]{1,0:T(8,128)S(1)}, f32[64,2048]{1,0:T(8,128)S(1)}) custom-call(bf16[192,2048]{1,0:T(8,128)(2,1)S(1)} %get-tuple-element.95.stack_ref.refs_4_, f32[64,192]{1,0:T(8,128)S(1)} %get-tuple-element.136.m.mix_ref.refs_5_, f32[64,128]{1,0:T(8,128)S(1)} %get-tuple-element.139.search_ref), custom_call_target="tpu_custom_call" | custom-call | tf_op jit(solution)/shard_map/pallas_call | solution.py:20
  44.7 0.4 collective-permute-start.19
  45.1 3.0 %collective-permute-start.18 = (f32[64,128]{1,0:T(8,128)S(1)}, f32[64,128]{1,0:T(8,128)S(1)}, u32[]{:S(2)}, u32[]{:S(2)}) collective-permute-start(f32[64,128]{1,0:T(8,128)S(1)} %add.22.refs_0_), channel_id=1, source_target_pairs={{0,24},{2,26},{4,28},{6,30},{8,16},{10,18},{12,20},{14,22},{16,8},... | collective-permute-start | bytes 98312 | tf_op jit(solution)/shard_map/ppermute | solution.py:228
  48.1 1.4 %collective-permute-start.16 = (f32[64,128]{1,0:T(8,128)S(1)}, f32[64,128]{1,0:T(8,128)S(1)}, u32[]{:S(2)}, u32[]{:S(2)}) collective-permute-start(f32[64,128]{1,0:T(8,128)S(1)} %add.22.refs_0_), channel_id=1, source_target_pairs={{0,8},{2,10},{4,12},{6,14},{8,0},{10,2},{12,4},{14,6},{16,24},{18,... | collective-permute-start | bytes 98312 | tf_op jit(solution)/shard_map/ppermute | solution.py:228
  49.5 3.4 %shard_map.120 = (f32[64,64]{1,0:T(8,128)S(1)}, f32[64,128]{1,0:T(8,128)S(1)}) custom-call(f32[64,128]{1,0:T(8,128)S(1)} %get-tuple-element.98.refs_0_, f32[64,128]{1,0:T(8,128)S(1)} %collective-permute-done.19.refs_1_), custom_call_target="tpu_custom_call" | custom-call | tf_op jit(solution)/shard_map/pallas_call | solution.py:20
  52.9 0.3 shard_map.121.refs_0_
  53.2 1.8 %collective-permute-start.22 = (bf16[256,128]{1,0:T(8,128)(2,1)S(1)}, bf16[256,128]{1,0:T(8,128)(2,1)S(1)}, u32[]{:S(2)}, u32[]{:S(2)}) collective-permute-start(bf16[256,128]{1,0:T(8,128)(2,1)S(1)} %shard_map.121.refs_0_), channel_id=1, source_target_pairs={{0,6},{2,4},{4,2},{6,0},{8,14},{10,12},{12,10},{14,8},{16,22},{18,... | collective-permute-start | bytes 196616 | tf_op jit(solution)/shard_map/ppermute | solution.py:228
  55.0 0.9 %collective-permute-start.21 = (bf16[256,128]{1,0:T(8,128)(2,1)S(1)}, bf16[256,128]{1,0:T(8,128)(2,1)S(1)}, u32[]{:S(2)}, u32[]{:S(2)}) collective-permute-start(bf16[256,128]{1,0:T(8,128)(2,1)S(1)} %shard_map.121.refs_0_), channel_id=1, source_target_pairs={{0,4},{2,6},{4,0},{6,2},{8,12},{10,14},{12,8},{14,10},{16,20},{18,... | collective-permute-start | bytes 196616 | tf_op jit(solution)/shard_map/ppermute | solution.py:228
  55.9 0.8 %collective-permute-start.20 = (bf16[256,128]{1,0:T(8,128)(2,1)S(1)}, bf16[256,128]{1,0:T(8,128)(2,1)S(1)}, u32[]{:S(2)}, u32[]{:S(2)}) collective-permute-start(bf16[256,128]{1,0:T(8,128)(2,1)S(1)} %shard_map.121.refs_0_), channel_id=1, source_target_pairs={{0,2},{2,0},{4,6},{6,4},{8,10},{10,8},{12,14},{14,12},{16,18},{18,... | collective-permute-start | bytes 196616 | tf_op jit(solution)/shard_map/ppermute | solution.py:228
  56.7 0.6 shard_map.122
  57.4 1.6 %collective-permute-done.22.refs_3_ = bf16[256,128]{1,0:T(8,128)(2,1)S(1)} collective-permute-done((bf16[256,128]{1,0:T(8,128)(2,1)S(1)}, bf16[256,128]{1,0:T(8,128)(2,1)S(1)}, u32[]{:S(2)}, u32[]{:S(2)}) %collective-permute-start.22) | collective-permute-done | bytes 65568 | tf_op jit(solution)/shard_map/ppermute | solution.py:228
  59.0 0.5 collective-permute-done.21.refs_2_
  59.5 0.7 collective-permute-done.20.refs_1_
  60.2 0.4 shard_map.123
  60.6 1.2 %collective-permute-done.23.refs_1_ = f32[64,128]{1,0:T(8,128)S(1)} collective-permute-done((f32[64,128]{1,0:T(8,128)S(1)}, f32[64,128]{1,0:T(8,128)S(1)}, u32[]{:S(2)}, u32[]{:S(2)}) %collective-permute-start.23) | collective-permute-done | bytes 32800 | tf_op jit(solution)/shard_map/ppermute | solution.py:228
  61.8 1.1 %shard_map.124 = (bf16[192,2048]{1,0:T(8,128)(2,1)S(1)}, f32[64,128]{1,0:T(8,128)S(1)}, f32[64,128]{1,0:T(8,128)S(1)}) custom-call(s32[1]{0:T(128)} %bitcast.place_ref.p, bf16[2048,256]{1,0:T(8,128)(2,1)S(1)} %shard_map.111.dense_ref.t, f32[64,192]{1,0:T(8,128)S(1)} %get-tuple-element.135.m.mix_ref.refs_5_, f32[64,128]{1,0:T(8,128)S(1)} %get-tuple-element.108.refs_0_, ...), custom_call_target="tpu_custom_call" | custom-call | tf_op jit(solution)/shard_map/pallas_call | solution.py:20
  63.0 0.2 collective-permute-start.24
  63.2 1.1 %shard_map.125 = (f32[64,128]{1,0:T(8,128)S(1)}, f32[64,2048]{1,0:T(8,128)S(1)}) custom-call(bf16[192,2048]{1,0:T(8,128)(2,1)S(1)} %get-tuple-element.113.stack_ref.refs_4_, f32[64,192]{1,0:T(8,128)S(1)} %get-tuple-element.135.m.mix_ref.refs_5_, f32[64,128]{1,0:T(8,128)S(1)} %get-tuple-element.137.search_ref), custom_call_target="tpu_custom_call" | custom-call | tf_op jit(solution)/shard_map/pallas_call | solution.py:20
  64.3 0.4 collective-permute-start.25
  64.8 3.0 %collective-permute-start.28 = (f32[64,128]{1,0:T(8,128)S(1)}, f32[64,128]{1,0:T(8,128)S(1)}, u32[]{:S(2)}, u32[]{:S(2)}) collective-permute-start(f32[64,128]{1,0:T(8,128)S(1)} %add.23.refs_0_), channel_id=1, source_target_pairs={{0,24},{2,26},{4,28},{6,30},{8,16},{10,18},{12,20},{14,22},{16,8},... | collective-permute-start | bytes 98312 | tf_op jit(solution)/shard_map/ppermute | solution.py:228
  67.8 1.4 %collective-permute-start.26 = (f32[64,128]{1,0:T(8,128)S(1)}, f32[64,128]{1,0:T(8,128)S(1)}, u32[]{:S(2)}, u32[]{:S(2)}) collective-permute-start(f32[64,128]{1,0:T(8,128)S(1)} %add.23.refs_0_), channel_id=1, source_target_pairs={{0,8},{2,10},{4,12},{6,14},{8,0},{10,2},{12,4},{14,6},{16,24},{18,... | collective-permute-start | bytes 98312 | tf_op jit(solution)/shard_map/ppermute | solution.py:228
  69.2 3.4 %shard_map.126 = (f32[64,64]{1,0:T(8,128)S(1)}, f32[64,128]{1,0:T(8,128)S(1)}) custom-call(f32[64,128]{1,0:T(8,128)S(1)} %get-tuple-element.115.refs_0_, f32[64,128]{1,0:T(8,128)S(1)} %collective-permute-done.25.refs_1_), custom_call_target="tpu_custom_call" | custom-call | tf_op jit(solution)/shard_map/pallas_call | solution.py:20
  72.6 0.3 shard_map.128
  72.8 1.5 %collective-permute-start.31 = (bf16[256,128]{1,0:T(8,128)(2,1)S(1)}, bf16[256,128]{1,0:T(8,128)(2,1)S(1)}, u32[]{:S(2)}, u32[]{:S(2)}) collective-permute-start(bf16[256,128]{1,0:T(8,128)(2,1)S(1)} %get-tuple-element.127.refs_0_), channel_id=1, source_target_pairs={{0,6},{2,4},{4,2},{6,0},{8,14},{10,12},{12,10},{14,8},{16,22},{18,... | collective-permute-start | bytes 196616 | tf_op jit(solution)/shard_map/ppermute | solution.py:228
  74.3 0.9 %collective-permute-start.30 = (bf16[256,128]{1,0:T(8,128)(2,1)S(1)}, bf16[256,128]{1,0:T(8,128)(2,1)S(1)}, u32[]{:S(2)}, u32[]{:S(2)}) collective-permute-start(bf16[256,128]{1,0:T(8,128)(2,1)S(1)} %get-tuple-element.127.refs_0_), channel_id=1, source_target_pairs={{0,4},{2,6},{4,0},{6,2},{8,12},{10,14},{12,8},{14,10},{16,20},{18,... | collective-permute-start | bytes 196616 | tf_op jit(solution)/shard_map/ppermute | solution.py:228
  75.2 1.2 %collective-permute-start.29 = (bf16[256,128]{1,0:T(8,128)(2,1)S(1)}, bf16[256,128]{1,0:T(8,128)(2,1)S(1)}, u32[]{:S(2)}, u32[]{:S(2)}) collective-permute-start(bf16[256,128]{1,0:T(8,128)(2,1)S(1)} %get-tuple-element.127.refs_0_), channel_id=1, source_target_pairs={{0,2},{2,0},{4,6},{6,4},{8,10},{10,8},{12,14},{14,12},{16,18},{18,... | collective-permute-start | bytes 196616 | tf_op jit(solution)/shard_map/ppermute | solution.py:228
  76.4 1.2 %shard_map.127 = (bf16[192,2048]{1,0:T(8,128)(2,1)S(1)}, f32[64,64]{1,0:T(8,128)S(1)}, f32[64,128]{1,0:T(8,128)}, f32[64,128]{1,0:T(8,128)}) custom-call(f32[64,128]{1,0:T(8,128)S(1)} %get-tuple-element.115.refs_0_, f32[64,128]{1,0:T(8,128)S(1)} %collective-permute-done.25.refs_1_, f32[64,64]{1,0:T(8,128)S(1)} %get-tuple-element.119.refs_2_.refs_4_, ...), custom_call_target="tpu_custom_call" | custom-call | tf_op jit(solution)/shard_map/pallas_call | solution.py:20
  77.6 1.1 %collective-permute-done.31.refs_3_ = bf16[256,128]{1,0:T(8,128)(2,1)S(1)} collective-permute-done((bf16[256,128]{1,0:T(8,128)(2,1)S(1)}, bf16[256,128]{1,0:T(8,128)(2,1)S(1)}, u32[]{:S(2)}, u32[]{:S(2)}) %collective-permute-start.31) | collective-permute-done | bytes 65568 | tf_op jit(solution)/shard_map/ppermute | solution.py:228
  78.6 0.4 collective-permute-done.30.refs_2_
  79.0 0.4 collective-permute-done.29.refs_1_
  79.5 0.4 shard_map.129.refs_0_
  79.9 1.2 %collective-permute-done.32.refs_1_ = f32[64,128]{1,0:T(8,128)S(1)} collective-permute-done((f32[64,128]{1,0:T(8,128)S(1)}, f32[64,128]{1,0:T(8,128)S(1)}, u32[]{:S(2)}, u32[]{:S(2)}) %collective-permute-start.32) | collective-permute-done | bytes 32800 | tf_op jit(solution)/shard_map/ppermute | solution.py:228
  81.1 1.0 %shard_map.130 = (f32[64,128]{1,0:T(8,128)}, f32[64,64]{1,0:T(8,128)}) custom-call(f32[64,128]{1,0:T(8,128)S(1)} %shard_map.129.refs_0_, f32[64,128]{1,0:T(8,128)S(1)} %collective-permute-done.32.refs_1_, f32[64,64]{1,0:T(8,128)S(1)} %get-tuple-element.129.refs_2_, f32[64,128]{1,0:T(8,128)S(1)} %copy-done.1, f32[64,128]{1,0:T(8,128)S(1)} %get-tuple-element.130.refs_4_), custom_call_target="tpu_custom_call" | custom-call | tf_op jit(solution)/shard_map/pallas_call | solution.py:20
  (42 shorter events, 0.7 us)
Async XLA Ops:
  1.4 9.0 %collective-permute-start.2 = (bf16[1,192,128]{2,1,0:T(8,128)(2,1)S(1)}, bf16[1,192,128]{2,1,0:T(8,128)(2,1)S(1)}, u32[]{:S(2)}, u32[]{:S(2)}) collective-permute-start(bf16[1,192,128]{2,1,0:T(8,128)(2,1)S(1)} %maximum_bitcast_fusion), channel_id=1, source_target_pairs={{0,24},{2,26},{4,28},{6,30},{8,16},{10,18},{12,20},{14,22},{16,8},... | collective-permute-start | bytes 147464 | tf_op jit(solution)/shard_map/ppermute | solution.py:228
  6.4 5.0 %collective-permute-start.1 = (bf16[1,192,128]{2,1,0:T(8,128)(2,1)S(1)}, bf16[1,192,128]{2,1,0:T(8,128)(2,1)S(1)}, u32[]{:S(2)}, u32[]{:S(2)}) collective-permute-start(bf16[1,192,128]{2,1,0:T(8,128)(2,1)S(1)} %maximum_bitcast_fusion), channel_id=1, source_target_pairs={{0,16},{2,18},{4,20},{6,22},{8,24},{10,26},{12,28},{14,30},{16,0},... | collective-permute-start | bytes 147464 | tf_op jit(solution)/shard_map/ppermute | solution.py:228
  6.4 5.0 %collective-permute-start = (bf16[1,192,128]{2,1,0:T(8,128)(2,1)S(1)}, bf16[1,192,128]{2,1,0:T(8,128)(2,1)S(1)}, u32[]{:S(2)}, u32[]{:S(2)}) collective-permute-start(bf16[1,192,128]{2,1,0:T(8,128)(2,1)S(1)} %maximum_bitcast_fusion), channel_id=1, source_target_pairs={{0,8},{2,10},{4,12},{6,14},{8,0},{10,2},{12,4},{14,6},{16,24},{18,... | collective-permute-start | bytes 147464 | tf_op jit(solution)/shard_map/ppermute | solution.py:228
  7.0 0.7 copy-start.4
  7.1 0.7 copy-start.5
  7.8 1.2 %copy-start = (bf16[1,1,2,16,128,128]{5,4,3,2,1,0:T(8,128)(2,1)S(1)}, bf16[1,1,2,16,128,128]{5,4,3,2,1,0:T(8,128)(2,1)}, u32[]{:S(2)}) copy-start(bf16[1,1,2,16,128,128]{5,4,3,2,1,0:T(8,128)(2,1)} %param.8) | copy-start | bytes 3145732
  10.4 4.6 %copy-start.2 = (f32[3,64,192]{2,1,0:T(8,128)S(1)}, f32[3,64,192]{2,1,0:T(8,128)}, u32[]{:S(2)}) copy-start(f32[3,64,192]{2,1,0:T(8,128)} %param.14) | copy-start | bytes 442372
  11.5 8.5 %collective-permute-start.5 = (bf16[4,192,128]{2,1,0:T(8,128)(2,1)S(1)}, bf16[4,192,128]{2,1,0:T(8,128)(2,1)S(1)}, u32[]{:S(2)}, u32[]{:S(2)}) collective-permute-start(bf16[4,192,128]{2,1,0:T(8,128)(2,1)S(1)} %pad_maximum_fusion.refs_0_), channel_id=1, source_target_pairs={{0,6},{2,4},{4,2},{6,0},{8,14},{10,12},{12,10},{14,8},{16,22},{18,... | collective-permute-start | bytes 589832 | tf_op jit(solution)/shard_map/ppermute | solution.py:228
  14.0 8.4 %collective-permute-start.4 = (bf16[4,192,128]{2,1,0:T(8,128)(2,1)S(1)}, bf16[4,192,128]{2,1,0:T(8,128)(2,1)S(1)}, u32[]{:S(2)}, u32[]{:S(2)}) collective-permute-start(bf16[4,192,128]{2,1,0:T(8,128)(2,1)S(1)} %pad_maximum_fusion.refs_0_), channel_id=1, source_target_pairs={{0,4},{2,6},{4,0},{6,2},{8,12},{10,14},{12,8},{14,10},{16,20},{18,... | collective-permute-start | bytes 589832 | tf_op jit(solution)/shard_map/ppermute | solution.py:228
  14.5 8.0 %collective-permute-start.3 = (bf16[4,192,128]{2,1,0:T(8,128)(2,1)S(1)}, bf16[4,192,128]{2,1,0:T(8,128)(2,1)S(1)}, u32[]{:S(2)}, u32[]{:S(2)}) collective-permute-start(bf16[4,192,128]{2,1,0:T(8,128)(2,1)S(1)} %pad_maximum_fusion.refs_0_), channel_id=1, source_target_pairs={{0,2},{2,0},{4,6},{6,4},{8,10},{10,8},{12,14},{14,12},{16,18},{18,... | collective-permute-start | bytes 589832 | tf_op jit(solution)/shard_map/ppermute | solution.py:228
  22.5 0.9 %copy-start.3 = (f32[3,64,128]{2,1,0:T(8,128)S(1)}, f32[3,64,128]{2,1,0:T(8,128)}, u32[]{:S(2)}) copy-start(f32[3,64,128]{2,1,0:T(8,128)} %param.15) | copy-start | bytes 294916
  23.2 1.3 %collective-permute-start.6 = (f32[64,128]{1,0:T(8,128)S(1)}, f32[64,128]{1,0:T(8,128)S(1)}, u32[]{:S(2)}, u32[]{:S(2)}) collective-permute-start(f32[64,128]{1,0:T(8,128)S(1)} %get-tuple-element.75), channel_id=1, source_target_pairs={{0,1},{1,0},{2,3},{3,2},{4,5},{5,4},{6,7},{7,6},{8,9},{9,8},{10,11... | collective-permute-start | bytes 98312 | tf_op jit(solution)/shard_map/ppermute | solution.py:228
  24.5 4.9 %collective-permute-start.10 = (f32[64,128]{1,0:T(8,128)S(1)}, f32[64,128]{1,0:T(8,128)S(1)}, u32[]{:S(2)}, u32[]{:S(2)}) collective-permute-start(f32[64,128]{1,0:T(8,128)S(1)} %get-tuple-element.79.refs_0_), channel_id=1, source_target_pairs={{0,1},{1,0},{2,3},{3,2},{4,5},{5,4},{6,7},{7,6},{8,9},{9,8},{10,11... | collective-permute-start | bytes 98312 | tf_op jit(solution)/shard_map/ppermute | solution.py:228
  25.1 7.8 %collective-permute-start.9 = (f32[64,128]{1,0:T(8,128)S(1)}, f32[64,128]{1,0:T(8,128)S(1)}, u32[]{:S(2)}, u32[]{:S(2)}) collective-permute-start(f32[64,128]{1,0:T(8,128)S(1)} %add.21.refs_0_), channel_id=1, source_target_pairs={{0,24},{2,26},{4,28},{6,30},{8,16},{10,18},{12,20},{14,22},{16,8},... | collective-permute-start | bytes 98312 | tf_op jit(solution)/shard_map/ppermute | solution.py:228
  28.8 4.8 %collective-permute-start.8 = (f32[64,128]{1,0:T(8,128)S(1)}, f32[64,128]{1,0:T(8,128)S(1)}, u32[]{:S(2)}, u32[]{:S(2)}) collective-permute-start(f32[64,128]{1,0:T(8,128)S(1)} %add.21.refs_0_), channel_id=1, source_target_pairs={{0,16},{2,18},{4,20},{6,22},{8,24},{10,26},{12,28},{14,30},{16,0},... | collective-permute-start | bytes 98312 | tf_op jit(solution)/shard_map/ppermute | solution.py:228
  28.8 4.8 %collective-permute-start.7 = (f32[64,128]{1,0:T(8,128)S(1)}, f32[64,128]{1,0:T(8,128)S(1)}, u32[]{:S(2)}, u32[]{:S(2)}) collective-permute-start(f32[64,128]{1,0:T(8,128)S(1)} %add.21.refs_0_), channel_id=1, source_target_pairs={{0,8},{2,10},{4,12},{6,14},{8,0},{10,2},{12,4},{14,6},{16,24},{18,... | collective-permute-start | bytes 98312 | tf_op jit(solution)/shard_map/ppermute | solution.py:228
  33.9 5.2 %collective-permute-start.13 = (bf16[256,128]{1,0:T(8,128)(2,1)S(1)}, bf16[256,128]{1,0:T(8,128)(2,1)S(1)}, u32[]{:S(2)}, u32[]{:S(2)}) collective-permute-start(bf16[256,128]{1,0:T(8,128)(2,1)S(1)} %shard_map.115.refs_0_), channel_id=1, source_target_pairs={{0,6},{2,4},{4,2},{6,0},{8,14},{10,12},{12,10},{14,8},{16,22},{18,... | collective-permute-start | bytes 196616 | tf_op jit(solution)/shard_map/ppermute | solution.py:228
  35.4 4.4 %collective-permute-start.12 = (bf16[256,128]{1,0:T(8,128)(2,1)S(1)}, bf16[256,128]{1,0:T(8,128)(2,1)S(1)}, u32[]{:S(2)}, u32[]{:S(2)}) collective-permute-start(bf16[256,128]{1,0:T(8,128)(2,1)S(1)} %shard_map.115.refs_0_), channel_id=1, source_target_pairs={{0,4},{2,6},{4,0},{6,2},{8,12},{10,14},{12,8},{14,10},{16,20},{18,... | collective-permute-start | bytes 196616 | tf_op jit(solution)/shard_map/ppermute | solution.py:228
  36.3 4.3 %collective-permute-start.11 = (bf16[256,128]{1,0:T(8,128)(2,1)S(1)}, bf16[256,128]{1,0:T(8,128)(2,1)S(1)}, u32[]{:S(2)}, u32[]{:S(2)}) collective-permute-start(bf16[256,128]{1,0:T(8,128)(2,1)S(1)} %shard_map.115.refs_0_), channel_id=1, source_target_pairs={{0,2},{2,0},{4,6},{6,4},{8,10},{10,8},{12,14},{14,12},{16,18},{18,... | collective-permute-start | bytes 196616 | tf_op jit(solution)/shard_map/ppermute | solution.py:228
  40.9 1.3 %collective-permute-start.14 = (f32[64,128]{1,0:T(8,128)S(1)}, f32[64,128]{1,0:T(8,128)S(1)}, u32[]{:S(2)}, u32[]{:S(2)}) collective-permute-start(f32[64,128]{1,0:T(8,128)S(1)} %get-tuple-element.89.refs_0_), channel_id=1, source_target_pairs={{0,1},{1,0},{2,3},{3,2},{4,5},{5,4},{6,7},{7,6},{8,9},{9,8},{10,11... | collective-permute-start | bytes 98312 | tf_op jit(solution)/shard_map/ppermute | solution.py:228
  43.3 1.4 %collective-permute-start.15 = (f32[64,128]{1,0:T(8,128)S(1)}, f32[64,128]{1,0:T(8,128)S(1)}, u32[]{:S(2)}, u32[]{:S(2)}) collective-permute-start(f32[64,128]{1,0:T(8,128)S(1)} %get-tuple-element.94), channel_id=1, source_target_pairs={{0,1},{1,0},{2,3},{3,2},{4,5},{5,4},{6,7},{7,6},{8,9},{9,8},{10,11... | collective-permute-start | bytes 98312 | tf_op jit(solution)/shard_map/ppermute | solution.py:228
  44.7 4.8 %collective-permute-start.19 = (f32[64,128]{1,0:T(8,128)S(1)}, f32[64,128]{1,0:T(8,128)S(1)}, u32[]{:S(2)}, u32[]{:S(2)}) collective-permute-start(f32[64,128]{1,0:T(8,128)S(1)} %get-tuple-element.98.refs_0_), channel_id=1, source_target_pairs={{0,1},{1,0},{2,3},{3,2},{4,5},{5,4},{6,7},{7,6},{8,9},{9,8},{10,11... | collective-permute-start | bytes 98312 | tf_op jit(solution)/shard_map/ppermute | solution.py:228
  45.1 7.8 %collective-permute-start.18 = (f32[64,128]{1,0:T(8,128)S(1)}, f32[64,128]{1,0:T(8,128)S(1)}, u32[]{:S(2)}, u32[]{:S(2)}) collective-permute-start(f32[64,128]{1,0:T(8,128)S(1)} %add.22.refs_0_), channel_id=1, source_target_pairs={{0,24},{2,26},{4,28},{6,30},{8,16},{10,18},{12,20},{14,22},{16,8},... | collective-permute-start | bytes 98312 | tf_op jit(solution)/shard_map/ppermute | solution.py:228
  48.1 4.8 %collective-permute-start.17 = (f32[64,128]{1,0:T(8,128)S(1)}, f32[64,128]{1,0:T(8,128)S(1)}, u32[]{:S(2)}, u32[]{:S(2)}) collective-permute-start(f32[64,128]{1,0:T(8,128)S(1)} %add.22.refs_0_), channel_id=1, source_target_pairs={{0,16},{2,18},{4,20},{6,22},{8,24},{10,26},{12,28},{14,30},{16,0},... | collective-permute-start | bytes 98312 | tf_op jit(solution)/shard_map/ppermute | solution.py:228
  48.1 4.8 %collective-permute-start.16 = (f32[64,128]{1,0:T(8,128)S(1)}, f32[64,128]{1,0:T(8,128)S(1)}, u32[]{:S(2)}, u32[]{:S(2)}) collective-permute-start(f32[64,128]{1,0:T(8,128)S(1)} %add.22.refs_0_), channel_id=1, source_target_pairs={{0,8},{2,10},{4,12},{6,14},{8,0},{10,2},{12,4},{14,6},{16,24},{18,... | collective-permute-start | bytes 98312 | tf_op jit(solution)/shard_map/ppermute | solution.py:228
  53.2 5.8 %collective-permute-start.22 = (bf16[256,128]{1,0:T(8,128)(2,1)S(1)}, bf16[256,128]{1,0:T(8,128)(2,1)S(1)}, u32[]{:S(2)}, u32[]{:S(2)}) collective-permute-start(bf16[256,128]{1,0:T(8,128)(2,1)S(1)} %shard_map.121.refs_0_), channel_id=1, source_target_pairs={{0,6},{2,4},{4,2},{6,0},{8,14},{10,12},{12,10},{14,8},{16,22},{18,... | collective-permute-start | bytes 196616 | tf_op jit(solution)/shard_map/ppermute | solution.py:228
  55.0 4.5 %collective-permute-start.21 = (bf16[256,128]{1,0:T(8,128)(2,1)S(1)}, bf16[256,128]{1,0:T(8,128)(2,1)S(1)}, u32[]{:S(2)}, u32[]{:S(2)}) collective-permute-start(bf16[256,128]{1,0:T(8,128)(2,1)S(1)} %shard_map.121.refs_0_), channel_id=1, source_target_pairs={{0,4},{2,6},{4,0},{6,2},{8,12},{10,14},{12,8},{14,10},{16,20},{18,... | collective-permute-start | bytes 196616 | tf_op jit(solution)/shard_map/ppermute | solution.py:228
  55.9 4.3 %collective-permute-start.20 = (bf16[256,128]{1,0:T(8,128)(2,1)S(1)}, bf16[256,128]{1,0:T(8,128)(2,1)S(1)}, u32[]{:S(2)}, u32[]{:S(2)}) collective-permute-start(bf16[256,128]{1,0:T(8,128)(2,1)S(1)} %shard_map.121.refs_0_), channel_id=1, source_target_pairs={{0,2},{2,0},{4,6},{6,4},{8,10},{10,8},{12,14},{14,12},{16,18},{18,... | collective-permute-start | bytes 196616 | tf_op jit(solution)/shard_map/ppermute | solution.py:228
  60.6 1.3 %collective-permute-start.23 = (f32[64,128]{1,0:T(8,128)S(1)}, f32[64,128]{1,0:T(8,128)S(1)}, u32[]{:S(2)}, u32[]{:S(2)}) collective-permute-start(f32[64,128]{1,0:T(8,128)S(1)} %get-tuple-element.108.refs_0_), channel_id=1, source_target_pairs={{0,1},{1,0},{2,3},{3,2},{4,5},{5,4},{6,7},{7,6},{8,9},{9,8},{10,11... | collective-permute-start | bytes 98312 | tf_op jit(solution)/shard_map/ppermute | solution.py:228
  63.0 1.4 %collective-permute-start.24 = (f32[64,128]{1,0:T(8,128)S(1)}, f32[64,128]{1,0:T(8,128)S(1)}, u32[]{:S(2)}, u32[]{:S(2)}) collective-permute-start(f32[64,128]{1,0:T(8,128)S(1)} %get-tuple-element.112), channel_id=1, source_target_pairs={{0,1},{1,0},{2,3},{3,2},{4,5},{5,4},{6,7},{7,6},{8,9},{9,8},{10,11... | collective-permute-start | bytes 98312 | tf_op jit(solution)/shard_map/ppermute | solution.py:228
  64.3 4.8 %collective-permute-start.25 = (f32[64,128]{1,0:T(8,128)S(1)}, f32[64,128]{1,0:T(8,128)S(1)}, u32[]{:S(2)}, u32[]{:S(2)}) collective-permute-start(f32[64,128]{1,0:T(8,128)S(1)} %get-tuple-element.115.refs_0_), channel_id=1, source_target_pairs={{0,1},{1,0},{2,3},{3,2},{4,5},{5,4},{6,7},{7,6},{8,9},{9,8},{10,11... | collective-permute-start | bytes 98312 | tf_op jit(solution)/shard_map/ppermute | solution.py:228
  64.8 7.8 %collective-permute-start.28 = (f32[64,128]{1,0:T(8,128)S(1)}, f32[64,128]{1,0:T(8,128)S(1)}, u32[]{:S(2)}, u32[]{:S(2)}) collective-permute-start(f32[64,128]{1,0:T(8,128)S(1)} %add.23.refs_0_), channel_id=1, source_target_pairs={{0,24},{2,26},{4,28},{6,30},{8,16},{10,18},{12,20},{14,22},{16,8},... | collective-permute-start | bytes 98312 | tf_op jit(solution)/shard_map/ppermute | solution.py:228
  67.7 4.8 %collective-permute-start.27 = (f32[64,128]{1,0:T(8,128)S(1)}, f32[64,128]{1,0:T(8,128)S(1)}, u32[]{:S(2)}, u32[]{:S(2)}) collective-permute-start(f32[64,128]{1,0:T(8,128)S(1)} %add.23.refs_0_), channel_id=1, source_target_pairs={{0,16},{2,18},{4,20},{6,22},{8,24},{10,26},{12,28},{14,30},{16,0},... | collective-permute-start | bytes 98312 | tf_op jit(solution)/shard_map/ppermute | solution.py:228
  67.8 4.8 %collective-permute-start.26 = (f32[64,128]{1,0:T(8,128)S(1)}, f32[64,128]{1,0:T(8,128)S(1)}, u32[]{:S(2)}, u32[]{:S(2)}) collective-permute-start(f32[64,128]{1,0:T(8,128)S(1)} %add.23.refs_0_), channel_id=1, source_target_pairs={{0,8},{2,10},{4,12},{6,14},{8,0},{10,2},{12,4},{14,6},{16,24},{18,... | collective-permute-start | bytes 98312 | tf_op jit(solution)/shard_map/ppermute | solution.py:228
  72.8 5.8 %collective-permute-start.31 = (bf16[256,128]{1,0:T(8,128)(2,1)S(1)}, bf16[256,128]{1,0:T(8,128)(2,1)S(1)}, u32[]{:S(2)}, u32[]{:S(2)}) collective-permute-start(bf16[256,128]{1,0:T(8,128)(2,1)S(1)} %get-tuple-element.127.refs_0_), channel_id=1, source_target_pairs={{0,6},{2,4},{4,2},{6,0},{8,14},{10,12},{12,10},{14,8},{16,22},{18,... | collective-permute-start | bytes 196616 | tf_op jit(solution)/shard_map/ppermute | solution.py:228
  74.3 4.7 %collective-permute-start.30 = (bf16[256,128]{1,0:T(8,128)(2,1)S(1)}, bf16[256,128]{1,0:T(8,128)(2,1)S(1)}, u32[]{:S(2)}, u32[]{:S(2)}) collective-permute-start(bf16[256,128]{1,0:T(8,128)(2,1)S(1)} %get-tuple-element.127.refs_0_), channel_id=1, source_target_pairs={{0,4},{2,6},{4,0},{6,2},{8,12},{10,14},{12,8},{14,10},{16,20},{18,... | collective-permute-start | bytes 196616 | tf_op jit(solution)/shard_map/ppermute | solution.py:228
  75.2 4.3 %collective-permute-start.29 = (bf16[256,128]{1,0:T(8,128)(2,1)S(1)}, bf16[256,128]{1,0:T(8,128)(2,1)S(1)}, u32[]{:S(2)}, u32[]{:S(2)}) collective-permute-start(bf16[256,128]{1,0:T(8,128)(2,1)S(1)} %get-tuple-element.127.refs_0_), channel_id=1, source_target_pairs={{0,2},{2,0},{4,6},{6,4},{8,10},{10,8},{12,14},{14,12},{16,18},{18,... | collective-permute-start | bytes 196616 | tf_op jit(solution)/shard_map/ppermute | solution.py:228
  79.5 1.7 %copy-start.1 = (f32[64,128]{1,0:T(8,128)S(1)}, f32[64,128]{1,0:T(8,128)}, u32[]{:S(2)}) copy-start(f32[64,128]{1,0:T(8,128)} %get-tuple-element.65.refs_3_) | copy-start | bytes 98308
  79.8 1.3 %collective-permute-start.32 = (f32[64,128]{1,0:T(8,128)S(1)}, f32[64,128]{1,0:T(8,128)S(1)}, u32[]{:S(2)}, u32[]{:S(2)}) collective-permute-start(f32[64,128]{1,0:T(8,128)S(1)} %shard_map.129.refs_0_), channel_id=1, source_target_pairs={{0,1},{1,0},{2,3},{3,2},{4,5},{5,4},{6,7},{7,6},{8,9},{9,8},{10,11... | collective-permute-start | bytes 98312 | tf_op jit(solution)/shard_map/ppermute | solution.py:228

commit v6 on v5

--- a/solution.py
+++ b/solution.py
@@ -141,45 +141,69 @@
 def factor_kernel(nodes, packs, inverse_ref, scale_ref):
     vecs = inverse_ref.shape[0]
     total = sum(ref[...] for ref in packs) / nodes
-    scale_ref[...] = jnp.broadcast_to(lax.rsqrt(total[:, vecs : vecs + 1] + epsilon), scale_ref.shape)
+    scale_ref[...] = lax.rsqrt(jnp.maximum(total, 0.0) + epsilon)
     row_ids = lax.broadcasted_iota(jnp.int32, (vecs, 2 * vecs), 0)
     lane_ids = lax.broadcasted_iota(jnp.int32, (vecs, 2 * vecs), 1)
     diagonal = jnp.where(lane_ids == row_ids, total, 0.0)
-    down = lax.rsqrt(jnp.sum(diagonal, axis=1, keepdims=True))
     across = lax.rsqrt(jnp.sum(diagonal, axis=0, keepdims=True))
-    work = jnp.where(lane_ids < vecs, total * down * across, jnp.where(lane_ids == row_ids + vecs, down, 0.0))
-    height = 8
-    tiles = [work[t : t + height] for t in range(0, vecs, height)]
-    shape = tiles[0].shape
+    height, step = 8, 4
+    shape = (height, 2 * vecs)
     ids = lax.broadcasted_iota(jnp.int32, shape, 0)
-    for j in range(0, vecs, 2):
+    lanes = lax.broadcasted_iota(jnp.int32, shape, 1)
+
+    def lane(tile, index):
+        return jnp.take_along_axis(tile, index, axis=1)
+
+    tiles = []
+    for t in range(0, vecs, height):
+        tile = total[t : t + height]
+        down = lax.rsqrt(lane(tile, ids + t))
+        unit = jnp.where(lanes == ids + (t + vecs), down, 0.0)
+        tiles.append(jnp.where(lanes < vecs, tile * down * across, unit))
+    done = [None] * len(tiles)
+    for j in range(0, vecs, step):
         t, s = divmod(j, height)
-        top, under = tiles[t][s : s + 1], tiles[t][s + 1 : s + 2]
+        rows = [jnp.broadcast_to(tiles[t][s + m : s + m + 1], shape) for m in range(step)]
         columns = [
-            [jnp.broadcast_to(tile[:, k : k + 1], shape) for k in (j, j + 1)] for tile in tiles[t:]
+            [lane(tile, jnp.full(shape, k, jnp.int32)) for k in range(j, j + step)] for tile in tiles[t:]
         ]
-        a = columns[0][0][s : s + 1]
-        b = columns[0][0][s + 1 : s + 2]
-        c = columns[0][1][s + 1 : s + 2]
-        determinant = 1.0 / (a * c - b * b)
-        a, b, c = a * determinant, b * determinant, c * determinant
+
+        def pivot(m, n):
+            return jnp.broadcast_to(columns[0][n][s + m : s + m + 1], shape)
+
+        p00, p10, p11 = pivot(0, 0), pivot(1, 0), pivot(1, 1)
+        q20, q21, q30, q31 = pivot(2, 0), pivot(2, 1), pivot(3, 0), pivot(3, 1)
+        w22, w32, w33 = pivot(2, 2), pivot(3, 2), pivot(3, 3)
+        scale = 1.0 / (p00 * p11 - p10 * p10)
+        i00, i10, i11 = p11 * scale, -p10 * scale, p00 * scale
+        e20, e21 = q20 * i00 + q21 * i10, q20 * i10 + q21 * i11
+        e30, e31 = q30 * i00 + q31 * i10, q30 * i10 + q31 * i11
+        s22 = w22 - (e20 * q20 + e21 * q21)
+        s32 = w32 - (e30 * q20 + e31 * q21)
+        s33 = w33 - (e30 * q30 + e31 * q31)
+        scale = 1.0 / (s22 * s33 - s32 * s32)
+        u22, u32, u33 = s33 * scale, -s32 * scale, s22 * scale
+        below2 = rows[2] - (e20 * rows[0] + e21 * rows[1])
+        below3 = rows[3] - (e30 * rows[0] + e31 * rows[1])
+        y2, y3 = below2 * u22 + below3 * u32, below2 * u32 + below3 * u33
+        z0 = rows[0] - (y2 * q20 + y3 * q30)
+        z1 = rows[1] - (y2 * q21 + y3 * q31)
+        y0, y1 = z0 * i00 + z1 * i10, z0 * i10 + z1 * i11
         for u in range(t, len(tiles)):
-            if u == t and s == height - 2:
+            if u == t and s + step == height:
                 continue
-            x, y = columns[u - t]
-            one, two = x * c - y * b, y * a - x * b
+            x0, x1, x2, x3 = columns[u - t]
+            less = (x0 * y0 + x1 * y1) + (x2 * y2 + x3 * y3)
             if u == t:
-                one, two = jnp.where(ids > s + 1, one, 0.0), jnp.where(ids > s + 1, two, 0.0)
-            tiles[u] = tiles[u] - one * top - two * under
-    work = jnp.concatenate(tiles, axis=0)
-    above = jnp.concatenate([work[:1], work[:-1]], axis=0)
-    odd = row_ids % 2 == 1
-    pivots = jnp.sum(jnp.where(lane_ids == row_ids, work, 0.0), axis=1, keepdims=True)
-    beside = jnp.sum(jnp.where(lane_ids == row_ids - 1, work, 0.0), axis=1, keepdims=True)
-    firsts = jnp.concatenate([pivots[:1], pivots[:-1]], axis=0)
-    ratio = jnp.where(odd[:, :1], beside / firsts, 0.0)
-    inverse = (work - ratio * above) * lax.rsqrt(pivots - ratio * beside)
-    inverse_ref[...] = inverse[:, vecs:]
+                less = jnp.where(ids >= s + step, less, 0.0)
+            tiles[u] = tiles[u] - less
+        ratio = p10 / p00
+        finished = [rows[0], rows[1] - ratio * rows[0], below2, below3 - (s32 / s22) * below2]
+        roots = [p00, p11 - ratio * p10, s22, s33 - (s32 / s22) * s32]
+        for m in range(step):
+            value = finished[m] * lax.rsqrt(roots[m])
+            done[t] = value if done[t] is None else jnp.where(ids >= s + m, value, done[t])
+    inverse_ref[...] = jnp.concatenate(done, axis=0)[:, vecs:]
 
 
 def basis_kernel(nodes, packs, inverse_ref, scale_ref, stack_ref, mix_ref, search_ref, basis_ref, gram_ref, dirs_ref, *own_basis):
@@ -188,7 +212,7 @@
     total = sum(ref[...] for ref in packs)[:, :vecs] / nodes
     gram_ref[...] = dot_nt(dot_nn(inverse, total), inverse)
     edge = dirs_ref.shape[1]
-    dirs_ref[...] = (search_ref[:, :edge] * scale_ref[:, :1]).astype(dirs_ref.dtype)
+    dirs_ref[...] = (search_ref[:, :edge] * scale_ref[:, vecs : vecs + 1]).astype(dirs_ref.dtype)
     basis = times_stack(dot_nn(inverse, mix_ref[...]), stack_ref[...])
     basis_ref[...] = pieces(basis)
     if own_basis:

time: 82.5 us -> 80.8 us (0.979)
  Pallas kernels: 23.3 us -> 19.8 us
  waiting for transfers between devices: 20 us -> 21.3 us
    pallas_call x20, Pallas kernels: 23.3 us -> 19.8 us  [call(): pl.pallas_call(kernel, out_shape=[jax.ShapeDtypeStruct(shape, kind) for s...]
    ppermute x33, waiting for transfers between devices: 20 us -> 21.3 us  [swap(): return lax.ppermute(value, axis, [(i, i ^ by) for i in range(size)])]
  transfers between devices with their start and end apart: 33 -> 33, of which waited for: 17 -> 20; matrix products, arithmetic and copies ran while one was open for 0% -> 0% of each run, Pallas kernels for 21% -> 17%
where the time goes in v6:
time: 80.8 us; the launch traced here: 80.6 us
  starting transfers between devices  35.6 us (44%)
  waiting for transfers between devices  21.3 us (26%)
  Pallas kernels  19.8 us (25%)
  local copies, waits for them, and re-layouts  2 us (2%)
  other arithmetic  0.87 us (1%)
  between operations  0.87 us (1%)
    ppermute x33, starting transfers between devices, swap(): return lax.ppermute(value, axis, [(i, i ^ by) for i in range(size)])  35.6 us
    ppermute x33, waiting for transfers between devices, swap(): return lax.ppermute(value, axis, [(i, i ^ by) for i in range(size)])  21.3 us
    pallas_call x20, Pallas kernels, call(): pl.pallas_call(kernel, out_shape=[jax.ShapeDtypeStruct(shape, kind) for s...  19.8 us
    unnamed x12, local copies, waits for them, and re-layouts  1.98 us
  transfers between devices with their start and end apart: 33, of which 20 were waited for; matrix products, arithmetic and copies ran while one was open for 0% of the time, Pallas kernels for 17%

profile of v6, /device:TPU:0, one launch (start us, length us, event | category | flops | bytes accessed | tf_op | source)
XLA Modules:
  0.0 80.6 jit_solution(6169701377642604089)
XLA Ops:
  0.6 0.8 maximum_bitcast_fusion
  1.4 5.0 %collective-permute-start.2 = (bf16[1,192,128]{2,1,0:T(8,128)(2,1)S(1)}, bf16[1,192,128]{2,1,0:T(8,128)(2,1)S(1)}, u32[]{:S(2)}, u32[]{:S(2)}) collective-permute-start(bf16[1,192,128]{2,1,0:T(8,128)(2,1)S(1)} %maximum_bitcast_fusion), channel_id=1, source_target_pairs={{0,24},{2,26},{4,28},{6,30},{8,16},{10,18},{12,20},{14,22},{16,8},... | collective-permute-start | bytes 147464 | tf_op jit(solution)/shard_map/ppermute | solution.py:252
  6.4 0.6 collective-permute-start
  7.1 0.7 copy-done.4
  7.8 1.2 %copy-done = bf16[1,1,2,16,128,128]{5,4,3,2,1,0:T(8,128)(2,1)S(1)} copy-done((bf16[1,1,2,16,128,128]{5,4,3,2,1,0:T(8,128)(2,1)S(1)}, bf16[1,1,2,16,128,128]{5,4,3,2,1,0:T(8,128)(2,1)}, u32[]{:S(2)}) %copy-start) | copy-done | bytes 1048600
  9.0 1.5 %shard_map.111.dense_ref.t = bf16[2048,256]{1,0:T(8,128)(2,1)S(1)} custom-call(s32[2,16]{1,0:T(2,128)S(1)} %compare_select_fusion.slots_ref, bf16[2,16,128,128]{3,2,1,0:T(8,128)(2,1)S(1)} %bitcast.25), custom_call_target="tpu_custom_call" | custom-call | tf_op jit(solution)/shard_map/pallas_call | solution.py:20
  10.6 0.9 %collective-permute-done.1 = bf16[1,192,128]{2,1,0:T(8,128)(2,1)S(1)} collective-permute-done((bf16[1,192,128]{2,1,0:T(8,128)(2,1)S(1)}, bf16[1,192,128]{2,1,0:T(8,128)(2,1)S(1)}, u32[]{:S(2)}, u32[]{:S(2)}) %collective-permute-start.1) | collective-permute-done | bytes 49184 | tf_op jit(solution)/shard_map/ppermute | solution.py:252
  11.5 2.5 %collective-permute-start.5 = (bf16[4,192,128]{2,1,0:T(8,128)(2,1)S(1)}, bf16[4,192,128]{2,1,0:T(8,128)(2,1)S(1)}, u32[]{:S(2)}, u32[]{:S(2)}) collective-permute-start(bf16[4,192,128]{2,1,0:T(8,128)(2,1)S(1)} %pad_maximum_fusion.refs_0_), channel_id=1, source_target_pairs={{0,6},{2,4},{4,2},{6,0},{8,14},{10,12},{12,10},{14,8},{16,22},{18,... | collective-permute-start | bytes 589832 | tf_op jit(solution)/shard_map/ppermute | solution.py:252
  14.0 0.5 collective-permute-start.4
  14.5 0.5 collective-permute-start.3
  15.0 4.9 %collective-permute-done.5.refs_3_ = bf16[4,192,128]{2,1,0:T(8,128)(2,1)S(1)} collective-permute-done((bf16[4,192,128]{2,1,0:T(8,128)(2,1)S(1)}, bf16[4,192,128]{2,1,0:T(8,128)(2,1)S(1)}, u32[]{:S(2)}, u32[]{:S(2)}) %collective-permute-start.5) | collective-permute-done | bytes 196640 | tf_op jit(solution)/shard_map/ppermute | solution.py:252
  19.9 2.5 %collective-permute-done.4.refs_2_ = bf16[4,192,128]{2,1,0:T(8,128)(2,1)S(1)} collective-permute-done((bf16[4,192,128]{2,1,0:T(8,128)(2,1)S(1)}, bf16[4,192,128]{2,1,0:T(8,128)(2,1)S(1)}, u32[]{:S(2)}, u32[]{:S(2)}) %collective-permute-start.4) | collective-permute-done | bytes 196640 | tf_op jit(solution)/shard_map/ppermute | solution.py:252
  22.5 0.7 shard_map.112
  23.4 1.1 %shard_map.113 = (f32[64,128]{1,0:T(8,128)S(1)}, f32[64,2048]{1,0:T(8,128)S(1)}) custom-call(bf16[192,2048]{1,0:T(8,128)(2,1)S(1)} %get-tuple-element.76.stack_ref.refs_4_, f32[64,192]{1,0:T(8,128)S(1)} %get-tuple-element.134.mix_ref.refs_5_, f32[64,128]{1,0:T(8,128)S(1)} %get-tuple-element.138.search_ref), custom_call_target="tpu_custom_call" | custom-call | tf_op jit(solution)/shard_map/pallas_call | solution.py:20
  24.5 0.5 collective-permute-start.10
  25.1 4.3 %collective-permute-start.9 = (f32[64,128]{1,0:T(8,128)S(1)}, f32[64,128]{1,0:T(8,128)S(1)}, u32[]{:S(2)}, u32[]{:S(2)}) collective-permute-start(f32[64,128]{1,0:T(8,128)S(1)} %add.21.refs_0_), channel_id=1, source_target_pairs={{0,24},{2,26},{4,28},{6,30},{8,16},{10,18},{12,20},{14,22},{16,8},... | collective-permute-start | bytes 98312 | tf_op jit(solution)/shard_map/ppermute | solution.py:252
  29.3 0.6 collective-permute-start.7
  30.0 2.2 %shard_map.114 = (f32[64,64]{1,0:T(8,128)S(1)}, f32[64,128]{1,0:T(8,128)S(1)}) custom-call(f32[64,128]{1,0:T(8,128)S(1)} %get-tuple-element.79.refs_0_, f32[64,128]{1,0:T(8,128)S(1)} %collective-permute-done.10.refs_1_), custom_call_target="tpu_custom_call" | custom-call | tf_op jit(solution)/shard_map/pallas_call | solution.py:20
  32.2 2.0 %collective-permute-done.8.refs_2_ = f32[64,128]{1,0:T(8,128)S(1)} collective-permute-done((f32[64,128]{1,0:T(8,128)S(1)}, f32[64,128]{1,0:T(8,128)S(1)}, u32[]{:S(2)}, u32[]{:S(2)}) %collective-permute-start.8) | collective-permute-done | bytes 32800 | tf_op jit(solution)/shard_map/ppermute | solution.py:252
  34.2 0.3 shard_map.115.refs_0_
  34.4 1.2 %collective-permute-start.13 = (bf16[256,128]{1,0:T(8,128)(2,1)S(1)}, bf16[256,128]{1,0:T(8,128)(2,1)S(1)}, u32[]{:S(2)}, u32[]{:S(2)}) collective-permute-start(bf16[256,128]{1,0:T(8,128)(2,1)S(1)} %shard_map.115.refs_0_), channel_id=1, source_target_pairs={{0,6},{2,4},{4,2},{6,0},{8,14},{10,12},{12,10},{14,8},{16,22},{18,... | collective-permute-start | bytes 196616 | tf_op jit(solution)/shard_map/ppermute | solution.py:252
  35.7 0.6 collective-permute-start.12
  36.3 1.7 %collective-permute-start.11 = (bf16[256,128]{1,0:T(8,128)(2,1)S(1)}, bf16[256,128]{1,0:T(8,128)(2,1)S(1)}, u32[]{:S(2)}, u32[]{:S(2)}) collective-permute-start(bf16[256,128]{1,0:T(8,128)(2,1)S(1)} %shard_map.115.refs_0_), channel_id=1, source_target_pairs={{0,2},{2,0},{4,6},{6,4},{8,10},{10,8},{12,14},{14,12},{16,18},{18,... | collective-permute-start | bytes 196616 | tf_op jit(solution)/shard_map/ppermute | solution.py:252
  38.0 0.6 shard_map.116
  38.6 1.1 %collective-permute-done.13.refs_3_ = bf16[256,128]{1,0:T(8,128)(2,1)S(1)} collective-permute-done((bf16[256,128]{1,0:T(8,128)(2,1)S(1)}, bf16[256,128]{1,0:T(8,128)(2,1)S(1)}, u32[]{:S(2)}, u32[]{:S(2)}) %collective-permute-start.13) | collective-permute-done | bytes 65568 | tf_op jit(solution)/shard_map/ppermute | solution.py:252
  39.7 0.7 collective-permute-done.12.refs_2_
  40.5 0.4 shard_map.117
  41.0 1.2 %collective-permute-done.14.refs_1_ = f32[64,128]{1,0:T(8,128)S(1)} collective-permute-done((f32[64,128]{1,0:T(8,128)S(1)}, f32[64,128]{1,0:T(8,128)S(1)}, u32[]{:S(2)}, u32[]{:S(2)}) %collective-permute-start.14) | collective-permute-done | bytes 32800 | tf_op jit(solution)/shard_map/ppermute | solution.py:252
  42.2 1.1 %shard_map.118 = (bf16[192,2048]{1,0:T(8,128)(2,1)S(1)}, f32[64,128]{1,0:T(8,128)S(1)}, f32[64,128]{1,0:T(8,128)S(1)}) custom-call(s32[1]{0:T(128)} %bitcast.place_ref.p, bf16[2048,256]{1,0:T(8,128)(2,1)S(1)} %shard_map.111.dense_ref.t, f32[64,192]{1,0:T(8,128)S(1)} %get-tuple-element.136.m.mix_ref.refs_5_, f32[64,128]{1,0:T(8,128)S(1)} %get-tuple-element.89.refs_0_, ...), custom_call_target="tpu_custom_call" | custom-call | tf_op jit(solution)/shard_map/pallas_call | solution.py:20
  43.3 0.2 collective-permute-start.15
  43.5 1.1 %shard_map.119 = (f32[64,128]{1,0:T(8,128)S(1)}, f32[64,2048]{1,0:T(8,128)S(1)}) custom-call(bf16[192,2048]{1,0:T(8,128)(2,1)S(1)} %get-tuple-element.95.stack_ref.refs_4_, f32[64,192]{1,0:T(8,128)S(1)} %get-tuple-element.136.m.mix_ref.refs_5_, f32[64,128]{1,0:T(8,128)S(1)} %get-tuple-element.139.search_ref), custom_call_target="tpu_custom_call" | custom-call | tf_op jit(solution)/shard_map/pallas_call | solution.py:20
  44.7 0.4 collective-permute-start.19
  45.1 1.8 %collective-permute-start.18 = (f32[64,128]{1,0:T(8,128)S(1)}, f32[64,128]{1,0:T(8,128)S(1)}, u32[]{:S(2)}, u32[]{:S(2)}) collective-permute-start(f32[64,128]{1,0:T(8,128)S(1)} %add.22.refs_0_), channel_id=1, source_target_pairs={{0,24},{2,26},{4,28},{6,30},{8,16},{10,18},{12,20},{14,22},{16,8},... | collective-permute-start | bytes 98312 | tf_op jit(solution)/shard_map/ppermute | solution.py:252
  46.9 0.3 collective-permute-start.17
  47.2 2.3 %collective-permute-start.16 = (f32[64,128]{1,0:T(8,128)S(1)}, f32[64,128]{1,0:T(8,128)S(1)}, u32[]{:S(2)}, u32[]{:S(2)}) collective-permute-start(f32[64,128]{1,0:T(8,128)S(1)} %add.22.refs_0_), channel_id=1, source_target_pairs={{0,8},{2,10},{4,12},{6,14},{8,0},{10,2},{12,4},{14,6},{16,24},{18,... | collective-permute-start | bytes 98312 | tf_op jit(solution)/shard_map/ppermute | solution.py:252
  49.5 2.2 %shard_map.120 = (f32[64,64]{1,0:T(8,128)S(1)}, f32[64,128]{1,0:T(8,128)S(1)}) custom-call(f32[64,128]{1,0:T(8,128)S(1)} %get-tuple-element.98.refs_0_, f32[64,128]{1,0:T(8,128)S(1)} %collective-permute-done.19.refs_1_), custom_call_target="tpu_custom_call" | custom-call | tf_op jit(solution)/shard_map/pallas_call | solution.py:20
  51.9 0.2 shard_map.121.refs_0_
  52.1 1.8 %collective-permute-start.22 = (bf16[256,128]{1,0:T(8,128)(2,1)S(1)}, bf16[256,128]{1,0:T(8,128)(2,1)S(1)}, u32[]{:S(2)}, u32[]{:S(2)}) collective-permute-start(bf16[256,128]{1,0:T(8,128)(2,1)S(1)} %shard_map.121.refs_0_), channel_id=1, source_target_pairs={{0,6},{2,4},{4,2},{6,0},{8,14},{10,12},{12,10},{14,8},{16,22},{18,... | collective-permute-start | bytes 196616 | tf_op jit(solution)/shard_map/ppermute | solution.py:252
  54.0 1.4 %collective-permute-start.21 = (bf16[256,128]{1,0:T(8,128)(2,1)S(1)}, bf16[256,128]{1,0:T(8,128)(2,1)S(1)}, u32[]{:S(2)}, u32[]{:S(2)}) collective-permute-start(bf16[256,128]{1,0:T(8,128)(2,1)S(1)} %shard_map.121.refs_0_), channel_id=1, source_target_pairs={{0,4},{2,6},{4,0},{6,2},{8,12},{10,14},{12,8},{14,10},{16,20},{18,... | collective-permute-start | bytes 196616 | tf_op jit(solution)/shard_map/ppermute | solution.py:252
  55.4 0.3 collective-permute-start.20
  55.7 0.6 shard_map.122
  56.3 1.6 %collective-permute-done.22.refs_3_ = bf16[256,128]{1,0:T(8,128)(2,1)S(1)} collective-permute-done((bf16[256,128]{1,0:T(8,128)(2,1)S(1)}, bf16[256,128]{1,0:T(8,128)(2,1)S(1)}, u32[]{:S(2)}, u32[]{:S(2)}) %collective-permute-start.22) | collective-permute-done | bytes 65568 | tf_op jit(solution)/shard_map/ppermute | solution.py:252
  57.9 0.5 collective-permute-done.21.refs_2_
  58.4 1.2 %collective-permute-done.20.refs_1_ = bf16[256,128]{1,0:T(8,128)(2,1)S(1)} collective-permute-done((bf16[256,128]{1,0:T(8,128)(2,1)S(1)}, bf16[256,128]{1,0:T(8,128)(2,1)S(1)}, u32[]{:S(2)}, u32[]{:S(2)}) %collective-permute-start.20) | collective-permute-done | bytes 65568 | tf_op jit(solution)/shard_map/ppermute | solution.py:252
  59.7 0.4 shard_map.123
  60.1 1.2 %collective-permute-done.23.refs_1_ = f32[64,128]{1,0:T(8,128)S(1)} collective-permute-done((f32[64,128]{1,0:T(8,128)S(1)}, f32[64,128]{1,0:T(8,128)S(1)}, u32[]{:S(2)}, u32[]{:S(2)}) %collective-permute-start.23) | collective-permute-done | bytes 32800 | tf_op jit(solution)/shard_map/ppermute | solution.py:252
  61.3 1.1 %shard_map.124 = (bf16[192,2048]{1,0:T(8,128)(2,1)S(1)}, f32[64,128]{1,0:T(8,128)S(1)}, f32[64,128]{1,0:T(8,128)S(1)}) custom-call(s32[1]{0:T(128)} %bitcast.place_ref.p, bf16[2048,256]{1,0:T(8,128)(2,1)S(1)} %shard_map.111.dense_ref.t, f32[64,192]{1,0:T(8,128)S(1)} %get-tuple-element.135.m.mix_ref.refs_5_, f32[64,128]{1,0:T(8,128)S(1)} %get-tuple-element.108.refs_0_, ...), custom_call_target="tpu_custom_call" | custom-call | tf_op jit(solution)/shard_map/pallas_call | solution.py:20
  62.7 1.1 %shard_map.125 = (f32[64,128]{1,0:T(8,128)S(1)}, f32[64,2048]{1,0:T(8,128)S(1)}) custom-call(bf16[192,2048]{1,0:T(8,128)(2,1)S(1)} %get-tuple-element.113.stack_ref.refs_4_, f32[64,192]{1,0:T(8,128)S(1)} %get-tuple-element.135.m.mix_ref.refs_5_, f32[64,128]{1,0:T(8,128)S(1)} %get-tuple-element.137.search_ref), custom_call_target="tpu_custom_call" | custom-call | tf_op jit(solution)/shard_map/pallas_call | solution.py:20
  63.8 0.4 collective-permute-start.25
  64.3 2.4 %collective-permute-start.28 = (f32[64,128]{1,0:T(8,128)S(1)}, f32[64,128]{1,0:T(8,128)S(1)}, u32[]{:S(2)}, u32[]{:S(2)}) collective-permute-start(f32[64,128]{1,0:T(8,128)S(1)} %add.23.refs_0_), channel_id=1, source_target_pairs={{0,24},{2,26},{4,28},{6,30},{8,16},{10,18},{12,20},{14,22},{16,8},... | collective-permute-start | bytes 98312 | tf_op jit(solution)/shard_map/ppermute | solution.py:252
  66.6 0.6 collective-permute-start.27
  67.2 1.4 %collective-permute-start.26 = (f32[64,128]{1,0:T(8,128)S(1)}, f32[64,128]{1,0:T(8,128)S(1)}, u32[]{:S(2)}, u32[]{:S(2)}) collective-permute-start(f32[64,128]{1,0:T(8,128)S(1)} %add.23.refs_0_), channel_id=1, source_target_pairs={{0,8},{2,10},{4,12},{6,14},{8,0},{10,2},{12,4},{14,6},{16,24},{18,... | collective-permute-start | bytes 98312 | tf_op jit(solution)/shard_map/ppermute | solution.py:252
  68.7 2.2 %shard_map.126 = (f32[64,64]{1,0:T(8,128)S(1)}, f32[64,128]{1,0:T(8,128)S(1)}) custom-call(f32[64,128]{1,0:T(8,128)S(1)} %get-tuple-element.115.refs_0_, f32[64,128]{1,0:T(8,128)S(1)} %collective-permute-done.25.refs_1_), custom_call_target="tpu_custom_call" | custom-call | tf_op jit(solution)/shard_map/pallas_call | solution.py:20
  70.9 0.6 collective-permute-done.27.refs_2_
  71.5 0.3 shard_map.128
  71.8 1.2 %collective-permute-start.31 = (bf16[256,128]{1,0:T(8,128)(2,1)S(1)}, bf16[256,128]{1,0:T(8,128)(2,1)S(1)}, u32[]{:S(2)}, u32[]{:S(2)}) collective-permute-start(bf16[256,128]{1,0:T(8,128)(2,1)S(1)} %get-tuple-element.127.refs_0_), channel_id=1, source_target_pairs={{0,6},{2,4},{4,2},{6,0},{8,14},{10,12},{12,10},{14,8},{16,22},{18,... | collective-permute-start | bytes 196616 | tf_op jit(solution)/shard_map/ppermute | solution.py:252
  73.0 0.6 collective-permute-start.30
  73.6 1.7 %collective-permute-start.29 = (bf16[256,128]{1,0:T(8,128)(2,1)S(1)}, bf16[256,128]{1,0:T(8,128)(2,1)S(1)}, u32[]{:S(2)}, u32[]{:S(2)}) collective-permute-start(bf16[256,128]{1,0:T(8,128)(2,1)S(1)} %get-tuple-element.127.refs_0_), channel_id=1, source_target_pairs={{0,2},{2,0},{4,6},{6,4},{8,10},{10,8},{12,14},{14,12},{16,18},{18,... | collective-permute-start | bytes 196616 | tf_op jit(solution)/shard_map/ppermute | solution.py:252
  75.3 1.2 %shard_map.127 = (bf16[192,2048]{1,0:T(8,128)(2,1)S(1)}, f32[64,64]{1,0:T(8,128)S(1)}, f32[64,128]{1,0:T(8,128)}, f32[64,128]{1,0:T(8,128)}) custom-call(f32[64,128]{1,0:T(8,128)S(1)} %get-tuple-element.115.refs_0_, f32[64,128]{1,0:T(8,128)S(1)} %collective-permute-done.25.refs_1_, f32[64,64]{1,0:T(8,128)S(1)} %get-tuple-element.119.refs_2_.refs_4_, ...), custom_call_target="tpu_custom_call" | custom-call | tf_op jit(solution)/shard_map/pallas_call | solution.py:20
  76.5 0.5 collective-permute-done.31.refs_3_
  77.0 0.7 collective-permute-done.30.refs_2_
  77.9 0.4 shard_map.129.refs_0_
  78.3 1.2 %collective-permute-done.32.refs_1_ = f32[64,128]{1,0:T(8,128)S(1)} collective-permute-done((f32[64,128]{1,0:T(8,128)S(1)}, f32[64,128]{1,0:T(8,128)S(1)}, u32[]{:S(2)}, u32[]{:S(2)}) %collective-permute-start.32) | collective-permute-done | bytes 32800 | tf_op jit(solution)/shard_map/ppermute | solution.py:252
  79.5 1.0 %shard_map.130 = (f32[64,128]{1,0:T(8,128)}, f32[64,64]{1,0:T(8,128)}) custom-call(f32[64,128]{1,0:T(8,128)S(1)} %shard_map.129.refs_0_, f32[64,128]{1,0:T(8,128)S(1)} %collective-permute-done.32.refs_1_, f32[64,64]{1,0:T(8,128)S(1)} %get-tuple-element.129.refs_2_, f32[64,128]{1,0:T(8,128)S(1)} %copy-done.1, f32[64,128]{1,0:T(8,128)S(1)} %get-tuple-element.130.refs_4_), custom_call_target="tpu_custom_call" | custom-call | tf_op jit(solution)/shard_map/pallas_call | solution.py:20
  (42 shorter events, 1.4 us)
Async XLA Ops:
  1.4 9.2 %collective-permute-start.2 = (bf16[1,192,128]{2,1,0:T(8,128)(2,1)S(1)}, bf16[1,192,128]{2,1,0:T(8,128)(2,1)S(1)}, u32[]{:S(2)}, u32[]{:S(2)}) collective-permute-start(bf16[1,192,128]{2,1,0:T(8,128)(2,1)S(1)} %maximum_bitcast_fusion), channel_id=1, source_target_pairs={{0,24},{2,26},{4,28},{6,30},{8,16},{10,18},{12,20},{14,22},{16,8},... | collective-permute-start | bytes 147464 | tf_op jit(solution)/shard_map/ppermute | solution.py:252
  6.4 5.0 %collective-permute-start.1 = (bf16[1,192,128]{2,1,0:T(8,128)(2,1)S(1)}, bf16[1,192,128]{2,1,0:T(8,128)(2,1)S(1)}, u32[]{:S(2)}, u32[]{:S(2)}) collective-permute-start(bf16[1,192,128]{2,1,0:T(8,128)(2,1)S(1)} %maximum_bitcast_fusion), channel_id=1, source_target_pairs={{0,16},{2,18},{4,20},{6,22},{8,24},{10,26},{12,28},{14,30},{16,0},... | collective-permute-start | bytes 147464 | tf_op jit(solution)/shard_map/ppermute | solution.py:252
  6.4 5.0 %collective-permute-start = (bf16[1,192,128]{2,1,0:T(8,128)(2,1)S(1)}, bf16[1,192,128]{2,1,0:T(8,128)(2,1)S(1)}, u32[]{:S(2)}, u32[]{:S(2)}) collective-permute-start(bf16[1,192,128]{2,1,0:T(8,128)(2,1)S(1)} %maximum_bitcast_fusion), channel_id=1, source_target_pairs={{0,8},{2,10},{4,12},{6,14},{8,0},{10,2},{12,4},{14,6},{16,24},{18,... | collective-permute-start | bytes 147464 | tf_op jit(solution)/shard_map/ppermute | solution.py:252
  7.0 0.7 copy-start.4
  7.1 0.7 copy-start.5
  7.8 1.2 %copy-start = (bf16[1,1,2,16,128,128]{5,4,3,2,1,0:T(8,128)(2,1)S(1)}, bf16[1,1,2,16,128,128]{5,4,3,2,1,0:T(8,128)(2,1)}, u32[]{:S(2)}) copy-start(bf16[1,1,2,16,128,128]{5,4,3,2,1,0:T(8,128)(2,1)} %param.8) | copy-start | bytes 3145732
  10.5 4.5 %copy-start.2 = (f32[3,64,192]{2,1,0:T(8,128)S(1)}, f32[3,64,192]{2,1,0:T(8,128)}, u32[]{:S(2)}) copy-start(f32[3,64,192]{2,1,0:T(8,128)} %param.14) | copy-start | bytes 442372
  11.5 8.5 %collective-permute-start.5 = (bf16[4,192,128]{2,1,0:T(8,128)(2,1)S(1)}, bf16[4,192,128]{2,1,0:T(8,128)(2,1)S(1)}, u32[]{:S(2)}, u32[]{:S(2)}) collective-permute-start(bf16[4,192,128]{2,1,0:T(8,128)(2,1)S(1)} %pad_maximum_fusion.refs_0_), channel_id=1, source_target_pairs={{0,6},{2,4},{4,2},{6,0},{8,14},{10,12},{12,10},{14,8},{16,22},{18,... | collective-permute-start | bytes 589832 | tf_op jit(solution)/shard_map/ppermute | solution.py:252
  14.0 8.4 %collective-permute-start.4 = (bf16[4,192,128]{2,1,0:T(8,128)(2,1)S(1)}, bf16[4,192,128]{2,1,0:T(8,128)(2,1)S(1)}, u32[]{:S(2)}, u32[]{:S(2)}) collective-permute-start(bf16[4,192,128]{2,1,0:T(8,128)(2,1)S(1)} %pad_maximum_fusion.refs_0_), channel_id=1, source_target_pairs={{0,4},{2,6},{4,0},{6,2},{8,12},{10,14},{12,8},{14,10},{16,20},{18,... | collective-permute-start | bytes 589832 | tf_op jit(solution)/shard_map/ppermute | solution.py:252
  14.5 8.0 %collective-permute-start.3 = (bf16[4,192,128]{2,1,0:T(8,128)(2,1)S(1)}, bf16[4,192,128]{2,1,0:T(8,128)(2,1)S(1)}, u32[]{:S(2)}, u32[]{:S(2)}) collective-permute-start(bf16[4,192,128]{2,1,0:T(8,128)(2,1)S(1)} %pad_maximum_fusion.refs_0_), channel_id=1, source_target_pairs={{0,2},{2,0},{4,6},{6,4},{8,10},{10,8},{12,14},{14,12},{16,18},{18,... | collective-permute-start | bytes 589832 | tf_op jit(solution)/shard_map/ppermute | solution.py:252
  22.5 0.9 %copy-start.3 = (f32[3,64,128]{2,1,0:T(8,128)S(1)}, f32[3,64,128]{2,1,0:T(8,128)}, u32[]{:S(2)}) copy-start(f32[3,64,128]{2,1,0:T(8,128)} %param.15) | copy-start | bytes 294916
  23.2 1.3 %collective-permute-start.6 = (f32[64,128]{1,0:T(8,128)S(1)}, f32[64,128]{1,0:T(8,128)S(1)}, u32[]{:S(2)}, u32[]{:S(2)}) collective-permute-start(f32[64,128]{1,0:T(8,128)S(1)} %get-tuple-element.75), channel_id=1, source_target_pairs={{0,1},{1,0},{2,3},{3,2},{4,5},{5,4},{6,7},{7,6},{8,9},{9,8},{10,11... | collective-permute-start | bytes 98312 | tf_op jit(solution)/shard_map/ppermute | solution.py:252
  24.5 5.4 %collective-permute-start.10 = (f32[64,128]{1,0:T(8,128)S(1)}, f32[64,128]{1,0:T(8,128)S(1)}, u32[]{:S(2)}, u32[]{:S(2)}) collective-permute-start(f32[64,128]{1,0:T(8,128)S(1)} %get-tuple-element.79.refs_0_), channel_id=1, source_target_pairs={{0,1},{1,0},{2,3},{3,2},{4,5},{5,4},{6,7},{7,6},{8,9},{9,8},{10,11... | collective-permute-start | bytes 98312 | tf_op jit(solution)/shard_map/ppermute | solution.py:252
  25.1 7.1 %collective-permute-start.9 = (f32[64,128]{1,0:T(8,128)S(1)}, f32[64,128]{1,0:T(8,128)S(1)}, u32[]{:S(2)}, u32[]{:S(2)}) collective-permute-start(f32[64,128]{1,0:T(8,128)S(1)} %add.21.refs_0_), channel_id=1, source_target_pairs={{0,24},{2,26},{4,28},{6,30},{8,16},{10,18},{12,20},{14,22},{16,8},... | collective-permute-start | bytes 98312 | tf_op jit(solution)/shard_map/ppermute | solution.py:252
  29.3 4.8 %collective-permute-start.8 = (f32[64,128]{1,0:T(8,128)S(1)}, f32[64,128]{1,0:T(8,128)S(1)}, u32[]{:S(2)}, u32[]{:S(2)}) collective-permute-start(f32[64,128]{1,0:T(8,128)S(1)} %add.21.refs_0_), channel_id=1, source_target_pairs={{0,16},{2,18},{4,20},{6,22},{8,24},{10,26},{12,28},{14,30},{16,0},... | collective-permute-start | bytes 98312 | tf_op jit(solution)/shard_map/ppermute | solution.py:252
  29.3 4.8 %collective-permute-start.7 = (f32[64,128]{1,0:T(8,128)S(1)}, f32[64,128]{1,0:T(8,128)S(1)}, u32[]{:S(2)}, u32[]{:S(2)}) collective-permute-start(f32[64,128]{1,0:T(8,128)S(1)} %add.21.refs_0_), channel_id=1, source_target_pairs={{0,8},{2,10},{4,12},{6,14},{8,0},{10,2},{12,4},{14,6},{16,24},{18,... | collective-permute-start | bytes 98312 | tf_op jit(solution)/shard_map/ppermute | solution.py:252
  34.4 5.3 %collective-permute-start.13 = (bf16[256,128]{1,0:T(8,128)(2,1)S(1)}, bf16[256,128]{1,0:T(8,128)(2,1)S(1)}, u32[]{:S(2)}, u32[]{:S(2)}) collective-permute-start(bf16[256,128]{1,0:T(8,128)(2,1)S(1)} %shard_map.115.refs_0_), channel_id=1, source_target_pairs={{0,6},{2,4},{4,2},{6,0},{8,14},{10,12},{12,10},{14,8},{16,22},{18,... | collective-permute-start | bytes 196616 | tf_op jit(solution)/shard_map/ppermute | solution.py:252
  35.7 4.7 %collective-permute-start.12 = (bf16[256,128]{1,0:T(8,128)(2,1)S(1)}, bf16[256,128]{1,0:T(8,128)(2,1)S(1)}, u32[]{:S(2)}, u32[]{:S(2)}) collective-permute-start(bf16[256,128]{1,0:T(8,128)(2,1)S(1)} %shard_map.115.refs_0_), channel_id=1, source_target_pairs={{0,4},{2,6},{4,0},{6,2},{8,12},{10,14},{12,8},{14,10},{16,20},{18,... | collective-permute-start | bytes 196616 | tf_op jit(solution)/shard_map/ppermute | solution.py:252
  36.3 4.3 %collective-permute-start.11 = (bf16[256,128]{1,0:T(8,128)(2,1)S(1)}, bf16[256,128]{1,0:T(8,128)(2,1)S(1)}, u32[]{:S(2)}, u32[]{:S(2)}) collective-permute-start(bf16[256,128]{1,0:T(8,128)(2,1)S(1)} %shard_map.115.refs_0_), channel_id=1, source_target_pairs={{0,2},{2,0},{4,6},{6,4},{8,10},{10,8},{12,14},{14,12},{16,18},{18,... | collective-permute-start | bytes 196616 | tf_op jit(solution)/shard_map/ppermute | solution.py:252
  40.9 1.3 %collective-permute-start.14 = (f32[64,128]{1,0:T(8,128)S(1)}, f32[64,128]{1,0:T(8,128)S(1)}, u32[]{:S(2)}, u32[]{:S(2)}) collective-permute-start(f32[64,128]{1,0:T(8,128)S(1)} %get-tuple-element.89.refs_0_), channel_id=1, source_target_pairs={{0,1},{1,0},{2,3},{3,2},{4,5},{5,4},{6,7},{7,6},{8,9},{9,8},{10,11... | collective-permute-start | bytes 98312 | tf_op jit(solution)/shard_map/ppermute | solution.py:252
  43.3 1.4 %collective-permute-start.15 = (f32[64,128]{1,0:T(8,128)S(1)}, f32[64,128]{1,0:T(8,128)S(1)}, u32[]{:S(2)}, u32[]{:S(2)}) collective-permute-start(f32[64,128]{1,0:T(8,128)S(1)} %get-tuple-element.94), channel_id=1, source_target_pairs={{0,1},{1,0},{2,3},{3,2},{4,5},{5,4},{6,7},{7,6},{8,9},{9,8},{10,11... | collective-permute-start | bytes 98312 | tf_op jit(solution)/shard_map/ppermute | solution.py:252
  44.7 4.8 %collective-permute-start.19 = (f32[64,128]{1,0:T(8,128)S(1)}, f32[64,128]{1,0:T(8,128)S(1)}, u32[]{:S(2)}, u32[]{:S(2)}) collective-permute-start(f32[64,128]{1,0:T(8,128)S(1)} %get-tuple-element.98.refs_0_), channel_id=1, source_target_pairs={{0,1},{1,0},{2,3},{3,2},{4,5},{5,4},{6,7},{7,6},{8,9},{9,8},{10,11... | collective-permute-start | bytes 98312 | tf_op jit(solution)/shard_map/ppermute | solution.py:252
  45.1 6.6 %collective-permute-start.18 = (f32[64,128]{1,0:T(8,128)S(1)}, f32[64,128]{1,0:T(8,128)S(1)}, u32[]{:S(2)}, u32[]{:S(2)}) collective-permute-start(f32[64,128]{1,0:T(8,128)S(1)} %add.22.refs_0_), channel_id=1, source_target_pairs={{0,24},{2,26},{4,28},{6,30},{8,16},{10,18},{12,20},{14,22},{16,8},... | collective-permute-start | bytes 98312 | tf_op jit(solution)/shard_map/ppermute | solution.py:252
  46.9 4.9 %collective-permute-start.17 = (f32[64,128]{1,0:T(8,128)S(1)}, f32[64,128]{1,0:T(8,128)S(1)}, u32[]{:S(2)}, u32[]{:S(2)}) collective-permute-start(f32[64,128]{1,0:T(8,128)S(1)} %add.22.refs_0_), channel_id=1, source_target_pairs={{0,16},{2,18},{4,20},{6,22},{8,24},{10,26},{12,28},{14,30},{16,0},... | collective-permute-start | bytes 98312 | tf_op jit(solution)/shard_map/ppermute | solution.py:252
  47.2 4.7 %collective-permute-start.16 = (f32[64,128]{1,0:T(8,128)S(1)}, f32[64,128]{1,0:T(8,128)S(1)}, u32[]{:S(2)}, u32[]{:S(2)}) collective-permute-start(f32[64,128]{1,0:T(8,128)S(1)} %add.22.refs_0_), channel_id=1, source_target_pairs={{0,8},{2,10},{4,12},{6,14},{8,0},{10,2},{12,4},{14,6},{16,24},{18,... | collective-permute-start | bytes 98312 | tf_op jit(solution)/shard_map/ppermute | solution.py:252
  52.1 5.8 %collective-permute-start.22 = (bf16[256,128]{1,0:T(8,128)(2,1)S(1)}, bf16[256,128]{1,0:T(8,128)(2,1)S(1)}, u32[]{:S(2)}, u32[]{:S(2)}) collective-permute-start(bf16[256,128]{1,0:T(8,128)(2,1)S(1)} %shard_map.121.refs_0_), channel_id=1, source_target_pairs={{0,6},{2,4},{4,2},{6,0},{8,14},{10,12},{12,10},{14,8},{16,22},{18,... | collective-permute-start | bytes 196616 | tf_op jit(solution)/shard_map/ppermute | solution.py:252
  54.0 4.5 %collective-permute-start.21 = (bf16[256,128]{1,0:T(8,128)(2,1)S(1)}, bf16[256,128]{1,0:T(8,128)(2,1)S(1)}, u32[]{:S(2)}, u32[]{:S(2)}) collective-permute-start(bf16[256,128]{1,0:T(8,128)(2,1)S(1)} %shard_map.121.refs_0_), channel_id=1, source_target_pairs={{0,4},{2,6},{4,0},{6,2},{8,12},{10,14},{12,8},{14,10},{16,20},{18,... | collective-permute-start | bytes 196616 | tf_op jit(solution)/shard_map/ppermute | solution.py:252
  55.4 4.3 %collective-permute-start.20 = (bf16[256,128]{1,0:T(8,128)(2,1)S(1)}, bf16[256,128]{1,0:T(8,128)(2,1)S(1)}, u32[]{:S(2)}, u32[]{:S(2)}) collective-permute-start(bf16[256,128]{1,0:T(8,128)(2,1)S(1)} %shard_map.121.refs_0_), channel_id=1, source_target_pairs={{0,2},{2,0},{4,6},{6,4},{8,10},{10,8},{12,14},{14,12},{16,18},{18,... | collective-permute-start | bytes 196616 | tf_op jit(solution)/shard_map/ppermute | solution.py:252
  60.1 1.3 %collective-permute-start.23 = (f32[64,128]{1,0:T(8,128)S(1)}, f32[64,128]{1,0:T(8,128)S(1)}, u32[]{:S(2)}, u32[]{:S(2)}) collective-permute-start(f32[64,128]{1,0:T(8,128)S(1)} %get-tuple-element.108.refs_0_), channel_id=1, source_target_pairs={{0,1},{1,0},{2,3},{3,2},{4,5},{5,4},{6,7},{7,6},{8,9},{9,8},{10,11... | collective-permute-start | bytes 98312 | tf_op jit(solution)/shard_map/ppermute | solution.py:252
  62.5 1.4 %collective-permute-start.24 = (f32[64,128]{1,0:T(8,128)S(1)}, f32[64,128]{1,0:T(8,128)S(1)}, u32[]{:S(2)}, u32[]{:S(2)}) collective-permute-start(f32[64,128]{1,0:T(8,128)S(1)} %get-tuple-element.112), channel_id=1, source_target_pairs={{0,1},{1,0},{2,3},{3,2},{4,5},{5,4},{6,7},{7,6},{8,9},{9,8},{10,11... | collective-permute-start | bytes 98312 | tf_op jit(solution)/shard_map/ppermute | solution.py:252
  63.8 4.8 %collective-permute-start.25 = (f32[64,128]{1,0:T(8,128)S(1)}, f32[64,128]{1,0:T(8,128)S(1)}, u32[]{:S(2)}, u32[]{:S(2)}) collective-permute-start(f32[64,128]{1,0:T(8,128)S(1)} %get-tuple-element.115.refs_0_), channel_id=1, source_target_pairs={{0,1},{1,0},{2,3},{3,2},{4,5},{5,4},{6,7},{7,6},{8,9},{9,8},{10,11... | collective-permute-start | bytes 98312 | tf_op jit(solution)/shard_map/ppermute | solution.py:252
  64.3 6.6 %collective-permute-start.28 = (f32[64,128]{1,0:T(8,128)S(1)}, f32[64,128]{1,0:T(8,128)S(1)}, u32[]{:S(2)}, u32[]{:S(2)}) collective-permute-start(f32[64,128]{1,0:T(8,128)S(1)} %add.23.refs_0_), channel_id=1, source_target_pairs={{0,24},{2,26},{4,28},{6,30},{8,16},{10,18},{12,20},{14,22},{16,8},... | collective-permute-start | bytes 98312 | tf_op jit(solution)/shard_map/ppermute | solution.py:252
  66.6 4.9 %collective-permute-start.27 = (f32[64,128]{1,0:T(8,128)S(1)}, f32[64,128]{1,0:T(8,128)S(1)}, u32[]{:S(2)}, u32[]{:S(2)}) collective-permute-start(f32[64,128]{1,0:T(8,128)S(1)} %add.23.refs_0_), channel_id=1, source_target_pairs={{0,16},{2,18},{4,20},{6,22},{8,24},{10,26},{12,28},{14,30},{16,0},... | collective-permute-start | bytes 98312 | tf_op jit(solution)/shard_map/ppermute | solution.py:252
  67.2 4.3 %collective-permute-start.26 = (f32[64,128]{1,0:T(8,128)S(1)}, f32[64,128]{1,0:T(8,128)S(1)}, u32[]{:S(2)}, u32[]{:S(2)}) collective-permute-start(f32[64,128]{1,0:T(8,128)S(1)} %add.23.refs_0_), channel_id=1, source_target_pairs={{0,8},{2,10},{4,12},{6,14},{8,0},{10,2},{12,4},{14,6},{16,24},{18,... | collective-permute-start | bytes 98312 | tf_op jit(solution)/shard_map/ppermute | solution.py:252
  71.8 5.3 %collective-permute-start.31 = (bf16[256,128]{1,0:T(8,128)(2,1)S(1)}, bf16[256,128]{1,0:T(8,128)(2,1)S(1)}, u32[]{:S(2)}, u32[]{:S(2)}) collective-permute-start(bf16[256,128]{1,0:T(8,128)(2,1)S(1)} %get-tuple-element.127.refs_0_), channel_id=1, source_target_pairs={{0,6},{2,4},{4,2},{6,0},{8,14},{10,12},{12,10},{14,8},{16,22},{18,... | collective-permute-start | bytes 196616 | tf_op jit(solution)/shard_map/ppermute | solution.py:252
  73.0 4.7 %collective-permute-start.30 = (bf16[256,128]{1,0:T(8,128)(2,1)S(1)}, bf16[256,128]{1,0:T(8,128)(2,1)S(1)}, u32[]{:S(2)}, u32[]{:S(2)}) collective-permute-start(bf16[256,128]{1,0:T(8,128)(2,1)S(1)} %get-tuple-element.127.refs_0_), channel_id=1, source_target_pairs={{0,4},{2,6},{4,0},{6,2},{8,12},{10,14},{12,8},{14,10},{16,20},{18,... | collective-permute-start | bytes 196616 | tf_op jit(solution)/shard_map/ppermute | solution.py:252
  73.6 4.3 %collective-permute-start.29 = (bf16[256,128]{1,0:T(8,128)(2,1)S(1)}, bf16[256,128]{1,0:T(8,128)(2,1)S(1)}, u32[]{:S(2)}, u32[]{:S(2)}) collective-permute-start(bf16[256,128]{1,0:T(8,128)(2,1)S(1)} %get-tuple-element.127.refs_0_), channel_id=1, source_target_pairs={{0,2},{2,0},{4,6},{6,4},{8,10},{10,8},{12,14},{14,12},{16,18},{18,... | collective-permute-start | bytes 196616 | tf_op jit(solution)/shard_map/ppermute | solution.py:252
  77.9 1.7 %copy-start.1 = (f32[64,128]{1,0:T(8,128)S(1)}, f32[64,128]{1,0:T(8,128)}, u32[]{:S(2)}) copy-start(f32[64,128]{1,0:T(8,128)} %get-tuple-element.65.refs_3_) | copy-start | bytes 98308
  78.3 1.3 %collective-permute-start.32 = (f32[64,128]{1,0:T(8,128)S(1)}, f32[64,128]{1,0:T(8,128)S(1)}, u32[]{:S(2)}, u32[]{:S(2)}) collective-permute-start(f32[64,128]{1,0:T(8,128)S(1)} %shard_map.129.refs_0_), channel_id=1, source_target_pairs={{0,1},{1,0},{2,3},{3,2},{4,5},{5,4},{6,7},{7,6},{8,9},{9,8},{10,11... | collective-permute-start | bytes 98312 | tf_op jit(solution)/shard_map/ppermute | solution.py:252

commit v7 on v6

--- a/solution.py
+++ b/solution.py
@@ -13,7 +13,7 @@
 bf16 = jnp.bfloat16
 
 
-def call(kernel, outs, args, smem=(), limit=16, scratch=()):
+def call(kernel, outs, args, smem=(), limit=16):
     specs = [
         pl.BlockSpec(memory_space=pltpu.SMEM if i in smem else pltpu.VMEM) for i in range(len(args))
     ]
@@ -22,7 +22,6 @@
         out_shape=[jax.ShapeDtypeStruct(shape, kind) for shape, kind in outs],
         in_specs=specs,
         out_specs=[pl.BlockSpec(memory_space=pltpu.VMEM) for _ in outs],
-        scratch_shapes=[pltpu.VMEM(shape, kind) for shape, kind in scratch],
         compiler_params=pltpu.CompilerParams(vmem_limit_bytes=limit << 20),
     )(*args)
 
@@ -35,6 +34,11 @@
     return jnp.concatenate([high, middle, low], axis=0)
 
 
+def halves(value):
+    high = value.astype(bf16)
+    return high, (value - high.astype(f32)).astype(bf16)
+
+
 def times_stack(weights, stack):
     rows = weights.shape[0]
     parts = jnp.dot(pieces(weights), stack, preferred_element_type=f32)
@@ -72,7 +76,11 @@
 
 def product(place_ref, dense_ref, mix_ref, stack, mine_refs):
     edge = mine_refs[0].shape[-1]
-    mixed = dot_nn(mix_ref[...], jnp.dot(stack, dense_ref[...], preferred_element_type=f32))
+    vecs = mix_ref.shape[0]
+    high, low = halves(jnp.dot(stack, dense_ref[...], preferred_element_type=f32))
+    weights = jnp.concatenate(halves(mix_ref[...]), axis=0)
+    mixed = jnp.dot(weights, high, preferred_element_type=f32)
+    mixed = mixed[:vecs] + mixed[vecs:] + jnp.dot(weights[:vecs], low, preferred_element_type=f32)
     if len(mine_refs) == 2:
         first = place_ref[0] == 0
         low, high = mixed[:, :edge], mixed[:, edge:]
@@ -94,20 +102,16 @@
     product(place_ref, dense_ref, mix_ref, stack_ref[...], mine_refs)
 
 
-def residual_terms(crosses, gram_ref):
+def residual_scale(q, square):
+    return lax.rsqrt(jnp.maximum(square - jnp.sum((q * q).T, axis=1, keepdims=True), 0.0) + epsilon)
+
+
+def next_kernel(place_ref, dense_ref, mix_ref, crosses, basis_ref, wide_ref, dirs_ref, stack_ref, *mine_refs):
+    vecs = wide_ref.shape[0]
     both = sum(ref[...] for ref in crosses)
-    vecs = both.shape[0]
     q = both[:, :vecs]
-    taken = q * (2.0 * q - dot_nn(gram_ref[...], q))
-    square = both[:, vecs : vecs + 1] - jnp.sum(taken.T, axis=1, keepdims=True)
-    return q, lax.rsqrt(jnp.maximum(square, 0.0) + epsilon)
-
-
-def next_kernel(place_ref, dense_ref, mix_ref, crosses, gram_ref, basis_ref, wide_ref, dirs_ref, stack_ref, *mine_refs):
-    vecs = wide_ref.shape[0]
-    q, scale = residual_terms(crosses, gram_ref)
-    high = q.astype(bf16)
-    low = (q - high.astype(f32)).astype(bf16)
+    scale = residual_scale(q, both[:, vecs : vecs + 1])
+    high, low = halves(q)
     terms = jnp.concatenate([high, high, low], axis=0)
     basis = jnp.concatenate([basis_ref[: 2 * vecs], basis_ref[:vecs]], axis=0)
     part = lax.dot_general(terms, basis, (((0,), (0,)), ((), ())), preferred_element_type=f32)
@@ -117,21 +121,13 @@
     product(place_ref, dense_ref, mix_ref, stack_ref[...], mine_refs)
 
 
-def last_kernel(crosses, gram_ref, basis_ref, own_ref, resid_ref, rayleigh_ref):
-    vecs = own_ref.shape[0]
-    q, scale = residual_terms(crosses, gram_ref)
-    resid_ref[...] = (dot_tn(q, basis_ref[...]) - own_ref[...]) * scale
-    row_ids = lax.broadcasted_iota(jnp.int32, (vecs, vecs), 0)
-    lane_ids = lax.broadcasted_iota(jnp.int32, (vecs, vecs), 1)
-    rayleigh_ref[...] = jnp.where(row_ids == lane_ids, 1.0, 0.0) - q
-
-
-def gram_kernel(stack_ref, mix_ref, search_ref, pack_ref, search_out):
-    wide = search_out.shape[1]
-    vecs = mix_ref.shape[0]
+def gram_kernel(stack_ref, mix_ref, search_ref, pack_ref, search_out, *own_rotated):
+    vecs, edge = mix_ref.shape[0], search_out.shape[1]
     rotated = times_stack(mix_ref[...], stack_ref[...])
     search = times_stack(search_ref[...], stack_ref[vecs:])
-    search_out[...] = search
+    search_out[...] = search[:, :edge]
+    if own_rotated:
+        own_rotated[0][...] = rotated[:, :edge]
     square = jnp.sum(search * search, axis=1, keepdims=True)
     pack_ref[...] = jnp.concatenate(
         [dot_nt(rotated, rotated), jnp.broadcast_to(square, (vecs, vecs))], axis=1
@@ -206,25 +202,41 @@
     inverse_ref[...] = jnp.concatenate(done, axis=0)[:, vecs:]
 
 
-def basis_kernel(nodes, packs, inverse_ref, scale_ref, stack_ref, mix_ref, search_ref, basis_ref, gram_ref, dirs_ref, *own_basis):
+def basis_kernel(inverse_ref, scale_ref, stack_ref, mix_ref, search_ref, basis_ref, dirs_ref):
     vecs = mix_ref.shape[0]
+    dirs_ref[...] = (search_ref[...] * scale_ref[:, vecs : vecs + 1]).astype(bf16)
+    basis = times_stack(dot_nn(inverse_ref[...], mix_ref[...]), stack_ref[...])
+    basis_ref[...] = pieces(basis)
+
+
+def terms_kernel(rotated_ref, adj_ref, terms_ref):
+    adj = adj_ref[...]
+    terms_ref[...] = jnp.concatenate([dot_nt(rotated_ref[...], adj), dot_nt(adj, adj)], axis=1)
+
+
+def own_kernel(inverse_ref, scale_ref, rotated_ref, search_ref, basis_ref, dirs_ref):
+    vecs = inverse_ref.shape[0]
+    basis_ref[...] = dot_nn(inverse_ref[...], rotated_ref[...])
+    dirs_ref[...] = search_ref[...] * scale_ref[:, vecs : vecs + 1]
+
+
+def last_kernel(nodes, terms, inverse_ref, rotated_ref, adj_ref, resid_ref, rayleigh_ref):
+    vecs = inverse_ref.shape[0]
     inverse = inverse_ref[...]
-    total = sum(ref[...] for ref in packs)[:, :vecs] / nodes
-    gram_ref[...] = dot_nt(dot_nn(inverse, total), inverse)
-    edge = dirs_ref.shape[1]
-    dirs_ref[...] = (search_ref[:, :edge] * scale_ref[:, vecs : vecs + 1]).astype(dirs_ref.dtype)
-    basis = times_stack(dot_nn(inverse, mix_ref[...]), stack_ref[...])
-    basis_ref[...] = pieces(basis)
-    if own_basis:
-        own_basis[0][...] = basis[:, :edge]
+    total = sum(ref[...] for ref in terms) / nodes
+    q = dot_nt(dot_nn(inverse, total[:, :vecs]), inverse)
+    square = jnp.sum(dot_nn(inverse, total[:, vecs:]) * inverse, axis=1, keepdims=True)
+    raw = dot_nn(dot_tn(q, inverse), rotated_ref[...]) - dot_nn(inverse, adj_ref[...])
+    resid_ref[...] = raw * residual_scale(q, square)
+    row_ids = lax.broadcasted_iota(jnp.int32, (vecs, vecs), 0)
+    lane_ids = lax.broadcasted_iota(jnp.int32, (vecs, vecs), 1)
+    rayleigh_ref[...] = jnp.where(row_ids == lane_ids, 1.0, 0.0) - q
 
 
 def solve_kernel(parts, *refs):
-    part_refs, inverse_ref, blocks_ref, own_ref = refs[:parts], refs[parts], refs[parts + 1], refs[parts + 2 :]
+    part_refs, inverse_ref, blocks_ref = refs[:parts], refs[parts], refs[parts + 1]
     vecs, edge = part_refs[0].shape
     solved = dot_nn(inverse_ref[...], jnp.concatenate([ref[...] for ref in part_refs], axis=1))
-    if own_ref:
-        own_ref[0][...] = solved[:, :edge]
     for i in range(parts):
         blocks_ref[i * vecs : (i + 1) * vecs, :] = solved[:, i * edge : (i + 1) * edge].astype(bf16)
 
@@ -319,7 +331,7 @@
                 limit=limit,
             )
         else:
-            crosses, gram, basis, wide_adj, dirs = state
+            crosses, basis, wide_adj, dirs = state
             count = len(crosses)
 
             def kernel(p, t, m, *refs):
@@ -328,13 +340,14 @@
             stack, *mine = call(
                 kernel,
                 [stack_out] + mine_outs,
-                [place, dense, mixing] + crosses + [gram, basis] + wide_adj + [dirs],
+                [place, dense, mixing] + crosses + [basis, wide_adj, dirs],
                 smem=(0,),
                 limit=limit,
             )
-        pack, search = call(
+        own_out = ((vecs, edge), f32)
+        pack, search, *rotated = call(
             gram_kernel,
-            [((vecs, 2 * vecs), f32), ((vecs, wide), f32)],
+            [((vecs, 2 * vecs), f32)] + ([own_out, own_out] if last else [((vecs, wide), f32)]),
             [stack, mixing, ritz_search[sweep]],
             limit=limit,
         )
@@ -353,51 +366,45 @@
         inverse, scale = call(
             kernel_factor, [((vecs, vecs), f32), ((vecs, 2 * vecs), f32)], packs
         )
+        if last:
+            break
         far_parts = far_values(rotated_adj, near)
         far_parts, inverse = lax.optimization_barrier((far_parts, inverse))
-        held, *own_adj = call(
+        held, = call(
             functools.partial(solve_kernel, len(far_parts)),
-            [((len(far_parts) * vecs, edge), bf16)] + [((vecs, edge), f32)] * last,
+            [((len(far_parts) * vecs, edge), bf16)],
             far_parts + [inverse],
             limit=limit,
         )
         adj_parts = near_values(held, near)
-
-        def kernel_basis(*refs):
-            basis_kernel(nodes, refs[:pack_count], *refs[pack_count:])
-
-        basis, gram, dirs, *own_basis = call(
-            kernel_basis,
-            [
-                ((3 * vecs, wide), bf16),
-                ((vecs, vecs), f32),
-                ((vecs, edge), f32) if last else ((vecs, wide), bf16),
-            ]
-            + [((vecs, edge), f32)] * last,
-            packs + [inverse, scale, stack, mixing, search],
+        basis, dirs = call(
+            basis_kernel,
+            [((3 * vecs, wide), bf16), ((vecs, wide), bf16)],
+            [inverse, scale, stack, mixing, search],
             limit=limit,
         )
-        wide_out = [((vecs, wide), bf16)]
-        cross, *wide_adj = call(
+        cross, wide_adj = call(
             functools.partial(cross_kernel, nodes, near),
-            [((vecs, 2 * vecs), f32)] + ([] if last else wide_out),
+            [((vecs, 2 * vecs), f32), ((vecs, wide), bf16)],
             adj_parts + [basis],
             limit=limit,
-            scratch=wide_out if last else [],
         )
-        crosses = panel_terms(cross)
-        state = (crosses, gram, basis, wide_adj, dirs)
-    count = len(crosses)
+        state = (panel_terms(cross), basis, wide_adj, dirs)
+
+    rotated = rotated[0]
+    terms, = call(terms_kernel, [((vecs, 2 * vecs), f32)], [rotated, rotated_adj])
+    far_parts, inverse = lax.optimization_barrier((far_values(terms, near), inverse))
+    own_basis, own_dirs = call(own_kernel, [own_out, own_out], [inverse, scale, rotated, search])
+    terms = panel_terms(sum(near_values(sum(far_parts), near)))
+    count = len(terms)
 
     def kernel_last(*refs):
-        last_kernel(refs[:count], *refs[count:])
+        last_kernel(nodes, refs[:count], *refs[count:])
 
     resid, rayleigh = call(
-        kernel_last,
-        [((vecs, edge), f32), ((vecs, vecs), f32)],
-        crosses + [gram] + own_basis + own_adj,
-    )
-    return (own_basis[0], resid, dirs, rayleigh)
+        kernel_last, [own_out, ((vecs, vecs), f32)], terms + [inverse, rotated, rotated_adj]
+    )
+    return (own_basis, resid, own_dirs, rayleigh)
 
 
 def solution(mesh):

time: 80.8 us -> 80 us (0.990)
    pallas_call x20 -> x19, Pallas kernels: 19.8 us -> 19.1 us  [call(): pl.pallas_call(kernel, out_shape=[jax.ShapeDtypeStruct(shape, kind) for s...]
    unnamed x12 -> x10, local copies, waits for them, and re-layouts: 1.98 us -> 2.12 us
  transfers between devices with their start and end apart: 33 -> 33, of which waited for: 20 -> 20; matrix products, arithmetic and copies ran while one was open for 0% -> 0% of each run, Pallas kernels for 17% -> 18%
where the time goes in v7:
time: 80 us; the launch traced here: 80.1 us
  starting transfers between devices  35 us (44%)
  waiting for transfers between devices  22.1 us (28%)
  Pallas kernels  19.1 us (24%)
  local copies, waits for them, and re-layouts  2.14 us (3%)
  other arithmetic  0.89 us (1%)
  between operations  0.86 us (1%)
    ppermute x33, starting transfers between devices, swap(): return lax.ppermute(value, axis, [(i, i ^ by) for i in range(size)])  35 us
    ppermute x33, waiting for transfers between devices, swap(): return lax.ppermute(value, axis, [(i, i ^ by) for i in range(size)])  22.1 us
    pallas_call x19, Pallas kernels, call(): pl.pallas_call(kernel, out_shape=[jax.ShapeDtypeStruct(shape, kind) for s...  19.1 us
    unnamed x10, local copies, waits for them, and re-layouts  2.12 us
  transfers between devices with their start and end apart: 33, of which 20 were waited for; matrix products, arithmetic and copies ran while one was open for 0% of the time, Pallas kernels for 18%

profile of v7, /device:TPU:0, one launch (start us, length us, event | category | flops | bytes accessed | tf_op | source)
XLA Modules:
  0.0 80.1 jit_solution(15014686563144490857)
XLA Ops:
  0.6 0.8 maximum_bitcast_fusion
  1.4 5.0 %collective-permute-start.2 = (bf16[1,192,128]{2,1,0:T(8,128)(2,1)S(1)}, bf16[1,192,128]{2,1,0:T(8,128)(2,1)S(1)}, u32[]{:S(2)}, u32[]{:S(2)}) collective-permute-start(bf16[1,192,128]{2,1,0:T(8,128)(2,1)S(1)} %maximum_bitcast_fusion), channel_id=1, source_target_pairs={{0,24},{2,26},{4,28},{6,30},{8,16},{10,18},{12,20},{14,22},{16,8},... | collective-permute-start | bytes 147464 | tf_op jit(solution)/shard_map/ppermute | solution.py:264
  6.4 0.6 collective-permute-start
  7.1 0.7 copy-done.3
  7.8 1.2 %copy-done = bf16[1,1,2,16,128,128]{5,4,3,2,1,0:T(8,128)(2,1)S(1)} copy-done((bf16[1,1,2,16,128,128]{5,4,3,2,1,0:T(8,128)(2,1)S(1)}, bf16[1,1,2,16,128,128]{5,4,3,2,1,0:T(8,128)(2,1)}, u32[]{:S(2)}) %copy-start) | copy-done | bytes 1048600
  9.0 1.9 %shard_map.111.dense_ref.t = bf16[2048,256]{1,0:T(8,128)(2,1)S(1)} custom-call(s32[2,16]{1,0:T(2,128)S(1)} %compare_select_fusion.slots_ref, bf16[2,16,128,128]{3,2,1,0:T(8,128)(2,1)S(1)} %bitcast.25), custom_call_target="tpu_custom_call" | custom-call | tf_op jit(solution)/shard_map/pallas_call | solution.py:20
  10.9 0.5 collective-permute-done.1
  11.5 2.5 %collective-permute-start.5 = (bf16[4,192,128]{2,1,0:T(8,128)(2,1)S(1)}, bf16[4,192,128]{2,1,0:T(8,128)(2,1)S(1)}, u32[]{:S(2)}, u32[]{:S(2)}) collective-permute-start(bf16[4,192,128]{2,1,0:T(8,128)(2,1)S(1)} %pad_maximum_fusion.refs_0_), channel_id=1, source_target_pairs={{0,6},{2,4},{4,2},{6,0},{8,14},{10,12},{12,10},{14,8},{16,22},{18,... | collective-permute-start | bytes 589832 | tf_op jit(solution)/shard_map/ppermute | solution.py:264
  14.0 0.5 collective-permute-start.4
  14.5 0.5 collective-permute-start.3
  15.0 4.9 %collective-permute-done.5.refs_3_ = bf16[4,192,128]{2,1,0:T(8,128)(2,1)S(1)} collective-permute-done((bf16[4,192,128]{2,1,0:T(8,128)(2,1)S(1)}, bf16[4,192,128]{2,1,0:T(8,128)(2,1)S(1)}, u32[]{:S(2)}, u32[]{:S(2)}) %collective-permute-start.5) | collective-permute-done | bytes 196640 | tf_op jit(solution)/shard_map/ppermute | solution.py:264
  19.9 2.5 %collective-permute-done.4.refs_2_ = bf16[4,192,128]{2,1,0:T(8,128)(2,1)S(1)} collective-permute-done((bf16[4,192,128]{2,1,0:T(8,128)(2,1)S(1)}, bf16[4,192,128]{2,1,0:T(8,128)(2,1)S(1)}, u32[]{:S(2)}, u32[]{:S(2)}) %collective-permute-start.4) | collective-permute-done | bytes 196640 | tf_op jit(solution)/shard_map/ppermute | solution.py:264
  22.5 0.6 shard_map.112
  23.4 1.1 %shard_map.113 = (f32[64,128]{1,0:T(8,128)S(1)}, f32[64,2048]{1,0:T(8,128)S(1)}) custom-call(bf16[192,2048]{1,0:T(8,128)(2,1)S(1)} %get-tuple-element.71.stack_ref, f32[64,192]{1,0:T(8,128)S(1)} %get-tuple-element.124.mix_ref, f32[64,128]{1,0:T(8,128)S(1)} %get-tuple-element.128.search_ref), custom_call_target="tpu_custom_call" | custom-call | tf_op jit(solution)/shard_map/pallas_call | solution.py:20
  24.5 0.4 collective-permute-start.10
  24.9 3.2 %collective-permute-start.9 = (f32[64,128]{1,0:T(8,128)S(1)}, f32[64,128]{1,0:T(8,128)S(1)}, u32[]{:S(2)}, u32[]{:S(2)}) collective-permute-start(f32[64,128]{1,0:T(8,128)S(1)} %add.39.refs_0_), channel_id=1, source_target_pairs={{0,24},{2,26},{4,28},{6,30},{8,16},{10,18},{12,20},{14,22},{16,8},... | collective-permute-start | bytes 98312 | tf_op jit(solution)/shard_map/ppermute | solution.py:264
  28.2 0.4 collective-permute-start.8
  28.6 0.7 collective-permute-start.7
  29.3 2.2 %shard_map.114 = (f32[64,64]{1,0:T(8,128)S(1)}, f32[64,128]{1,0:T(8,128)S(1)}) custom-call(f32[64,128]{1,0:T(8,128)S(1)} %get-tuple-element.74.refs_0_, f32[64,128]{1,0:T(8,128)S(1)} %collective-permute-done.10.refs_1_), custom_call_target="tpu_custom_call" | custom-call | tf_op jit(solution)/shard_map/pallas_call | solution.py:20
  31.5 1.5 %collective-permute-done.8.refs_2_ = f32[64,128]{1,0:T(8,128)S(1)} collective-permute-done((f32[64,128]{1,0:T(8,128)S(1)}, f32[64,128]{1,0:T(8,128)S(1)}, u32[]{:S(2)}, u32[]{:S(2)}) %collective-permute-start.8) | collective-permute-done | bytes 32800 | tf_op jit(solution)/shard_map/ppermute | solution.py:264
  33.0 0.3 shard_map.115.refs_0_
  33.2 1.9 %collective-permute-start.13 = (bf16[256,128]{1,0:T(8,128)(2,1)S(1)}, bf16[256,128]{1,0:T(8,128)(2,1)S(1)}, u32[]{:S(2)}, u32[]{:S(2)}) collective-permute-start(bf16[256,128]{1,0:T(8,128)(2,1)S(1)} %shard_map.115.refs_0_), channel_id=1, source_target_pairs={{0,6},{2,4},{4,2},{6,0},{8,14},{10,12},{12,10},{14,8},{16,22},{18,... | collective-permute-start | bytes 196616 | tf_op jit(solution)/shard_map/ppermute | solution.py:264
  35.1 1.4 %collective-permute-start.12 = (bf16[256,128]{1,0:T(8,128)(2,1)S(1)}, bf16[256,128]{1,0:T(8,128)(2,1)S(1)}, u32[]{:S(2)}, u32[]{:S(2)}) collective-permute-start(bf16[256,128]{1,0:T(8,128)(2,1)S(1)} %shard_map.115.refs_0_), channel_id=1, source_target_pairs={{0,4},{2,6},{4,0},{6,2},{8,12},{10,14},{12,8},{14,10},{16,20},{18,... | collective-permute-start | bytes 196616 | tf_op jit(solution)/shard_map/ppermute | solution.py:264
  36.5 0.2 collective-permute-start.11
  36.8 0.6 shard_map.116
  37.4 1.4 %collective-permute-done.13.refs_3_ = bf16[256,128]{1,0:T(8,128)(2,1)S(1)} collective-permute-done((bf16[256,128]{1,0:T(8,128)(2,1)S(1)}, bf16[256,128]{1,0:T(8,128)(2,1)S(1)}, u32[]{:S(2)}, u32[]{:S(2)}) %collective-permute-start.13) | collective-permute-done | bytes 65568 | tf_op jit(solution)/shard_map/ppermute | solution.py:264
  38.8 0.7 collective-permute-done.12.refs_2_
  39.5 1.3 %collective-permute-done.11.refs_1_ = bf16[256,128]{1,0:T(8,128)(2,1)S(1)} collective-permute-done((bf16[256,128]{1,0:T(8,128)(2,1)S(1)}, bf16[256,128]{1,0:T(8,128)(2,1)S(1)}, u32[]{:S(2)}, u32[]{:S(2)}) %collective-permute-start.11) | collective-permute-done | bytes 65568 | tf_op jit(solution)/shard_map/ppermute | solution.py:264
  40.8 0.4 shard_map.117
  41.3 1.2 %collective-permute-done.14.refs_1_ = f32[64,128]{1,0:T(8,128)S(1)} collective-permute-done((f32[64,128]{1,0:T(8,128)S(1)}, f32[64,128]{1,0:T(8,128)S(1)}, u32[]{:S(2)}, u32[]{:S(2)}) %collective-permute-start.14) | collective-permute-done | bytes 32800 | tf_op jit(solution)/shard_map/ppermute | solution.py:264
  42.5 0.9 %shard_map.118 = (bf16[192,2048]{1,0:T(8,128)(2,1)S(1)}, f32[64,128]{1,0:T(8,128)S(1)}, f32[64,128]{1,0:T(8,128)S(1)}) custom-call(s32[1]{0:T(128)} %bitcast.place_ref.p, bf16[2048,256]{1,0:T(8,128)(2,1)S(1)} %shard_map.111.dense_ref.t, f32[64,192]{1,0:T(8,128)S(1)} %get-tuple-element.126.m.mix_ref, f32[64,128]{1,0:T(8,128)S(1)} %get-tuple-element.84.refs_0_, ...), custom_call_target="tpu_custom_call" | custom-call | tf_op jit(solution)/shard_map/pallas_call | solution.py:20
  43.6 1.1 %shard_map.119 = (f32[64,128]{1,0:T(8,128)S(1)}, f32[64,2048]{1,0:T(8,128)S(1)}) custom-call(bf16[192,2048]{1,0:T(8,128)(2,1)S(1)} %get-tuple-element.89.stack_ref, f32[64,192]{1,0:T(8,128)S(1)} %get-tuple-element.126.m.mix_ref, f32[64,128]{1,0:T(8,128)S(1)} %get-tuple-element.129.search_ref), custom_call_target="tpu_custom_call" | custom-call | tf_op jit(solution)/shard_map/pallas_call | solution.py:20
  44.7 0.4 collective-permute-start.19
  45.1 1.8 %collective-permute-start.18 = (f32[64,128]{1,0:T(8,128)S(1)}, f32[64,128]{1,0:T(8,128)S(1)}, u32[]{:S(2)}, u32[]{:S(2)}) collective-permute-start(f32[64,128]{1,0:T(8,128)S(1)} %add.40.refs_0_), channel_id=1, source_target_pairs={{0,24},{2,26},{4,28},{6,30},{8,16},{10,18},{12,20},{14,22},{16,8},... | collective-permute-start | bytes 98312 | tf_op jit(solution)/shard_map/ppermute | solution.py:264
  46.9 0.3 collective-permute-start.17
  47.2 2.3 %collective-permute-start.16 = (f32[64,128]{1,0:T(8,128)S(1)}, f32[64,128]{1,0:T(8,128)S(1)}, u32[]{:S(2)}, u32[]{:S(2)}) collective-permute-start(f32[64,128]{1,0:T(8,128)S(1)} %add.40.refs_0_), channel_id=1, source_target_pairs={{0,8},{2,10},{4,12},{6,14},{8,0},{10,2},{12,4},{14,6},{16,24},{18,... | collective-permute-start | bytes 98312 | tf_op jit(solution)/shard_map/ppermute | solution.py:264
  49.5 2.2 %shard_map.120 = (f32[64,64]{1,0:T(8,128)S(1)}, f32[64,128]{1,0:T(8,128)S(1)}) custom-call(f32[64,128]{1,0:T(8,128)S(1)} %get-tuple-element.92.refs_0_, f32[64,128]{1,0:T(8,128)S(1)} %collective-permute-done.19.refs_1_), custom_call_target="tpu_custom_call" | custom-call | tf_op jit(solution)/shard_map/pallas_call | solution.py:20
  51.9 0.3 shard_map.121.refs_0_
  52.2 0.9 %collective-permute-start.22 = (bf16[256,128]{1,0:T(8,128)(2,1)S(1)}, bf16[256,128]{1,0:T(8,128)(2,1)S(1)}, u32[]{:S(2)}, u32[]{:S(2)}) collective-permute-start(bf16[256,128]{1,0:T(8,128)(2,1)S(1)} %shard_map.121.refs_0_), channel_id=1, source_target_pairs={{0,6},{2,4},{4,2},{6,0},{8,14},{10,12},{12,10},{14,8},{16,22},{18,... | collective-permute-start | bytes 196616 | tf_op jit(solution)/shard_map/ppermute | solution.py:264
  53.0 0.9 %collective-permute-start.21 = (bf16[256,128]{1,0:T(8,128)(2,1)S(1)}, bf16[256,128]{1,0:T(8,128)(2,1)S(1)}, u32[]{:S(2)}, u32[]{:S(2)}) collective-permute-start(bf16[256,128]{1,0:T(8,128)(2,1)S(1)} %shard_map.121.refs_0_), channel_id=1, source_target_pairs={{0,4},{2,6},{4,0},{6,2},{8,12},{10,14},{12,8},{14,10},{16,20},{18,... | collective-permute-start | bytes 196616 | tf_op jit(solution)/shard_map/ppermute | solution.py:264
  54.0 1.8 %collective-permute-start.20 = (bf16[256,128]{1,0:T(8,128)(2,1)S(1)}, bf16[256,128]{1,0:T(8,128)(2,1)S(1)}, u32[]{:S(2)}, u32[]{:S(2)}) collective-permute-start(bf16[256,128]{1,0:T(8,128)(2,1)S(1)} %shard_map.121.refs_0_), channel_id=1, source_target_pairs={{0,2},{2,0},{4,6},{6,4},{8,10},{10,8},{12,14},{14,12},{16,18},{18,... | collective-permute-start | bytes 196616 | tf_op jit(solution)/shard_map/ppermute | solution.py:264
  55.7 0.6 shard_map.122
  56.3 1.2 %collective-permute-done.22.refs_3_ = bf16[256,128]{1,0:T(8,128)(2,1)S(1)} collective-permute-done((bf16[256,128]{1,0:T(8,128)(2,1)S(1)}, bf16[256,128]{1,0:T(8,128)(2,1)S(1)}, u32[]{:S(2)}, u32[]{:S(2)}) %collective-permute-start.22) | collective-permute-done | bytes 65568 | tf_op jit(solution)/shard_map/ppermute | solution.py:264
  57.5 0.5 collective-permute-done.21.refs_2_
  58.2 0.4 shard_map.123
  58.7 1.2 %collective-permute-done.23.refs_1_ = f32[64,128]{1,0:T(8,128)S(1)} collective-permute-done((f32[64,128]{1,0:T(8,128)S(1)}, f32[64,128]{1,0:T(8,128)S(1)}, u32[]{:S(2)}, u32[]{:S(2)}) %collective-permute-start.23) | collective-permute-done | bytes 32800 | tf_op jit(solution)/shard_map/ppermute | solution.py:264
  59.9 0.9 %shard_map.124 = (bf16[192,2048]{1,0:T(8,128)(2,1)S(1)}, f32[64,128]{1,0:T(8,128)S(1)}, f32[64,128]{1,0:T(8,128)S(1)}) custom-call(s32[1]{0:T(128)} %bitcast.place_ref.p, bf16[2048,256]{1,0:T(8,128)(2,1)S(1)} %shard_map.111.dense_ref.t, f32[64,192]{1,0:T(8,128)S(1)} %get-tuple-element.125.m.mix_ref, f32[64,128]{1,0:T(8,128)S(1)} %get-tuple-element.102.refs_0_, ...), custom_call_target="tpu_custom_call" | custom-call | tf_op jit(solution)/shard_map/pallas_call | solution.py:20
  61.0 1.1 %shard_map.125 = (f32[64,128]{1,0:T(8,128)S(1)}, f32[64,128]{1,0:T(8,128)S(1)}, f32[64,128]{1,0:T(8,128)S(1)}) custom-call(bf16[192,2048]{1,0:T(8,128)(2,1)S(1)} %get-tuple-element.105.stack_ref, f32[64,192]{1,0:T(8,128)S(1)} %get-tuple-element.125.m.mix_ref, f32[64,128]{1,0:T(8,128)S(1)} %get-tuple-element.127.search_ref), custom_call_target="tpu_custom_call" | custom-call | tf_op jit(solution)/shard_map/pallas_call | solution.py:20
  62.1 0.4 collective-permute-start.28
  62.5 0.3 shard_map.126
  62.8 2.4 %collective-permute-start.27 = (f32[64,128]{1,0:T(8,128)S(1)}, f32[64,128]{1,0:T(8,128)S(1)}, u32[]{:S(2)}, u32[]{:S(2)}) collective-permute-start(f32[64,128]{1,0:T(8,128)S(1)} %shard_map.126), channel_id=1, source_target_pairs={{0,24},{2,26},{4,28},{6,30},{8,16},{10,18},{12,20},{14,22},{16,8},... | collective-permute-start | bytes 98312 | tf_op jit(solution)/shard_map/ppermute | solution.py:264
  65.3 0.6 collective-permute-start.26
  65.9 1.4 %collective-permute-start.25 = (f32[64,128]{1,0:T(8,128)S(1)}, f32[64,128]{1,0:T(8,128)S(1)}, u32[]{:S(2)}, u32[]{:S(2)}) collective-permute-start(f32[64,128]{1,0:T(8,128)S(1)} %shard_map.126), channel_id=1, source_target_pairs={{0,8},{2,10},{4,12},{6,14},{8,0},{10,2},{12,4},{14,6},{16,24},{18,... | collective-permute-start | bytes 98312 | tf_op jit(solution)/shard_map/ppermute | solution.py:264
  67.3 2.2 %shard_map.127 = (f32[64,64]{1,0:T(8,128)S(1)}, f32[64,128]{1,0:T(8,128)S(1)}) custom-call(f32[64,128]{1,0:T(8,128)S(1)} %get-tuple-element.111.refs_0_, f32[64,128]{1,0:T(8,128)S(1)} %collective-permute-done.28.refs_1_), custom_call_target="tpu_custom_call" | custom-call | tf_op jit(solution)/shard_map/pallas_call | solution.py:20
  69.5 0.7 collective-permute-done.26
  70.2 1.9 %collective-permute-start.31 = (f32[64,128]{1,0:T(8,128)S(1)}, f32[64,128]{1,0:T(8,128)S(1)}, u32[]{:S(2)}, u32[]{:S(2)}) collective-permute-start(f32[64,128]{1,0:T(8,128)S(1)} %add_add_fusion.1), channel_id=1, source_target_pairs={{0,6},{2,4},{4,2},{6,0},{8,14},{10,12},{12,10},{14,8},{16,22},{18,... | collective-permute-start | bytes 98312 | tf_op jit(solution)/shard_map/ppermute | solution.py:264
  72.0 1.4 %collective-permute-start.30 = (f32[64,128]{1,0:T(8,128)S(1)}, f32[64,128]{1,0:T(8,128)S(1)}, u32[]{:S(2)}, u32[]{:S(2)}) collective-permute-start(f32[64,128]{1,0:T(8,128)S(1)} %add_add_fusion.1), channel_id=1, source_target_pairs={{0,4},{2,6},{4,0},{6,2},{8,12},{10,14},{12,8},{14,10},{16,20},{18,... | collective-permute-start | bytes 98312 | tf_op jit(solution)/shard_map/ppermute | solution.py:264
  73.5 0.2 collective-permute-start.29
  73.7 1.4 %collective-permute-done.31 = f32[64,128]{1,0:T(8,128)S(1)} collective-permute-done((f32[64,128]{1,0:T(8,128)S(1)}, f32[64,128]{1,0:T(8,128)S(1)}, u32[]{:S(2)}, u32[]{:S(2)}) %collective-permute-start.31) | collective-permute-done | bytes 32800 | tf_op jit(solution)/shard_map/ppermute | solution.py:264
  75.1 0.9 %collective-permute-done.30 = f32[64,128]{1,0:T(8,128)S(1)} collective-permute-done((f32[64,128]{1,0:T(8,128)S(1)}, f32[64,128]{1,0:T(8,128)S(1)}, u32[]{:S(2)}, u32[]{:S(2)}) %collective-permute-start.30) | collective-permute-done | bytes 32800 | tf_op jit(solution)/shard_map/ppermute | solution.py:264
  76.0 1.4 %collective-permute-done.29 = f32[64,128]{1,0:T(8,128)S(1)} collective-permute-done((f32[64,128]{1,0:T(8,128)S(1)}, f32[64,128]{1,0:T(8,128)S(1)}, u32[]{:S(2)}, u32[]{:S(2)}) %collective-permute-start.29) | collective-permute-done | bytes 32800 | tf_op jit(solution)/shard_map/ppermute | solution.py:264
  77.5 0.8 shard_map.128
  78.3 0.4 collective-permute-done.32.refs_1_
  78.7 1.4 %shard_map.129 = (f32[64,128]{1,0:T(8,128)}, f32[64,64]{1,0:T(8,128)}) custom-call(f32[64,128]{1,0:T(8,128)S(1)} %add_add_fusion.refs_0_, f32[64,128]{1,0:T(8,128)S(1)} %collective-permute-done.32.refs_1_, f32[64,64]{1,0:T(8,128)S(1)} %get-tuple-element.113.inverse_ref.refs_2_, f32[64,128]{1,0:T(8,128)S(1)} %get-tuple-element.106.rotated_ref.refs_3_, ...), custom_call_target="tpu_custom_call" | custom-call | tf_op jit(solution)/shard_map/pallas_call | solution.py:20
  (41 shorter events, 1.7 us)
Async XLA Ops:
  1.4 9.5 %collective-permute-start.2 = (bf16[1,192,128]{2,1,0:T(8,128)(2,1)S(1)}, bf16[1,192,128]{2,1,0:T(8,128)(2,1)S(1)}, u32[]{:S(2)}, u32[]{:S(2)}) collective-permute-start(bf16[1,192,128]{2,1,0:T(8,128)(2,1)S(1)} %maximum_bitcast_fusion), channel_id=1, source_target_pairs={{0,24},{2,26},{4,28},{6,30},{8,16},{10,18},{12,20},{14,22},{16,8},... | collective-permute-start | bytes 147464 | tf_op jit(solution)/shard_map/ppermute | solution.py:264
  6.4 5.0 %collective-permute-start.1 = (bf16[1,192,128]{2,1,0:T(8,128)(2,1)S(1)}, bf16[1,192,128]{2,1,0:T(8,128)(2,1)S(1)}, u32[]{:S(2)}, u32[]{:S(2)}) collective-permute-start(bf16[1,192,128]{2,1,0:T(8,128)(2,1)S(1)} %maximum_bitcast_fusion), channel_id=1, source_target_pairs={{0,16},{2,18},{4,20},{6,22},{8,24},{10,26},{12,28},{14,30},{16,0},... | collective-permute-start | bytes 147464 | tf_op jit(solution)/shard_map/ppermute | solution.py:264
  6.4 5.0 %collective-permute-start = (bf16[1,192,128]{2,1,0:T(8,128)(2,1)S(1)}, bf16[1,192,128]{2,1,0:T(8,128)(2,1)S(1)}, u32[]{:S(2)}, u32[]{:S(2)}) collective-permute-start(bf16[1,192,128]{2,1,0:T(8,128)(2,1)S(1)} %maximum_bitcast_fusion), channel_id=1, source_target_pairs={{0,8},{2,10},{4,12},{6,14},{8,0},{10,2},{12,4},{14,6},{16,24},{18,... | collective-permute-start | bytes 147464 | tf_op jit(solution)/shard_map/ppermute | solution.py:264
  7.0 0.7 copy-start.3
  7.1 0.7 copy-start.4
  7.8 1.2 %copy-start = (bf16[1,1,2,16,128,128]{5,4,3,2,1,0:T(8,128)(2,1)S(1)}, bf16[1,1,2,16,128,128]{5,4,3,2,1,0:T(8,128)(2,1)}, u32[]{:S(2)}) copy-start(bf16[1,1,2,16,128,128]{5,4,3,2,1,0:T(8,128)(2,1)} %param.8) | copy-start | bytes 3145732
  10.9 4.1 %copy-start.1 = (f32[3,64,192]{2,1,0:T(8,128)S(1)}, f32[3,64,192]{2,1,0:T(8,128)}, u32[]{:S(2)}) copy-start(f32[3,64,192]{2,1,0:T(8,128)} %param.14) | copy-start | bytes 442372
  11.5 8.5 %collective-permute-start.5 = (bf16[4,192,128]{2,1,0:T(8,128)(2,1)S(1)}, bf16[4,192,128]{2,1,0:T(8,128)(2,1)S(1)}, u32[]{:S(2)}, u32[]{:S(2)}) collective-permute-start(bf16[4,192,128]{2,1,0:T(8,128)(2,1)S(1)} %pad_maximum_fusion.refs_0_), channel_id=1, source_target_pairs={{0,6},{2,4},{4,2},{6,0},{8,14},{10,12},{12,10},{14,8},{16,22},{18,... | collective-permute-start | bytes 589832 | tf_op jit(solution)/shard_map/ppermute | solution.py:264
  14.0 8.4 %collective-permute-start.4 = (bf16[4,192,128]{2,1,0:T(8,128)(2,1)S(1)}, bf16[4,192,128]{2,1,0:T(8,128)(2,1)S(1)}, u32[]{:S(2)}, u32[]{:S(2)}) collective-permute-start(bf16[4,192,128]{2,1,0:T(8,128)(2,1)S(1)} %pad_maximum_fusion.refs_0_), channel_id=1, source_target_pairs={{0,4},{2,6},{4,0},{6,2},{8,12},{10,14},{12,8},{14,10},{16,20},{18,... | collective-permute-start | bytes 589832 | tf_op jit(solution)/shard_map/ppermute | solution.py:264
  14.5 8.0 %collective-permute-start.3 = (bf16[4,192,128]{2,1,0:T(8,128)(2,1)S(1)}, bf16[4,192,128]{2,1,0:T(8,128)(2,1)S(1)}, u32[]{:S(2)}, u32[]{:S(2)}) collective-permute-start(bf16[4,192,128]{2,1,0:T(8,128)(2,1)S(1)} %pad_maximum_fusion.refs_0_), channel_id=1, source_target_pairs={{0,2},{2,0},{4,6},{6,4},{8,10},{10,8},{12,14},{14,12},{16,18},{18,... | collective-permute-start | bytes 589832 | tf_op jit(solution)/shard_map/ppermute | solution.py:264
  22.5 0.9 %copy-start.2 = (f32[3,64,128]{2,1,0:T(8,128)S(1)}, f32[3,64,128]{2,1,0:T(8,128)}, u32[]{:S(2)}) copy-start(f32[3,64,128]{2,1,0:T(8,128)} %param.15) | copy-start | bytes 294916
  23.1 1.4 %collective-permute-start.6 = (f32[64,128]{1,0:T(8,128)S(1)}, f32[64,128]{1,0:T(8,128)S(1)}, u32[]{:S(2)}, u32[]{:S(2)}) collective-permute-start(f32[64,128]{1,0:T(8,128)S(1)} %get-tuple-element.70), channel_id=1, source_target_pairs={{0,1},{1,0},{2,3},{3,2},{4,5},{5,4},{6,7},{7,6},{8,9},{9,8},{10,11... | collective-permute-start | bytes 98312 | tf_op jit(solution)/shard_map/ppermute | solution.py:264
  24.5 4.8 %collective-permute-start.10 = (f32[64,128]{1,0:T(8,128)S(1)}, f32[64,128]{1,0:T(8,128)S(1)}, u32[]{:S(2)}, u32[]{:S(2)}) collective-permute-start(f32[64,128]{1,0:T(8,128)S(1)} %get-tuple-element.74.refs_0_), channel_id=1, source_target_pairs={{0,1},{1,0},{2,3},{3,2},{4,5},{5,4},{6,7},{7,6},{8,9},{9,8},{10,11... | collective-permute-start | bytes 98312 | tf_op jit(solution)/shard_map/ppermute | solution.py:264
  24.9 6.6 %collective-permute-start.9 = (f32[64,128]{1,0:T(8,128)S(1)}, f32[64,128]{1,0:T(8,128)S(1)}, u32[]{:S(2)}, u32[]{:S(2)}) collective-permute-start(f32[64,128]{1,0:T(8,128)S(1)} %add.39.refs_0_), channel_id=1, source_target_pairs={{0,24},{2,26},{4,28},{6,30},{8,16},{10,18},{12,20},{14,22},{16,8},... | collective-permute-start | bytes 98312 | tf_op jit(solution)/shard_map/ppermute | solution.py:264
  28.2 4.8 %collective-permute-start.8 = (f32[64,128]{1,0:T(8,128)S(1)}, f32[64,128]{1,0:T(8,128)S(1)}, u32[]{:S(2)}, u32[]{:S(2)}) collective-permute-start(f32[64,128]{1,0:T(8,128)S(1)} %add.39.refs_0_), channel_id=1, source_target_pairs={{0,16},{2,18},{4,20},{6,22},{8,24},{10,26},{12,28},{14,30},{16,0},... | collective-permute-start | bytes 98312 | tf_op jit(solution)/shard_map/ppermute | solution.py:264
  28.6 4.4 %collective-permute-start.7 = (f32[64,128]{1,0:T(8,128)S(1)}, f32[64,128]{1,0:T(8,128)S(1)}, u32[]{:S(2)}, u32[]{:S(2)}) collective-permute-start(f32[64,128]{1,0:T(8,128)S(1)} %add.39.refs_0_), channel_id=1, source_target_pairs={{0,8},{2,10},{4,12},{6,14},{8,0},{10,2},{12,4},{14,6},{16,24},{18,... | collective-permute-start | bytes 98312 | tf_op jit(solution)/shard_map/ppermute | solution.py:264
  33.2 5.6 %collective-permute-start.13 = (bf16[256,128]{1,0:T(8,128)(2,1)S(1)}, bf16[256,128]{1,0:T(8,128)(2,1)S(1)}, u32[]{:S(2)}, u32[]{:S(2)}) collective-permute-start(bf16[256,128]{1,0:T(8,128)(2,1)S(1)} %shard_map.115.refs_0_), channel_id=1, source_target_pairs={{0,6},{2,4},{4,2},{6,0},{8,14},{10,12},{12,10},{14,8},{16,22},{18,... | collective-permute-start | bytes 196616 | tf_op jit(solution)/shard_map/ppermute | solution.py:264
  35.1 4.4 %collective-permute-start.12 = (bf16[256,128]{1,0:T(8,128)(2,1)S(1)}, bf16[256,128]{1,0:T(8,128)(2,1)S(1)}, u32[]{:S(2)}, u32[]{:S(2)}) collective-permute-start(bf16[256,128]{1,0:T(8,128)(2,1)S(1)} %shard_map.115.refs_0_), channel_id=1, source_target_pairs={{0,4},{2,6},{4,0},{6,2},{8,12},{10,14},{12,8},{14,10},{16,20},{18,... | collective-permute-start | bytes 196616 | tf_op jit(solution)/shard_map/ppermute | solution.py:264
  36.5 4.3 %collective-permute-start.11 = (bf16[256,128]{1,0:T(8,128)(2,1)S(1)}, bf16[256,128]{1,0:T(8,128)(2,1)S(1)}, u32[]{:S(2)}, u32[]{:S(2)}) collective-permute-start(bf16[256,128]{1,0:T(8,128)(2,1)S(1)} %shard_map.115.refs_0_), channel_id=1, source_target_pairs={{0,2},{2,0},{4,6},{6,4},{8,10},{10,8},{12,14},{14,12},{16,18},{18,... | collective-permute-start | bytes 196616 | tf_op jit(solution)/shard_map/ppermute | solution.py:264
  41.2 1.3 %collective-permute-start.14 = (f32[64,128]{1,0:T(8,128)S(1)}, f32[64,128]{1,0:T(8,128)S(1)}, u32[]{:S(2)}, u32[]{:S(2)}) collective-permute-start(f32[64,128]{1,0:T(8,128)S(1)} %get-tuple-element.84.refs_0_), channel_id=1, source_target_pairs={{0,1},{1,0},{2,3},{3,2},{4,5},{5,4},{6,7},{7,6},{8,9},{9,8},{10,11... | collective-permute-start | bytes 98312 | tf_op jit(solution)/shard_map/ppermute | solution.py:264
  43.3 1.4 %collective-permute-start.15 = (f32[64,128]{1,0:T(8,128)S(1)}, f32[64,128]{1,0:T(8,128)S(1)}, u32[]{:S(2)}, u32[]{:S(2)}) collective-permute-start(f32[64,128]{1,0:T(8,128)S(1)} %get-tuple-element.88), channel_id=1, source_target_pairs={{0,1},{1,0},{2,3},{3,2},{4,5},{5,4},{6,7},{7,6},{8,9},{9,8},{10,11... | collective-permute-start | bytes 98312 | tf_op jit(solution)/shard_map/ppermute | solution.py:264
  44.7 4.8 %collective-permute-start.19 = (f32[64,128]{1,0:T(8,128)S(1)}, f32[64,128]{1,0:T(8,128)S(1)}, u32[]{:S(2)}, u32[]{:S(2)}) collective-permute-start(f32[64,128]{1,0:T(8,128)S(1)} %get-tuple-element.92.refs_0_), channel_id=1, source_target_pairs={{0,1},{1,0},{2,3},{3,2},{4,5},{5,4},{6,7},{7,6},{8,9},{9,8},{10,11... | collective-permute-start | bytes 98312 | tf_op jit(solution)/shard_map/ppermute | solution.py:264
  45.1 6.6 %collective-permute-start.18 = (f32[64,128]{1,0:T(8,128)S(1)}, f32[64,128]{1,0:T(8,128)S(1)}, u32[]{:S(2)}, u32[]{:S(2)}) collective-permute-start(f32[64,128]{1,0:T(8,128)S(1)} %add.40.refs_0_), channel_id=1, source_target_pairs={{0,24},{2,26},{4,28},{6,30},{8,16},{10,18},{12,20},{14,22},{16,8},... | collective-permute-start | bytes 98312 | tf_op jit(solution)/shard_map/ppermute | solution.py:264
  46.9 4.9 %collective-permute-start.17 = (f32[64,128]{1,0:T(8,128)S(1)}, f32[64,128]{1,0:T(8,128)S(1)}, u32[]{:S(2)}, u32[]{:S(2)}) collective-permute-start(f32[64,128]{1,0:T(8,128)S(1)} %add.40.refs_0_), channel_id=1, source_target_pairs={{0,16},{2,18},{4,20},{6,22},{8,24},{10,26},{12,28},{14,30},{16,0},... | collective-permute-start | bytes 98312 | tf_op jit(solution)/shard_map/ppermute | solution.py:264
  47.2 4.7 %collective-permute-start.16 = (f32[64,128]{1,0:T(8,128)S(1)}, f32[64,128]{1,0:T(8,128)S(1)}, u32[]{:S(2)}, u32[]{:S(2)}) collective-permute-start(f32[64,128]{1,0:T(8,128)S(1)} %add.40.refs_0_), channel_id=1, source_target_pairs={{0,8},{2,10},{4,12},{6,14},{8,0},{10,2},{12,4},{14,6},{16,24},{18,... | collective-permute-start | bytes 98312 | tf_op jit(solution)/shard_map/ppermute | solution.py:264
  52.2 5.3 %collective-permute-start.22 = (bf16[256,128]{1,0:T(8,128)(2,1)S(1)}, bf16[256,128]{1,0:T(8,128)(2,1)S(1)}, u32[]{:S(2)}, u32[]{:S(2)}) collective-permute-start(bf16[256,128]{1,0:T(8,128)(2,1)S(1)} %shard_map.121.refs_0_), channel_id=1, source_target_pairs={{0,6},{2,4},{4,2},{6,0},{8,14},{10,12},{12,10},{14,8},{16,22},{18,... | collective-permute-start | bytes 196616 | tf_op jit(solution)/shard_map/ppermute | solution.py:264
  53.0 5.0 %collective-permute-start.21 = (bf16[256,128]{1,0:T(8,128)(2,1)S(1)}, bf16[256,128]{1,0:T(8,128)(2,1)S(1)}, u32[]{:S(2)}, u32[]{:S(2)}) collective-permute-start(bf16[256,128]{1,0:T(8,128)(2,1)S(1)} %shard_map.121.refs_0_), channel_id=1, source_target_pairs={{0,4},{2,6},{4,0},{6,2},{8,12},{10,14},{12,8},{14,10},{16,20},{18,... | collective-permute-start | bytes 196616 | tf_op jit(solution)/shard_map/ppermute | solution.py:264
  54.0 4.3 %collective-permute-start.20 = (bf16[256,128]{1,0:T(8,128)(2,1)S(1)}, bf16[256,128]{1,0:T(8,128)(2,1)S(1)}, u32[]{:S(2)}, u32[]{:S(2)}) collective-permute-start(bf16[256,128]{1,0:T(8,128)(2,1)S(1)} %shard_map.121.refs_0_), channel_id=1, source_target_pairs={{0,2},{2,0},{4,6},{6,4},{8,10},{10,8},{12,14},{14,12},{16,18},{18,... | collective-permute-start | bytes 196616 | tf_op jit(solution)/shard_map/ppermute | solution.py:264
  58.6 1.3 %collective-permute-start.23 = (f32[64,128]{1,0:T(8,128)S(1)}, f32[64,128]{1,0:T(8,128)S(1)}, u32[]{:S(2)}, u32[]{:S(2)}) collective-permute-start(f32[64,128]{1,0:T(8,128)S(1)} %get-tuple-element.102.refs_0_), channel_id=1, source_target_pairs={{0,1},{1,0},{2,3},{3,2},{4,5},{5,4},{6,7},{7,6},{8,9},{9,8},{10,11... | collective-permute-start | bytes 98312 | tf_op jit(solution)/shard_map/ppermute | solution.py:264
  60.8 1.4 %collective-permute-start.24 = (f32[64,128]{1,0:T(8,128)S(1)}, f32[64,128]{1,0:T(8,128)S(1)}, u32[]{:S(2)}, u32[]{:S(2)}) collective-permute-start(f32[64,128]{1,0:T(8,128)S(1)} %get-tuple-element.108), channel_id=1, source_target_pairs={{0,1},{1,0},{2,3},{3,2},{4,5},{5,4},{6,7},{7,6},{8,9},{9,8},{10,11... | collective-permute-start | bytes 98312 | tf_op jit(solution)/shard_map/ppermute | solution.py:264
  62.1 5.2 %collective-permute-start.28 = (f32[64,128]{1,0:T(8,128)S(1)}, f32[64,128]{1,0:T(8,128)S(1)}, u32[]{:S(2)}, u32[]{:S(2)}) collective-permute-start(f32[64,128]{1,0:T(8,128)S(1)} %get-tuple-element.111.refs_0_), channel_id=1, source_target_pairs={{0,1},{1,0},{2,3},{3,2},{4,5},{5,4},{6,7},{7,6},{8,9},{9,8},{10,11... | collective-permute-start | bytes 98312 | tf_op jit(solution)/shard_map/ppermute | solution.py:264
  62.8 6.7 %collective-permute-start.27 = (f32[64,128]{1,0:T(8,128)S(1)}, f32[64,128]{1,0:T(8,128)S(1)}, u32[]{:S(2)}, u32[]{:S(2)}) collective-permute-start(f32[64,128]{1,0:T(8,128)S(1)} %shard_map.126), channel_id=1, source_target_pairs={{0,24},{2,26},{4,28},{6,30},{8,16},{10,18},{12,20},{14,22},{16,8},... | collective-permute-start | bytes 98312 | tf_op jit(solution)/shard_map/ppermute | solution.py:264
  65.3 4.9 %collective-permute-start.26 = (f32[64,128]{1,0:T(8,128)S(1)}, f32[64,128]{1,0:T(8,128)S(1)}, u32[]{:S(2)}, u32[]{:S(2)}) collective-permute-start(f32[64,128]{1,0:T(8,128)S(1)} %shard_map.126), channel_id=1, source_target_pairs={{0,16},{2,18},{4,20},{6,22},{8,24},{10,26},{12,28},{14,30},{16,0},... | collective-permute-start | bytes 98312 | tf_op jit(solution)/shard_map/ppermute | solution.py:264
  65.9 4.3 %collective-permute-start.25 = (f32[64,128]{1,0:T(8,128)S(1)}, f32[64,128]{1,0:T(8,128)S(1)}, u32[]{:S(2)}, u32[]{:S(2)}) collective-permute-start(f32[64,128]{1,0:T(8,128)S(1)} %shard_map.126), channel_id=1, source_target_pairs={{0,8},{2,10},{4,12},{6,14},{8,0},{10,2},{12,4},{14,6},{16,24},{18,... | collective-permute-start | bytes 98312 | tf_op jit(solution)/shard_map/ppermute | solution.py:264
  70.2 4.9 %collective-permute-start.31 = (f32[64,128]{1,0:T(8,128)S(1)}, f32[64,128]{1,0:T(8,128)S(1)}, u32[]{:S(2)}, u32[]{:S(2)}) collective-permute-start(f32[64,128]{1,0:T(8,128)S(1)} %add_add_fusion.1), channel_id=1, source_target_pairs={{0,6},{2,4},{4,2},{6,0},{8,14},{10,12},{12,10},{14,8},{16,22},{18,... | collective-permute-start | bytes 98312 | tf_op jit(solution)/shard_map/ppermute | solution.py:264
  72.0 3.9 %collective-permute-start.30 = (f32[64,128]{1,0:T(8,128)S(1)}, f32[64,128]{1,0:T(8,128)S(1)}, u32[]{:S(2)}, u32[]{:S(2)}) collective-permute-start(f32[64,128]{1,0:T(8,128)S(1)} %add_add_fusion.1), channel_id=1, source_target_pairs={{0,4},{2,6},{4,0},{6,2},{8,12},{10,14},{12,8},{14,10},{16,20},{18,... | collective-permute-start | bytes 98312 | tf_op jit(solution)/shard_map/ppermute | solution.py:264
  73.5 3.9 %collective-permute-start.29 = (f32[64,128]{1,0:T(8,128)S(1)}, f32[64,128]{1,0:T(8,128)S(1)}, u32[]{:S(2)}, u32[]{:S(2)}) collective-permute-start(f32[64,128]{1,0:T(8,128)S(1)} %add_add_fusion.1), channel_id=1, source_target_pairs={{0,2},{2,0},{4,6},{6,4},{8,10},{10,8},{12,14},{14,12},{16,18},{18,... | collective-permute-start | bytes 98312 | tf_op jit(solution)/shard_map/ppermute | solution.py:264
  77.4 1.3 %collective-permute-start.32 = (f32[64,128]{1,0:T(8,128)S(1)}, f32[64,128]{1,0:T(8,128)S(1)}, u32[]{:S(2)}, u32[]{:S(2)}) collective-permute-start(f32[64,128]{1,0:T(8,128)S(1)} %add_add_fusion.refs_0_), channel_id=1, source_target_pairs={{0,1},{1,0},{2,3},{3,2},{4,5},{5,4},{6,7},{7,6},{8,9},{9,8},{10,11... | collective-permute-start | bytes 98312 | tf_op jit(solution)/shard_map/ppermute | solution.py:264

commit v8 on v7

--- a/solution.py
+++ b/solution.py
@@ -214,19 +214,22 @@
     terms_ref[...] = jnp.concatenate([dot_nt(rotated_ref[...], adj), dot_nt(adj, adj)], axis=1)
 
 
-def own_kernel(inverse_ref, scale_ref, rotated_ref, search_ref, basis_ref, dirs_ref):
-    vecs = inverse_ref.shape[0]
-    basis_ref[...] = dot_nn(inverse_ref[...], rotated_ref[...])
+def own_kernel(inverse_ref, scale_ref, rotated_ref, adj_ref, search_ref, basis_ref, dirs_ref, both_ref):
+    vecs, edge = rotated_ref.shape
+    both = dot_nn(inverse_ref[...], jnp.concatenate([rotated_ref[...], adj_ref[...]], axis=1))
+    both_ref[...] = both
+    basis_ref[...] = both[:, :edge]
     dirs_ref[...] = search_ref[...] * scale_ref[:, vecs : vecs + 1]
 
 
-def last_kernel(nodes, terms, inverse_ref, rotated_ref, adj_ref, resid_ref, rayleigh_ref):
-    vecs = inverse_ref.shape[0]
+def last_kernel(nodes, terms, inverse_ref, both_ref, resid_ref, rayleigh_ref):
+    vecs, edge = resid_ref.shape
     inverse = inverse_ref[...]
     total = sum(ref[...] for ref in terms) / nodes
-    q = dot_nt(dot_nn(inverse, total[:, :vecs]), inverse)
+    turned = dot_nn(inverse, total[:, :vecs])
     square = jnp.sum(dot_nn(inverse, total[:, vecs:]) * inverse, axis=1, keepdims=True)
-    raw = dot_nn(dot_tn(q, inverse), rotated_ref[...]) - dot_nn(inverse, adj_ref[...])
+    q = dot_nt(turned, inverse)
+    raw = dot_tn(q, both_ref[:, :edge]) - both_ref[:, edge:]
     resid_ref[...] = raw * residual_scale(q, square)
     row_ids = lax.broadcasted_iota(jnp.int32, (vecs, vecs), 0)
     lane_ids = lax.broadcasted_iota(jnp.int32, (vecs, vecs), 1)
@@ -310,18 +313,23 @@
         mine_outs = [((blocks, vecs, edge), f32)]
     stack_out = ((3 * vecs, wide), bf16)
     limit = 16 if wide <= 4096 else 56
+
+    start = jnp.concatenate([start_basis, start_resid, start_search], axis=0)[None]
+    sweeps = ritz_basis.shape[0]
+    held = jnp.concatenate(far_values(start, near), axis=0)
+    held, slot_ids, tile_set, ritz_basis, ritz_search = lax.optimization_barrier(
+        (held, slot_ids, tile_set, ritz_basis, ritz_search)
+    )
+    parts = near_values(held, near)
     dense, = call(
         layout_kernel, [((wide, blocks * edge), bf16)], [slot_ids, tile_set], smem=(0,), limit=limit
     )
-
-    start = jnp.concatenate([start_basis, start_resid, start_search], axis=0)[None]
-    parts = near_values(jnp.concatenate(far_values(start, near), axis=0), near)
-    parts, dense = lax.optimization_barrier((parts, dense))
+    ritz = [(ritz_basis[sweep], ritz_search[sweep]) for sweep in range(sweeps)]
+    parts, dense, ritz = lax.optimization_barrier((parts, dense, ritz))
     state = None
-    sweeps = ritz_basis.shape[0]
     for sweep in range(sweeps):
         last = sweep == sweeps - 1
-        mixing = ritz_basis[sweep]
+        mixing, seeking = ritz[sweep]
         if state is None:
             stack, *mine = call(
                 functools.partial(first_kernel, near),
@@ -348,7 +356,7 @@
         pack, search, *rotated = call(
             gram_kernel,
             [((vecs, 2 * vecs), f32)] + ([own_out, own_out] if last else [((vecs, wide), f32)]),
-            [stack, mixing, ritz_search[sweep]],
+            [stack, mixing, seeking],
             limit=limit,
         )
         if panels == 2:
@@ -394,7 +402,11 @@
     rotated = rotated[0]
     terms, = call(terms_kernel, [((vecs, 2 * vecs), f32)], [rotated, rotated_adj])
     far_parts, inverse = lax.optimization_barrier((far_values(terms, near), inverse))
-    own_basis, own_dirs = call(own_kernel, [own_out, own_out], [inverse, scale, rotated, search])
+    own_basis, own_dirs, both = call(
+        own_kernel,
+        [own_out, own_out, ((vecs, 2 * edge), f32)],
+        [inverse, scale, rotated, rotated_adj, search],
+    )
     terms = panel_terms(sum(near_values(sum(far_parts), near)))
     count = len(terms)
 
@@ -402,7 +414,7 @@
         last_kernel(nodes, refs[:count], *refs[count:])
 
     resid, rayleigh = call(
-        kernel_last, [own_out, ((vecs, vecs), f32)], terms + [inverse, rotated, rotated_adj]
+        kernel_last, [own_out, ((vecs, vecs), f32)], terms + [inverse, both]
     )
     return (own_basis, resid, own_dirs, rayleigh)
 

time: 80 us -> 78.8 us (0.985)
  Pallas kernels: 19.1 us -> 18.3 us
  waiting for transfers between devices: 22.1 us -> 21.3 us
    pallas_call x19, Pallas kernels: 19.1 us -> 18.3 us  [call(): pl.pallas_call(kernel, out_shape=[jax.ShapeDtypeStruct(shape, kind) for s...]
  transfers between devices with their start and end apart: 33 -> 33, of which waited for: 20 -> 24; matrix products, arithmetic and copies ran while one was open for 0% -> 0% of each run, Pallas kernels for 18% -> 17%
where the time goes in v8:
time: 78.8 us; the launch traced here: 78.4 us
  starting transfers between devices  35.2 us (45%)
  waiting for transfers between devices  21.3 us (27%)
  Pallas kernels  18.3 us (23%)
  local copies, waits for them, and re-layouts  1.93 us (2%)
  other arithmetic  0.89 us (1%)
  between operations  0.85 us (1%)
    ppermute x33, starting transfers between devices, swap(): return lax.ppermute(value, axis, [(i, i ^ by) for i in range(size)])  35.2 us
    ppermute x33, waiting for transfers between devices, swap(): return lax.ppermute(value, axis, [(i, i ^ by) for i in range(size)])  21.3 us
    pallas_call x19, Pallas kernels, call(): pl.pallas_call(kernel, out_shape=[jax.ShapeDtypeStruct(shape, kind) for s...  18.3 us
    unnamed x10, local copies, waits for them, and re-layouts  1.91 us
  transfers between devices with their start and end apart: 33, of which 24 were waited for; matrix products, arithmetic and copies ran while one was open for 0% of the time, Pallas kernels for 17%

profile of v8, /device:TPU:0, one launch (start us, length us, event | category | flops | bytes accessed | tf_op | source)
XLA Modules:
  0.0 78.4 jit_solution(206660819850523110)
XLA Ops:
  0.6 0.8 maximum_bitcast_fusion
  1.4 5.0 %collective-permute-start.2 = (bf16[1,192,128]{2,1,0:T(8,128)(2,1)S(1)}, bf16[1,192,128]{2,1,0:T(8,128)(2,1)S(1)}, u32[]{:S(2)}, u32[]{:S(2)}) collective-permute-start(bf16[1,192,128]{2,1,0:T(8,128)(2,1)S(1)} %maximum_bitcast_fusion), channel_id=1, source_target_pairs={{0,24},{2,26},{4,28},{6,30},{8,16},{10,18},{12,20},{14,22},{16,8},... | collective-permute-start | bytes 147464 | tf_op jit(solution)/shard_map/ppermute | solution.py:267
  6.4 0.6 collective-permute-start
  7.1 0.7 copy-done.3
  7.8 0.9 %collective-permute-done.2 = bf16[1,192,128]{2,1,0:T(8,128)(2,1)S(1)} collective-permute-done((bf16[1,192,128]{2,1,0:T(8,128)(2,1)S(1)}, bf16[1,192,128]{2,1,0:T(8,128)(2,1)S(1)}, u32[]{:S(2)}, u32[]{:S(2)}) %collective-permute-start.2) | collective-permute-done | bytes 49184 | tf_op jit(solution)/shard_map/ppermute | solution.py:267
  8.7 2.8 %collective-permute-done.1 = bf16[1,192,128]{2,1,0:T(8,128)(2,1)S(1)} collective-permute-done((bf16[1,192,128]{2,1,0:T(8,128)(2,1)S(1)}, bf16[1,192,128]{2,1,0:T(8,128)(2,1)S(1)}, u32[]{:S(2)}, u32[]{:S(2)}) %collective-permute-start.1) | collective-permute-done | bytes 49184 | tf_op jit(solution)/shard_map/ppermute | solution.py:267
  11.5 2.5 %collective-permute-start.5 = (bf16[4,192,128]{2,1,0:T(8,128)(2,1)S(1)}, bf16[4,192,128]{2,1,0:T(8,128)(2,1)S(1)}, u32[]{:S(2)}, u32[]{:S(2)}) collective-permute-start(bf16[4,192,128]{2,1,0:T(8,128)(2,1)S(1)} %pad_maximum_fusion.refs_0_), channel_id=1, source_target_pairs={{0,6},{2,4},{4,2},{6,0},{8,14},{10,12},{12,10},{14,8},{16,22},{18,... | collective-permute-start | bytes 589832 | tf_op jit(solution)/shard_map/ppermute | solution.py:267
  14.0 0.5 collective-permute-start.4
  14.5 0.5 collective-permute-start.3
  15.1 1.2 %copy-done = bf16[1,1,2,16,128,128]{5,4,3,2,1,0:T(8,128)(2,1)S(1)} copy-done((bf16[1,1,2,16,128,128]{5,4,3,2,1,0:T(8,128)(2,1)S(1)}, bf16[1,1,2,16,128,128]{5,4,3,2,1,0:T(8,128)(2,1)}, u32[]{:S(2)}) %copy-start) | copy-done | bytes 1048600
  16.3 1.2 %shard_map.111.dense_ref.t = bf16[2048,256]{1,0:T(8,128)(2,1)S(1)} custom-call(s32[2,16]{1,0:T(2,128)S(1)} %compare_select_fusion.slots_ref, bf16[2,16,128,128]{3,2,1,0:T(8,128)(2,1)S(1)} %bitcast.25), custom_call_target="tpu_custom_call" | custom-call | tf_op jit(solution)/shard_map/pallas_call | solution.py:20
  17.5 2.5 %collective-permute-done.5.refs_3_ = bf16[4,192,128]{2,1,0:T(8,128)(2,1)S(1)} collective-permute-done((bf16[4,192,128]{2,1,0:T(8,128)(2,1)S(1)}, bf16[4,192,128]{2,1,0:T(8,128)(2,1)S(1)}, u32[]{:S(2)}, u32[]{:S(2)}) %collective-permute-start.5) | collective-permute-done | bytes 196640 | tf_op jit(solution)/shard_map/ppermute | solution.py:267
  19.9 2.5 %collective-permute-done.4.refs_2_ = bf16[4,192,128]{2,1,0:T(8,128)(2,1)S(1)} collective-permute-done((bf16[4,192,128]{2,1,0:T(8,128)(2,1)S(1)}, bf16[4,192,128]{2,1,0:T(8,128)(2,1)S(1)}, u32[]{:S(2)}, u32[]{:S(2)}) %collective-permute-start.4) | collective-permute-done | bytes 196640 | tf_op jit(solution)/shard_map/ppermute | solution.py:267
  22.5 0.6 shard_map.112
  23.2 1.1 %shard_map.113 = (f32[64,128]{1,0:T(8,128)S(1)}, f32[64,2048]{1,0:T(8,128)S(1)}) custom-call(bf16[192,2048]{1,0:T(8,128)(2,1)S(1)} %get-tuple-element.91.stack_ref, f32[64,192]{1,0:T(8,128)S(1)} %get-tuple-element.84.mix_ref, f32[64,128]{1,0:T(8,128)S(1)} %get-tuple-element.92.search_ref), custom_call_target="tpu_custom_call" | custom-call | tf_op jit(solution)/shard_map/pallas_call | solution.py:20
  24.4 0.5 collective-permute-start.10
  24.9 1.6 %collective-permute-start.9 = (f32[64,128]{1,0:T(8,128)S(1)}, f32[64,128]{1,0:T(8,128)S(1)}, u32[]{:S(2)}, u32[]{:S(2)}) collective-permute-start(f32[64,128]{1,0:T(8,128)S(1)} %add.39.refs_0_), channel_id=1, source_target_pairs={{0,24},{2,26},{4,28},{6,30},{8,16},{10,18},{12,20},{14,22},{16,8},... | collective-permute-start | bytes 98312 | tf_op jit(solution)/shard_map/ppermute | solution.py:267
  26.5 0.6 collective-permute-start.8
  27.1 2.2 %collective-permute-start.7 = (f32[64,128]{1,0:T(8,128)S(1)}, f32[64,128]{1,0:T(8,128)S(1)}, u32[]{:S(2)}, u32[]{:S(2)}) collective-permute-start(f32[64,128]{1,0:T(8,128)S(1)} %add.39.refs_0_), channel_id=1, source_target_pairs={{0,8},{2,10},{4,12},{6,14},{8,0},{10,2},{12,4},{14,6},{16,24},{18,... | collective-permute-start | bytes 98312 | tf_op jit(solution)/shard_map/ppermute | solution.py:267
  29.3 2.2 %shard_map.114 = (f32[64,64]{1,0:T(8,128)S(1)}, f32[64,128]{1,0:T(8,128)S(1)}) custom-call(f32[64,128]{1,0:T(8,128)S(1)} %get-tuple-element.95.refs_0_, f32[64,128]{1,0:T(8,128)S(1)} %collective-permute-done.10.refs_1_), custom_call_target="tpu_custom_call" | custom-call | tf_op jit(solution)/shard_map/pallas_call | solution.py:20
  32.0 1.7 %collective-permute-start.13 = (bf16[256,128]{1,0:T(8,128)(2,1)S(1)}, bf16[256,128]{1,0:T(8,128)(2,1)S(1)}, u32[]{:S(2)}, u32[]{:S(2)}) collective-permute-start(bf16[256,128]{1,0:T(8,128)(2,1)S(1)} %shard_map.115.refs_0_), channel_id=1, source_target_pairs={{0,6},{2,4},{4,2},{6,0},{8,14},{10,12},{12,10},{14,8},{16,22},{18,... | collective-permute-start | bytes 196616 | tf_op jit(solution)/shard_map/ppermute | solution.py:267
  33.7 1.3 %collective-permute-start.12 = (bf16[256,128]{1,0:T(8,128)(2,1)S(1)}, bf16[256,128]{1,0:T(8,128)(2,1)S(1)}, u32[]{:S(2)}, u32[]{:S(2)}) collective-permute-start(bf16[256,128]{1,0:T(8,128)(2,1)S(1)} %shard_map.115.refs_0_), channel_id=1, source_target_pairs={{0,4},{2,6},{4,0},{6,2},{8,12},{10,14},{12,8},{14,10},{16,20},{18,... | collective-permute-start | bytes 196616 | tf_op jit(solution)/shard_map/ppermute | solution.py:267
  35.0 0.5 collective-permute-start.11
  35.5 0.6 shard_map.116
  36.1 1.4 %collective-permute-done.13.refs_3_ = bf16[256,128]{1,0:T(8,128)(2,1)S(1)} collective-permute-done((bf16[256,128]{1,0:T(8,128)(2,1)S(1)}, bf16[256,128]{1,0:T(8,128)(2,1)S(1)}, u32[]{:S(2)}, u32[]{:S(2)}) %collective-permute-start.13) | collective-permute-done | bytes 65568 | tf_op jit(solution)/shard_map/ppermute | solution.py:267
  37.6 0.5 collective-permute-done.12.refs_2_
  38.1 1.1 %collective-permute-done.11.refs_1_ = bf16[256,128]{1,0:T(8,128)(2,1)S(1)} collective-permute-done((bf16[256,128]{1,0:T(8,128)(2,1)S(1)}, bf16[256,128]{1,0:T(8,128)(2,1)S(1)}, u32[]{:S(2)}, u32[]{:S(2)}) %collective-permute-start.11) | collective-permute-done | bytes 65568 | tf_op jit(solution)/shard_map/ppermute | solution.py:267
  39.2 0.4 shard_map.117
  39.7 1.2 %collective-permute-done.14.refs_1_ = f32[64,128]{1,0:T(8,128)S(1)} collective-permute-done((f32[64,128]{1,0:T(8,128)S(1)}, f32[64,128]{1,0:T(8,128)S(1)}, u32[]{:S(2)}, u32[]{:S(2)}) %collective-permute-start.14) | collective-permute-done | bytes 32800 | tf_op jit(solution)/shard_map/ppermute | solution.py:267
  40.9 0.9 %shard_map.118 = (bf16[192,2048]{1,0:T(8,128)(2,1)S(1)}, f32[64,128]{1,0:T(8,128)S(1)}, f32[64,128]{1,0:T(8,128)S(1)}) custom-call(s32[1]{0:T(128)} %bitcast.place_ref.p, bf16[2048,256]{1,0:T(8,128)(2,1)S(1)} %shard_map.111.dense_ref.t, f32[64,192]{1,0:T(8,128)S(1)} %get-tuple-element.83.m.mix_ref, f32[64,128]{1,0:T(8,128)S(1)} %get-tuple-element.105.refs_0_, ...), custom_call_target="tpu_custom_call" | custom-call | tf_op jit(solution)/shard_map/pallas_call | solution.py:20
  42.0 1.1 %shard_map.119 = (f32[64,128]{1,0:T(8,128)S(1)}, f32[64,2048]{1,0:T(8,128)S(1)}) custom-call(bf16[192,2048]{1,0:T(8,128)(2,1)S(1)} %get-tuple-element.110.stack_ref, f32[64,192]{1,0:T(8,128)S(1)} %get-tuple-element.83.m.mix_ref, f32[64,128]{1,0:T(8,128)S(1)} %get-tuple-element.111.search_ref), custom_call_target="tpu_custom_call" | custom-call | tf_op jit(solution)/shard_map/pallas_call | solution.py:20
  43.2 0.4 collective-permute-start.19
  43.6 1.8 %collective-permute-start.18 = (f32[64,128]{1,0:T(8,128)S(1)}, f32[64,128]{1,0:T(8,128)S(1)}, u32[]{:S(2)}, u32[]{:S(2)}) collective-permute-start(f32[64,128]{1,0:T(8,128)S(1)} %add.40.refs_0_), channel_id=1, source_target_pairs={{0,24},{2,26},{4,28},{6,30},{8,16},{10,18},{12,20},{14,22},{16,8},... | collective-permute-start | bytes 98312 | tf_op jit(solution)/shard_map/ppermute | solution.py:267
  45.4 1.1 %collective-permute-start.17 = (f32[64,128]{1,0:T(8,128)S(1)}, f32[64,128]{1,0:T(8,128)S(1)}, u32[]{:S(2)}, u32[]{:S(2)}) collective-permute-start(f32[64,128]{1,0:T(8,128)S(1)} %add.40.refs_0_), channel_id=1, source_target_pairs={{0,16},{2,18},{4,20},{6,22},{8,24},{10,26},{12,28},{14,30},{16,0},... | collective-permute-start | bytes 98312 | tf_op jit(solution)/shard_map/ppermute | solution.py:267
  46.5 1.4 %collective-permute-start.16 = (f32[64,128]{1,0:T(8,128)S(1)}, f32[64,128]{1,0:T(8,128)S(1)}, u32[]{:S(2)}, u32[]{:S(2)}) collective-permute-start(f32[64,128]{1,0:T(8,128)S(1)} %add.40.refs_0_), channel_id=1, source_target_pairs={{0,8},{2,10},{4,12},{6,14},{8,0},{10,2},{12,4},{14,6},{16,24},{18,... | collective-permute-start | bytes 98312 | tf_op jit(solution)/shard_map/ppermute | solution.py:267
  48.0 2.2 %shard_map.120 = (f32[64,64]{1,0:T(8,128)S(1)}, f32[64,128]{1,0:T(8,128)S(1)}) custom-call(f32[64,128]{1,0:T(8,128)S(1)} %get-tuple-element.114.refs_0_, f32[64,128]{1,0:T(8,128)S(1)} %collective-permute-done.19.refs_1_), custom_call_target="tpu_custom_call" | custom-call | tf_op jit(solution)/shard_map/pallas_call | solution.py:20
  50.2 0.4 collective-permute-done.17.refs_2_
  50.6 0.3 collective-permute-done.16.refs_1_
  50.9 0.3 shard_map.121.refs_0_
  51.1 1.5 %collective-permute-start.22 = (bf16[256,128]{1,0:T(8,128)(2,1)S(1)}, bf16[256,128]{1,0:T(8,128)(2,1)S(1)}, u32[]{:S(2)}, u32[]{:S(2)}) collective-permute-start(bf16[256,128]{1,0:T(8,128)(2,1)S(1)} %shard_map.121.refs_0_), channel_id=1, source_target_pairs={{0,6},{2,4},{4,2},{6,0},{8,14},{10,12},{12,10},{14,8},{16,22},{18,... | collective-permute-start | bytes 196616 | tf_op jit(solution)/shard_map/ppermute | solution.py:267
  52.6 0.6 collective-permute-start.21
  53.2 1.5 %collective-permute-start.20 = (bf16[256,128]{1,0:T(8,128)(2,1)S(1)}, bf16[256,128]{1,0:T(8,128)(2,1)S(1)}, u32[]{:S(2)}, u32[]{:S(2)}) collective-permute-start(bf16[256,128]{1,0:T(8,128)(2,1)S(1)} %shard_map.121.refs_0_), channel_id=1, source_target_pairs={{0,2},{2,0},{4,6},{6,4},{8,10},{10,8},{12,14},{14,12},{16,18},{18,... | collective-permute-start | bytes 196616 | tf_op jit(solution)/shard_map/ppermute | solution.py:267
  54.7 0.6 shard_map.122
  55.3 1.8 %collective-permute-done.22.refs_3_ = bf16[256,128]{1,0:T(8,128)(2,1)S(1)} collective-permute-done((bf16[256,128]{1,0:T(8,128)(2,1)S(1)}, bf16[256,128]{1,0:T(8,128)(2,1)S(1)}, u32[]{:S(2)}, u32[]{:S(2)}) %collective-permute-start.22) | collective-permute-done | bytes 65568 | tf_op jit(solution)/shard_map/ppermute | solution.py:267
  57.1 0.3 collective-permute-done.21.refs_2_
  57.5 0.4 shard_map.123
  57.9 1.2 %collective-permute-done.23.refs_1_ = f32[64,128]{1,0:T(8,128)S(1)} collective-permute-done((f32[64,128]{1,0:T(8,128)S(1)}, f32[64,128]{1,0:T(8,128)S(1)}, u32[]{:S(2)}, u32[]{:S(2)}) %collective-permute-start.23) | collective-permute-done | bytes 32800 | tf_op jit(solution)/shard_map/ppermute | solution.py:267
  59.1 0.9 %shard_map.124 = (bf16[192,2048]{1,0:T(8,128)(2,1)S(1)}, f32[64,128]{1,0:T(8,128)S(1)}, f32[64,128]{1,0:T(8,128)S(1)}) custom-call(s32[1]{0:T(128)} %bitcast.place_ref.p, bf16[2048,256]{1,0:T(8,128)(2,1)S(1)} %shard_map.111.dense_ref.t, f32[64,192]{1,0:T(8,128)S(1)} %get-tuple-element.82.m.mix_ref, f32[64,128]{1,0:T(8,128)S(1)} %get-tuple-element.124.refs_0_, ...), custom_call_target="tpu_custom_call" | custom-call | tf_op jit(solution)/shard_map/pallas_call | solution.py:20
  60.2 1.1 %shard_map.125 = (f32[64,128]{1,0:T(8,128)S(1)}, f32[64,128]{1,0:T(8,128)S(1)}, f32[64,128]{1,0:T(8,128)S(1)}) custom-call(bf16[192,2048]{1,0:T(8,128)(2,1)S(1)} %get-tuple-element.127.stack_ref, f32[64,192]{1,0:T(8,128)S(1)} %get-tuple-element.82.m.mix_ref, f32[64,128]{1,0:T(8,128)S(1)} %get-tuple-element.128.search_ref), custom_call_target="tpu_custom_call" | custom-call | tf_op jit(solution)/shard_map/pallas_call | solution.py:20
  61.4 0.4 collective-permute-start.28
  61.8 0.3 shard_map.126
  62.1 1.8 %collective-permute-start.27 = (f32[64,128]{1,0:T(8,128)S(1)}, f32[64,128]{1,0:T(8,128)S(1)}, u32[]{:S(2)}, u32[]{:S(2)}) collective-permute-start(f32[64,128]{1,0:T(8,128)S(1)} %shard_map.126), channel_id=1, source_target_pairs={{0,24},{2,26},{4,28},{6,30},{8,16},{10,18},{12,20},{14,22},{16,8},... | collective-permute-start | bytes 98312 | tf_op jit(solution)/shard_map/ppermute | solution.py:267
  63.8 0.8 collective-permute-start.26
  64.6 1.9 %collective-permute-start.25 = (f32[64,128]{1,0:T(8,128)S(1)}, f32[64,128]{1,0:T(8,128)S(1)}, u32[]{:S(2)}, u32[]{:S(2)}) collective-permute-start(f32[64,128]{1,0:T(8,128)S(1)} %shard_map.126), channel_id=1, source_target_pairs={{0,8},{2,10},{4,12},{6,14},{8,0},{10,2},{12,4},{14,6},{16,24},{18,... | collective-permute-start | bytes 98312 | tf_op jit(solution)/shard_map/ppermute | solution.py:267
  66.5 2.2 %shard_map.127 = (f32[64,64]{1,0:T(8,128)S(1)}, f32[64,128]{1,0:T(8,128)S(1)}) custom-call(f32[64,128]{1,0:T(8,128)S(1)} %get-tuple-element.134.refs_0_, f32[64,128]{1,0:T(8,128)S(1)} %collective-permute-done.28.refs_1_), custom_call_target="tpu_custom_call" | custom-call | tf_op jit(solution)/shard_map/pallas_call | solution.py:20
  69.0 1.7 %collective-permute-start.31 = (f32[64,128]{1,0:T(8,128)S(1)}, f32[64,128]{1,0:T(8,128)S(1)}, u32[]{:S(2)}, u32[]{:S(2)}) collective-permute-start(f32[64,128]{1,0:T(8,128)S(1)} %add_add_fusion.1), channel_id=1, source_target_pairs={{0,6},{2,4},{4,2},{6,0},{8,14},{10,12},{12,10},{14,8},{16,22},{18,... | collective-permute-start | bytes 98312 | tf_op jit(solution)/shard_map/ppermute | solution.py:267
  70.7 1.3 %collective-permute-start.30 = (f32[64,128]{1,0:T(8,128)S(1)}, f32[64,128]{1,0:T(8,128)S(1)}, u32[]{:S(2)}, u32[]{:S(2)}) collective-permute-start(f32[64,128]{1,0:T(8,128)S(1)} %add_add_fusion.1), channel_id=1, source_target_pairs={{0,4},{2,6},{4,0},{6,2},{8,12},{10,14},{12,8},{14,10},{16,20},{18,... | collective-permute-start | bytes 98312 | tf_op jit(solution)/shard_map/ppermute | solution.py:267
  72.0 0.5 collective-permute-start.29
  72.5 1.3 %collective-permute-done.31 = f32[64,128]{1,0:T(8,128)S(1)} collective-permute-done((f32[64,128]{1,0:T(8,128)S(1)}, f32[64,128]{1,0:T(8,128)S(1)}, u32[]{:S(2)}, u32[]{:S(2)}) %collective-permute-start.31) | collective-permute-done | bytes 32800 | tf_op jit(solution)/shard_map/ppermute | solution.py:267
  73.9 0.8 collective-permute-done.30
  74.6 1.3 %collective-permute-done.29 = f32[64,128]{1,0:T(8,128)S(1)} collective-permute-done((f32[64,128]{1,0:T(8,128)S(1)}, f32[64,128]{1,0:T(8,128)S(1)}, u32[]{:S(2)}, u32[]{:S(2)}) %collective-permute-start.29) | collective-permute-done | bytes 32800 | tf_op jit(solution)/shard_map/ppermute | solution.py:267
  76.0 0.8 %shard_map.128 = (f32[64,128]{1,0:T(8,128)}, f32[64,128]{1,0:T(8,128)}, f32[64,256]{1,0:T(8,128)S(1)}) custom-call(f32[64,64]{1,0:T(8,128)S(1)} %get-tuple-element.136.inverse_ref.refs_2_, f32[64,128]{1,0:T(8,128)S(1)} %get-tuple-element.137.scale_ref, f32[64,128]{1,0:T(8,128)S(1)} %get-tuple-element.129.rotated_ref, f32[64,128]{1,0:T(8,128)S(1)} %add.41.adj_ref, ...), custom_call_target="tpu_custom_call" | custom-call | tf_op jit(solution)/shard_map/pallas_call | solution.py:20
  76.8 0.4 collective-permute-done.32.refs_1_
  77.2 1.2 %shard_map.129 = (f32[64,128]{1,0:T(8,128)}, f32[64,64]{1,0:T(8,128)}) custom-call(f32[64,128]{1,0:T(8,128)S(1)} %add_add_fusion.refs_0_, f32[64,128]{1,0:T(8,128)S(1)} %collective-permute-done.32.refs_1_, f32[64,64]{1,0:T(8,128)S(1)} %get-tuple-element.136.inverse_ref.refs_2_, f32[64,256]{1,0:T(8,128)S(1)} %get-tuple-element.144.refs_3_), custom_call_target="tpu_custom_call" | custom-call | tf_op jit(solution)/shard_map/pallas_call | solution.py:20
  (41 shorter events, 1.9 us)
Async XLA Ops:
  1.4 7.3 %collective-permute-start.2 = (bf16[1,192,128]{2,1,0:T(8,128)(2,1)S(1)}, bf16[1,192,128]{2,1,0:T(8,128)(2,1)S(1)}, u32[]{:S(2)}, u32[]{:S(2)}) collective-permute-start(bf16[1,192,128]{2,1,0:T(8,128)(2,1)S(1)} %maximum_bitcast_fusion), channel_id=1, source_target_pairs={{0,24},{2,26},{4,28},{6,30},{8,16},{10,18},{12,20},{14,22},{16,8},... | collective-permute-start | bytes 147464 | tf_op jit(solution)/shard_map/ppermute | solution.py:267
  6.4 5.0 %collective-permute-start.1 = (bf16[1,192,128]{2,1,0:T(8,128)(2,1)S(1)}, bf16[1,192,128]{2,1,0:T(8,128)(2,1)S(1)}, u32[]{:S(2)}, u32[]{:S(2)}) collective-permute-start(bf16[1,192,128]{2,1,0:T(8,128)(2,1)S(1)} %maximum_bitcast_fusion), channel_id=1, source_target_pairs={{0,16},{2,18},{4,20},{6,22},{8,24},{10,26},{12,28},{14,30},{16,0},... | collective-permute-start | bytes 147464 | tf_op jit(solution)/shard_map/ppermute | solution.py:267
  6.4 5.0 %collective-permute-start = (bf16[1,192,128]{2,1,0:T(8,128)(2,1)S(1)}, bf16[1,192,128]{2,1,0:T(8,128)(2,1)S(1)}, u32[]{:S(2)}, u32[]{:S(2)}) collective-permute-start(bf16[1,192,128]{2,1,0:T(8,128)(2,1)S(1)} %maximum_bitcast_fusion), channel_id=1, source_target_pairs={{0,8},{2,10},{4,12},{6,14},{8,0},{10,2},{12,4},{14,6},{16,24},{18,... | collective-permute-start | bytes 147464 | tf_op jit(solution)/shard_map/ppermute | solution.py:267
  7.0 0.7 copy-start.3
  7.1 0.7 copy-start.4
  7.8 7.2 %copy-start.1 = (f32[3,64,192]{2,1,0:T(8,128)S(1)}, f32[3,64,192]{2,1,0:T(8,128)}, u32[]{:S(2)}) copy-start(f32[3,64,192]{2,1,0:T(8,128)} %param.14) | copy-start | bytes 442372
  11.5 8.5 %collective-permute-start.5 = (bf16[4,192,128]{2,1,0:T(8,128)(2,1)S(1)}, bf16[4,192,128]{2,1,0:T(8,128)(2,1)S(1)}, u32[]{:S(2)}, u32[]{:S(2)}) collective-permute-start(bf16[4,192,128]{2,1,0:T(8,128)(2,1)S(1)} %pad_maximum_fusion.refs_0_), channel_id=1, source_target_pairs={{0,6},{2,4},{4,2},{6,0},{8,14},{10,12},{12,10},{14,8},{16,22},{18,... | collective-permute-start | bytes 589832 | tf_op jit(solution)/shard_map/ppermute | solution.py:267
  14.0 8.4 %collective-permute-start.4 = (bf16[4,192,128]{2,1,0:T(8,128)(2,1)S(1)}, bf16[4,192,128]{2,1,0:T(8,128)(2,1)S(1)}, u32[]{:S(2)}, u32[]{:S(2)}) collective-permute-start(bf16[4,192,128]{2,1,0:T(8,128)(2,1)S(1)} %pad_maximum_fusion.refs_0_), channel_id=1, source_target_pairs={{0,4},{2,6},{4,0},{6,2},{8,12},{10,14},{12,8},{14,10},{16,20},{18,... | collective-permute-start | bytes 589832 | tf_op jit(solution)/shard_map/ppermute | solution.py:267
  14.5 8.0 %collective-permute-start.3 = (bf16[4,192,128]{2,1,0:T(8,128)(2,1)S(1)}, bf16[4,192,128]{2,1,0:T(8,128)(2,1)S(1)}, u32[]{:S(2)}, u32[]{:S(2)}) collective-permute-start(bf16[4,192,128]{2,1,0:T(8,128)(2,1)S(1)} %pad_maximum_fusion.refs_0_), channel_id=1, source_target_pairs={{0,2},{2,0},{4,6},{6,4},{8,10},{10,8},{12,14},{14,12},{16,18},{18,... | collective-permute-start | bytes 589832 | tf_op jit(solution)/shard_map/ppermute | solution.py:267
  15.0 1.2 %copy-start = (bf16[1,1,2,16,128,128]{5,4,3,2,1,0:T(8,128)(2,1)S(1)}, bf16[1,1,2,16,128,128]{5,4,3,2,1,0:T(8,128)(2,1)}, u32[]{:S(2)}) copy-start(bf16[1,1,2,16,128,128]{5,4,3,2,1,0:T(8,128)(2,1)} %param.8) | copy-start | bytes 3145732
  16.3 1.2 %copy-start.2 = (f32[3,64,128]{2,1,0:T(8,128)S(1)}, f32[3,64,128]{2,1,0:T(8,128)}, u32[]{:S(2)}) copy-start(f32[3,64,128]{2,1,0:T(8,128)} %param.15) | copy-start | bytes 294916
  23.1 1.3 %collective-permute-start.6 = (f32[64,128]{1,0:T(8,128)S(1)}, f32[64,128]{1,0:T(8,128)S(1)}, u32[]{:S(2)}, u32[]{:S(2)}) collective-permute-start(f32[64,128]{1,0:T(8,128)S(1)} %get-tuple-element.90), channel_id=1, source_target_pairs={{0,1},{1,0},{2,3},{3,2},{4,5},{5,4},{6,7},{7,6},{8,9},{9,8},{10,11... | collective-permute-start | bytes 98312 | tf_op jit(solution)/shard_map/ppermute | solution.py:267
  24.4 4.9 %collective-permute-start.10 = (f32[64,128]{1,0:T(8,128)S(1)}, f32[64,128]{1,0:T(8,128)S(1)}, u32[]{:S(2)}, u32[]{:S(2)}) collective-permute-start(f32[64,128]{1,0:T(8,128)S(1)} %get-tuple-element.95.refs_0_), channel_id=1, source_target_pairs={{0,1},{1,0},{2,3},{3,2},{4,5},{5,4},{6,7},{7,6},{8,9},{9,8},{10,11... | collective-permute-start | bytes 98312 | tf_op jit(solution)/shard_map/ppermute | solution.py:267
  24.9 6.6 %collective-permute-start.9 = (f32[64,128]{1,0:T(8,128)S(1)}, f32[64,128]{1,0:T(8,128)S(1)}, u32[]{:S(2)}, u32[]{:S(2)}) collective-permute-start(f32[64,128]{1,0:T(8,128)S(1)} %add.39.refs_0_), channel_id=1, source_target_pairs={{0,24},{2,26},{4,28},{6,30},{8,16},{10,18},{12,20},{14,22},{16,8},... | collective-permute-start | bytes 98312 | tf_op jit(solution)/shard_map/ppermute | solution.py:267
  26.5 5.1 %collective-permute-start.8 = (f32[64,128]{1,0:T(8,128)S(1)}, f32[64,128]{1,0:T(8,128)S(1)}, u32[]{:S(2)}, u32[]{:S(2)}) collective-permute-start(f32[64,128]{1,0:T(8,128)S(1)} %add.39.refs_0_), channel_id=1, source_target_pairs={{0,16},{2,18},{4,20},{6,22},{8,24},{10,26},{12,28},{14,30},{16,0},... | collective-permute-start | bytes 98312 | tf_op jit(solution)/shard_map/ppermute | solution.py:267
  27.1 4.6 %collective-permute-start.7 = (f32[64,128]{1,0:T(8,128)S(1)}, f32[64,128]{1,0:T(8,128)S(1)}, u32[]{:S(2)}, u32[]{:S(2)}) collective-permute-start(f32[64,128]{1,0:T(8,128)S(1)} %add.39.refs_0_), channel_id=1, source_target_pairs={{0,8},{2,10},{4,12},{6,14},{8,0},{10,2},{12,4},{14,6},{16,24},{18,... | collective-permute-start | bytes 98312 | tf_op jit(solution)/shard_map/ppermute | solution.py:267
  32.0 5.6 %collective-permute-start.13 = (bf16[256,128]{1,0:T(8,128)(2,1)S(1)}, bf16[256,128]{1,0:T(8,128)(2,1)S(1)}, u32[]{:S(2)}, u32[]{:S(2)}) collective-permute-start(bf16[256,128]{1,0:T(8,128)(2,1)S(1)} %shard_map.115.refs_0_), channel_id=1, source_target_pairs={{0,6},{2,4},{4,2},{6,0},{8,14},{10,12},{12,10},{14,8},{16,22},{18,... | collective-permute-start | bytes 196616 | tf_op jit(solution)/shard_map/ppermute | solution.py:267
  33.7 4.4 %collective-permute-start.12 = (bf16[256,128]{1,0:T(8,128)(2,1)S(1)}, bf16[256,128]{1,0:T(8,128)(2,1)S(1)}, u32[]{:S(2)}, u32[]{:S(2)}) collective-permute-start(bf16[256,128]{1,0:T(8,128)(2,1)S(1)} %shard_map.115.refs_0_), channel_id=1, source_target_pairs={{0,4},{2,6},{4,0},{6,2},{8,12},{10,14},{12,8},{14,10},{16,20},{18,... | collective-permute-start | bytes 196616 | tf_op jit(solution)/shard_map/ppermute | solution.py:267
  35.0 4.3 %collective-permute-start.11 = (bf16[256,128]{1,0:T(8,128)(2,1)S(1)}, bf16[256,128]{1,0:T(8,128)(2,1)S(1)}, u32[]{:S(2)}, u32[]{:S(2)}) collective-permute-start(bf16[256,128]{1,0:T(8,128)(2,1)S(1)} %shard_map.115.refs_0_), channel_id=1, source_target_pairs={{0,2},{2,0},{4,6},{6,4},{8,10},{10,8},{12,14},{14,12},{16,18},{18,... | collective-permute-start | bytes 196616 | tf_op jit(solution)/shard_map/ppermute | solution.py:267
  39.6 1.3 %collective-permute-start.14 = (f32[64,128]{1,0:T(8,128)S(1)}, f32[64,128]{1,0:T(8,128)S(1)}, u32[]{:S(2)}, u32[]{:S(2)}) collective-permute-start(f32[64,128]{1,0:T(8,128)S(1)} %get-tuple-element.105.refs_0_), channel_id=1, source_target_pairs={{0,1},{1,0},{2,3},{3,2},{4,5},{5,4},{6,7},{7,6},{8,9},{9,8},{10,11... | collective-permute-start | bytes 98312 | tf_op jit(solution)/shard_map/ppermute | solution.py:267
  41.8 1.4 %collective-permute-start.15 = (f32[64,128]{1,0:T(8,128)S(1)}, f32[64,128]{1,0:T(8,128)S(1)}, u32[]{:S(2)}, u32[]{:S(2)}) collective-permute-start(f32[64,128]{1,0:T(8,128)S(1)} %get-tuple-element.109), channel_id=1, source_target_pairs={{0,1},{1,0},{2,3},{3,2},{4,5},{5,4},{6,7},{7,6},{8,9},{9,8},{10,11... | collective-permute-start | bytes 98312 | tf_op jit(solution)/shard_map/ppermute | solution.py:267
  43.2 4.8 %collective-permute-start.19 = (f32[64,128]{1,0:T(8,128)S(1)}, f32[64,128]{1,0:T(8,128)S(1)}, u32[]{:S(2)}, u32[]{:S(2)}) collective-permute-start(f32[64,128]{1,0:T(8,128)S(1)} %get-tuple-element.114.refs_0_), channel_id=1, source_target_pairs={{0,1},{1,0},{2,3},{3,2},{4,5},{5,4},{6,7},{7,6},{8,9},{9,8},{10,11... | collective-permute-start | bytes 98312 | tf_op jit(solution)/shard_map/ppermute | solution.py:267
  43.6 6.6 %collective-permute-start.18 = (f32[64,128]{1,0:T(8,128)S(1)}, f32[64,128]{1,0:T(8,128)S(1)}, u32[]{:S(2)}, u32[]{:S(2)}) collective-permute-start(f32[64,128]{1,0:T(8,128)S(1)} %add.40.refs_0_), channel_id=1, source_target_pairs={{0,24},{2,26},{4,28},{6,30},{8,16},{10,18},{12,20},{14,22},{16,8},... | collective-permute-start | bytes 98312 | tf_op jit(solution)/shard_map/ppermute | solution.py:267
  45.4 5.2 %collective-permute-start.17 = (f32[64,128]{1,0:T(8,128)S(1)}, f32[64,128]{1,0:T(8,128)S(1)}, u32[]{:S(2)}, u32[]{:S(2)}) collective-permute-start(f32[64,128]{1,0:T(8,128)S(1)} %add.40.refs_0_), channel_id=1, source_target_pairs={{0,16},{2,18},{4,20},{6,22},{8,24},{10,26},{12,28},{14,30},{16,0},... | collective-permute-start | bytes 98312 | tf_op jit(solution)/shard_map/ppermute | solution.py:267
  46.5 4.3 %collective-permute-start.16 = (f32[64,128]{1,0:T(8,128)S(1)}, f32[64,128]{1,0:T(8,128)S(1)}, u32[]{:S(2)}, u32[]{:S(2)}) collective-permute-start(f32[64,128]{1,0:T(8,128)S(1)} %add.40.refs_0_), channel_id=1, source_target_pairs={{0,8},{2,10},{4,12},{6,14},{8,0},{10,2},{12,4},{14,6},{16,24},{18,... | collective-permute-start | bytes 98312 | tf_op jit(solution)/shard_map/ppermute | solution.py:267
  51.1 5.9 %collective-permute-start.22 = (bf16[256,128]{1,0:T(8,128)(2,1)S(1)}, bf16[256,128]{1,0:T(8,128)(2,1)S(1)}, u32[]{:S(2)}, u32[]{:S(2)}) collective-permute-start(bf16[256,128]{1,0:T(8,128)(2,1)S(1)} %shard_map.121.refs_0_), channel_id=1, source_target_pairs={{0,6},{2,4},{4,2},{6,0},{8,14},{10,12},{12,10},{14,8},{16,22},{18,... | collective-permute-start | bytes 196616 | tf_op jit(solution)/shard_map/ppermute | solution.py:267
  52.6 4.7 %collective-permute-start.21 = (bf16[256,128]{1,0:T(8,128)(2,1)S(1)}, bf16[256,128]{1,0:T(8,128)(2,1)S(1)}, u32[]{:S(2)}, u32[]{:S(2)}) collective-permute-start(bf16[256,128]{1,0:T(8,128)(2,1)S(1)} %shard_map.121.refs_0_), channel_id=1, source_target_pairs={{0,4},{2,6},{4,0},{6,2},{8,12},{10,14},{12,8},{14,10},{16,20},{18,... | collective-permute-start | bytes 196616 | tf_op jit(solution)/shard_map/ppermute | solution.py:267
  53.2 4.3 %collective-permute-start.20 = (bf16[256,128]{1,0:T(8,128)(2,1)S(1)}, bf16[256,128]{1,0:T(8,128)(2,1)S(1)}, u32[]{:S(2)}, u32[]{:S(2)}) collective-permute-start(bf16[256,128]{1,0:T(8,128)(2,1)S(1)} %shard_map.121.refs_0_), channel_id=1, source_target_pairs={{0,2},{2,0},{4,6},{6,4},{8,10},{10,8},{12,14},{14,12},{16,18},{18,... | collective-permute-start | bytes 196616 | tf_op jit(solution)/shard_map/ppermute | solution.py:267
  57.8 1.3 %collective-permute-start.23 = (f32[64,128]{1,0:T(8,128)S(1)}, f32[64,128]{1,0:T(8,128)S(1)}, u32[]{:S(2)}, u32[]{:S(2)}) collective-permute-start(f32[64,128]{1,0:T(8,128)S(1)} %get-tuple-element.124.refs_0_), channel_id=1, source_target_pairs={{0,1},{1,0},{2,3},{3,2},{4,5},{5,4},{6,7},{7,6},{8,9},{9,8},{10,11... | collective-permute-start | bytes 98312 | tf_op jit(solution)/shard_map/ppermute | solution.py:267
  60.0 1.4 %collective-permute-start.24 = (f32[64,128]{1,0:T(8,128)S(1)}, f32[64,128]{1,0:T(8,128)S(1)}, u32[]{:S(2)}, u32[]{:S(2)}) collective-permute-start(f32[64,128]{1,0:T(8,128)S(1)} %get-tuple-element.131), channel_id=1, source_target_pairs={{0,1},{1,0},{2,3},{3,2},{4,5},{5,4},{6,7},{7,6},{8,9},{9,8},{10,11... | collective-permute-start | bytes 98312 | tf_op jit(solution)/shard_map/ppermute | solution.py:267
  61.4 5.2 %collective-permute-start.28 = (f32[64,128]{1,0:T(8,128)S(1)}, f32[64,128]{1,0:T(8,128)S(1)}, u32[]{:S(2)}, u32[]{:S(2)}) collective-permute-start(f32[64,128]{1,0:T(8,128)S(1)} %get-tuple-element.134.refs_0_), channel_id=1, source_target_pairs={{0,1},{1,0},{2,3},{3,2},{4,5},{5,4},{6,7},{7,6},{8,9},{9,8},{10,11... | collective-permute-start | bytes 98312 | tf_op jit(solution)/shard_map/ppermute | solution.py:267
  62.1 6.7 %collective-permute-start.27 = (f32[64,128]{1,0:T(8,128)S(1)}, f32[64,128]{1,0:T(8,128)S(1)}, u32[]{:S(2)}, u32[]{:S(2)}) collective-permute-start(f32[64,128]{1,0:T(8,128)S(1)} %shard_map.126), channel_id=1, source_target_pairs={{0,24},{2,26},{4,28},{6,30},{8,16},{10,18},{12,20},{14,22},{16,8},... | collective-permute-start | bytes 98312 | tf_op jit(solution)/shard_map/ppermute | solution.py:267
  63.8 5.0 %collective-permute-start.26 = (f32[64,128]{1,0:T(8,128)S(1)}, f32[64,128]{1,0:T(8,128)S(1)}, u32[]{:S(2)}, u32[]{:S(2)}) collective-permute-start(f32[64,128]{1,0:T(8,128)S(1)} %shard_map.126), channel_id=1, source_target_pairs={{0,16},{2,18},{4,20},{6,22},{8,24},{10,26},{12,28},{14,30},{16,0},... | collective-permute-start | bytes 98312 | tf_op jit(solution)/shard_map/ppermute | solution.py:267
  64.6 4.4 %collective-permute-start.25 = (f32[64,128]{1,0:T(8,128)S(1)}, f32[64,128]{1,0:T(8,128)S(1)}, u32[]{:S(2)}, u32[]{:S(2)}) collective-permute-start(f32[64,128]{1,0:T(8,128)S(1)} %shard_map.126), channel_id=1, source_target_pairs={{0,8},{2,10},{4,12},{6,14},{8,0},{10,2},{12,4},{14,6},{16,24},{18,... | collective-permute-start | bytes 98312 | tf_op jit(solution)/shard_map/ppermute | solution.py:267
  69.0 4.9 %collective-permute-start.31 = (f32[64,128]{1,0:T(8,128)S(1)}, f32[64,128]{1,0:T(8,128)S(1)}, u32[]{:S(2)}, u32[]{:S(2)}) collective-permute-start(f32[64,128]{1,0:T(8,128)S(1)} %add_add_fusion.1), channel_id=1, source_target_pairs={{0,6},{2,4},{4,2},{6,0},{8,14},{10,12},{12,10},{14,8},{16,22},{18,... | collective-permute-start | bytes 98312 | tf_op jit(solution)/shard_map/ppermute | solution.py:267
  70.7 3.9 %collective-permute-start.30 = (f32[64,128]{1,0:T(8,128)S(1)}, f32[64,128]{1,0:T(8,128)S(1)}, u32[]{:S(2)}, u32[]{:S(2)}) collective-permute-start(f32[64,128]{1,0:T(8,128)S(1)} %add_add_fusion.1), channel_id=1, source_target_pairs={{0,4},{2,6},{4,0},{6,2},{8,12},{10,14},{12,8},{14,10},{16,20},{18,... | collective-permute-start | bytes 98312 | tf_op jit(solution)/shard_map/ppermute | solution.py:267
  72.0 3.9 %collective-permute-start.29 = (f32[64,128]{1,0:T(8,128)S(1)}, f32[64,128]{1,0:T(8,128)S(1)}, u32[]{:S(2)}, u32[]{:S(2)}) collective-permute-start(f32[64,128]{1,0:T(8,128)S(1)} %add_add_fusion.1), channel_id=1, source_target_pairs={{0,2},{2,0},{4,6},{6,4},{8,10},{10,8},{12,14},{14,12},{16,18},{18,... | collective-permute-start | bytes 98312 | tf_op jit(solution)/shard_map/ppermute | solution.py:267
  75.9 1.3 %collective-permute-start.32 = (f32[64,128]{1,0:T(8,128)S(1)}, f32[64,128]{1,0:T(8,128)S(1)}, u32[]{:S(2)}, u32[]{:S(2)}) collective-permute-start(f32[64,128]{1,0:T(8,128)S(1)} %add_add_fusion.refs_0_), channel_id=1, source_target_pairs={{0,1},{1,0},{2,3},{3,2},{4,5},{5,4},{6,7},{7,6},{8,9},{9,8},{10,11... | collective-permute-start | bytes 98312 | tf_op jit(solution)/shard_map/ppermute | solution.py:267

commit v9 on v8

--- a/solution.py
+++ b/solution.py
@@ -13,7 +13,7 @@
 bf16 = jnp.bfloat16
 
 
-def call(kernel, outs, args, smem=(), limit=16):
+def call(kernel, outs, args, smem=(), limit=16, scratch=()):
     specs = [
         pl.BlockSpec(memory_space=pltpu.SMEM if i in smem else pltpu.VMEM) for i in range(len(args))
     ]
@@ -22,6 +22,7 @@
         out_shape=[jax.ShapeDtypeStruct(shape, kind) for shape, kind in outs],
         in_specs=specs,
         out_specs=[pl.BlockSpec(memory_space=pltpu.VMEM) for _ in outs],
+        scratch_shapes=[pltpu.VMEM(shape, kind) for shape, kind in scratch],
         compiler_params=pltpu.CompilerParams(vmem_limit_bytes=limit << 20),
     )(*args)
 
@@ -74,10 +75,10 @@
                 dense_ref[pl.ds(start, edge), b * edge : (b + 1) * edge] = tiles_ref[b, s].T
 
 
-def product(place_ref, dense_ref, mix_ref, stack, mine_refs):
+def send_parts(place_ref, mix_ref, image, mine_refs):
     edge = mine_refs[0].shape[-1]
     vecs = mix_ref.shape[0]
-    high, low = halves(jnp.dot(stack, dense_ref[...], preferred_element_type=f32))
+    high, low = halves(image)
     weights = jnp.concatenate(halves(mix_ref[...]), axis=0)
     mixed = jnp.dot(weights, high, preferred_element_type=f32)
     mixed = mixed[:vecs] + mixed[vecs:] + jnp.dot(weights[:vecs], low, preferred_element_type=f32)
@@ -96,48 +97,84 @@
     edge = mine_refs[0].shape[-1]
     at = 0
     for ref in part_refs:
-        for i in range(ref.shape[0]):
-            stack_ref[:, at : at + edge] = ref[i]
+        far = ref.shape[0]
+        for i in range(far):
+            stack_ref[:, at : at + edge] = ref[-i % far]
             at += edge
-    product(place_ref, dense_ref, mix_ref, stack_ref[...], mine_refs)
+    image = jnp.dot(stack_ref[...], dense_ref[...], preferred_element_type=f32)
+    send_parts(place_ref, mix_ref, image, mine_refs)
 
 
 def residual_scale(q, square):
     return lax.rsqrt(jnp.maximum(square - jnp.sum((q * q).T, axis=1, keepdims=True), 0.0) + epsilon)
 
 
-def next_kernel(place_ref, dense_ref, mix_ref, crosses, basis_ref, wide_ref, dirs_ref, stack_ref, *mine_refs):
-    vecs = wide_ref.shape[0]
+def cross_terms(crosses):
     both = sum(ref[...] for ref in crosses)
+    vecs = both.shape[0]
     q = both[:, :vecs]
     scale = residual_scale(q, both[:, vecs : vecs + 1])
-    high, low = halves(q)
-    terms = jnp.concatenate([high, high, low], axis=0)
-    basis = jnp.concatenate([basis_ref[: 2 * vecs], basis_ref[:vecs]], axis=0)
+    at = vecs + vecs // 2
+    return q, scale, lax.rsqrt(both[:, at : at + 1] + epsilon)
+
+
+def ahead_kernel(basis_ref, wide_ref, search_ref, dense_ref, image_ref):
+    vecs = wide_ref.shape[0]
+    rows = jnp.concatenate([basis_ref[:vecs], wide_ref[...], search_ref[...].astype(bf16)], axis=0)
+    image_ref[...] = jnp.dot(rows, dense_ref[...], preferred_element_type=f32)
+
+
+def mix_kernel(place_ref, mix_ref, crosses, image_ref, *mine_refs):
+    vecs = mix_ref.shape[0]
+    q, scale, step = cross_terms(crosses)
+    basis = image_ref[:vecs]
+    raw = dot_tn(q, basis) - image_ref[vecs : 2 * vecs]
+    image = jnp.concatenate([basis, raw * scale, image_ref[2 * vecs :] * step], axis=0)
+    send_parts(place_ref, mix_ref, image, mine_refs)
+
+
+def gram_terms(stack, mix_ref, pack_ref, search_refs):
+    vecs = mix_ref.shape[0]
+    rotated = times_stack(mix_ref[...], stack)
+    square = jnp.zeros((vecs, vecs), f32)
+    if search_refs:
+        weights_ref, search_out, own_rotated = search_refs
+        edge = search_out.shape[1]
+        search = times_stack(weights_ref[...], stack[vecs:])
+        search_out[...] = search[:, :edge]
+        own_rotated[...] = rotated[:, :edge]
+        square = jnp.broadcast_to(jnp.sum(search * search, axis=1, keepdims=True), square.shape)
+    split = jnp.concatenate(halves(rotated), axis=0)
+    gram = lax.dot_general(split, split, (((1,), (1,)), ((), ())), preferred_element_type=f32)
+    gram = gram[:vecs] + gram[vecs:]
+    pack_ref[...] = jnp.concatenate([gram[:, :vecs] + gram[:, vecs:], square], axis=1)
+
+
+def gram_kernel(stack_ref, mix_ref, pack_ref):
+    gram_terms(stack_ref[...], mix_ref, pack_ref, ())
+
+
+def stack_kernel(last, mix_ref, crosses, basis_ref, wide_ref, found_ref, *refs):
+    vecs = wide_ref.shape[0]
+    if last:
+        weights, pack_ref, outs, stack_ref = refs[:1], refs[1], refs[2:4], refs[4]
+    else:
+        weights, pack_ref, outs, stack_ref = (), refs[0], (), refs[1]
+    q, scale, step = cross_terms(crosses)
+    terms = jnp.concatenate([*halves(q), q.astype(bf16)], axis=0)
+    basis = jnp.concatenate([basis_ref[:vecs], basis_ref[:vecs], basis_ref[vecs : 2 * vecs]], axis=0)
     part = lax.dot_general(terms, basis, (((0,), (0,)), ((), ())), preferred_element_type=f32)
     stack_ref[:vecs] = basis_ref[:vecs]
     stack_ref[vecs : 2 * vecs] = ((part - wide_ref[...].astype(f32)) * scale).astype(bf16)
-    stack_ref[2 * vecs :] = dirs_ref[...]
-    product(place_ref, dense_ref, mix_ref, stack_ref[...], mine_refs)
-
-
-def gram_kernel(stack_ref, mix_ref, search_ref, pack_ref, search_out, *own_rotated):
-    vecs, edge = mix_ref.shape[0], search_out.shape[1]
-    rotated = times_stack(mix_ref[...], stack_ref[...])
-    search = times_stack(search_ref[...], stack_ref[vecs:])
-    search_out[...] = search[:, :edge]
-    if own_rotated:
-        own_rotated[0][...] = rotated[:, :edge]
-    square = jnp.sum(search * search, axis=1, keepdims=True)
-    pack_ref[...] = jnp.concatenate(
-        [dot_nt(rotated, rotated), jnp.broadcast_to(square, (vecs, vecs))], axis=1
-    )
-
-
-def factor_kernel(nodes, packs, inverse_ref, scale_ref):
+    stack_ref[2 * vecs :] = (found_ref[...] * step).astype(bf16)
+    gram_terms(stack_ref[...], mix_ref, pack_ref, (*weights, *outs))
+
+
+def factor_kernel(nodes, packs, inverse_ref, *scale_ref):
     vecs = inverse_ref.shape[0]
     total = sum(ref[...] for ref in packs) / nodes
-    scale_ref[...] = lax.rsqrt(jnp.maximum(total, 0.0) + epsilon)
+    if scale_ref:
+        scale_ref[0][...] = lax.rsqrt(jnp.maximum(total, 0.0) + epsilon)
     row_ids = lax.broadcasted_iota(jnp.int32, (vecs, 2 * vecs), 0)
     lane_ids = lax.broadcasted_iota(jnp.int32, (vecs, 2 * vecs), 1)
     diagonal = jnp.where(lane_ids == row_ids, total, 0.0)
@@ -202,9 +239,11 @@
     inverse_ref[...] = jnp.concatenate(done, axis=0)[:, vecs:]
 
 
-def basis_kernel(inverse_ref, scale_ref, stack_ref, mix_ref, search_ref, basis_ref, dirs_ref):
+def basis_kernel(inverse_ref, stack_ref, mix_ref, weights_ref, basis_ref, search_ref, square_ref):
     vecs = mix_ref.shape[0]
-    dirs_ref[...] = (search_ref[...] * scale_ref[:, vecs : vecs + 1]).astype(bf16)
+    search = times_stack(weights_ref[...], stack_ref[vecs:])
+    search_ref[...] = search
+    square_ref[...] = jnp.broadcast_to(jnp.sum(search * search, axis=1, keepdims=True), square_ref.shape)
     basis = times_stack(dot_nn(inverse_ref[...], mix_ref[...]), stack_ref[...])
     basis_ref[...] = pieces(basis)
 
@@ -245,7 +284,7 @@
 
 
 def cross_kernel(nodes, parts, *refs):
-    part_refs, basis_ref, cross_ref, wide_ref = refs[:parts], refs[parts], refs[parts + 1], refs[parts + 2]
+    part_refs, (basis_ref, search_ref, cross_ref, wide_ref) = refs[:parts], refs[parts:]
     vecs = wide_ref.shape[0]
     edge = part_refs[0].shape[1]
     at = 0
@@ -259,7 +298,9 @@
     cross = cross[:vecs] + cross[vecs : 2 * vecs] + cross[2 * vecs :]
     values = wide_ref[...].astype(f32)
     square = jnp.sum(values * values, axis=1, keepdims=True)
-    cross_ref[...] = jnp.concatenate([cross, jnp.broadcast_to(square, cross.shape)], axis=1) / nodes
+    half = (vecs, vecs // 2)
+    squares = [jnp.broadcast_to(square, half), jnp.broadcast_to(search_ref[:, :1], half)]
+    cross_ref[...] = jnp.concatenate([cross, *squares], axis=1) / nodes
 
 
 def swap(value, by, axis):
@@ -275,11 +316,11 @@
 
 def far_values(value, near):
     far = lax.axis_size("rows") // near
-    return [value] + [swap(value, near * i, "rows") for i in range(1, far)]
+    return [value] + [swap(value, near * i, "rows") for i in range(far - 1, 0, -1)]
 
 
 def near_values(held, near):
-    return [held] + [swap(held, i, "rows") for i in range(1, near)]
+    return [held] + [swap(held, i, "rows") for i in range(near - 1, 0, -1)]
 
 
 def body(
@@ -302,7 +343,8 @@
     wide = rows * edge
     near = 4
     away = columns ^ lax.axis_index("rows")
-    position = (away % near) * (rows // near) + away // near
+    far = rows // near
+    position = (-away % near) * far + -(away // near) % far
     in_use = jnp.arange(slots, dtype=jnp.int32)[None, :] < counts[:, None]
     slot_ids = jnp.where(in_use, position, rows).astype(jnp.int32)
     place = lax.axis_index("panel").astype(jnp.int32).reshape(1)
@@ -316,7 +358,8 @@
 
     start = jnp.concatenate([start_basis, start_resid, start_search], axis=0)[None]
     sweeps = ritz_basis.shape[0]
-    held = jnp.concatenate(far_values(start, near), axis=0)
+    first_parts = far_values(start, near)
+    held = jnp.concatenate(first_parts[:1] + first_parts[:0:-1], axis=0)
     held, slot_ids, tile_set, ritz_basis, ritz_search = lax.optimization_barrier(
         (held, slot_ids, tile_set, ritz_basis, ritz_search)
     )
@@ -339,26 +382,32 @@
                 limit=limit,
             )
         else:
-            crosses, basis, wide_adj, dirs = state
+            crosses, basis, wide_adj, search, image = state
             count = len(crosses)
 
-            def kernel(p, t, m, *refs):
-                next_kernel(p, t, m, refs[:count], *refs[count:])
-
-            stack, *mine = call(
-                kernel,
-                [stack_out] + mine_outs,
-                [place, dense, mixing] + crosses + [basis, wide_adj, dirs],
-                smem=(0,),
-                limit=limit,
+            def kernel_mix(p, m, *refs):
+                mix_kernel(p, m, refs[:count], *refs[count:])
+
+            mine = call(
+                kernel_mix, mine_outs, [place, mixing] + crosses + [image], smem=(0,), limit=limit
             )
         own_out = ((vecs, edge), f32)
-        pack, search, *rotated = call(
-            gram_kernel,
-            [((vecs, 2 * vecs), f32)] + ([own_out, own_out] if last else [((vecs, wide), f32)]),
-            [stack, mixing, seeking],
-            limit=limit,
-        )
+        pack_out = ((vecs, 2 * vecs), f32)
+        if state is None:
+            pack, = call(gram_kernel, [pack_out], [stack, mixing], limit=limit)
+        else:
+
+            def kernel_stack(m, *refs):
+                stack_kernel(last, m, refs[:count], *refs[count:])
+
+            pack, *rest = call(
+                kernel_stack,
+                [pack_out] + ([own_out, own_out] if last else [stack_out]),
+                [mixing] + crosses + [basis, wide_adj, search] + [seeking] * last,
+                limit=limit,
+                scratch=[stack_out] * last,
+            )
+            stack = rest[0]
         if panels == 2:
             other = swap(mine[1], 1, "panel")
             other, pack = lax.optimization_barrier((other, pack))
@@ -371,8 +420,8 @@
         def kernel_factor(*refs):
             factor_kernel(nodes, refs[:pack_count], *refs[pack_count:])
 
-        inverse, scale = call(
-            kernel_factor, [((vecs, vecs), f32), ((vecs, 2 * vecs), f32)], packs
+        inverse, *scale = call(
+            kernel_factor, [((vecs, vecs), f32)] + [((vecs, 2 * vecs), f32)] * last, packs
         )
         if last:
             break
@@ -385,29 +434,35 @@
             limit=limit,
         )
         adj_parts = near_values(held, near)
-        basis, dirs = call(
+        basis, search, square = call(
             basis_kernel,
-            [((3 * vecs, wide), bf16), ((vecs, wide), bf16)],
-            [inverse, scale, stack, mixing, search],
+            [((3 * vecs, wide), bf16), ((vecs, wide), f32), own_out],
+            [inverse, stack, mixing, seeking],
             limit=limit,
         )
         cross, wide_adj = call(
             functools.partial(cross_kernel, nodes, near),
-            [((vecs, 2 * vecs), f32), ((vecs, wide), bf16)],
-            adj_parts + [basis],
+            [pack_out, ((vecs, wide), bf16)],
+            adj_parts + [basis, square],
             limit=limit,
         )
-        state = (panel_terms(cross), basis, wide_adj, dirs)
-
-    rotated = rotated[0]
+        image, = call(
+            ahead_kernel,
+            [((3 * vecs, blocks * edge), f32)],
+            [basis, wide_adj, search, dense],
+            limit=limit,
+        )
+        state = (panel_terms(cross), basis, wide_adj, search, image)
+
+    search, rotated = rest
     terms, = call(terms_kernel, [((vecs, 2 * vecs), f32)], [rotated, rotated_adj])
     far_parts, inverse = lax.optimization_barrier((far_values(terms, near), inverse))
     own_basis, own_dirs, both = call(
         own_kernel,
         [own_out, own_out, ((vecs, 2 * edge), f32)],
-        [inverse, scale, rotated, rotated_adj, search],
-    )
-    terms = panel_terms(sum(near_values(sum(far_parts), near)))
+        [inverse, *scale, rotated, rotated_adj, search],
+    )
+    terms = panel_terms(sum(near_values(sum(far_parts), near)[::-1]))
     count = len(terms)
 
     def kernel_last(*refs):

time: 78.8 us -> 77.7 us (0.986)
    pallas_call x19 -> x21, Pallas kernels: 18.3 us -> 18.2 us  [call(): pl.pallas_call(kernel, out_shape=[jax.ShapeDtypeStruct(shape, kind) for s...]
  transfers between devices with their start and end apart: 33 -> 33, of which waited for: 24 -> 23; matrix products, arithmetic and copies ran while one was open for 0% -> 0% of each run, Pallas kernels for 17% -> 18%
where the time goes in v9:
time: 77.7 us; the launch traced here: 77.4 us
  starting transfers between devices  34.8 us (45%)
  waiting for transfers between devices  20.6 us (27%)
  Pallas kernels  18.2 us (23%)
  local copies, waits for them, and re-layouts  1.93 us (2%)
  other arithmetic  0.89 us (1%)
  between operations  0.88 us (1%)
    ppermute x33, starting transfers between devices, swap(): return lax.ppermute(value, axis, [(i, i ^ by) for i in range(size)])  34.8 us
    ppermute x33, waiting for transfers between devices, swap(): return lax.ppermute(value, axis, [(i, i ^ by) for i in range(size)])  20.6 us
    pallas_call x21, Pallas kernels, call(): pl.pallas_call(kernel, out_shape=[jax.ShapeDtypeStruct(shape, kind) for s...  18.2 us
    unnamed x10, local copies, waits for them, and re-layouts  1.91 us
  transfers between devices with their start and end apart: 33, of which 23 were waited for; matrix products, arithmetic and copies ran while one was open for 0% of the time, Pallas kernels for 18%

profile of v9, /device:TPU:0, one launch (start us, length us, event | category | flops | bytes accessed | tf_op | source)
XLA Modules:
  0.0 77.4 jit_solution(5198713573442740139)
XLA Ops:
  0.6 0.8 maximum_bitcast_fusion
  1.4 5.0 %collective-permute-start.2 = (bf16[1,192,128]{2,1,0:T(8,128)(2,1)S(1)}, bf16[1,192,128]{2,1,0:T(8,128)(2,1)S(1)}, u32[]{:S(2)}, u32[]{:S(2)}) collective-permute-start(bf16[1,192,128]{2,1,0:T(8,128)(2,1)S(1)} %maximum_bitcast_fusion), channel_id=1, source_target_pairs={{0,24},{2,26},{4,28},{6,30},{8,16},{10,18},{12,20},{14,22},{16,8},... | collective-permute-start | bytes 147464 | tf_op jit(solution)/shard_map/ppermute | solution.py:308
  6.4 0.6 collective-permute-start
  7.1 0.7 copy-done.3
  7.8 0.9 %collective-permute-done.2 = bf16[1,192,128]{2,1,0:T(8,128)(2,1)S(1)} collective-permute-done((bf16[1,192,128]{2,1,0:T(8,128)(2,1)S(1)}, bf16[1,192,128]{2,1,0:T(8,128)(2,1)S(1)}, u32[]{:S(2)}, u32[]{:S(2)}) %collective-permute-start.2) | collective-permute-done | bytes 49184 | tf_op jit(solution)/shard_map/ppermute | solution.py:308
  8.7 2.8 %collective-permute-done.1 = bf16[1,192,128]{2,1,0:T(8,128)(2,1)S(1)} collective-permute-done((bf16[1,192,128]{2,1,0:T(8,128)(2,1)S(1)}, bf16[1,192,128]{2,1,0:T(8,128)(2,1)S(1)}, u32[]{:S(2)}, u32[]{:S(2)}) %collective-permute-start.1) | collective-permute-done | bytes 49184 | tf_op jit(solution)/shard_map/ppermute | solution.py:308
  11.5 2.5 %collective-permute-start.3 = (bf16[4,192,128]{2,1,0:T(8,128)(2,1)S(1)}, bf16[4,192,128]{2,1,0:T(8,128)(2,1)S(1)}, u32[]{:S(2)}, u32[]{:S(2)}) collective-permute-start(bf16[4,192,128]{2,1,0:T(8,128)(2,1)S(1)} %pad_maximum_fusion.refs_0_), channel_id=1, source_target_pairs={{0,6},{2,4},{4,2},{6,0},{8,14},{10,12},{12,10},{14,8},{16,22},{18,... | collective-permute-start | bytes 589832 | tf_op jit(solution)/shard_map/ppermute | solution.py:308
  14.0 0.5 collective-permute-start.4
  14.5 0.5 collective-permute-start.5
  15.1 1.2 %copy-done = bf16[1,1,2,16,128,128]{5,4,3,2,1,0:T(8,128)(2,1)S(1)} copy-done((bf16[1,1,2,16,128,128]{5,4,3,2,1,0:T(8,128)(2,1)S(1)}, bf16[1,1,2,16,128,128]{5,4,3,2,1,0:T(8,128)(2,1)}, u32[]{:S(2)}) %copy-start) | copy-done | bytes 1048600
  16.3 1.1 %shard_map.111.dense_ref = bf16[2048,256]{1,0:T(8,128)(2,1)S(1)} custom-call(s32[2,16]{1,0:T(2,128)S(1)} %compare_select_fusion.4.slots_ref, bf16[2,16,128,128]{3,2,1,0:T(8,128)(2,1)S(1)} %bitcast.28), custom_call_target="tpu_custom_call" | custom-call | tf_op jit(solution)/shard_map/pallas_call | solution.py:20
  17.4 2.6 %collective-permute-done.3.refs_1_ = bf16[4,192,128]{2,1,0:T(8,128)(2,1)S(1)} collective-permute-done((bf16[4,192,128]{2,1,0:T(8,128)(2,1)S(1)}, bf16[4,192,128]{2,1,0:T(8,128)(2,1)S(1)}, u32[]{:S(2)}, u32[]{:S(2)}) %collective-permute-start.3) | collective-permute-done | bytes 196640 | tf_op jit(solution)/shard_map/ppermute | solution.py:308
  19.9 2.5 %collective-permute-done.4.refs_2_ = bf16[4,192,128]{2,1,0:T(8,128)(2,1)S(1)} collective-permute-done((bf16[4,192,128]{2,1,0:T(8,128)(2,1)S(1)}, bf16[4,192,128]{2,1,0:T(8,128)(2,1)S(1)}, u32[]{:S(2)}, u32[]{:S(2)}) %collective-permute-start.4) | collective-permute-done | bytes 196640 | tf_op jit(solution)/shard_map/ppermute | solution.py:308
  22.5 0.6 shard_map.112
  23.2 0.7 shard_map.113.refs_0_
  23.9 0.5 collective-permute-done.6
  24.6 1.6 %collective-permute-start.7 = (f32[64,128]{1,0:T(8,128)S(1)}, f32[64,128]{1,0:T(8,128)S(1)}, u32[]{:S(2)}, u32[]{:S(2)}) collective-permute-start(f32[64,128]{1,0:T(8,128)S(1)} %add.44.refs_0_), channel_id=1, source_target_pairs={{0,24},{2,26},{4,28},{6,30},{8,16},{10,18},{12,20},{14,22},{16,8},... | collective-permute-start | bytes 98312 | tf_op jit(solution)/shard_map/ppermute | solution.py:308
  26.1 0.6 collective-permute-start.8
  26.7 2.2 %collective-permute-start.9 = (f32[64,128]{1,0:T(8,128)S(1)}, f32[64,128]{1,0:T(8,128)S(1)}, u32[]{:S(2)}, u32[]{:S(2)}) collective-permute-start(f32[64,128]{1,0:T(8,128)S(1)} %add.44.refs_0_), channel_id=1, source_target_pairs={{0,8},{2,10},{4,12},{6,14},{8,0},{10,2},{12,4},{14,6},{16,24},{18,... | collective-permute-start | bytes 98312 | tf_op jit(solution)/shard_map/ppermute | solution.py:308
  28.9 2.2 %shard_map.114.refs_4_.inverse_ref = f32[64,64]{1,0:T(8,128)S(1)} custom-call(f32[64,128]{1,0:T(8,128)S(1)} %shard_map.113.refs_0_, f32[64,128]{1,0:T(8,128)S(1)} %collective-permute-done.10.refs_1_), custom_call_target="tpu_custom_call" | custom-call | tf_op jit(solution)/shard_map/pallas_call | solution.py:20
  31.1 0.3 collective-permute-done.8.refs_2_
  31.7 1.7 %collective-permute-start.11 = (bf16[256,128]{1,0:T(8,128)(2,1)S(1)}, bf16[256,128]{1,0:T(8,128)(2,1)S(1)}, u32[]{:S(2)}, u32[]{:S(2)}) collective-permute-start(bf16[256,128]{1,0:T(8,128)(2,1)S(1)} %shard_map.115.refs_0_), channel_id=1, source_target_pairs={{0,6},{2,4},{4,2},{6,0},{8,14},{10,12},{12,10},{14,8},{16,22},{18,... | collective-permute-start | bytes 196616 | tf_op jit(solution)/shard_map/ppermute | solution.py:308
  33.4 1.3 %collective-permute-start.12 = (bf16[256,128]{1,0:T(8,128)(2,1)S(1)}, bf16[256,128]{1,0:T(8,128)(2,1)S(1)}, u32[]{:S(2)}, u32[]{:S(2)}) collective-permute-start(bf16[256,128]{1,0:T(8,128)(2,1)S(1)} %shard_map.115.refs_0_), channel_id=1, source_target_pairs={{0,4},{2,6},{4,0},{6,2},{8,12},{10,14},{12,8},{14,10},{16,20},{18,... | collective-permute-start | bytes 196616 | tf_op jit(solution)/shard_map/ppermute | solution.py:308
  34.7 0.5 collective-permute-start.13
  35.3 0.9 %shard_map.116 = (bf16[192,2048]{1,0:T(8,128)(2,1)S(1)}, f32[64,2048]{1,0:T(8,128)S(1)}, f32[64,128]{1,0:T(8,128)S(1)}) custom-call(f32[64,64]{1,0:T(8,128)S(1)} %shard_map.114.refs_4_.inverse_ref, bf16[192,2048]{1,0:T(8,128)(2,1)S(1)} %get-tuple-element.85.stack_ref, f32[64,192]{1,0:T(8,128)S(1)} %get-tuple-element.78.mix_ref, ...), custom_call_target="tpu_custom_call" | custom-call | tf_op jit(solution)/shard_map/pallas_call | solution.py:20
  36.1 0.9 %collective-permute-done.11.refs_1_ = bf16[256,128]{1,0:T(8,128)(2,1)S(1)} collective-permute-done((bf16[256,128]{1,0:T(8,128)(2,1)S(1)}, bf16[256,128]{1,0:T(8,128)(2,1)S(1)}, u32[]{:S(2)}, u32[]{:S(2)}) %collective-permute-start.11) | collective-permute-done | bytes 65568 | tf_op jit(solution)/shard_map/ppermute | solution.py:308
  37.0 1.0 %collective-permute-done.12.refs_2_ = bf16[256,128]{1,0:T(8,128)(2,1)S(1)} collective-permute-done((bf16[256,128]{1,0:T(8,128)(2,1)S(1)}, bf16[256,128]{1,0:T(8,128)(2,1)S(1)}, u32[]{:S(2)}, u32[]{:S(2)}) %collective-permute-start.12) | collective-permute-done | bytes 65568 | tf_op jit(solution)/shard_map/ppermute | solution.py:308
  38.1 1.0 %collective-permute-done.13.refs_3_ = bf16[256,128]{1,0:T(8,128)(2,1)S(1)} collective-permute-done((bf16[256,128]{1,0:T(8,128)(2,1)S(1)}, bf16[256,128]{1,0:T(8,128)(2,1)S(1)}, u32[]{:S(2)}, u32[]{:S(2)}) %collective-permute-start.13) | collective-permute-done | bytes 65568 | tf_op jit(solution)/shard_map/ppermute | solution.py:308
  39.0 0.4 shard_map.117
  39.5 0.4 shard_map.118.refs_2_
  39.9 0.8 %collective-permute-done.14.refs_1_ = f32[64,128]{1,0:T(8,128)S(1)} collective-permute-done((f32[64,128]{1,0:T(8,128)S(1)}, f32[64,128]{1,0:T(8,128)S(1)}, u32[]{:S(2)}, u32[]{:S(2)}) %collective-permute-start.14) | collective-permute-done | bytes 32800 | tf_op jit(solution)/shard_map/ppermute | solution.py:308
  40.7 0.5 shard_map.119
  41.4 1.1 %shard_map.120 = (f32[64,128]{1,0:T(8,128)S(1)}, bf16[192,2048]{1,0:T(8,128)(2,1)S(1)}) custom-call(f32[64,192]{1,0:T(8,128)S(1)} %get-tuple-element.76.m.mix_ref, f32[64,128]{1,0:T(8,128)S(1)} %get-tuple-element.96.refs_0_, f32[64,128]{1,0:T(8,128)S(1)} %collective-permute-done.14.refs_1_, ...), custom_call_target="tpu_custom_call" | custom-call | tf_op jit(solution)/shard_map/pallas_call | solution.py:20
  42.5 0.4 collective-permute-start.19
  42.9 1.7 %collective-permute-start.16 = (f32[64,128]{1,0:T(8,128)S(1)}, f32[64,128]{1,0:T(8,128)S(1)}, u32[]{:S(2)}, u32[]{:S(2)}) collective-permute-start(f32[64,128]{1,0:T(8,128)S(1)} %add.45.refs_0_), channel_id=1, source_target_pairs={{0,24},{2,26},{4,28},{6,30},{8,16},{10,18},{12,20},{14,22},{16,8},... | collective-permute-start | bytes 98312 | tf_op jit(solution)/shard_map/ppermute | solution.py:308
  44.6 1.1 %collective-permute-start.17 = (f32[64,128]{1,0:T(8,128)S(1)}, f32[64,128]{1,0:T(8,128)S(1)}, u32[]{:S(2)}, u32[]{:S(2)}) collective-permute-start(f32[64,128]{1,0:T(8,128)S(1)} %add.45.refs_0_), channel_id=1, source_target_pairs={{0,16},{2,18},{4,20},{6,22},{8,24},{10,26},{12,28},{14,30},{16,0},... | collective-permute-start | bytes 98312 | tf_op jit(solution)/shard_map/ppermute | solution.py:308
  45.8 1.5 %collective-permute-start.18 = (f32[64,128]{1,0:T(8,128)S(1)}, f32[64,128]{1,0:T(8,128)S(1)}, u32[]{:S(2)}, u32[]{:S(2)}) collective-permute-start(f32[64,128]{1,0:T(8,128)S(1)} %add.45.refs_0_), channel_id=1, source_target_pairs={{0,8},{2,10},{4,12},{6,14},{8,0},{10,2},{12,4},{14,6},{16,24},{18,... | collective-permute-start | bytes 98312 | tf_op jit(solution)/shard_map/ppermute | solution.py:308
  47.3 2.2 %shard_map.121.refs_4_.inverse_ref = f32[64,64]{1,0:T(8,128)S(1)} custom-call(f32[64,128]{1,0:T(8,128)S(1)} %get-tuple-element.103.refs_0_, f32[64,128]{1,0:T(8,128)S(1)} %collective-permute-done.19.refs_1_), custom_call_target="tpu_custom_call" | custom-call | tf_op jit(solution)/shard_map/pallas_call | solution.py:20
  49.5 0.3 collective-permute-done.17.refs_2_
  49.8 0.3 collective-permute-done.18.refs_3_
  50.4 1.5 %collective-permute-start.20 = (bf16[256,128]{1,0:T(8,128)(2,1)S(1)}, bf16[256,128]{1,0:T(8,128)(2,1)S(1)}, u32[]{:S(2)}, u32[]{:S(2)}) collective-permute-start(bf16[256,128]{1,0:T(8,128)(2,1)S(1)} %shard_map.122.refs_0_), channel_id=1, source_target_pairs={{0,6},{2,4},{4,2},{6,0},{8,14},{10,12},{12,10},{14,8},{16,22},{18,... | collective-permute-start | bytes 196616 | tf_op jit(solution)/shard_map/ppermute | solution.py:308
  51.8 0.6 collective-permute-start.21
  52.4 1.5 %collective-permute-start.22 = (bf16[256,128]{1,0:T(8,128)(2,1)S(1)}, bf16[256,128]{1,0:T(8,128)(2,1)S(1)}, u32[]{:S(2)}, u32[]{:S(2)}) collective-permute-start(bf16[256,128]{1,0:T(8,128)(2,1)S(1)} %shard_map.122.refs_0_), channel_id=1, source_target_pairs={{0,2},{2,0},{4,6},{6,4},{8,10},{10,8},{12,14},{14,12},{16,18},{18,... | collective-permute-start | bytes 196616 | tf_op jit(solution)/shard_map/ppermute | solution.py:308
  53.9 0.9 %shard_map.123 = (bf16[192,2048]{1,0:T(8,128)(2,1)S(1)}, f32[64,2048]{1,0:T(8,128)S(1)}, f32[64,128]{1,0:T(8,128)S(1)}) custom-call(f32[64,64]{1,0:T(8,128)S(1)} %shard_map.121.refs_4_.inverse_ref, bf16[192,2048]{1,0:T(8,128)(2,1)S(1)} %get-tuple-element.109.stack_ref, f32[64,192]{1,0:T(8,128)S(1)} %get-tuple-element.76.m.mix_ref, ...), custom_call_target="tpu_custom_call" | custom-call | tf_op jit(solution)/shard_map/pallas_call | solution.py:20
  54.8 1.5 %collective-permute-done.20.refs_1_ = bf16[256,128]{1,0:T(8,128)(2,1)S(1)} collective-permute-done((bf16[256,128]{1,0:T(8,128)(2,1)S(1)}, bf16[256,128]{1,0:T(8,128)(2,1)S(1)}, u32[]{:S(2)}, u32[]{:S(2)}) %collective-permute-start.20) | collective-permute-done | bytes 65568 | tf_op jit(solution)/shard_map/ppermute | solution.py:308
  56.7 0.4 shard_map.124
  57.2 0.4 shard_map.126.refs_2_
  57.6 0.8 %collective-permute-done.23.refs_1_ = f32[64,128]{1,0:T(8,128)S(1)} collective-permute-done((f32[64,128]{1,0:T(8,128)S(1)}, f32[64,128]{1,0:T(8,128)S(1)}, u32[]{:S(2)}, u32[]{:S(2)}) %collective-permute-start.23) | collective-permute-done | bytes 32800 | tf_op jit(solution)/shard_map/ppermute | solution.py:308
  58.4 0.5 shard_map.127
  59.1 1.1 %shard_map.125 = (f32[64,128]{1,0:T(8,128)S(1)}, f32[64,128]{1,0:T(8,128)S(1)}, f32[64,128]{1,0:T(8,128)S(1)}) custom-call(f32[64,192]{1,0:T(8,128)S(1)} %get-tuple-element.75.m, f32[64,128]{1,0:T(8,128)S(1)} %get-tuple-element.113.refs_0_, f32[64,128]{1,0:T(8,128)S(1)} %collective-permute-done.23.refs_1_, ...), custom_call_target="tpu_custom_call" | custom-call | tf_op jit(solution)/shard_map/pallas_call | solution.py:20
  60.2 0.4 collective-permute-start.28
  61.0 1.8 %collective-permute-start.25 = (f32[64,128]{1,0:T(8,128)S(1)}, f32[64,128]{1,0:T(8,128)S(1)}, u32[]{:S(2)}, u32[]{:S(2)}) collective-permute-start(f32[64,128]{1,0:T(8,128)S(1)} %shard_map.128), channel_id=1, source_target_pairs={{0,24},{2,26},{4,28},{6,30},{8,16},{10,18},{12,20},{14,22},{16,8},... | collective-permute-start | bytes 98312 | tf_op jit(solution)/shard_map/ppermute | solution.py:308
  62.7 0.9 %collective-permute-start.26 = (f32[64,128]{1,0:T(8,128)S(1)}, f32[64,128]{1,0:T(8,128)S(1)}, u32[]{:S(2)}, u32[]{:S(2)}) collective-permute-start(f32[64,128]{1,0:T(8,128)S(1)} %shard_map.128), channel_id=1, source_target_pairs={{0,16},{2,18},{4,20},{6,22},{8,24},{10,26},{12,28},{14,30},{16,0},... | collective-permute-start | bytes 98312 | tf_op jit(solution)/shard_map/ppermute | solution.py:308
  63.6 1.8 %collective-permute-start.27 = (f32[64,128]{1,0:T(8,128)S(1)}, f32[64,128]{1,0:T(8,128)S(1)}, u32[]{:S(2)}, u32[]{:S(2)}) collective-permute-start(f32[64,128]{1,0:T(8,128)S(1)} %shard_map.128), channel_id=1, source_target_pairs={{0,8},{2,10},{4,12},{6,14},{8,0},{10,2},{12,4},{14,6},{16,24},{18,... | collective-permute-start | bytes 98312 | tf_op jit(solution)/shard_map/ppermute | solution.py:308
  65.4 2.2 %shard_map.129 = (f32[64,64]{1,0:T(8,128)S(1)}, f32[64,128]{1,0:T(8,128)S(1)}) custom-call(f32[64,128]{1,0:T(8,128)S(1)} %get-tuple-element.122.refs_0_, f32[64,128]{1,0:T(8,128)S(1)} %collective-permute-done.28.refs_1_), custom_call_target="tpu_custom_call" | custom-call | tf_op jit(solution)/shard_map/pallas_call | solution.py:20
  68.0 1.7 %collective-permute-start.31 = (f32[64,128]{1,0:T(8,128)S(1)}, f32[64,128]{1,0:T(8,128)S(1)}, u32[]{:S(2)}, u32[]{:S(2)}) collective-permute-start(f32[64,128]{1,0:T(8,128)S(1)} %add_add_fusion.1), channel_id=1, source_target_pairs={{0,6},{2,4},{4,2},{6,0},{8,14},{10,12},{12,10},{14,8},{16,22},{18,... | collective-permute-start | bytes 98312 | tf_op jit(solution)/shard_map/ppermute | solution.py:308
  69.7 1.2 %collective-permute-start.29 = (f32[64,128]{1,0:T(8,128)S(1)}, f32[64,128]{1,0:T(8,128)S(1)}, u32[]{:S(2)}, u32[]{:S(2)}) collective-permute-start(f32[64,128]{1,0:T(8,128)S(1)} %add_add_fusion.1), channel_id=1, source_target_pairs={{0,2},{2,0},{4,6},{6,4},{8,10},{10,8},{12,14},{14,12},{16,18},{18,... | collective-permute-start | bytes 98312 | tf_op jit(solution)/shard_map/ppermute | solution.py:308
  70.9 0.6 collective-permute-start.30
  71.6 1.6 %collective-permute-done.31 = f32[64,128]{1,0:T(8,128)S(1)} collective-permute-done((f32[64,128]{1,0:T(8,128)S(1)}, f32[64,128]{1,0:T(8,128)S(1)}, u32[]{:S(2)}, u32[]{:S(2)}) %collective-permute-start.31) | collective-permute-done | bytes 32800 | tf_op jit(solution)/shard_map/ppermute | solution.py:308
  73.2 0.5 collective-permute-done.29
  73.6 1.2 %collective-permute-done.30 = f32[64,128]{1,0:T(8,128)S(1)} collective-permute-done((f32[64,128]{1,0:T(8,128)S(1)}, f32[64,128]{1,0:T(8,128)S(1)}, u32[]{:S(2)}, u32[]{:S(2)}) %collective-permute-start.30) | collective-permute-done | bytes 32800 | tf_op jit(solution)/shard_map/ppermute | solution.py:308
  74.9 0.8 %shard_map.130 = (f32[64,128]{1,0:T(8,128)}, f32[64,128]{1,0:T(8,128)}, f32[64,256]{1,0:T(8,128)S(1)}) custom-call(f32[64,64]{1,0:T(8,128)S(1)} %get-tuple-element.124.inverse_ref.refs_2_, f32[64,128]{1,0:T(8,128)S(1)} %get-tuple-element.125.scale_ref, f32[64,128]{1,0:T(8,128)S(1)} %get-tuple-element.117.rotated_ref, f32[64,128]{1,0:T(8,128)S(1)} %add.46.adj_ref, ...), custom_call_target="tpu_custom_call" | custom-call | tf_op jit(solution)/shard_map/pallas_call | solution.py:20
  75.8 0.4 collective-permute-done.32.refs_1_
  76.1 1.2 %shard_map.131 = (f32[64,128]{1,0:T(8,128)}, f32[64,64]{1,0:T(8,128)}) custom-call(f32[64,128]{1,0:T(8,128)S(1)} %add_add_fusion.refs_0_, f32[64,128]{1,0:T(8,128)S(1)} %collective-permute-done.32.refs_1_, f32[64,64]{1,0:T(8,128)S(1)} %get-tuple-element.124.inverse_ref.refs_2_, f32[64,256]{1,0:T(8,128)S(1)} %get-tuple-element.132.refs_3_), custom_call_target="tpu_custom_call" | custom-call | tf_op jit(solution)/shard_map/pallas_call | solution.py:20
  (43 shorter events, 2.8 us)
Async XLA Ops:
  1.4 7.3 %collective-permute-start.2 = (bf16[1,192,128]{2,1,0:T(8,128)(2,1)S(1)}, bf16[1,192,128]{2,1,0:T(8,128)(2,1)S(1)}, u32[]{:S(2)}, u32[]{:S(2)}) collective-permute-start(bf16[1,192,128]{2,1,0:T(8,128)(2,1)S(1)} %maximum_bitcast_fusion), channel_id=1, source_target_pairs={{0,24},{2,26},{4,28},{6,30},{8,16},{10,18},{12,20},{14,22},{16,8},... | collective-permute-start | bytes 147464 | tf_op jit(solution)/shard_map/ppermute | solution.py:308
  6.4 5.0 %collective-permute-start.1 = (bf16[1,192,128]{2,1,0:T(8,128)(2,1)S(1)}, bf16[1,192,128]{2,1,0:T(8,128)(2,1)S(1)}, u32[]{:S(2)}, u32[]{:S(2)}) collective-permute-start(bf16[1,192,128]{2,1,0:T(8,128)(2,1)S(1)} %maximum_bitcast_fusion), channel_id=1, source_target_pairs={{0,16},{2,18},{4,20},{6,22},{8,24},{10,26},{12,28},{14,30},{16,0},... | collective-permute-start | bytes 147464 | tf_op jit(solution)/shard_map/ppermute | solution.py:308
  6.4 5.0 %collective-permute-start = (bf16[1,192,128]{2,1,0:T(8,128)(2,1)S(1)}, bf16[1,192,128]{2,1,0:T(8,128)(2,1)S(1)}, u32[]{:S(2)}, u32[]{:S(2)}) collective-permute-start(bf16[1,192,128]{2,1,0:T(8,128)(2,1)S(1)} %maximum_bitcast_fusion), channel_id=1, source_target_pairs={{0,8},{2,10},{4,12},{6,14},{8,0},{10,2},{12,4},{14,6},{16,24},{18,... | collective-permute-start | bytes 147464 | tf_op jit(solution)/shard_map/ppermute | solution.py:308
  7.0 0.7 copy-start.3
  7.1 0.7 copy-start.4
  7.8 7.2 %copy-start.1 = (f32[3,64,192]{2,1,0:T(8,128)S(1)}, f32[3,64,192]{2,1,0:T(8,128)}, u32[]{:S(2)}) copy-start(f32[3,64,192]{2,1,0:T(8,128)} %param.14) | copy-start | bytes 442372
  11.5 8.5 %collective-permute-start.3 = (bf16[4,192,128]{2,1,0:T(8,128)(2,1)S(1)}, bf16[4,192,128]{2,1,0:T(8,128)(2,1)S(1)}, u32[]{:S(2)}, u32[]{:S(2)}) collective-permute-start(bf16[4,192,128]{2,1,0:T(8,128)(2,1)S(1)} %pad_maximum_fusion.refs_0_), channel_id=1, source_target_pairs={{0,6},{2,4},{4,2},{6,0},{8,14},{10,12},{12,10},{14,8},{16,22},{18,... | collective-permute-start | bytes 589832 | tf_op jit(solution)/shard_map/ppermute | solution.py:308
  14.0 8.4 %collective-permute-start.4 = (bf16[4,192,128]{2,1,0:T(8,128)(2,1)S(1)}, bf16[4,192,128]{2,1,0:T(8,128)(2,1)S(1)}, u32[]{:S(2)}, u32[]{:S(2)}) collective-permute-start(bf16[4,192,128]{2,1,0:T(8,128)(2,1)S(1)} %pad_maximum_fusion.refs_0_), channel_id=1, source_target_pairs={{0,4},{2,6},{4,0},{6,2},{8,12},{10,14},{12,8},{14,10},{16,20},{18,... | collective-permute-start | bytes 589832 | tf_op jit(solution)/shard_map/ppermute | solution.py:308
  14.5 8.0 %collective-permute-start.5 = (bf16[4,192,128]{2,1,0:T(8,128)(2,1)S(1)}, bf16[4,192,128]{2,1,0:T(8,128)(2,1)S(1)}, u32[]{:S(2)}, u32[]{:S(2)}) collective-permute-start(bf16[4,192,128]{2,1,0:T(8,128)(2,1)S(1)} %pad_maximum_fusion.refs_0_), channel_id=1, source_target_pairs={{0,2},{2,0},{4,6},{6,4},{8,10},{10,8},{12,14},{14,12},{16,18},{18,... | collective-permute-start | bytes 589832 | tf_op jit(solution)/shard_map/ppermute | solution.py:308
  15.0 1.2 %copy-start = (bf16[1,1,2,16,128,128]{5,4,3,2,1,0:T(8,128)(2,1)S(1)}, bf16[1,1,2,16,128,128]{5,4,3,2,1,0:T(8,128)(2,1)}, u32[]{:S(2)}) copy-start(bf16[1,1,2,16,128,128]{5,4,3,2,1,0:T(8,128)(2,1)} %param.8) | copy-start | bytes 3145732
  16.3 1.1 %copy-start.2 = (f32[3,64,128]{2,1,0:T(8,128)S(1)}, f32[3,64,128]{2,1,0:T(8,128)}, u32[]{:S(2)}) copy-start(f32[3,64,128]{2,1,0:T(8,128)} %param.15) | copy-start | bytes 294916
  23.1 1.3 %collective-permute-start.6 = (f32[64,128]{1,0:T(8,128)S(1)}, f32[64,128]{1,0:T(8,128)S(1)}, u32[]{:S(2)}, u32[]{:S(2)}) collective-permute-start(f32[64,128]{1,0:T(8,128)S(1)} %get-tuple-element.84), channel_id=1, source_target_pairs={{0,1},{1,0},{2,3},{3,2},{4,5},{5,4},{6,7},{7,6},{8,9},{9,8},{10,11... | collective-permute-start | bytes 98312 | tf_op jit(solution)/shard_map/ppermute | solution.py:308
  24.4 4.6 %collective-permute-start.10 = (f32[64,128]{1,0:T(8,128)S(1)}, f32[64,128]{1,0:T(8,128)S(1)}, u32[]{:S(2)}, u32[]{:S(2)}) collective-permute-start(f32[64,128]{1,0:T(8,128)S(1)} %shard_map.113.refs_0_), channel_id=1, source_target_pairs={{0,1},{1,0},{2,3},{3,2},{4,5},{5,4},{6,7},{7,6},{8,9},{9,8},{10,11... | collective-permute-start | bytes 98312 | tf_op jit(solution)/shard_map/ppermute | solution.py:308
  24.6 6.6 %collective-permute-start.7 = (f32[64,128]{1,0:T(8,128)S(1)}, f32[64,128]{1,0:T(8,128)S(1)}, u32[]{:S(2)}, u32[]{:S(2)}) collective-permute-start(f32[64,128]{1,0:T(8,128)S(1)} %add.44.refs_0_), channel_id=1, source_target_pairs={{0,24},{2,26},{4,28},{6,30},{8,16},{10,18},{12,20},{14,22},{16,8},... | collective-permute-start | bytes 98312 | tf_op jit(solution)/shard_map/ppermute | solution.py:308
  26.1 5.3 %collective-permute-start.8 = (f32[64,128]{1,0:T(8,128)S(1)}, f32[64,128]{1,0:T(8,128)S(1)}, u32[]{:S(2)}, u32[]{:S(2)}) collective-permute-start(f32[64,128]{1,0:T(8,128)S(1)} %add.44.refs_0_), channel_id=1, source_target_pairs={{0,16},{2,18},{4,20},{6,22},{8,24},{10,26},{12,28},{14,30},{16,0},... | collective-permute-start | bytes 98312 | tf_op jit(solution)/shard_map/ppermute | solution.py:308
  26.7 4.7 %collective-permute-start.9 = (f32[64,128]{1,0:T(8,128)S(1)}, f32[64,128]{1,0:T(8,128)S(1)}, u32[]{:S(2)}, u32[]{:S(2)}) collective-permute-start(f32[64,128]{1,0:T(8,128)S(1)} %add.44.refs_0_), channel_id=1, source_target_pairs={{0,8},{2,10},{4,12},{6,14},{8,0},{10,2},{12,4},{14,6},{16,24},{18,... | collective-permute-start | bytes 98312 | tf_op jit(solution)/shard_map/ppermute | solution.py:308
  31.7 5.3 %collective-permute-start.11 = (bf16[256,128]{1,0:T(8,128)(2,1)S(1)}, bf16[256,128]{1,0:T(8,128)(2,1)S(1)}, u32[]{:S(2)}, u32[]{:S(2)}) collective-permute-start(bf16[256,128]{1,0:T(8,128)(2,1)S(1)} %shard_map.115.refs_0_), channel_id=1, source_target_pairs={{0,6},{2,4},{4,2},{6,0},{8,14},{10,12},{12,10},{14,8},{16,22},{18,... | collective-permute-start | bytes 196616 | tf_op jit(solution)/shard_map/ppermute | solution.py:308
  33.4 4.6 %collective-permute-start.12 = (bf16[256,128]{1,0:T(8,128)(2,1)S(1)}, bf16[256,128]{1,0:T(8,128)(2,1)S(1)}, u32[]{:S(2)}, u32[]{:S(2)}) collective-permute-start(bf16[256,128]{1,0:T(8,128)(2,1)S(1)} %shard_map.115.refs_0_), channel_id=1, source_target_pairs={{0,4},{2,6},{4,0},{6,2},{8,12},{10,14},{12,8},{14,10},{16,20},{18,... | collective-permute-start | bytes 196616 | tf_op jit(solution)/shard_map/ppermute | solution.py:308
  34.7 4.3 %collective-permute-start.13 = (bf16[256,128]{1,0:T(8,128)(2,1)S(1)}, bf16[256,128]{1,0:T(8,128)(2,1)S(1)}, u32[]{:S(2)}, u32[]{:S(2)}) collective-permute-start(bf16[256,128]{1,0:T(8,128)(2,1)S(1)} %shard_map.115.refs_0_), channel_id=1, source_target_pairs={{0,2},{2,0},{4,6},{6,4},{8,10},{10,8},{12,14},{14,12},{16,18},{18,... | collective-permute-start | bytes 196616 | tf_op jit(solution)/shard_map/ppermute | solution.py:308
  39.4 1.3 %collective-permute-start.14 = (f32[64,128]{1,0:T(8,128)S(1)}, f32[64,128]{1,0:T(8,128)S(1)}, u32[]{:S(2)}, u32[]{:S(2)}) collective-permute-start(f32[64,128]{1,0:T(8,128)S(1)} %get-tuple-element.96.refs_0_), channel_id=1, source_target_pairs={{0,1},{1,0},{2,3},{3,2},{4,5},{5,4},{6,7},{7,6},{8,9},{9,8},{10,11... | collective-permute-start | bytes 98312 | tf_op jit(solution)/shard_map/ppermute | solution.py:308
  41.2 1.3 %collective-permute-start.15 = (f32[64,128]{1,0:T(8,128)S(1)}, f32[64,128]{1,0:T(8,128)S(1)}, u32[]{:S(2)}, u32[]{:S(2)}) collective-permute-start(f32[64,128]{1,0:T(8,128)S(1)} %get-tuple-element.100), channel_id=1, source_target_pairs={{0,1},{1,0},{2,3},{3,2},{4,5},{5,4},{6,7},{7,6},{8,9},{9,8},{10,11... | collective-permute-start | bytes 98312 | tf_op jit(solution)/shard_map/ppermute | solution.py:308
  42.5 4.8 %collective-permute-start.19 = (f32[64,128]{1,0:T(8,128)S(1)}, f32[64,128]{1,0:T(8,128)S(1)}, u32[]{:S(2)}, u32[]{:S(2)}) collective-permute-start(f32[64,128]{1,0:T(8,128)S(1)} %get-tuple-element.103.refs_0_), channel_id=1, source_target_pairs={{0,1},{1,0},{2,3},{3,2},{4,5},{5,4},{6,7},{7,6},{8,9},{9,8},{10,11... | collective-permute-start | bytes 98312 | tf_op jit(solution)/shard_map/ppermute | solution.py:308
  42.9 6.6 %collective-permute-start.16 = (f32[64,128]{1,0:T(8,128)S(1)}, f32[64,128]{1,0:T(8,128)S(1)}, u32[]{:S(2)}, u32[]{:S(2)}) collective-permute-start(f32[64,128]{1,0:T(8,128)S(1)} %add.45.refs_0_), channel_id=1, source_target_pairs={{0,24},{2,26},{4,28},{6,30},{8,16},{10,18},{12,20},{14,22},{16,8},... | collective-permute-start | bytes 98312 | tf_op jit(solution)/shard_map/ppermute | solution.py:308
  44.6 5.2 %collective-permute-start.17 = (f32[64,128]{1,0:T(8,128)S(1)}, f32[64,128]{1,0:T(8,128)S(1)}, u32[]{:S(2)}, u32[]{:S(2)}) collective-permute-start(f32[64,128]{1,0:T(8,128)S(1)} %add.45.refs_0_), channel_id=1, source_target_pairs={{0,16},{2,18},{4,20},{6,22},{8,24},{10,26},{12,28},{14,30},{16,0},... | collective-permute-start | bytes 98312 | tf_op jit(solution)/shard_map/ppermute | solution.py:308
  45.8 4.3 %collective-permute-start.18 = (f32[64,128]{1,0:T(8,128)S(1)}, f32[64,128]{1,0:T(8,128)S(1)}, u32[]{:S(2)}, u32[]{:S(2)}) collective-permute-start(f32[64,128]{1,0:T(8,128)S(1)} %add.45.refs_0_), channel_id=1, source_target_pairs={{0,8},{2,10},{4,12},{6,14},{8,0},{10,2},{12,4},{14,6},{16,24},{18,... | collective-permute-start | bytes 98312 | tf_op jit(solution)/shard_map/ppermute | solution.py:308
  50.4 5.9 %collective-permute-start.20 = (bf16[256,128]{1,0:T(8,128)(2,1)S(1)}, bf16[256,128]{1,0:T(8,128)(2,1)S(1)}, u32[]{:S(2)}, u32[]{:S(2)}) collective-permute-start(bf16[256,128]{1,0:T(8,128)(2,1)S(1)} %shard_map.122.refs_0_), channel_id=1, source_target_pairs={{0,6},{2,4},{4,2},{6,0},{8,14},{10,12},{12,10},{14,8},{16,22},{18,... | collective-permute-start | bytes 196616 | tf_op jit(solution)/shard_map/ppermute | solution.py:308
  51.8 4.7 %collective-permute-start.21 = (bf16[256,128]{1,0:T(8,128)(2,1)S(1)}, bf16[256,128]{1,0:T(8,128)(2,1)S(1)}, u32[]{:S(2)}, u32[]{:S(2)}) collective-permute-start(bf16[256,128]{1,0:T(8,128)(2,1)S(1)} %shard_map.122.refs_0_), channel_id=1, source_target_pairs={{0,4},{2,6},{4,0},{6,2},{8,12},{10,14},{12,8},{14,10},{16,20},{18,... | collective-permute-start | bytes 196616 | tf_op jit(solution)/shard_map/ppermute | solution.py:308
  52.4 4.3 %collective-permute-start.22 = (bf16[256,128]{1,0:T(8,128)(2,1)S(1)}, bf16[256,128]{1,0:T(8,128)(2,1)S(1)}, u32[]{:S(2)}, u32[]{:S(2)}) collective-permute-start(bf16[256,128]{1,0:T(8,128)(2,1)S(1)} %shard_map.122.refs_0_), channel_id=1, source_target_pairs={{0,2},{2,0},{4,6},{6,4},{8,10},{10,8},{12,14},{14,12},{16,18},{18,... | collective-permute-start | bytes 196616 | tf_op jit(solution)/shard_map/ppermute | solution.py:308
  57.1 1.3 %collective-permute-start.23 = (f32[64,128]{1,0:T(8,128)S(1)}, f32[64,128]{1,0:T(8,128)S(1)}, u32[]{:S(2)}, u32[]{:S(2)}) collective-permute-start(f32[64,128]{1,0:T(8,128)S(1)} %get-tuple-element.113.refs_0_), channel_id=1, source_target_pairs={{0,1},{1,0},{2,3},{3,2},{4,5},{5,4},{6,7},{7,6},{8,9},{9,8},{10,11... | collective-permute-start | bytes 98312 | tf_op jit(solution)/shard_map/ppermute | solution.py:308
  58.9 1.4 %collective-permute-start.24 = (f32[64,128]{1,0:T(8,128)S(1)}, f32[64,128]{1,0:T(8,128)S(1)}, u32[]{:S(2)}, u32[]{:S(2)}) collective-permute-start(f32[64,128]{1,0:T(8,128)S(1)} %get-tuple-element.119), channel_id=1, source_target_pairs={{0,1},{1,0},{2,3},{3,2},{4,5},{5,4},{6,7},{7,6},{8,9},{9,8},{10,11... | collective-permute-start | bytes 98312 | tf_op jit(solution)/shard_map/ppermute | solution.py:308
  60.2 5.2 %collective-permute-start.28 = (f32[64,128]{1,0:T(8,128)S(1)}, f32[64,128]{1,0:T(8,128)S(1)}, u32[]{:S(2)}, u32[]{:S(2)}) collective-permute-start(f32[64,128]{1,0:T(8,128)S(1)} %get-tuple-element.122.refs_0_), channel_id=1, source_target_pairs={{0,1},{1,0},{2,3},{3,2},{4,5},{5,4},{6,7},{7,6},{8,9},{9,8},{10,11... | collective-permute-start | bytes 98312 | tf_op jit(solution)/shard_map/ppermute | solution.py:308
  61.0 6.7 %collective-permute-start.25 = (f32[64,128]{1,0:T(8,128)S(1)}, f32[64,128]{1,0:T(8,128)S(1)}, u32[]{:S(2)}, u32[]{:S(2)}) collective-permute-start(f32[64,128]{1,0:T(8,128)S(1)} %shard_map.128), channel_id=1, source_target_pairs={{0,24},{2,26},{4,28},{6,30},{8,16},{10,18},{12,20},{14,22},{16,8},... | collective-permute-start | bytes 98312 | tf_op jit(solution)/shard_map/ppermute | solution.py:308
  62.7 5.0 %collective-permute-start.26 = (f32[64,128]{1,0:T(8,128)S(1)}, f32[64,128]{1,0:T(8,128)S(1)}, u32[]{:S(2)}, u32[]{:S(2)}) collective-permute-start(f32[64,128]{1,0:T(8,128)S(1)} %shard_map.128), channel_id=1, source_target_pairs={{0,16},{2,18},{4,20},{6,22},{8,24},{10,26},{12,28},{14,30},{16,0},... | collective-permute-start | bytes 98312 | tf_op jit(solution)/shard_map/ppermute | solution.py:308
  63.6 4.4 %collective-permute-start.27 = (f32[64,128]{1,0:T(8,128)S(1)}, f32[64,128]{1,0:T(8,128)S(1)}, u32[]{:S(2)}, u32[]{:S(2)}) collective-permute-start(f32[64,128]{1,0:T(8,128)S(1)} %shard_map.128), channel_id=1, source_target_pairs={{0,8},{2,10},{4,12},{6,14},{8,0},{10,2},{12,4},{14,6},{16,24},{18,... | collective-permute-start | bytes 98312 | tf_op jit(solution)/shard_map/ppermute | solution.py:308
  68.0 5.2 %collective-permute-start.31 = (f32[64,128]{1,0:T(8,128)S(1)}, f32[64,128]{1,0:T(8,128)S(1)}, u32[]{:S(2)}, u32[]{:S(2)}) collective-permute-start(f32[64,128]{1,0:T(8,128)S(1)} %add_add_fusion.1), channel_id=1, source_target_pairs={{0,6},{2,4},{4,2},{6,0},{8,14},{10,12},{12,10},{14,8},{16,22},{18,... | collective-permute-start | bytes 98312 | tf_op jit(solution)/shard_map/ppermute | solution.py:308
  69.7 3.9 %collective-permute-start.29 = (f32[64,128]{1,0:T(8,128)S(1)}, f32[64,128]{1,0:T(8,128)S(1)}, u32[]{:S(2)}, u32[]{:S(2)}) collective-permute-start(f32[64,128]{1,0:T(8,128)S(1)} %add_add_fusion.1), channel_id=1, source_target_pairs={{0,2},{2,0},{4,6},{6,4},{8,10},{10,8},{12,14},{14,12},{16,18},{18,... | collective-permute-start | bytes 98312 | tf_op jit(solution)/shard_map/ppermute | solution.py:308
  70.9 3.9 %collective-permute-start.30 = (f32[64,128]{1,0:T(8,128)S(1)}, f32[64,128]{1,0:T(8,128)S(1)}, u32[]{:S(2)}, u32[]{:S(2)}) collective-permute-start(f32[64,128]{1,0:T(8,128)S(1)} %add_add_fusion.1), channel_id=1, source_target_pairs={{0,4},{2,6},{4,0},{6,2},{8,12},{10,14},{12,8},{14,10},{16,20},{18,... | collective-permute-start | bytes 98312 | tf_op jit(solution)/shard_map/ppermute | solution.py:308
  74.9 1.3 %collective-permute-start.32 = (f32[64,128]{1,0:T(8,128)S(1)}, f32[64,128]{1,0:T(8,128)S(1)}, u32[]{:S(2)}, u32[]{:S(2)}) collective-permute-start(f32[64,128]{1,0:T(8,128)S(1)} %add_add_fusion.refs_0_), channel_id=1, source_target_pairs={{0,1},{1,0},{2,3},{3,2},{4,5},{5,4},{6,7},{7,6},{8,9},{9,8},{10,11... | collective-permute-start | bytes 98312 | tf_op jit(solution)/shard_map/ppermute | solution.py:308

commit v10 on v9

--- a/solution.py
+++ b/solution.py
@@ -128,7 +128,15 @@
     vecs = mix_ref.shape[0]
     q, scale, step = cross_terms(crosses)
     basis = image_ref[:vecs]
-    raw = dot_tn(q, basis) - image_ref[vecs : 2 * vecs]
+    q_high, q_low = halves(q)
+    high, low = halves(basis)
+    raw = lax.dot_general(
+        jnp.concatenate([q_high, q_high, q_low], axis=0),
+        jnp.concatenate([high, low, high], axis=0),
+        (((0,), (0,)), ((), ())),
+        preferred_element_type=f32,
+    )
+    raw = raw - image_ref[vecs : 2 * vecs]
     image = jnp.concatenate([basis, raw * scale, image_ref[2 * vecs :] * step], axis=0)
     send_parts(place_ref, mix_ref, image, mine_refs)
 
@@ -342,11 +350,6 @@
     nodes = start_basis.shape[1] * rows * panels
     wide = rows * edge
     near = 4
-    away = columns ^ lax.axis_index("rows")
-    far = rows // near
-    position = (-away % near) * far + -(away // near) % far
-    in_use = jnp.arange(slots, dtype=jnp.int32)[None, :] < counts[:, None]
-    slot_ids = jnp.where(in_use, position, rows).astype(jnp.int32)
     place = lax.axis_index("panel").astype(jnp.int32).reshape(1)
 
     if panels == 2:
@@ -360,9 +363,14 @@
     sweeps = ritz_basis.shape[0]
     first_parts = far_values(start, near)
     held = jnp.concatenate(first_parts[:1] + first_parts[:0:-1], axis=0)
-    held, slot_ids, tile_set, ritz_basis, ritz_search = lax.optimization_barrier(
-        (held, slot_ids, tile_set, ritz_basis, ritz_search)
-    )
+    held, counts, columns, tile_set, ritz_basis, ritz_search = lax.optimization_barrier(
+        (held, counts, columns, tile_set, ritz_basis, ritz_search)
+    )
+    away = columns ^ lax.axis_index("rows")
+    far = rows // near
+    position = (-away % near) * far + -(away // near) % far
+    in_use = jnp.arange(slots, dtype=jnp.int32)[None, :] < counts[:, None]
+    slot_ids = jnp.where(in_use, position, rows).astype(jnp.int32)
     parts = near_values(held, near)
     dense, = call(
         layout_kernel, [((wide, blocks * edge), bf16)], [slot_ids, tile_set], smem=(0,), limit=limit

time: 77.7 us -> 77.7 us (level)
  Pallas kernels: 18.2 us -> 19.3 us
    pallas_call x21, Pallas kernels: 18.2 us -> 19.3 us  [call(): pl.pallas_call(kernel, out_shape=[jax.ShapeDtypeStruct(shape, kind) for s...]
  transfers between devices with their start and end apart: 33 -> 33, of which waited for: 23 -> 23; matrix products, arithmetic and copies ran while one was open for 0% -> 0% of each run, Pallas kernels for 18% -> 20%
where the time goes in v10:
time: 77.7 us; the launch traced here: 77.3 us
  starting transfers between devices  34.8 us (45%)
  waiting for transfers between devices  20.1 us (26%)
  Pallas kernels  19.3 us (25%)
  local copies, waits for them, and re-layouts  1.27 us (2%)
  other arithmetic  0.9 us (1%)
  between operations  0.9 us (1%)
    ppermute x33, starting transfers between devices, swap(): return lax.ppermute(value, axis, [(i, i ^ by) for i in range(size)])  34.8 us
    ppermute x33, waiting for transfers between devices, swap(): return lax.ppermute(value, axis, [(i, i ^ by) for i in range(size)])  20.1 us
    pallas_call x21, Pallas kernels, call(): pl.pallas_call(kernel, out_shape=[jax.ShapeDtypeStruct(shape, kind) for s...  19.3 us
  transfers between devices with their start and end apart: 33, of which 23 were waited for; matrix products, arithmetic and copies ran while one was open for 0% of the time, Pallas kernels for 20%

profile of v10, /device:TPU:0, one launch (start us, length us, event | category | flops | bytes accessed | tf_op | source)
XLA Modules:
  0.0 77.3 jit_solution(3103483607102589863)
XLA Ops:
  0.6 0.8 maximum_bitcast_fusion
  1.4 5.0 %collective-permute-start.2 = (bf16[1,192,128]{2,1,0:T(8,128)(2,1)S(1)}, bf16[1,192,128]{2,1,0:T(8,128)(2,1)S(1)}, u32[]{:S(2)}, u32[]{:S(2)}) collective-permute-start(bf16[1,192,128]{2,1,0:T(8,128)(2,1)S(1)} %maximum_bitcast_fusion), channel_id=1, source_target_pairs={{0,24},{2,26},{4,28},{6,30},{8,16},{10,18},{12,20},{14,22},{16,8},... | collective-permute-start | bytes 147464 | tf_op jit(solution)/shard_map/ppermute | solution.py:316
  6.4 0.6 collective-permute-start
  7.1 1.6 %collective-permute-done.2 = bf16[1,192,128]{2,1,0:T(8,128)(2,1)S(1)} collective-permute-done((bf16[1,192,128]{2,1,0:T(8,128)(2,1)S(1)}, bf16[1,192,128]{2,1,0:T(8,128)(2,1)S(1)}, u32[]{:S(2)}, u32[]{:S(2)}) %collective-permute-start.2) | collective-permute-done | bytes 49184 | tf_op jit(solution)/shard_map/ppermute | solution.py:316
  8.7 2.8 %collective-permute-done.1 = bf16[1,192,128]{2,1,0:T(8,128)(2,1)S(1)} collective-permute-done((bf16[1,192,128]{2,1,0:T(8,128)(2,1)S(1)}, bf16[1,192,128]{2,1,0:T(8,128)(2,1)S(1)}, u32[]{:S(2)}, u32[]{:S(2)}) %collective-permute-start.1) | collective-permute-done | bytes 49184 | tf_op jit(solution)/shard_map/ppermute | solution.py:316
  11.5 2.5 %collective-permute-start.3 = (bf16[4,192,128]{2,1,0:T(8,128)(2,1)S(1)}, bf16[4,192,128]{2,1,0:T(8,128)(2,1)S(1)}, u32[]{:S(2)}, u32[]{:S(2)}) collective-permute-start(bf16[4,192,128]{2,1,0:T(8,128)(2,1)S(1)} %pad_maximum_fusion.refs_0_), channel_id=1, source_target_pairs={{0,6},{2,4},{4,2},{6,0},{8,14},{10,12},{12,10},{14,8},{16,22},{18,... | collective-permute-start | bytes 589832 | tf_op jit(solution)/shard_map/ppermute | solution.py:316
  14.0 0.5 collective-permute-start.4
  14.5 0.5 collective-permute-start.5
  15.2 1.2 %copy-done = bf16[1,1,2,16,128,128]{5,4,3,2,1,0:T(8,128)(2,1)S(1)} copy-done((bf16[1,1,2,16,128,128]{5,4,3,2,1,0:T(8,128)(2,1)S(1)}, bf16[1,1,2,16,128,128]{5,4,3,2,1,0:T(8,128)(2,1)}, u32[]{:S(2)}) %copy-start) | copy-done | bytes 1048600
  16.4 2.2 %shard_map.111.dense_ref = bf16[2048,256]{1,0:T(8,128)(2,1)S(1)} custom-call(s32[2,16]{1,0:T(2,128)S(1)} %compare_select_fusion.4.slots_ref, bf16[2,16,128,128]{3,2,1,0:T(8,128)(2,1)S(1)} %bitcast.18), custom_call_target="tpu_custom_call" | custom-call | tf_op jit(solution)/shard_map/pallas_call | solution.py:20
  18.7 1.3 %collective-permute-done.3.refs_1_ = bf16[4,192,128]{2,1,0:T(8,128)(2,1)S(1)} collective-permute-done((bf16[4,192,128]{2,1,0:T(8,128)(2,1)S(1)}, bf16[4,192,128]{2,1,0:T(8,128)(2,1)S(1)}, u32[]{:S(2)}, u32[]{:S(2)}) %collective-permute-start.3) | collective-permute-done | bytes 196640 | tf_op jit(solution)/shard_map/ppermute | solution.py:316
  20.0 2.5 %collective-permute-done.4.refs_2_ = bf16[4,192,128]{2,1,0:T(8,128)(2,1)S(1)} collective-permute-done((bf16[4,192,128]{2,1,0:T(8,128)(2,1)S(1)}, bf16[4,192,128]{2,1,0:T(8,128)(2,1)S(1)}, u32[]{:S(2)}, u32[]{:S(2)}) %collective-permute-start.4) | collective-permute-done | bytes 196640 | tf_op jit(solution)/shard_map/ppermute | solution.py:316
  22.5 0.6 shard_map.112
  23.2 0.7 shard_map.113.refs_0_
  23.9 0.5 collective-permute-done.6
  24.6 1.6 %collective-permute-start.7 = (f32[64,128]{1,0:T(8,128)S(1)}, f32[64,128]{1,0:T(8,128)S(1)}, u32[]{:S(2)}, u32[]{:S(2)}) collective-permute-start(f32[64,128]{1,0:T(8,128)S(1)} %add.44.refs_0_), channel_id=1, source_target_pairs={{0,24},{2,26},{4,28},{6,30},{8,16},{10,18},{12,20},{14,22},{16,8},... | collective-permute-start | bytes 98312 | tf_op jit(solution)/shard_map/ppermute | solution.py:316
  26.2 0.6 collective-permute-start.8
  26.7 2.2 %collective-permute-start.9 = (f32[64,128]{1,0:T(8,128)S(1)}, f32[64,128]{1,0:T(8,128)S(1)}, u32[]{:S(2)}, u32[]{:S(2)}) collective-permute-start(f32[64,128]{1,0:T(8,128)S(1)} %add.44.refs_0_), channel_id=1, source_target_pairs={{0,8},{2,10},{4,12},{6,14},{8,0},{10,2},{12,4},{14,6},{16,24},{18,... | collective-permute-start | bytes 98312 | tf_op jit(solution)/shard_map/ppermute | solution.py:316
  29.0 2.2 %shard_map.114.refs_4_.inverse_ref = f32[64,64]{1,0:T(8,128)S(1)} custom-call(f32[64,128]{1,0:T(8,128)S(1)} %shard_map.113.refs_0_, f32[64,128]{1,0:T(8,128)S(1)} %collective-permute-done.10.refs_1_), custom_call_target="tpu_custom_call" | custom-call | tf_op jit(solution)/shard_map/pallas_call | solution.py:20
  31.2 0.3 collective-permute-done.8.refs_2_
  31.7 1.7 %collective-permute-start.11 = (bf16[256,128]{1,0:T(8,128)(2,1)S(1)}, bf16[256,128]{1,0:T(8,128)(2,1)S(1)}, u32[]{:S(2)}, u32[]{:S(2)}) collective-permute-start(bf16[256,128]{1,0:T(8,128)(2,1)S(1)} %shard_map.115.refs_0_), channel_id=1, source_target_pairs={{0,6},{2,4},{4,2},{6,0},{8,14},{10,12},{12,10},{14,8},{16,22},{18,... | collective-permute-start | bytes 196616 | tf_op jit(solution)/shard_map/ppermute | solution.py:316
  33.5 1.3 %collective-permute-start.12 = (bf16[256,128]{1,0:T(8,128)(2,1)S(1)}, bf16[256,128]{1,0:T(8,128)(2,1)S(1)}, u32[]{:S(2)}, u32[]{:S(2)}) collective-permute-start(bf16[256,128]{1,0:T(8,128)(2,1)S(1)} %shard_map.115.refs_0_), channel_id=1, source_target_pairs={{0,4},{2,6},{4,0},{6,2},{8,12},{10,14},{12,8},{14,10},{16,20},{18,... | collective-permute-start | bytes 196616 | tf_op jit(solution)/shard_map/ppermute | solution.py:316
  34.8 0.5 collective-permute-start.13
  35.3 0.9 %shard_map.116 = (bf16[192,2048]{1,0:T(8,128)(2,1)S(1)}, f32[64,2048]{1,0:T(8,128)S(1)}, f32[64,128]{1,0:T(8,128)S(1)}) custom-call(f32[64,64]{1,0:T(8,128)S(1)} %shard_map.114.refs_4_.inverse_ref, bf16[192,2048]{1,0:T(8,128)(2,1)S(1)} %get-tuple-element.87.stack_ref, f32[64,192]{1,0:T(8,128)S(1)} %get-tuple-element.80.mix_ref, ...), custom_call_target="tpu_custom_call" | custom-call | tf_op jit(solution)/shard_map/pallas_call | solution.py:20
  36.2 0.9 %collective-permute-done.11.refs_1_ = bf16[256,128]{1,0:T(8,128)(2,1)S(1)} collective-permute-done((bf16[256,128]{1,0:T(8,128)(2,1)S(1)}, bf16[256,128]{1,0:T(8,128)(2,1)S(1)}, u32[]{:S(2)}, u32[]{:S(2)}) %collective-permute-start.11) | collective-permute-done | bytes 65568 | tf_op jit(solution)/shard_map/ppermute | solution.py:316
  37.1 1.0 %collective-permute-done.12.refs_2_ = bf16[256,128]{1,0:T(8,128)(2,1)S(1)} collective-permute-done((bf16[256,128]{1,0:T(8,128)(2,1)S(1)}, bf16[256,128]{1,0:T(8,128)(2,1)S(1)}, u32[]{:S(2)}, u32[]{:S(2)}) %collective-permute-start.12) | collective-permute-done | bytes 65568 | tf_op jit(solution)/shard_map/ppermute | solution.py:316
  38.1 1.0 %collective-permute-done.13.refs_3_ = bf16[256,128]{1,0:T(8,128)(2,1)S(1)} collective-permute-done((bf16[256,128]{1,0:T(8,128)(2,1)S(1)}, bf16[256,128]{1,0:T(8,128)(2,1)S(1)}, u32[]{:S(2)}, u32[]{:S(2)}) %collective-permute-start.13) | collective-permute-done | bytes 65568 | tf_op jit(solution)/shard_map/ppermute | solution.py:316
  39.0 0.4 shard_map.117
  39.5 0.4 shard_map.118.refs_2_
  39.9 0.8 %collective-permute-done.14.refs_1_ = f32[64,128]{1,0:T(8,128)S(1)} collective-permute-done((f32[64,128]{1,0:T(8,128)S(1)}, f32[64,128]{1,0:T(8,128)S(1)}, u32[]{:S(2)}, u32[]{:S(2)}) %collective-permute-start.14) | collective-permute-done | bytes 32800 | tf_op jit(solution)/shard_map/ppermute | solution.py:316
  40.7 0.4 shard_map.119
  41.4 1.1 %shard_map.120 = (f32[64,128]{1,0:T(8,128)S(1)}, bf16[192,2048]{1,0:T(8,128)(2,1)S(1)}) custom-call(f32[64,192]{1,0:T(8,128)S(1)} %get-tuple-element.78.m.mix_ref, f32[64,128]{1,0:T(8,128)S(1)} %get-tuple-element.98.refs_0_, f32[64,128]{1,0:T(8,128)S(1)} %collective-permute-done.14.refs_1_, ...), custom_call_target="tpu_custom_call" | custom-call | tf_op jit(solution)/shard_map/pallas_call | solution.py:20
  42.5 0.4 collective-permute-start.19
  42.9 1.7 %collective-permute-start.16 = (f32[64,128]{1,0:T(8,128)S(1)}, f32[64,128]{1,0:T(8,128)S(1)}, u32[]{:S(2)}, u32[]{:S(2)}) collective-permute-start(f32[64,128]{1,0:T(8,128)S(1)} %add.45.refs_0_), channel_id=1, source_target_pairs={{0,24},{2,26},{4,28},{6,30},{8,16},{10,18},{12,20},{14,22},{16,8},... | collective-permute-start | bytes 98312 | tf_op jit(solution)/shard_map/ppermute | solution.py:316
  44.6 1.1 %collective-permute-start.17 = (f32[64,128]{1,0:T(8,128)S(1)}, f32[64,128]{1,0:T(8,128)S(1)}, u32[]{:S(2)}, u32[]{:S(2)}) collective-permute-start(f32[64,128]{1,0:T(8,128)S(1)} %add.45.refs_0_), channel_id=1, source_target_pairs={{0,16},{2,18},{4,20},{6,22},{8,24},{10,26},{12,28},{14,30},{16,0},... | collective-permute-start | bytes 98312 | tf_op jit(solution)/shard_map/ppermute | solution.py:316
  45.8 1.5 %collective-permute-start.18 = (f32[64,128]{1,0:T(8,128)S(1)}, f32[64,128]{1,0:T(8,128)S(1)}, u32[]{:S(2)}, u32[]{:S(2)}) collective-permute-start(f32[64,128]{1,0:T(8,128)S(1)} %add.45.refs_0_), channel_id=1, source_target_pairs={{0,8},{2,10},{4,12},{6,14},{8,0},{10,2},{12,4},{14,6},{16,24},{18,... | collective-permute-start | bytes 98312 | tf_op jit(solution)/shard_map/ppermute | solution.py:316
  47.3 2.2 %shard_map.121.refs_4_.inverse_ref = f32[64,64]{1,0:T(8,128)S(1)} custom-call(f32[64,128]{1,0:T(8,128)S(1)} %get-tuple-element.105.refs_0_, f32[64,128]{1,0:T(8,128)S(1)} %collective-permute-done.19.refs_1_), custom_call_target="tpu_custom_call" | custom-call | tf_op jit(solution)/shard_map/pallas_call | solution.py:20
  49.5 0.3 collective-permute-done.17.refs_2_
  49.8 0.3 collective-permute-done.18.refs_3_
  50.4 1.5 %collective-permute-start.20 = (bf16[256,128]{1,0:T(8,128)(2,1)S(1)}, bf16[256,128]{1,0:T(8,128)(2,1)S(1)}, u32[]{:S(2)}, u32[]{:S(2)}) collective-permute-start(bf16[256,128]{1,0:T(8,128)(2,1)S(1)} %shard_map.122.refs_0_), channel_id=1, source_target_pairs={{0,6},{2,4},{4,2},{6,0},{8,14},{10,12},{12,10},{14,8},{16,22},{18,... | collective-permute-start | bytes 196616 | tf_op jit(solution)/shard_map/ppermute | solution.py:316
  51.8 0.6 collective-permute-start.21
  52.4 1.5 %collective-permute-start.22 = (bf16[256,128]{1,0:T(8,128)(2,1)S(1)}, bf16[256,128]{1,0:T(8,128)(2,1)S(1)}, u32[]{:S(2)}, u32[]{:S(2)}) collective-permute-start(bf16[256,128]{1,0:T(8,128)(2,1)S(1)} %shard_map.122.refs_0_), channel_id=1, source_target_pairs={{0,2},{2,0},{4,6},{6,4},{8,10},{10,8},{12,14},{14,12},{16,18},{18,... | collective-permute-start | bytes 196616 | tf_op jit(solution)/shard_map/ppermute | solution.py:316
  53.9 0.8 %shard_map.123 = (bf16[192,2048]{1,0:T(8,128)(2,1)S(1)}, f32[64,2048]{1,0:T(8,128)S(1)}, f32[64,128]{1,0:T(8,128)S(1)}) custom-call(f32[64,64]{1,0:T(8,128)S(1)} %shard_map.121.refs_4_.inverse_ref, bf16[192,2048]{1,0:T(8,128)(2,1)S(1)} %get-tuple-element.111.stack_ref, f32[64,192]{1,0:T(8,128)S(1)} %get-tuple-element.78.m.mix_ref, ...), custom_call_target="tpu_custom_call" | custom-call | tf_op jit(solution)/shard_map/pallas_call | solution.py:20
  54.8 1.5 %collective-permute-done.20.refs_1_ = bf16[256,128]{1,0:T(8,128)(2,1)S(1)} collective-permute-done((bf16[256,128]{1,0:T(8,128)(2,1)S(1)}, bf16[256,128]{1,0:T(8,128)(2,1)S(1)}, u32[]{:S(2)}, u32[]{:S(2)}) %collective-permute-start.20) | collective-permute-done | bytes 65568 | tf_op jit(solution)/shard_map/ppermute | solution.py:316
  56.7 0.4 shard_map.124
  57.2 0.4 shard_map.126.refs_2_
  57.6 0.8 %collective-permute-done.23.refs_1_ = f32[64,128]{1,0:T(8,128)S(1)} collective-permute-done((f32[64,128]{1,0:T(8,128)S(1)}, f32[64,128]{1,0:T(8,128)S(1)}, u32[]{:S(2)}, u32[]{:S(2)}) %collective-permute-start.23) | collective-permute-done | bytes 32800 | tf_op jit(solution)/shard_map/ppermute | solution.py:316
  58.4 0.4 shard_map.127
  59.1 1.1 %shard_map.125 = (f32[64,128]{1,0:T(8,128)S(1)}, f32[64,128]{1,0:T(8,128)S(1)}, f32[64,128]{1,0:T(8,128)S(1)}) custom-call(f32[64,192]{1,0:T(8,128)S(1)} %get-tuple-element.77.m, f32[64,128]{1,0:T(8,128)S(1)} %get-tuple-element.115.refs_0_, f32[64,128]{1,0:T(8,128)S(1)} %collective-permute-done.23.refs_1_, ...), custom_call_target="tpu_custom_call" | custom-call | tf_op jit(solution)/shard_map/pallas_call | solution.py:20
  60.2 0.4 collective-permute-start.28
  60.6 0.3 shard_map.128
  60.9 1.8 %collective-permute-start.25 = (f32[64,128]{1,0:T(8,128)S(1)}, f32[64,128]{1,0:T(8,128)S(1)}, u32[]{:S(2)}, u32[]{:S(2)}) collective-permute-start(f32[64,128]{1,0:T(8,128)S(1)} %shard_map.128), channel_id=1, source_target_pairs={{0,24},{2,26},{4,28},{6,30},{8,16},{10,18},{12,20},{14,22},{16,8},... | collective-permute-start | bytes 98312 | tf_op jit(solution)/shard_map/ppermute | solution.py:316
  62.7 0.9 %collective-permute-start.26 = (f32[64,128]{1,0:T(8,128)S(1)}, f32[64,128]{1,0:T(8,128)S(1)}, u32[]{:S(2)}, u32[]{:S(2)}) collective-permute-start(f32[64,128]{1,0:T(8,128)S(1)} %shard_map.128), channel_id=1, source_target_pairs={{0,16},{2,18},{4,20},{6,22},{8,24},{10,26},{12,28},{14,30},{16,0},... | collective-permute-start | bytes 98312 | tf_op jit(solution)/shard_map/ppermute | solution.py:316
  63.5 1.8 %collective-permute-start.27 = (f32[64,128]{1,0:T(8,128)S(1)}, f32[64,128]{1,0:T(8,128)S(1)}, u32[]{:S(2)}, u32[]{:S(2)}) collective-permute-start(f32[64,128]{1,0:T(8,128)S(1)} %shard_map.128), channel_id=1, source_target_pairs={{0,8},{2,10},{4,12},{6,14},{8,0},{10,2},{12,4},{14,6},{16,24},{18,... | collective-permute-start | bytes 98312 | tf_op jit(solution)/shard_map/ppermute | solution.py:316
  65.4 2.2 %shard_map.129 = (f32[64,64]{1,0:T(8,128)S(1)}, f32[64,128]{1,0:T(8,128)S(1)}) custom-call(f32[64,128]{1,0:T(8,128)S(1)} %get-tuple-element.124.refs_0_, f32[64,128]{1,0:T(8,128)S(1)} %collective-permute-done.28.refs_1_), custom_call_target="tpu_custom_call" | custom-call | tf_op jit(solution)/shard_map/pallas_call | solution.py:20
  67.9 1.7 %collective-permute-start.31 = (f32[64,128]{1,0:T(8,128)S(1)}, f32[64,128]{1,0:T(8,128)S(1)}, u32[]{:S(2)}, u32[]{:S(2)}) collective-permute-start(f32[64,128]{1,0:T(8,128)S(1)} %add_add_fusion.1), channel_id=1, source_target_pairs={{0,6},{2,4},{4,2},{6,0},{8,14},{10,12},{12,10},{14,8},{16,22},{18,... | collective-permute-start | bytes 98312 | tf_op jit(solution)/shard_map/ppermute | solution.py:316
  69.6 1.2 %collective-permute-start.29 = (f32[64,128]{1,0:T(8,128)S(1)}, f32[64,128]{1,0:T(8,128)S(1)}, u32[]{:S(2)}, u32[]{:S(2)}) collective-permute-start(f32[64,128]{1,0:T(8,128)S(1)} %add_add_fusion.1), channel_id=1, source_target_pairs={{0,2},{2,0},{4,6},{6,4},{8,10},{10,8},{12,14},{14,12},{16,18},{18,... | collective-permute-start | bytes 98312 | tf_op jit(solution)/shard_map/ppermute | solution.py:316
  70.9 0.6 collective-permute-start.30
  71.5 1.6 %collective-permute-done.31 = f32[64,128]{1,0:T(8,128)S(1)} collective-permute-done((f32[64,128]{1,0:T(8,128)S(1)}, f32[64,128]{1,0:T(8,128)S(1)}, u32[]{:S(2)}, u32[]{:S(2)}) %collective-permute-start.31) | collective-permute-done | bytes 32800 | tf_op jit(solution)/shard_map/ppermute | solution.py:316
  73.1 0.5 collective-permute-done.29
  73.5 1.2 %collective-permute-done.30 = f32[64,128]{1,0:T(8,128)S(1)} collective-permute-done((f32[64,128]{1,0:T(8,128)S(1)}, f32[64,128]{1,0:T(8,128)S(1)}, u32[]{:S(2)}, u32[]{:S(2)}) %collective-permute-start.30) | collective-permute-done | bytes 32800 | tf_op jit(solution)/shard_map/ppermute | solution.py:316
  74.9 0.8 %shard_map.130 = (f32[64,128]{1,0:T(8,128)}, f32[64,128]{1,0:T(8,128)}, f32[64,256]{1,0:T(8,128)S(1)}) custom-call(f32[64,64]{1,0:T(8,128)S(1)} %get-tuple-element.126.inverse_ref.refs_2_, f32[64,128]{1,0:T(8,128)S(1)} %get-tuple-element.127.scale_ref, f32[64,128]{1,0:T(8,128)S(1)} %get-tuple-element.119.rotated_ref, f32[64,128]{1,0:T(8,128)S(1)} %add.46.adj_ref, ...), custom_call_target="tpu_custom_call" | custom-call | tf_op jit(solution)/shard_map/pallas_call | solution.py:20
  75.7 0.4 collective-permute-done.32.refs_1_
  76.1 1.2 %shard_map.131 = (f32[64,128]{1,0:T(8,128)}, f32[64,64]{1,0:T(8,128)}) custom-call(f32[64,128]{1,0:T(8,128)S(1)} %add_add_fusion.refs_0_, f32[64,128]{1,0:T(8,128)S(1)} %collective-permute-done.32.refs_1_, f32[64,64]{1,0:T(8,128)S(1)} %get-tuple-element.126.inverse_ref.refs_2_, f32[64,256]{1,0:T(8,128)S(1)} %get-tuple-element.134.refs_3_), custom_call_target="tpu_custom_call" | custom-call | tf_op jit(solution)/shard_map/pallas_call | solution.py:20
  (43 shorter events, 2.5 us)
Async XLA Ops:
  1.4 7.3 %collective-permute-start.2 = (bf16[1,192,128]{2,1,0:T(8,128)(2,1)S(1)}, bf16[1,192,128]{2,1,0:T(8,128)(2,1)S(1)}, u32[]{:S(2)}, u32[]{:S(2)}) collective-permute-start(bf16[1,192,128]{2,1,0:T(8,128)(2,1)S(1)} %maximum_bitcast_fusion), channel_id=1, source_target_pairs={{0,24},{2,26},{4,28},{6,30},{8,16},{10,18},{12,20},{14,22},{16,8},... | collective-permute-start | bytes 147464 | tf_op jit(solution)/shard_map/ppermute | solution.py:316
  6.4 5.0 %collective-permute-start.1 = (bf16[1,192,128]{2,1,0:T(8,128)(2,1)S(1)}, bf16[1,192,128]{2,1,0:T(8,128)(2,1)S(1)}, u32[]{:S(2)}, u32[]{:S(2)}) collective-permute-start(bf16[1,192,128]{2,1,0:T(8,128)(2,1)S(1)} %maximum_bitcast_fusion), channel_id=1, source_target_pairs={{0,16},{2,18},{4,20},{6,22},{8,24},{10,26},{12,28},{14,30},{16,0},... | collective-permute-start | bytes 147464 | tf_op jit(solution)/shard_map/ppermute | solution.py:316
  6.4 5.0 %collective-permute-start = (bf16[1,192,128]{2,1,0:T(8,128)(2,1)S(1)}, bf16[1,192,128]{2,1,0:T(8,128)(2,1)S(1)}, u32[]{:S(2)}, u32[]{:S(2)}) collective-permute-start(bf16[1,192,128]{2,1,0:T(8,128)(2,1)S(1)} %maximum_bitcast_fusion), channel_id=1, source_target_pairs={{0,8},{2,10},{4,12},{6,14},{8,0},{10,2},{12,4},{14,6},{16,24},{18,... | collective-permute-start | bytes 147464 | tf_op jit(solution)/shard_map/ppermute | solution.py:316
  7.0 8.0 %copy-start.1 = (f32[3,64,192]{2,1,0:T(8,128)S(1)}, f32[3,64,192]{2,1,0:T(8,128)}, u32[]{:S(2)}) copy-start(f32[3,64,192]{2,1,0:T(8,128)} %param.14) | copy-start | bytes 442372
  11.5 3.6 %copy-start.3 = (s32[1,1,2,16]{3,2,1,0:T(2,128)S(1)}, s32[1,1,2,16]{3,2,1,0:T(2,128)}, u32[]{:S(2)}) copy-start(s32[1,1,2,16]{3,2,1,0:T(2,128)} %param.10) | copy-start | bytes 388
  11.5 3.6 %copy-start.4 = (s32[1,1,2]{2,1,0:T(1,128)S(1)}, s32[1,1,2]{2,1,0:T(1,128)}, u32[]{:S(2)}) copy-start(s32[1,1,2]{2,1,0:T(1,128)} %param.9) | copy-start | bytes 28
  11.5 8.5 %collective-permute-start.3 = (bf16[4,192,128]{2,1,0:T(8,128)(2,1)S(1)}, bf16[4,192,128]{2,1,0:T(8,128)(2,1)S(1)}, u32[]{:S(2)}, u32[]{:S(2)}) collective-permute-start(bf16[4,192,128]{2,1,0:T(8,128)(2,1)S(1)} %pad_maximum_fusion.refs_0_), channel_id=1, source_target_pairs={{0,6},{2,4},{4,2},{6,0},{8,14},{10,12},{12,10},{14,8},{16,22},{18,... | collective-permute-start | bytes 589832 | tf_op jit(solution)/shard_map/ppermute | solution.py:316
  14.0 8.4 %collective-permute-start.4 = (bf16[4,192,128]{2,1,0:T(8,128)(2,1)S(1)}, bf16[4,192,128]{2,1,0:T(8,128)(2,1)S(1)}, u32[]{:S(2)}, u32[]{:S(2)}) collective-permute-start(bf16[4,192,128]{2,1,0:T(8,128)(2,1)S(1)} %pad_maximum_fusion.refs_0_), channel_id=1, source_target_pairs={{0,4},{2,6},{4,0},{6,2},{8,12},{10,14},{12,8},{14,10},{16,20},{18,... | collective-permute-start | bytes 589832 | tf_op jit(solution)/shard_map/ppermute | solution.py:316
  14.5 8.0 %collective-permute-start.5 = (bf16[4,192,128]{2,1,0:T(8,128)(2,1)S(1)}, bf16[4,192,128]{2,1,0:T(8,128)(2,1)S(1)}, u32[]{:S(2)}, u32[]{:S(2)}) collective-permute-start(bf16[4,192,128]{2,1,0:T(8,128)(2,1)S(1)} %pad_maximum_fusion.refs_0_), channel_id=1, source_target_pairs={{0,2},{2,0},{4,6},{6,4},{8,10},{10,8},{12,14},{14,12},{16,18},{18,... | collective-permute-start | bytes 589832 | tf_op jit(solution)/shard_map/ppermute | solution.py:316
  15.2 1.2 %copy-start = (bf16[1,1,2,16,128,128]{5,4,3,2,1,0:T(8,128)(2,1)S(1)}, bf16[1,1,2,16,128,128]{5,4,3,2,1,0:T(8,128)(2,1)}, u32[]{:S(2)}) copy-start(bf16[1,1,2,16,128,128]{5,4,3,2,1,0:T(8,128)(2,1)} %param.8) | copy-start | bytes 3145732
  16.4 2.3 %copy-start.2 = (f32[3,64,128]{2,1,0:T(8,128)S(1)}, f32[3,64,128]{2,1,0:T(8,128)}, u32[]{:S(2)}) copy-start(f32[3,64,128]{2,1,0:T(8,128)} %param.15) | copy-start | bytes 294916
  23.1 1.3 %collective-permute-start.6 = (f32[64,128]{1,0:T(8,128)S(1)}, f32[64,128]{1,0:T(8,128)S(1)}, u32[]{:S(2)}, u32[]{:S(2)}) collective-permute-start(f32[64,128]{1,0:T(8,128)S(1)} %get-tuple-element.86), channel_id=1, source_target_pairs={{0,1},{1,0},{2,3},{3,2},{4,5},{5,4},{6,7},{7,6},{8,9},{9,8},{10,11... | collective-permute-start | bytes 98312 | tf_op jit(solution)/shard_map/ppermute | solution.py:316
  24.4 4.6 %collective-permute-start.10 = (f32[64,128]{1,0:T(8,128)S(1)}, f32[64,128]{1,0:T(8,128)S(1)}, u32[]{:S(2)}, u32[]{:S(2)}) collective-permute-start(f32[64,128]{1,0:T(8,128)S(1)} %shard_map.113.refs_0_), channel_id=1, source_target_pairs={{0,1},{1,0},{2,3},{3,2},{4,5},{5,4},{6,7},{7,6},{8,9},{9,8},{10,11... | collective-permute-start | bytes 98312 | tf_op jit(solution)/shard_map/ppermute | solution.py:316
  24.6 6.6 %collective-permute-start.7 = (f32[64,128]{1,0:T(8,128)S(1)}, f32[64,128]{1,0:T(8,128)S(1)}, u32[]{:S(2)}, u32[]{:S(2)}) collective-permute-start(f32[64,128]{1,0:T(8,128)S(1)} %add.44.refs_0_), channel_id=1, source_target_pairs={{0,24},{2,26},{4,28},{6,30},{8,16},{10,18},{12,20},{14,22},{16,8},... | collective-permute-start | bytes 98312 | tf_op jit(solution)/shard_map/ppermute | solution.py:316
  26.2 5.3 %collective-permute-start.8 = (f32[64,128]{1,0:T(8,128)S(1)}, f32[64,128]{1,0:T(8,128)S(1)}, u32[]{:S(2)}, u32[]{:S(2)}) collective-permute-start(f32[64,128]{1,0:T(8,128)S(1)} %add.44.refs_0_), channel_id=1, source_target_pairs={{0,16},{2,18},{4,20},{6,22},{8,24},{10,26},{12,28},{14,30},{16,0},... | collective-permute-start | bytes 98312 | tf_op jit(solution)/shard_map/ppermute | solution.py:316
  26.7 4.7 %collective-permute-start.9 = (f32[64,128]{1,0:T(8,128)S(1)}, f32[64,128]{1,0:T(8,128)S(1)}, u32[]{:S(2)}, u32[]{:S(2)}) collective-permute-start(f32[64,128]{1,0:T(8,128)S(1)} %add.44.refs_0_), channel_id=1, source_target_pairs={{0,8},{2,10},{4,12},{6,14},{8,0},{10,2},{12,4},{14,6},{16,24},{18,... | collective-permute-start | bytes 98312 | tf_op jit(solution)/shard_map/ppermute | solution.py:316
  31.7 5.3 %collective-permute-start.11 = (bf16[256,128]{1,0:T(8,128)(2,1)S(1)}, bf16[256,128]{1,0:T(8,128)(2,1)S(1)}, u32[]{:S(2)}, u32[]{:S(2)}) collective-permute-start(bf16[256,128]{1,0:T(8,128)(2,1)S(1)} %shard_map.115.refs_0_), channel_id=1, source_target_pairs={{0,6},{2,4},{4,2},{6,0},{8,14},{10,12},{12,10},{14,8},{16,22},{18,... | collective-permute-start | bytes 196616 | tf_op jit(solution)/shard_map/ppermute | solution.py:316
  33.5 4.6 %collective-permute-start.12 = (bf16[256,128]{1,0:T(8,128)(2,1)S(1)}, bf16[256,128]{1,0:T(8,128)(2,1)S(1)}, u32[]{:S(2)}, u32[]{:S(2)}) collective-permute-start(bf16[256,128]{1,0:T(8,128)(2,1)S(1)} %shard_map.115.refs_0_), channel_id=1, source_target_pairs={{0,4},{2,6},{4,0},{6,2},{8,12},{10,14},{12,8},{14,10},{16,20},{18,... | collective-permute-start | bytes 196616 | tf_op jit(solution)/shard_map/ppermute | solution.py:316
  34.8 4.3 %collective-permute-start.13 = (bf16[256,128]{1,0:T(8,128)(2,1)S(1)}, bf16[256,128]{1,0:T(8,128)(2,1)S(1)}, u32[]{:S(2)}, u32[]{:S(2)}) collective-permute-start(bf16[256,128]{1,0:T(8,128)(2,1)S(1)} %shard_map.115.refs_0_), channel_id=1, source_target_pairs={{0,2},{2,0},{4,6},{6,4},{8,10},{10,8},{12,14},{14,12},{16,18},{18,... | collective-permute-start | bytes 196616 | tf_op jit(solution)/shard_map/ppermute | solution.py:316
  39.5 1.3 %collective-permute-start.14 = (f32[64,128]{1,0:T(8,128)S(1)}, f32[64,128]{1,0:T(8,128)S(1)}, u32[]{:S(2)}, u32[]{:S(2)}) collective-permute-start(f32[64,128]{1,0:T(8,128)S(1)} %get-tuple-element.98.refs_0_), channel_id=1, source_target_pairs={{0,1},{1,0},{2,3},{3,2},{4,5},{5,4},{6,7},{7,6},{8,9},{9,8},{10,11... | collective-permute-start | bytes 98312 | tf_op jit(solution)/shard_map/ppermute | solution.py:316
  41.2 1.3 %collective-permute-start.15 = (f32[64,128]{1,0:T(8,128)S(1)}, f32[64,128]{1,0:T(8,128)S(1)}, u32[]{:S(2)}, u32[]{:S(2)}) collective-permute-start(f32[64,128]{1,0:T(8,128)S(1)} %get-tuple-element.102), channel_id=1, source_target_pairs={{0,1},{1,0},{2,3},{3,2},{4,5},{5,4},{6,7},{7,6},{8,9},{9,8},{10,11... | collective-permute-start | bytes 98312 | tf_op jit(solution)/shard_map/ppermute | solution.py:316
  42.5 4.8 %collective-permute-start.19 = (f32[64,128]{1,0:T(8,128)S(1)}, f32[64,128]{1,0:T(8,128)S(1)}, u32[]{:S(2)}, u32[]{:S(2)}) collective-permute-start(f32[64,128]{1,0:T(8,128)S(1)} %get-tuple-element.105.refs_0_), channel_id=1, source_target_pairs={{0,1},{1,0},{2,3},{3,2},{4,5},{5,4},{6,7},{7,6},{8,9},{9,8},{10,11... | collective-permute-start | bytes 98312 | tf_op jit(solution)/shard_map/ppermute | solution.py:316
  42.9 6.6 %collective-permute-start.16 = (f32[64,128]{1,0:T(8,128)S(1)}, f32[64,128]{1,0:T(8,128)S(1)}, u32[]{:S(2)}, u32[]{:S(2)}) collective-permute-start(f32[64,128]{1,0:T(8,128)S(1)} %add.45.refs_0_), channel_id=1, source_target_pairs={{0,24},{2,26},{4,28},{6,30},{8,16},{10,18},{12,20},{14,22},{16,8},... | collective-permute-start | bytes 98312 | tf_op jit(solution)/shard_map/ppermute | solution.py:316
  44.6 5.2 %collective-permute-start.17 = (f32[64,128]{1,0:T(8,128)S(1)}, f32[64,128]{1,0:T(8,128)S(1)}, u32[]{:S(2)}, u32[]{:S(2)}) collective-permute-start(f32[64,128]{1,0:T(8,128)S(1)} %add.45.refs_0_), channel_id=1, source_target_pairs={{0,16},{2,18},{4,20},{6,22},{8,24},{10,26},{12,28},{14,30},{16,0},... | collective-permute-start | bytes 98312 | tf_op jit(solution)/shard_map/ppermute | solution.py:316
  45.8 4.3 %collective-permute-start.18 = (f32[64,128]{1,0:T(8,128)S(1)}, f32[64,128]{1,0:T(8,128)S(1)}, u32[]{:S(2)}, u32[]{:S(2)}) collective-permute-start(f32[64,128]{1,0:T(8,128)S(1)} %add.45.refs_0_), channel_id=1, source_target_pairs={{0,8},{2,10},{4,12},{6,14},{8,0},{10,2},{12,4},{14,6},{16,24},{18,... | collective-permute-start | bytes 98312 | tf_op jit(solution)/shard_map/ppermute | solution.py:316
  50.4 5.9 %collective-permute-start.20 = (bf16[256,128]{1,0:T(8,128)(2,1)S(1)}, bf16[256,128]{1,0:T(8,128)(2,1)S(1)}, u32[]{:S(2)}, u32[]{:S(2)}) collective-permute-start(bf16[256,128]{1,0:T(8,128)(2,1)S(1)} %shard_map.122.refs_0_), channel_id=1, source_target_pairs={{0,6},{2,4},{4,2},{6,0},{8,14},{10,12},{12,10},{14,8},{16,22},{18,... | collective-permute-start | bytes 196616 | tf_op jit(solution)/shard_map/ppermute | solution.py:316
  51.8 4.7 %collective-permute-start.21 = (bf16[256,128]{1,0:T(8,128)(2,1)S(1)}, bf16[256,128]{1,0:T(8,128)(2,1)S(1)}, u32[]{:S(2)}, u32[]{:S(2)}) collective-permute-start(bf16[256,128]{1,0:T(8,128)(2,1)S(1)} %shard_map.122.refs_0_), channel_id=1, source_target_pairs={{0,4},{2,6},{4,0},{6,2},{8,12},{10,14},{12,8},{14,10},{16,20},{18,... | collective-permute-start | bytes 196616 | tf_op jit(solution)/shard_map/ppermute | solution.py:316
  52.4 4.3 %collective-permute-start.22 = (bf16[256,128]{1,0:T(8,128)(2,1)S(1)}, bf16[256,128]{1,0:T(8,128)(2,1)S(1)}, u32[]{:S(2)}, u32[]{:S(2)}) collective-permute-start(bf16[256,128]{1,0:T(8,128)(2,1)S(1)} %shard_map.122.refs_0_), channel_id=1, source_target_pairs={{0,2},{2,0},{4,6},{6,4},{8,10},{10,8},{12,14},{14,12},{16,18},{18,... | collective-permute-start | bytes 196616 | tf_op jit(solution)/shard_map/ppermute | solution.py:316
  57.1 1.3 %collective-permute-start.23 = (f32[64,128]{1,0:T(8,128)S(1)}, f32[64,128]{1,0:T(8,128)S(1)}, u32[]{:S(2)}, u32[]{:S(2)}) collective-permute-start(f32[64,128]{1,0:T(8,128)S(1)} %get-tuple-element.115.refs_0_), channel_id=1, source_target_pairs={{0,1},{1,0},{2,3},{3,2},{4,5},{5,4},{6,7},{7,6},{8,9},{9,8},{10,11... | collective-permute-start | bytes 98312 | tf_op jit(solution)/shard_map/ppermute | solution.py:316
  58.8 1.4 %collective-permute-start.24 = (f32[64,128]{1,0:T(8,128)S(1)}, f32[64,128]{1,0:T(8,128)S(1)}, u32[]{:S(2)}, u32[]{:S(2)}) collective-permute-start(f32[64,128]{1,0:T(8,128)S(1)} %get-tuple-element.121), channel_id=1, source_target_pairs={{0,1},{1,0},{2,3},{3,2},{4,5},{5,4},{6,7},{7,6},{8,9},{9,8},{10,11... | collective-permute-start | bytes 98312 | tf_op jit(solution)/shard_map/ppermute | solution.py:316
  60.2 5.2 %collective-permute-start.28 = (f32[64,128]{1,0:T(8,128)S(1)}, f32[64,128]{1,0:T(8,128)S(1)}, u32[]{:S(2)}, u32[]{:S(2)}) collective-permute-start(f32[64,128]{1,0:T(8,128)S(1)} %get-tuple-element.124.refs_0_), channel_id=1, source_target_pairs={{0,1},{1,0},{2,3},{3,2},{4,5},{5,4},{6,7},{7,6},{8,9},{9,8},{10,11... | collective-permute-start | bytes 98312 | tf_op jit(solution)/shard_map/ppermute | solution.py:316
  60.9 6.7 %collective-permute-start.25 = (f32[64,128]{1,0:T(8,128)S(1)}, f32[64,128]{1,0:T(8,128)S(1)}, u32[]{:S(2)}, u32[]{:S(2)}) collective-permute-start(f32[64,128]{1,0:T(8,128)S(1)} %shard_map.128), channel_id=1, source_target_pairs={{0,24},{2,26},{4,28},{6,30},{8,16},{10,18},{12,20},{14,22},{16,8},... | collective-permute-start | bytes 98312 | tf_op jit(solution)/shard_map/ppermute | solution.py:316
  62.7 5.0 %collective-permute-start.26 = (f32[64,128]{1,0:T(8,128)S(1)}, f32[64,128]{1,0:T(8,128)S(1)}, u32[]{:S(2)}, u32[]{:S(2)}) collective-permute-start(f32[64,128]{1,0:T(8,128)S(1)} %shard_map.128), channel_id=1, source_target_pairs={{0,16},{2,18},{4,20},{6,22},{8,24},{10,26},{12,28},{14,30},{16,0},... | collective-permute-start | bytes 98312 | tf_op jit(solution)/shard_map/ppermute | solution.py:316
  63.5 4.4 %collective-permute-start.27 = (f32[64,128]{1,0:T(8,128)S(1)}, f32[64,128]{1,0:T(8,128)S(1)}, u32[]{:S(2)}, u32[]{:S(2)}) collective-permute-start(f32[64,128]{1,0:T(8,128)S(1)} %shard_map.128), channel_id=1, source_target_pairs={{0,8},{2,10},{4,12},{6,14},{8,0},{10,2},{12,4},{14,6},{16,24},{18,... | collective-permute-start | bytes 98312 | tf_op jit(solution)/shard_map/ppermute | solution.py:316
  67.9 5.1 %collective-permute-start.31 = (f32[64,128]{1,0:T(8,128)S(1)}, f32[64,128]{1,0:T(8,128)S(1)}, u32[]{:S(2)}, u32[]{:S(2)}) collective-permute-start(f32[64,128]{1,0:T(8,128)S(1)} %add_add_fusion.1), channel_id=1, source_target_pairs={{0,6},{2,4},{4,2},{6,0},{8,14},{10,12},{12,10},{14,8},{16,22},{18,... | collective-permute-start | bytes 98312 | tf_op jit(solution)/shard_map/ppermute | solution.py:316
  69.6 3.9 %collective-permute-start.29 = (f32[64,128]{1,0:T(8,128)S(1)}, f32[64,128]{1,0:T(8,128)S(1)}, u32[]{:S(2)}, u32[]{:S(2)}) collective-permute-start(f32[64,128]{1,0:T(8,128)S(1)} %add_add_fusion.1), channel_id=1, source_target_pairs={{0,2},{2,0},{4,6},{6,4},{8,10},{10,8},{12,14},{14,12},{16,18},{18,... | collective-permute-start | bytes 98312 | tf_op jit(solution)/shard_map/ppermute | solution.py:316
  70.9 3.9 %collective-permute-start.30 = (f32[64,128]{1,0:T(8,128)S(1)}, f32[64,128]{1,0:T(8,128)S(1)}, u32[]{:S(2)}, u32[]{:S(2)}) collective-permute-start(f32[64,128]{1,0:T(8,128)S(1)} %add_add_fusion.1), channel_id=1, source_target_pairs={{0,4},{2,6},{4,0},{6,2},{8,12},{10,14},{12,8},{14,10},{16,20},{18,... | collective-permute-start | bytes 98312 | tf_op jit(solution)/shard_map/ppermute | solution.py:316
  74.8 1.3 %collective-permute-start.32 = (f32[64,128]{1,0:T(8,128)S(1)}, f32[64,128]{1,0:T(8,128)S(1)}, u32[]{:S(2)}, u32[]{:S(2)}) collective-permute-start(f32[64,128]{1,0:T(8,128)S(1)} %add_add_fusion.refs_0_), channel_id=1, source_target_pairs={{0,1},{1,0},{2,3},{3,2},{4,5},{5,4},{6,7},{7,6},{8,9},{9,8},{10,11... | collective-permute-start | bytes 98312 | tf_op jit(solution)/shard_map/ppermute | solution.py:316

commit v11 on v10

--- a/solution.py
+++ b/solution.py
@@ -253,7 +253,7 @@
     search_ref[...] = search
     square_ref[...] = jnp.broadcast_to(jnp.sum(search * search, axis=1, keepdims=True), square_ref.shape)
     basis = times_stack(dot_nn(inverse_ref[...], mix_ref[...]), stack_ref[...])
-    basis_ref[...] = pieces(basis)
+    basis_ref[...] = jnp.concatenate(halves(basis), axis=0)
 
 
 def terms_kernel(rotated_ref, adj_ref, terms_ref):
@@ -303,7 +303,7 @@
     cross = lax.dot_general(
         basis_ref[...], wide_ref[...], (((1,), (1,)), ((), ())), preferred_element_type=f32
     )
-    cross = cross[:vecs] + cross[vecs : 2 * vecs] + cross[2 * vecs :]
+    cross = cross[:vecs] + cross[vecs:]
     values = wide_ref[...].astype(f32)
     square = jnp.sum(values * values, axis=1, keepdims=True)
     half = (vecs, vecs // 2)
@@ -444,7 +444,7 @@
         adj_parts = near_values(held, near)
         basis, search, square = call(
             basis_kernel,
-            [((3 * vecs, wide), bf16), ((vecs, wide), f32), own_out],
+            [((2 * vecs, wide), bf16), ((vecs, wide), f32), own_out],
             [inverse, stack, mixing, seeking],
             limit=limit,
         )

time: 77.7 us -> 77.5 us (level)
  Pallas kernels: 19.3 us -> 18.1 us
  waiting for transfers between devices: 20.1 us -> 21.1 us
    pallas_call x21, Pallas kernels: 19.3 us -> 18.1 us  [call(): pl.pallas_call(kernel, out_shape=[jax.ShapeDtypeStruct(shape, kind) for s...]
    ppermute x33, waiting for transfers between devices: 20.1 us -> 21.1 us  [swap(): return lax.ppermute(value, axis, [(i, i ^ by) for i in range(size)])]
  transfers between devices with their start and end apart: 33 -> 33, of which waited for: 23 -> 23; matrix products, arithmetic and copies ran while one was open for 0% -> 0% of each run, Pallas kernels for 20% -> 19%
where the time goes in v11:
time: 77.5 us; the launch traced here: 77.1 us
  starting transfers between devices  34.8 us (45%)
  waiting for transfers between devices  21.1 us (27%)
  Pallas kernels  18.1 us (23%)
  local copies, waits for them, and re-layouts  1.27 us (2%)
  other arithmetic  0.9 us (1%)
  between operations  0.9 us (1%)
    ppermute x33, starting transfers between devices, swap(): return lax.ppermute(value, axis, [(i, i ^ by) for i in range(size)])  34.8 us
    ppermute x33, waiting for transfers between devices, swap(): return lax.ppermute(value, axis, [(i, i ^ by) for i in range(size)])  21.1 us
    pallas_call x21, Pallas kernels, call(): pl.pallas_call(kernel, out_shape=[jax.ShapeDtypeStruct(shape, kind) for s...  18.1 us
  transfers between devices with their start and end apart: 33, of which 23 were waited for; matrix products, arithmetic and copies ran while one was open for 0% of the time, Pallas kernels for 19%

profile of v11, /device:TPU:0, one launch (start us, length us, event | category | flops | bytes accessed | tf_op | source)
XLA Modules:
  0.0 77.1 jit_solution(10572692588271850564)
XLA Ops:
  0.6 0.8 maximum_bitcast_fusion
  1.4 5.0 %collective-permute-start.2 = (bf16[1,192,128]{2,1,0:T(8,128)(2,1)S(1)}, bf16[1,192,128]{2,1,0:T(8,128)(2,1)S(1)}, u32[]{:S(2)}, u32[]{:S(2)}) collective-permute-start(bf16[1,192,128]{2,1,0:T(8,128)(2,1)S(1)} %maximum_bitcast_fusion), channel_id=1, source_target_pairs={{0,24},{2,26},{4,28},{6,30},{8,16},{10,18},{12,20},{14,22},{16,8},... | collective-permute-start | bytes 147464 | tf_op jit(solution)/shard_map/ppermute | solution.py:316
  6.4 0.6 collective-permute-start
  7.1 1.6 %collective-permute-done.2 = bf16[1,192,128]{2,1,0:T(8,128)(2,1)S(1)} collective-permute-done((bf16[1,192,128]{2,1,0:T(8,128)(2,1)S(1)}, bf16[1,192,128]{2,1,0:T(8,128)(2,1)S(1)}, u32[]{:S(2)}, u32[]{:S(2)}) %collective-permute-start.2) | collective-permute-done | bytes 49184 | tf_op jit(solution)/shard_map/ppermute | solution.py:316
  8.7 2.8 %collective-permute-done.1 = bf16[1,192,128]{2,1,0:T(8,128)(2,1)S(1)} collective-permute-done((bf16[1,192,128]{2,1,0:T(8,128)(2,1)S(1)}, bf16[1,192,128]{2,1,0:T(8,128)(2,1)S(1)}, u32[]{:S(2)}, u32[]{:S(2)}) %collective-permute-start.1) | collective-permute-done | bytes 49184 | tf_op jit(solution)/shard_map/ppermute | solution.py:316
  11.5 2.5 %collective-permute-start.3 = (bf16[4,192,128]{2,1,0:T(8,128)(2,1)S(1)}, bf16[4,192,128]{2,1,0:T(8,128)(2,1)S(1)}, u32[]{:S(2)}, u32[]{:S(2)}) collective-permute-start(bf16[4,192,128]{2,1,0:T(8,128)(2,1)S(1)} %pad_maximum_fusion.refs_0_), channel_id=1, source_target_pairs={{0,6},{2,4},{4,2},{6,0},{8,14},{10,12},{12,10},{14,8},{16,22},{18,... | collective-permute-start | bytes 589832 | tf_op jit(solution)/shard_map/ppermute | solution.py:316
  14.0 0.5 collective-permute-start.4
  14.5 0.5 collective-permute-start.5
  15.2 1.2 %copy-done = bf16[1,1,2,16,128,128]{5,4,3,2,1,0:T(8,128)(2,1)S(1)} copy-done((bf16[1,1,2,16,128,128]{5,4,3,2,1,0:T(8,128)(2,1)S(1)}, bf16[1,1,2,16,128,128]{5,4,3,2,1,0:T(8,128)(2,1)}, u32[]{:S(2)}) %copy-start) | copy-done | bytes 1048600
  16.4 1.2 %shard_map.111.dense_ref = bf16[2048,256]{1,0:T(8,128)(2,1)S(1)} custom-call(s32[2,16]{1,0:T(2,128)S(1)} %compare_select_fusion.4.slots_ref, bf16[2,16,128,128]{3,2,1,0:T(8,128)(2,1)S(1)} %bitcast.18), custom_call_target="tpu_custom_call" | custom-call | tf_op jit(solution)/shard_map/pallas_call | solution.py:20
  17.7 2.3 %collective-permute-done.3.refs_1_ = bf16[4,192,128]{2,1,0:T(8,128)(2,1)S(1)} collective-permute-done((bf16[4,192,128]{2,1,0:T(8,128)(2,1)S(1)}, bf16[4,192,128]{2,1,0:T(8,128)(2,1)S(1)}, u32[]{:S(2)}, u32[]{:S(2)}) %collective-permute-start.3) | collective-permute-done | bytes 196640 | tf_op jit(solution)/shard_map/ppermute | solution.py:316
  20.0 2.5 %collective-permute-done.4.refs_2_ = bf16[4,192,128]{2,1,0:T(8,128)(2,1)S(1)} collective-permute-done((bf16[4,192,128]{2,1,0:T(8,128)(2,1)S(1)}, bf16[4,192,128]{2,1,0:T(8,128)(2,1)S(1)}, u32[]{:S(2)}, u32[]{:S(2)}) %collective-permute-start.4) | collective-permute-done | bytes 196640 | tf_op jit(solution)/shard_map/ppermute | solution.py:316
  22.5 0.6 shard_map.112
  23.2 0.7 shard_map.113.refs_0_
  23.9 0.5 collective-permute-done.6
  24.6 1.6 %collective-permute-start.7 = (f32[64,128]{1,0:T(8,128)S(1)}, f32[64,128]{1,0:T(8,128)S(1)}, u32[]{:S(2)}, u32[]{:S(2)}) collective-permute-start(f32[64,128]{1,0:T(8,128)S(1)} %add.44.refs_0_), channel_id=1, source_target_pairs={{0,24},{2,26},{4,28},{6,30},{8,16},{10,18},{12,20},{14,22},{16,8},... | collective-permute-start | bytes 98312 | tf_op jit(solution)/shard_map/ppermute | solution.py:316
  26.2 0.6 collective-permute-start.8
  26.7 2.2 %collective-permute-start.9 = (f32[64,128]{1,0:T(8,128)S(1)}, f32[64,128]{1,0:T(8,128)S(1)}, u32[]{:S(2)}, u32[]{:S(2)}) collective-permute-start(f32[64,128]{1,0:T(8,128)S(1)} %add.44.refs_0_), channel_id=1, source_target_pairs={{0,8},{2,10},{4,12},{6,14},{8,0},{10,2},{12,4},{14,6},{16,24},{18,... | collective-permute-start | bytes 98312 | tf_op jit(solution)/shard_map/ppermute | solution.py:316
  29.0 2.2 %shard_map.114.refs_4_.inverse_ref = f32[64,64]{1,0:T(8,128)S(1)} custom-call(f32[64,128]{1,0:T(8,128)S(1)} %shard_map.113.refs_0_, f32[64,128]{1,0:T(8,128)S(1)} %collective-permute-done.10.refs_1_), custom_call_target="tpu_custom_call" | custom-call | tf_op jit(solution)/shard_map/pallas_call | solution.py:20
  31.2 0.3 collective-permute-done.8.refs_2_
  31.7 1.7 %collective-permute-start.11 = (bf16[256,128]{1,0:T(8,128)(2,1)S(1)}, bf16[256,128]{1,0:T(8,128)(2,1)S(1)}, u32[]{:S(2)}, u32[]{:S(2)}) collective-permute-start(bf16[256,128]{1,0:T(8,128)(2,1)S(1)} %shard_map.115.refs_0_), channel_id=1, source_target_pairs={{0,6},{2,4},{4,2},{6,0},{8,14},{10,12},{12,10},{14,8},{16,22},{18,... | collective-permute-start | bytes 196616 | tf_op jit(solution)/shard_map/ppermute | solution.py:316
  33.5 1.3 %collective-permute-start.12 = (bf16[256,128]{1,0:T(8,128)(2,1)S(1)}, bf16[256,128]{1,0:T(8,128)(2,1)S(1)}, u32[]{:S(2)}, u32[]{:S(2)}) collective-permute-start(bf16[256,128]{1,0:T(8,128)(2,1)S(1)} %shard_map.115.refs_0_), channel_id=1, source_target_pairs={{0,4},{2,6},{4,0},{6,2},{8,12},{10,14},{12,8},{14,10},{16,20},{18,... | collective-permute-start | bytes 196616 | tf_op jit(solution)/shard_map/ppermute | solution.py:316
  34.8 0.5 collective-permute-start.13
  35.3 0.8 %shard_map.116 = (bf16[128,2048]{1,0:T(8,128)(2,1)S(1)}, f32[64,2048]{1,0:T(8,128)S(1)}, f32[64,128]{1,0:T(8,128)S(1)}) custom-call(f32[64,64]{1,0:T(8,128)S(1)} %shard_map.114.refs_4_.inverse_ref, bf16[192,2048]{1,0:T(8,128)(2,1)S(1)} %get-tuple-element.87.stack_ref, f32[64,192]{1,0:T(8,128)S(1)} %get-tuple-element.80.mix_ref, ...), custom_call_target="tpu_custom_call" | custom-call | tf_op jit(solution)/shard_map/pallas_call | solution.py:20
  36.1 0.9 %collective-permute-done.11.refs_1_ = bf16[256,128]{1,0:T(8,128)(2,1)S(1)} collective-permute-done((bf16[256,128]{1,0:T(8,128)(2,1)S(1)}, bf16[256,128]{1,0:T(8,128)(2,1)S(1)}, u32[]{:S(2)}, u32[]{:S(2)}) %collective-permute-start.11) | collective-permute-done | bytes 65568 | tf_op jit(solution)/shard_map/ppermute | solution.py:316
  37.1 1.0 %collective-permute-done.12.refs_2_ = bf16[256,128]{1,0:T(8,128)(2,1)S(1)} collective-permute-done((bf16[256,128]{1,0:T(8,128)(2,1)S(1)}, bf16[256,128]{1,0:T(8,128)(2,1)S(1)}, u32[]{:S(2)}, u32[]{:S(2)}) %collective-permute-start.12) | collective-permute-done | bytes 65568 | tf_op jit(solution)/shard_map/ppermute | solution.py:316
  38.1 1.0 %collective-permute-done.13.refs_3_ = bf16[256,128]{1,0:T(8,128)(2,1)S(1)} collective-permute-done((bf16[256,128]{1,0:T(8,128)(2,1)S(1)}, bf16[256,128]{1,0:T(8,128)(2,1)S(1)}, u32[]{:S(2)}, u32[]{:S(2)}) %collective-permute-start.13) | collective-permute-done | bytes 65568 | tf_op jit(solution)/shard_map/ppermute | solution.py:316
  39.0 0.3 shard_map.117
  39.5 0.4 shard_map.118.refs_2_
  39.8 0.8 %collective-permute-done.14.refs_1_ = f32[64,128]{1,0:T(8,128)S(1)} collective-permute-done((f32[64,128]{1,0:T(8,128)S(1)}, f32[64,128]{1,0:T(8,128)S(1)}, u32[]{:S(2)}, u32[]{:S(2)}) %collective-permute-start.14) | collective-permute-done | bytes 32800 | tf_op jit(solution)/shard_map/ppermute | solution.py:316
  40.6 0.4 shard_map.119
  41.3 1.1 %shard_map.120 = (f32[64,128]{1,0:T(8,128)S(1)}, bf16[192,2048]{1,0:T(8,128)(2,1)S(1)}) custom-call(f32[64,192]{1,0:T(8,128)S(1)} %get-tuple-element.78.m.mix_ref, f32[64,128]{1,0:T(8,128)S(1)} %get-tuple-element.98.refs_0_, f32[64,128]{1,0:T(8,128)S(1)} %collective-permute-done.14.refs_1_, ...), custom_call_target="tpu_custom_call" | custom-call | tf_op jit(solution)/shard_map/pallas_call | solution.py:20
  42.4 0.4 collective-permute-start.19
  42.8 1.7 %collective-permute-start.16 = (f32[64,128]{1,0:T(8,128)S(1)}, f32[64,128]{1,0:T(8,128)S(1)}, u32[]{:S(2)}, u32[]{:S(2)}) collective-permute-start(f32[64,128]{1,0:T(8,128)S(1)} %add.45.refs_0_), channel_id=1, source_target_pairs={{0,24},{2,26},{4,28},{6,30},{8,16},{10,18},{12,20},{14,22},{16,8},... | collective-permute-start | bytes 98312 | tf_op jit(solution)/shard_map/ppermute | solution.py:316
  44.5 1.1 %collective-permute-start.17 = (f32[64,128]{1,0:T(8,128)S(1)}, f32[64,128]{1,0:T(8,128)S(1)}, u32[]{:S(2)}, u32[]{:S(2)}) collective-permute-start(f32[64,128]{1,0:T(8,128)S(1)} %add.45.refs_0_), channel_id=1, source_target_pairs={{0,16},{2,18},{4,20},{6,22},{8,24},{10,26},{12,28},{14,30},{16,0},... | collective-permute-start | bytes 98312 | tf_op jit(solution)/shard_map/ppermute | solution.py:316
  45.7 1.5 %collective-permute-start.18 = (f32[64,128]{1,0:T(8,128)S(1)}, f32[64,128]{1,0:T(8,128)S(1)}, u32[]{:S(2)}, u32[]{:S(2)}) collective-permute-start(f32[64,128]{1,0:T(8,128)S(1)} %add.45.refs_0_), channel_id=1, source_target_pairs={{0,8},{2,10},{4,12},{6,14},{8,0},{10,2},{12,4},{14,6},{16,24},{18,... | collective-permute-start | bytes 98312 | tf_op jit(solution)/shard_map/ppermute | solution.py:316
  47.2 2.2 %shard_map.121.refs_4_.inverse_ref = f32[64,64]{1,0:T(8,128)S(1)} custom-call(f32[64,128]{1,0:T(8,128)S(1)} %get-tuple-element.105.refs_0_, f32[64,128]{1,0:T(8,128)S(1)} %collective-permute-done.19.refs_1_), custom_call_target="tpu_custom_call" | custom-call | tf_op jit(solution)/shard_map/pallas_call | solution.py:20
  49.4 0.3 collective-permute-done.17.refs_2_
  49.7 0.3 collective-permute-done.18.refs_3_
  50.3 1.5 %collective-permute-start.20 = (bf16[256,128]{1,0:T(8,128)(2,1)S(1)}, bf16[256,128]{1,0:T(8,128)(2,1)S(1)}, u32[]{:S(2)}, u32[]{:S(2)}) collective-permute-start(bf16[256,128]{1,0:T(8,128)(2,1)S(1)} %shard_map.122.refs_0_), channel_id=1, source_target_pairs={{0,6},{2,4},{4,2},{6,0},{8,14},{10,12},{12,10},{14,8},{16,22},{18,... | collective-permute-start | bytes 196616 | tf_op jit(solution)/shard_map/ppermute | solution.py:316
  51.7 0.6 collective-permute-start.21
  52.3 1.5 %collective-permute-start.22 = (bf16[256,128]{1,0:T(8,128)(2,1)S(1)}, bf16[256,128]{1,0:T(8,128)(2,1)S(1)}, u32[]{:S(2)}, u32[]{:S(2)}) collective-permute-start(bf16[256,128]{1,0:T(8,128)(2,1)S(1)} %shard_map.122.refs_0_), channel_id=1, source_target_pairs={{0,2},{2,0},{4,6},{6,4},{8,10},{10,8},{12,14},{14,12},{16,18},{18,... | collective-permute-start | bytes 196616 | tf_op jit(solution)/shard_map/ppermute | solution.py:316
  53.8 0.8 %shard_map.123 = (bf16[128,2048]{1,0:T(8,128)(2,1)S(1)}, f32[64,2048]{1,0:T(8,128)S(1)}, f32[64,128]{1,0:T(8,128)S(1)}) custom-call(f32[64,64]{1,0:T(8,128)S(1)} %shard_map.121.refs_4_.inverse_ref, bf16[192,2048]{1,0:T(8,128)(2,1)S(1)} %get-tuple-element.111.stack_ref, f32[64,192]{1,0:T(8,128)S(1)} %get-tuple-element.78.m.mix_ref, ...), custom_call_target="tpu_custom_call" | custom-call | tf_op jit(solution)/shard_map/pallas_call | solution.py:20
  54.7 1.5 %collective-permute-done.20.refs_1_ = bf16[256,128]{1,0:T(8,128)(2,1)S(1)} collective-permute-done((bf16[256,128]{1,0:T(8,128)(2,1)S(1)}, bf16[256,128]{1,0:T(8,128)(2,1)S(1)}, u32[]{:S(2)}, u32[]{:S(2)}) %collective-permute-start.20) | collective-permute-done | bytes 65568 | tf_op jit(solution)/shard_map/ppermute | solution.py:316
  56.6 0.3 shard_map.124
  57.0 0.4 shard_map.126.refs_2_
  57.4 0.8 %collective-permute-done.23.refs_1_ = f32[64,128]{1,0:T(8,128)S(1)} collective-permute-done((f32[64,128]{1,0:T(8,128)S(1)}, f32[64,128]{1,0:T(8,128)S(1)}, u32[]{:S(2)}, u32[]{:S(2)}) %collective-permute-start.23) | collective-permute-done | bytes 32800 | tf_op jit(solution)/shard_map/ppermute | solution.py:316
  58.2 0.4 shard_map.127
  58.9 1.1 %shard_map.125 = (f32[64,128]{1,0:T(8,128)S(1)}, f32[64,128]{1,0:T(8,128)S(1)}, f32[64,128]{1,0:T(8,128)S(1)}) custom-call(f32[64,192]{1,0:T(8,128)S(1)} %get-tuple-element.77.m, f32[64,128]{1,0:T(8,128)S(1)} %get-tuple-element.115.refs_0_, f32[64,128]{1,0:T(8,128)S(1)} %collective-permute-done.23.refs_1_, ...), custom_call_target="tpu_custom_call" | custom-call | tf_op jit(solution)/shard_map/pallas_call | solution.py:20
  60.0 0.4 collective-permute-start.28
  60.5 0.3 shard_map.128
  60.7 1.8 %collective-permute-start.25 = (f32[64,128]{1,0:T(8,128)S(1)}, f32[64,128]{1,0:T(8,128)S(1)}, u32[]{:S(2)}, u32[]{:S(2)}) collective-permute-start(f32[64,128]{1,0:T(8,128)S(1)} %shard_map.128), channel_id=1, source_target_pairs={{0,24},{2,26},{4,28},{6,30},{8,16},{10,18},{12,20},{14,22},{16,8},... | collective-permute-start | bytes 98312 | tf_op jit(solution)/shard_map/ppermute | solution.py:316
  62.5 0.8 %collective-permute-start.26 = (f32[64,128]{1,0:T(8,128)S(1)}, f32[64,128]{1,0:T(8,128)S(1)}, u32[]{:S(2)}, u32[]{:S(2)}) collective-permute-start(f32[64,128]{1,0:T(8,128)S(1)} %shard_map.128), channel_id=1, source_target_pairs={{0,16},{2,18},{4,20},{6,22},{8,24},{10,26},{12,28},{14,30},{16,0},... | collective-permute-start | bytes 98312 | tf_op jit(solution)/shard_map/ppermute | solution.py:316
  63.4 1.8 %collective-permute-start.27 = (f32[64,128]{1,0:T(8,128)S(1)}, f32[64,128]{1,0:T(8,128)S(1)}, u32[]{:S(2)}, u32[]{:S(2)}) collective-permute-start(f32[64,128]{1,0:T(8,128)S(1)} %shard_map.128), channel_id=1, source_target_pairs={{0,8},{2,10},{4,12},{6,14},{8,0},{10,2},{12,4},{14,6},{16,24},{18,... | collective-permute-start | bytes 98312 | tf_op jit(solution)/shard_map/ppermute | solution.py:316
  65.2 2.2 %shard_map.129 = (f32[64,64]{1,0:T(8,128)S(1)}, f32[64,128]{1,0:T(8,128)S(1)}) custom-call(f32[64,128]{1,0:T(8,128)S(1)} %get-tuple-element.124.refs_0_, f32[64,128]{1,0:T(8,128)S(1)} %collective-permute-done.28.refs_1_), custom_call_target="tpu_custom_call" | custom-call | tf_op jit(solution)/shard_map/pallas_call | solution.py:20
  67.8 1.7 %collective-permute-start.31 = (f32[64,128]{1,0:T(8,128)S(1)}, f32[64,128]{1,0:T(8,128)S(1)}, u32[]{:S(2)}, u32[]{:S(2)}) collective-permute-start(f32[64,128]{1,0:T(8,128)S(1)} %add_add_fusion.1), channel_id=1, source_target_pairs={{0,6},{2,4},{4,2},{6,0},{8,14},{10,12},{12,10},{14,8},{16,22},{18,... | collective-permute-start | bytes 98312 | tf_op jit(solution)/shard_map/ppermute | solution.py:316
  69.5 1.2 %collective-permute-start.29 = (f32[64,128]{1,0:T(8,128)S(1)}, f32[64,128]{1,0:T(8,128)S(1)}, u32[]{:S(2)}, u32[]{:S(2)}) collective-permute-start(f32[64,128]{1,0:T(8,128)S(1)} %add_add_fusion.1), channel_id=1, source_target_pairs={{0,2},{2,0},{4,6},{6,4},{8,10},{10,8},{12,14},{14,12},{16,18},{18,... | collective-permute-start | bytes 98312 | tf_op jit(solution)/shard_map/ppermute | solution.py:316
  70.7 0.6 collective-permute-start.30
  71.3 1.6 %collective-permute-done.31 = f32[64,128]{1,0:T(8,128)S(1)} collective-permute-done((f32[64,128]{1,0:T(8,128)S(1)}, f32[64,128]{1,0:T(8,128)S(1)}, u32[]{:S(2)}, u32[]{:S(2)}) %collective-permute-start.31) | collective-permute-done | bytes 32800 | tf_op jit(solution)/shard_map/ppermute | solution.py:316
  72.9 0.4 collective-permute-done.29
  73.4 1.2 %collective-permute-done.30 = f32[64,128]{1,0:T(8,128)S(1)} collective-permute-done((f32[64,128]{1,0:T(8,128)S(1)}, f32[64,128]{1,0:T(8,128)S(1)}, u32[]{:S(2)}, u32[]{:S(2)}) %collective-permute-start.30) | collective-permute-done | bytes 32800 | tf_op jit(solution)/shard_map/ppermute | solution.py:316
  74.7 0.8 %shard_map.130 = (f32[64,128]{1,0:T(8,128)}, f32[64,128]{1,0:T(8,128)}, f32[64,256]{1,0:T(8,128)S(1)}) custom-call(f32[64,64]{1,0:T(8,128)S(1)} %get-tuple-element.126.inverse_ref.refs_2_, f32[64,128]{1,0:T(8,128)S(1)} %get-tuple-element.127.scale_ref, f32[64,128]{1,0:T(8,128)S(1)} %get-tuple-element.119.rotated_ref, f32[64,128]{1,0:T(8,128)S(1)} %add.46.adj_ref, ...), custom_call_target="tpu_custom_call" | custom-call | tf_op jit(solution)/shard_map/pallas_call | solution.py:20
  75.5 0.4 collective-permute-done.32.refs_1_
  75.9 1.2 %shard_map.131 = (f32[64,128]{1,0:T(8,128)}, f32[64,64]{1,0:T(8,128)}) custom-call(f32[64,128]{1,0:T(8,128)S(1)} %add_add_fusion.refs_0_, f32[64,128]{1,0:T(8,128)S(1)} %collective-permute-done.32.refs_1_, f32[64,64]{1,0:T(8,128)S(1)} %get-tuple-element.126.inverse_ref.refs_2_, f32[64,256]{1,0:T(8,128)S(1)} %get-tuple-element.134.refs_3_), custom_call_target="tpu_custom_call" | custom-call | tf_op jit(solution)/shard_map/pallas_call | solution.py:20
  (43 shorter events, 2.5 us)
Async XLA Ops:
  1.4 7.3 %collective-permute-start.2 = (bf16[1,192,128]{2,1,0:T(8,128)(2,1)S(1)}, bf16[1,192,128]{2,1,0:T(8,128)(2,1)S(1)}, u32[]{:S(2)}, u32[]{:S(2)}) collective-permute-start(bf16[1,192,128]{2,1,0:T(8,128)(2,1)S(1)} %maximum_bitcast_fusion), channel_id=1, source_target_pairs={{0,24},{2,26},{4,28},{6,30},{8,16},{10,18},{12,20},{14,22},{16,8},... | collective-permute-start | bytes 147464 | tf_op jit(solution)/shard_map/ppermute | solution.py:316
  6.4 5.0 %collective-permute-start.1 = (bf16[1,192,128]{2,1,0:T(8,128)(2,1)S(1)}, bf16[1,192,128]{2,1,0:T(8,128)(2,1)S(1)}, u32[]{:S(2)}, u32[]{:S(2)}) collective-permute-start(bf16[1,192,128]{2,1,0:T(8,128)(2,1)S(1)} %maximum_bitcast_fusion), channel_id=1, source_target_pairs={{0,16},{2,18},{4,20},{6,22},{8,24},{10,26},{12,28},{14,30},{16,0},... | collective-permute-start | bytes 147464 | tf_op jit(solution)/shard_map/ppermute | solution.py:316
  6.4 5.0 %collective-permute-start = (bf16[1,192,128]{2,1,0:T(8,128)(2,1)S(1)}, bf16[1,192,128]{2,1,0:T(8,128)(2,1)S(1)}, u32[]{:S(2)}, u32[]{:S(2)}) collective-permute-start(bf16[1,192,128]{2,1,0:T(8,128)(2,1)S(1)} %maximum_bitcast_fusion), channel_id=1, source_target_pairs={{0,8},{2,10},{4,12},{6,14},{8,0},{10,2},{12,4},{14,6},{16,24},{18,... | collective-permute-start | bytes 147464 | tf_op jit(solution)/shard_map/ppermute | solution.py:316
  7.0 8.0 %copy-start.1 = (f32[3,64,192]{2,1,0:T(8,128)S(1)}, f32[3,64,192]{2,1,0:T(8,128)}, u32[]{:S(2)}) copy-start(f32[3,64,192]{2,1,0:T(8,128)} %param.14) | copy-start | bytes 442372
  11.5 3.6 %copy-start.3 = (s32[1,1,2,16]{3,2,1,0:T(2,128)S(1)}, s32[1,1,2,16]{3,2,1,0:T(2,128)}, u32[]{:S(2)}) copy-start(s32[1,1,2,16]{3,2,1,0:T(2,128)} %param.10) | copy-start | bytes 388
  11.5 3.6 %copy-start.4 = (s32[1,1,2]{2,1,0:T(1,128)S(1)}, s32[1,1,2]{2,1,0:T(1,128)}, u32[]{:S(2)}) copy-start(s32[1,1,2]{2,1,0:T(1,128)} %param.9) | copy-start | bytes 28
  11.5 8.5 %collective-permute-start.3 = (bf16[4,192,128]{2,1,0:T(8,128)(2,1)S(1)}, bf16[4,192,128]{2,1,0:T(8,128)(2,1)S(1)}, u32[]{:S(2)}, u32[]{:S(2)}) collective-permute-start(bf16[4,192,128]{2,1,0:T(8,128)(2,1)S(1)} %pad_maximum_fusion.refs_0_), channel_id=1, source_target_pairs={{0,6},{2,4},{4,2},{6,0},{8,14},{10,12},{12,10},{14,8},{16,22},{18,... | collective-permute-start | bytes 589832 | tf_op jit(solution)/shard_map/ppermute | solution.py:316
  14.0 8.4 %collective-permute-start.4 = (bf16[4,192,128]{2,1,0:T(8,128)(2,1)S(1)}, bf16[4,192,128]{2,1,0:T(8,128)(2,1)S(1)}, u32[]{:S(2)}, u32[]{:S(2)}) collective-permute-start(bf16[4,192,128]{2,1,0:T(8,128)(2,1)S(1)} %pad_maximum_fusion.refs_0_), channel_id=1, source_target_pairs={{0,4},{2,6},{4,0},{6,2},{8,12},{10,14},{12,8},{14,10},{16,20},{18,... | collective-permute-start | bytes 589832 | tf_op jit(solution)/shard_map/ppermute | solution.py:316
  14.5 8.0 %collective-permute-start.5 = (bf16[4,192,128]{2,1,0:T(8,128)(2,1)S(1)}, bf16[4,192,128]{2,1,0:T(8,128)(2,1)S(1)}, u32[]{:S(2)}, u32[]{:S(2)}) collective-permute-start(bf16[4,192,128]{2,1,0:T(8,128)(2,1)S(1)} %pad_maximum_fusion.refs_0_), channel_id=1, source_target_pairs={{0,2},{2,0},{4,6},{6,4},{8,10},{10,8},{12,14},{14,12},{16,18},{18,... | collective-permute-start | bytes 589832 | tf_op jit(solution)/shard_map/ppermute | solution.py:316
  15.2 1.2 %copy-start = (bf16[1,1,2,16,128,128]{5,4,3,2,1,0:T(8,128)(2,1)S(1)}, bf16[1,1,2,16,128,128]{5,4,3,2,1,0:T(8,128)(2,1)}, u32[]{:S(2)}) copy-start(bf16[1,1,2,16,128,128]{5,4,3,2,1,0:T(8,128)(2,1)} %param.8) | copy-start | bytes 3145732
  16.4 1.3 %copy-start.2 = (f32[3,64,128]{2,1,0:T(8,128)S(1)}, f32[3,64,128]{2,1,0:T(8,128)}, u32[]{:S(2)}) copy-start(f32[3,64,128]{2,1,0:T(8,128)} %param.15) | copy-start | bytes 294916
  23.1 1.3 %collective-permute-start.6 = (f32[64,128]{1,0:T(8,128)S(1)}, f32[64,128]{1,0:T(8,128)S(1)}, u32[]{:S(2)}, u32[]{:S(2)}) collective-permute-start(f32[64,128]{1,0:T(8,128)S(1)} %get-tuple-element.86), channel_id=1, source_target_pairs={{0,1},{1,0},{2,3},{3,2},{4,5},{5,4},{6,7},{7,6},{8,9},{9,8},{10,11... | collective-permute-start | bytes 98312 | tf_op jit(solution)/shard_map/ppermute | solution.py:316
  24.4 4.6 %collective-permute-start.10 = (f32[64,128]{1,0:T(8,128)S(1)}, f32[64,128]{1,0:T(8,128)S(1)}, u32[]{:S(2)}, u32[]{:S(2)}) collective-permute-start(f32[64,128]{1,0:T(8,128)S(1)} %shard_map.113.refs_0_), channel_id=1, source_target_pairs={{0,1},{1,0},{2,3},{3,2},{4,5},{5,4},{6,7},{7,6},{8,9},{9,8},{10,11... | collective-permute-start | bytes 98312 | tf_op jit(solution)/shard_map/ppermute | solution.py:316
  24.6 6.6 %collective-permute-start.7 = (f32[64,128]{1,0:T(8,128)S(1)}, f32[64,128]{1,0:T(8,128)S(1)}, u32[]{:S(2)}, u32[]{:S(2)}) collective-permute-start(f32[64,128]{1,0:T(8,128)S(1)} %add.44.refs_0_), channel_id=1, source_target_pairs={{0,24},{2,26},{4,28},{6,30},{8,16},{10,18},{12,20},{14,22},{16,8},... | collective-permute-start | bytes 98312 | tf_op jit(solution)/shard_map/ppermute | solution.py:316
  26.2 5.3 %collective-permute-start.8 = (f32[64,128]{1,0:T(8,128)S(1)}, f32[64,128]{1,0:T(8,128)S(1)}, u32[]{:S(2)}, u32[]{:S(2)}) collective-permute-start(f32[64,128]{1,0:T(8,128)S(1)} %add.44.refs_0_), channel_id=1, source_target_pairs={{0,16},{2,18},{4,20},{6,22},{8,24},{10,26},{12,28},{14,30},{16,0},... | collective-permute-start | bytes 98312 | tf_op jit(solution)/shard_map/ppermute | solution.py:316
  26.7 4.7 %collective-permute-start.9 = (f32[64,128]{1,0:T(8,128)S(1)}, f32[64,128]{1,0:T(8,128)S(1)}, u32[]{:S(2)}, u32[]{:S(2)}) collective-permute-start(f32[64,128]{1,0:T(8,128)S(1)} %add.44.refs_0_), channel_id=1, source_target_pairs={{0,8},{2,10},{4,12},{6,14},{8,0},{10,2},{12,4},{14,6},{16,24},{18,... | collective-permute-start | bytes 98312 | tf_op jit(solution)/shard_map/ppermute | solution.py:316
  31.7 5.3 %collective-permute-start.11 = (bf16[256,128]{1,0:T(8,128)(2,1)S(1)}, bf16[256,128]{1,0:T(8,128)(2,1)S(1)}, u32[]{:S(2)}, u32[]{:S(2)}) collective-permute-start(bf16[256,128]{1,0:T(8,128)(2,1)S(1)} %shard_map.115.refs_0_), channel_id=1, source_target_pairs={{0,6},{2,4},{4,2},{6,0},{8,14},{10,12},{12,10},{14,8},{16,22},{18,... | collective-permute-start | bytes 196616 | tf_op jit(solution)/shard_map/ppermute | solution.py:316
  33.5 4.6 %collective-permute-start.12 = (bf16[256,128]{1,0:T(8,128)(2,1)S(1)}, bf16[256,128]{1,0:T(8,128)(2,1)S(1)}, u32[]{:S(2)}, u32[]{:S(2)}) collective-permute-start(bf16[256,128]{1,0:T(8,128)(2,1)S(1)} %shard_map.115.refs_0_), channel_id=1, source_target_pairs={{0,4},{2,6},{4,0},{6,2},{8,12},{10,14},{12,8},{14,10},{16,20},{18,... | collective-permute-start | bytes 196616 | tf_op jit(solution)/shard_map/ppermute | solution.py:316
  34.8 4.3 %collective-permute-start.13 = (bf16[256,128]{1,0:T(8,128)(2,1)S(1)}, bf16[256,128]{1,0:T(8,128)(2,1)S(1)}, u32[]{:S(2)}, u32[]{:S(2)}) collective-permute-start(bf16[256,128]{1,0:T(8,128)(2,1)S(1)} %shard_map.115.refs_0_), channel_id=1, source_target_pairs={{0,2},{2,0},{4,6},{6,4},{8,10},{10,8},{12,14},{14,12},{16,18},{18,... | collective-permute-start | bytes 196616 | tf_op jit(solution)/shard_map/ppermute | solution.py:316
  39.4 1.3 %collective-permute-start.14 = (f32[64,128]{1,0:T(8,128)S(1)}, f32[64,128]{1,0:T(8,128)S(1)}, u32[]{:S(2)}, u32[]{:S(2)}) collective-permute-start(f32[64,128]{1,0:T(8,128)S(1)} %get-tuple-element.98.refs_0_), channel_id=1, source_target_pairs={{0,1},{1,0},{2,3},{3,2},{4,5},{5,4},{6,7},{7,6},{8,9},{9,8},{10,11... | collective-permute-start | bytes 98312 | tf_op jit(solution)/shard_map/ppermute | solution.py:316
  41.1 1.3 %collective-permute-start.15 = (f32[64,128]{1,0:T(8,128)S(1)}, f32[64,128]{1,0:T(8,128)S(1)}, u32[]{:S(2)}, u32[]{:S(2)}) collective-permute-start(f32[64,128]{1,0:T(8,128)S(1)} %get-tuple-element.102), channel_id=1, source_target_pairs={{0,1},{1,0},{2,3},{3,2},{4,5},{5,4},{6,7},{7,6},{8,9},{9,8},{10,11... | collective-permute-start | bytes 98312 | tf_op jit(solution)/shard_map/ppermute | solution.py:316
  42.4 4.8 %collective-permute-start.19 = (f32[64,128]{1,0:T(8,128)S(1)}, f32[64,128]{1,0:T(8,128)S(1)}, u32[]{:S(2)}, u32[]{:S(2)}) collective-permute-start(f32[64,128]{1,0:T(8,128)S(1)} %get-tuple-element.105.refs_0_), channel_id=1, source_target_pairs={{0,1},{1,0},{2,3},{3,2},{4,5},{5,4},{6,7},{7,6},{8,9},{9,8},{10,11... | collective-permute-start | bytes 98312 | tf_op jit(solution)/shard_map/ppermute | solution.py:316
  42.8 6.6 %collective-permute-start.16 = (f32[64,128]{1,0:T(8,128)S(1)}, f32[64,128]{1,0:T(8,128)S(1)}, u32[]{:S(2)}, u32[]{:S(2)}) collective-permute-start(f32[64,128]{1,0:T(8,128)S(1)} %add.45.refs_0_), channel_id=1, source_target_pairs={{0,24},{2,26},{4,28},{6,30},{8,16},{10,18},{12,20},{14,22},{16,8},... | collective-permute-start | bytes 98312 | tf_op jit(solution)/shard_map/ppermute | solution.py:316
  44.5 5.2 %collective-permute-start.17 = (f32[64,128]{1,0:T(8,128)S(1)}, f32[64,128]{1,0:T(8,128)S(1)}, u32[]{:S(2)}, u32[]{:S(2)}) collective-permute-start(f32[64,128]{1,0:T(8,128)S(1)} %add.45.refs_0_), channel_id=1, source_target_pairs={{0,16},{2,18},{4,20},{6,22},{8,24},{10,26},{12,28},{14,30},{16,0},... | collective-permute-start | bytes 98312 | tf_op jit(solution)/shard_map/ppermute | solution.py:316
  45.7 4.3 %collective-permute-start.18 = (f32[64,128]{1,0:T(8,128)S(1)}, f32[64,128]{1,0:T(8,128)S(1)}, u32[]{:S(2)}, u32[]{:S(2)}) collective-permute-start(f32[64,128]{1,0:T(8,128)S(1)} %add.45.refs_0_), channel_id=1, source_target_pairs={{0,8},{2,10},{4,12},{6,14},{8,0},{10,2},{12,4},{14,6},{16,24},{18,... | collective-permute-start | bytes 98312 | tf_op jit(solution)/shard_map/ppermute | solution.py:316
  50.3 5.9 %collective-permute-start.20 = (bf16[256,128]{1,0:T(8,128)(2,1)S(1)}, bf16[256,128]{1,0:T(8,128)(2,1)S(1)}, u32[]{:S(2)}, u32[]{:S(2)}) collective-permute-start(bf16[256,128]{1,0:T(8,128)(2,1)S(1)} %shard_map.122.refs_0_), channel_id=1, source_target_pairs={{0,6},{2,4},{4,2},{6,0},{8,14},{10,12},{12,10},{14,8},{16,22},{18,... | collective-permute-start | bytes 196616 | tf_op jit(solution)/shard_map/ppermute | solution.py:316
  51.7 4.7 %collective-permute-start.21 = (bf16[256,128]{1,0:T(8,128)(2,1)S(1)}, bf16[256,128]{1,0:T(8,128)(2,1)S(1)}, u32[]{:S(2)}, u32[]{:S(2)}) collective-permute-start(bf16[256,128]{1,0:T(8,128)(2,1)S(1)} %shard_map.122.refs_0_), channel_id=1, source_target_pairs={{0,4},{2,6},{4,0},{6,2},{8,12},{10,14},{12,8},{14,10},{16,20},{18,... | collective-permute-start | bytes 196616 | tf_op jit(solution)/shard_map/ppermute | solution.py:316
  52.3 4.3 %collective-permute-start.22 = (bf16[256,128]{1,0:T(8,128)(2,1)S(1)}, bf16[256,128]{1,0:T(8,128)(2,1)S(1)}, u32[]{:S(2)}, u32[]{:S(2)}) collective-permute-start(bf16[256,128]{1,0:T(8,128)(2,1)S(1)} %shard_map.122.refs_0_), channel_id=1, source_target_pairs={{0,2},{2,0},{4,6},{6,4},{8,10},{10,8},{12,14},{14,12},{16,18},{18,... | collective-permute-start | bytes 196616 | tf_op jit(solution)/shard_map/ppermute | solution.py:316
  57.0 1.3 %collective-permute-start.23 = (f32[64,128]{1,0:T(8,128)S(1)}, f32[64,128]{1,0:T(8,128)S(1)}, u32[]{:S(2)}, u32[]{:S(2)}) collective-permute-start(f32[64,128]{1,0:T(8,128)S(1)} %get-tuple-element.115.refs_0_), channel_id=1, source_target_pairs={{0,1},{1,0},{2,3},{3,2},{4,5},{5,4},{6,7},{7,6},{8,9},{9,8},{10,11... | collective-permute-start | bytes 98312 | tf_op jit(solution)/shard_map/ppermute | solution.py:316
  58.7 1.4 %collective-permute-start.24 = (f32[64,128]{1,0:T(8,128)S(1)}, f32[64,128]{1,0:T(8,128)S(1)}, u32[]{:S(2)}, u32[]{:S(2)}) collective-permute-start(f32[64,128]{1,0:T(8,128)S(1)} %get-tuple-element.121), channel_id=1, source_target_pairs={{0,1},{1,0},{2,3},{3,2},{4,5},{5,4},{6,7},{7,6},{8,9},{9,8},{10,11... | collective-permute-start | bytes 98312 | tf_op jit(solution)/shard_map/ppermute | solution.py:316
  60.0 5.2 %collective-permute-start.28 = (f32[64,128]{1,0:T(8,128)S(1)}, f32[64,128]{1,0:T(8,128)S(1)}, u32[]{:S(2)}, u32[]{:S(2)}) collective-permute-start(f32[64,128]{1,0:T(8,128)S(1)} %get-tuple-element.124.refs_0_), channel_id=1, source_target_pairs={{0,1},{1,0},{2,3},{3,2},{4,5},{5,4},{6,7},{7,6},{8,9},{9,8},{10,11... | collective-permute-start | bytes 98312 | tf_op jit(solution)/shard_map/ppermute | solution.py:316
  60.7 6.7 %collective-permute-start.25 = (f32[64,128]{1,0:T(8,128)S(1)}, f32[64,128]{1,0:T(8,128)S(1)}, u32[]{:S(2)}, u32[]{:S(2)}) collective-permute-start(f32[64,128]{1,0:T(8,128)S(1)} %shard_map.128), channel_id=1, source_target_pairs={{0,24},{2,26},{4,28},{6,30},{8,16},{10,18},{12,20},{14,22},{16,8},... | collective-permute-start | bytes 98312 | tf_op jit(solution)/shard_map/ppermute | solution.py:316
  62.5 5.0 %collective-permute-start.26 = (f32[64,128]{1,0:T(8,128)S(1)}, f32[64,128]{1,0:T(8,128)S(1)}, u32[]{:S(2)}, u32[]{:S(2)}) collective-permute-start(f32[64,128]{1,0:T(8,128)S(1)} %shard_map.128), channel_id=1, source_target_pairs={{0,16},{2,18},{4,20},{6,22},{8,24},{10,26},{12,28},{14,30},{16,0},... | collective-permute-start | bytes 98312 | tf_op jit(solution)/shard_map/ppermute | solution.py:316
  63.4 4.4 %collective-permute-start.27 = (f32[64,128]{1,0:T(8,128)S(1)}, f32[64,128]{1,0:T(8,128)S(1)}, u32[]{:S(2)}, u32[]{:S(2)}) collective-permute-start(f32[64,128]{1,0:T(8,128)S(1)} %shard_map.128), channel_id=1, source_target_pairs={{0,8},{2,10},{4,12},{6,14},{8,0},{10,2},{12,4},{14,6},{16,24},{18,... | collective-permute-start | bytes 98312 | tf_op jit(solution)/shard_map/ppermute | solution.py:316
  67.8 5.2 %collective-permute-start.31 = (f32[64,128]{1,0:T(8,128)S(1)}, f32[64,128]{1,0:T(8,128)S(1)}, u32[]{:S(2)}, u32[]{:S(2)}) collective-permute-start(f32[64,128]{1,0:T(8,128)S(1)} %add_add_fusion.1), channel_id=1, source_target_pairs={{0,6},{2,4},{4,2},{6,0},{8,14},{10,12},{12,10},{14,8},{16,22},{18,... | collective-permute-start | bytes 98312 | tf_op jit(solution)/shard_map/ppermute | solution.py:316
  69.5 3.9 %collective-permute-start.29 = (f32[64,128]{1,0:T(8,128)S(1)}, f32[64,128]{1,0:T(8,128)S(1)}, u32[]{:S(2)}, u32[]{:S(2)}) collective-permute-start(f32[64,128]{1,0:T(8,128)S(1)} %add_add_fusion.1), channel_id=1, source_target_pairs={{0,2},{2,0},{4,6},{6,4},{8,10},{10,8},{12,14},{14,12},{16,18},{18,... | collective-permute-start | bytes 98312 | tf_op jit(solution)/shard_map/ppermute | solution.py:316
  70.7 3.9 %collective-permute-start.30 = (f32[64,128]{1,0:T(8,128)S(1)}, f32[64,128]{1,0:T(8,128)S(1)}, u32[]{:S(2)}, u32[]{:S(2)}) collective-permute-start(f32[64,128]{1,0:T(8,128)S(1)} %add_add_fusion.1), channel_id=1, source_target_pairs={{0,4},{2,6},{4,0},{6,2},{8,12},{10,14},{12,8},{14,10},{16,20},{18,... | collective-permute-start | bytes 98312 | tf_op jit(solution)/shard_map/ppermute | solution.py:316
  74.6 1.3 %collective-permute-start.32 = (f32[64,128]{1,0:T(8,128)S(1)}, f32[64,128]{1,0:T(8,128)S(1)}, u32[]{:S(2)}, u32[]{:S(2)}) collective-permute-start(f32[64,128]{1,0:T(8,128)S(1)} %add_add_fusion.refs_0_), channel_id=1, source_target_pairs={{0,1},{1,0},{2,3},{3,2},{4,5},{5,4},{6,7},{7,6},{8,9},{9,8},{10,11... | collective-permute-start | bytes 98312 | tf_op jit(solution)/shard_map/ppermute | solution.py:316

commit v12 on v11

--- a/solution.py
+++ b/solution.py
@@ -143,7 +143,9 @@
 
 def gram_terms(stack, mix_ref, pack_ref, search_refs):
     vecs = mix_ref.shape[0]
-    rotated = times_stack(mix_ref[...], stack)
+    weights = jnp.concatenate(halves(mix_ref[...]), axis=0)
+    rotated = jnp.dot(weights, stack, preferred_element_type=f32)
+    rotated = rotated[:vecs] + rotated[vecs:]
     square = jnp.zeros((vecs, vecs), f32)
     if search_refs:
         weights_ref, search_out, own_rotated = search_refs

time: 77.5 us -> 77.4 us (level)
  no operation moved by 1% of the time
where the time goes in v12:
time: 77.4 us; the launch traced here: 77 us
  starting transfers between devices  34.8 us (45%)
  waiting for transfers between devices  20.5 us (26%)
  Pallas kernels  18.7 us (24%)
  local copies, waits for them, and re-layouts  1.27 us (2%)
  other arithmetic  0.9 us (1%)
  between operations  0.88 us (1%)
    ppermute x33, starting transfers between devices, swap(): return lax.ppermute(value, axis, [(i, i ^ by) for i in range(size)])  34.8 us
    ppermute x33, waiting for transfers between devices, swap(): return lax.ppermute(value, axis, [(i, i ^ by) for i in range(size)])  20.5 us
    pallas_call x21, Pallas kernels, call(): pl.pallas_call(kernel, out_shape=[jax.ShapeDtypeStruct(shape, kind) for s...  18.7 us
  transfers between devices with their start and end apart: 33, of which 23 were waited for; matrix products, arithmetic and copies ran while one was open for 0% of the time, Pallas kernels for 19%

profile of v12, /device:TPU:0, one launch (start us, length us, event | category | flops | bytes accessed | tf_op | source)
XLA Modules:
  0.0 77.0 jit_solution(17544912304528330895)
XLA Ops:
  0.6 0.8 maximum_bitcast_fusion
  1.4 5.0 %collective-permute-start.2 = (bf16[1,192,128]{2,1,0:T(8,128)(2,1)S(1)}, bf16[1,192,128]{2,1,0:T(8,128)(2,1)S(1)}, u32[]{:S(2)}, u32[]{:S(2)}) collective-permute-start(bf16[1,192,128]{2,1,0:T(8,128)(2,1)S(1)} %maximum_bitcast_fusion), channel_id=1, source_target_pairs={{0,24},{2,26},{4,28},{6,30},{8,16},{10,18},{12,20},{14,22},{16,8},... | collective-permute-start | bytes 147464 | tf_op jit(solution)/shard_map/ppermute | solution.py:318
  6.4 0.6 collective-permute-start
  7.1 1.6 %collective-permute-done.2 = bf16[1,192,128]{2,1,0:T(8,128)(2,1)S(1)} collective-permute-done((bf16[1,192,128]{2,1,0:T(8,128)(2,1)S(1)}, bf16[1,192,128]{2,1,0:T(8,128)(2,1)S(1)}, u32[]{:S(2)}, u32[]{:S(2)}) %collective-permute-start.2) | collective-permute-done | bytes 49184 | tf_op jit(solution)/shard_map/ppermute | solution.py:318
  8.7 2.8 %collective-permute-done.1 = bf16[1,192,128]{2,1,0:T(8,128)(2,1)S(1)} collective-permute-done((bf16[1,192,128]{2,1,0:T(8,128)(2,1)S(1)}, bf16[1,192,128]{2,1,0:T(8,128)(2,1)S(1)}, u32[]{:S(2)}, u32[]{:S(2)}) %collective-permute-start.1) | collective-permute-done | bytes 49184 | tf_op jit(solution)/shard_map/ppermute | solution.py:318
  11.5 2.5 %collective-permute-start.3 = (bf16[4,192,128]{2,1,0:T(8,128)(2,1)S(1)}, bf16[4,192,128]{2,1,0:T(8,128)(2,1)S(1)}, u32[]{:S(2)}, u32[]{:S(2)}) collective-permute-start(bf16[4,192,128]{2,1,0:T(8,128)(2,1)S(1)} %pad_maximum_fusion.refs_0_), channel_id=1, source_target_pairs={{0,6},{2,4},{4,2},{6,0},{8,14},{10,12},{12,10},{14,8},{16,22},{18,... | collective-permute-start | bytes 589832 | tf_op jit(solution)/shard_map/ppermute | solution.py:318
  14.0 0.5 collective-permute-start.4
  14.5 0.5 collective-permute-start.5
  15.2 1.2 %copy-done = bf16[1,1,2,16,128,128]{5,4,3,2,1,0:T(8,128)(2,1)S(1)} copy-done((bf16[1,1,2,16,128,128]{5,4,3,2,1,0:T(8,128)(2,1)S(1)}, bf16[1,1,2,16,128,128]{5,4,3,2,1,0:T(8,128)(2,1)}, u32[]{:S(2)}) %copy-start) | copy-done | bytes 1048600
  16.4 2.0 %shard_map.111.dense_ref = bf16[2048,256]{1,0:T(8,128)(2,1)S(1)} custom-call(s32[2,16]{1,0:T(2,128)S(1)} %compare_select_fusion.4.slots_ref, bf16[2,16,128,128]{3,2,1,0:T(8,128)(2,1)S(1)} %bitcast.18), custom_call_target="tpu_custom_call" | custom-call | tf_op jit(solution)/shard_map/pallas_call | solution.py:20
  18.4 1.6 %collective-permute-done.3.refs_1_ = bf16[4,192,128]{2,1,0:T(8,128)(2,1)S(1)} collective-permute-done((bf16[4,192,128]{2,1,0:T(8,128)(2,1)S(1)}, bf16[4,192,128]{2,1,0:T(8,128)(2,1)S(1)}, u32[]{:S(2)}, u32[]{:S(2)}) %collective-permute-start.3) | collective-permute-done | bytes 196640 | tf_op jit(solution)/shard_map/ppermute | solution.py:318
  20.0 2.5 %collective-permute-done.4.refs_2_ = bf16[4,192,128]{2,1,0:T(8,128)(2,1)S(1)} collective-permute-done((bf16[4,192,128]{2,1,0:T(8,128)(2,1)S(1)}, bf16[4,192,128]{2,1,0:T(8,128)(2,1)S(1)}, u32[]{:S(2)}, u32[]{:S(2)}) %collective-permute-start.4) | collective-permute-done | bytes 196640 | tf_op jit(solution)/shard_map/ppermute | solution.py:318
  22.5 0.6 shard_map.112
  23.2 0.7 shard_map.113.refs_0_
  23.9 0.5 collective-permute-done.6
  24.6 1.6 %collective-permute-start.7 = (f32[64,128]{1,0:T(8,128)S(1)}, f32[64,128]{1,0:T(8,128)S(1)}, u32[]{:S(2)}, u32[]{:S(2)}) collective-permute-start(f32[64,128]{1,0:T(8,128)S(1)} %add.44.refs_0_), channel_id=1, source_target_pairs={{0,24},{2,26},{4,28},{6,30},{8,16},{10,18},{12,20},{14,22},{16,8},... | collective-permute-start | bytes 98312 | tf_op jit(solution)/shard_map/ppermute | solution.py:318
  26.2 0.6 collective-permute-start.8
  26.7 2.2 %collective-permute-start.9 = (f32[64,128]{1,0:T(8,128)S(1)}, f32[64,128]{1,0:T(8,128)S(1)}, u32[]{:S(2)}, u32[]{:S(2)}) collective-permute-start(f32[64,128]{1,0:T(8,128)S(1)} %add.44.refs_0_), channel_id=1, source_target_pairs={{0,8},{2,10},{4,12},{6,14},{8,0},{10,2},{12,4},{14,6},{16,24},{18,... | collective-permute-start | bytes 98312 | tf_op jit(solution)/shard_map/ppermute | solution.py:318
  29.0 2.2 %shard_map.114.refs_4_.inverse_ref = f32[64,64]{1,0:T(8,128)S(1)} custom-call(f32[64,128]{1,0:T(8,128)S(1)} %shard_map.113.refs_0_, f32[64,128]{1,0:T(8,128)S(1)} %collective-permute-done.10.refs_1_), custom_call_target="tpu_custom_call" | custom-call | tf_op jit(solution)/shard_map/pallas_call | solution.py:20
  31.2 0.3 collective-permute-done.8.refs_2_
  31.7 1.7 %collective-permute-start.11 = (bf16[256,128]{1,0:T(8,128)(2,1)S(1)}, bf16[256,128]{1,0:T(8,128)(2,1)S(1)}, u32[]{:S(2)}, u32[]{:S(2)}) collective-permute-start(bf16[256,128]{1,0:T(8,128)(2,1)S(1)} %shard_map.115.refs_0_), channel_id=1, source_target_pairs={{0,6},{2,4},{4,2},{6,0},{8,14},{10,12},{12,10},{14,8},{16,22},{18,... | collective-permute-start | bytes 196616 | tf_op jit(solution)/shard_map/ppermute | solution.py:318
  33.5 1.3 %collective-permute-start.12 = (bf16[256,128]{1,0:T(8,128)(2,1)S(1)}, bf16[256,128]{1,0:T(8,128)(2,1)S(1)}, u32[]{:S(2)}, u32[]{:S(2)}) collective-permute-start(bf16[256,128]{1,0:T(8,128)(2,1)S(1)} %shard_map.115.refs_0_), channel_id=1, source_target_pairs={{0,4},{2,6},{4,0},{6,2},{8,12},{10,14},{12,8},{14,10},{16,20},{18,... | collective-permute-start | bytes 196616 | tf_op jit(solution)/shard_map/ppermute | solution.py:318
  34.8 0.5 collective-permute-start.13
  35.3 0.8 %shard_map.116 = (bf16[128,2048]{1,0:T(8,128)(2,1)S(1)}, f32[64,2048]{1,0:T(8,128)S(1)}, f32[64,128]{1,0:T(8,128)S(1)}) custom-call(f32[64,64]{1,0:T(8,128)S(1)} %shard_map.114.refs_4_.inverse_ref, bf16[192,2048]{1,0:T(8,128)(2,1)S(1)} %get-tuple-element.87.stack_ref, f32[64,192]{1,0:T(8,128)S(1)} %get-tuple-element.80.mix_ref, ...), custom_call_target="tpu_custom_call" | custom-call | tf_op jit(solution)/shard_map/pallas_call | solution.py:20
  36.1 0.9 %collective-permute-done.11.refs_1_ = bf16[256,128]{1,0:T(8,128)(2,1)S(1)} collective-permute-done((bf16[256,128]{1,0:T(8,128)(2,1)S(1)}, bf16[256,128]{1,0:T(8,128)(2,1)S(1)}, u32[]{:S(2)}, u32[]{:S(2)}) %collective-permute-start.11) | collective-permute-done | bytes 65568 | tf_op jit(solution)/shard_map/ppermute | solution.py:318
  37.1 1.0 %collective-permute-done.12.refs_2_ = bf16[256,128]{1,0:T(8,128)(2,1)S(1)} collective-permute-done((bf16[256,128]{1,0:T(8,128)(2,1)S(1)}, bf16[256,128]{1,0:T(8,128)(2,1)S(1)}, u32[]{:S(2)}, u32[]{:S(2)}) %collective-permute-start.12) | collective-permute-done | bytes 65568 | tf_op jit(solution)/shard_map/ppermute | solution.py:318
  38.1 1.0 %collective-permute-done.13.refs_3_ = bf16[256,128]{1,0:T(8,128)(2,1)S(1)} collective-permute-done((bf16[256,128]{1,0:T(8,128)(2,1)S(1)}, bf16[256,128]{1,0:T(8,128)(2,1)S(1)}, u32[]{:S(2)}, u32[]{:S(2)}) %collective-permute-start.13) | collective-permute-done | bytes 65568 | tf_op jit(solution)/shard_map/ppermute | solution.py:318
  39.0 0.3 shard_map.117
  39.5 0.4 shard_map.118.refs_2_
  39.8 0.8 %collective-permute-done.14.refs_1_ = f32[64,128]{1,0:T(8,128)S(1)} collective-permute-done((f32[64,128]{1,0:T(8,128)S(1)}, f32[64,128]{1,0:T(8,128)S(1)}, u32[]{:S(2)}, u32[]{:S(2)}) %collective-permute-start.14) | collective-permute-done | bytes 32800 | tf_op jit(solution)/shard_map/ppermute | solution.py:318
  40.6 0.4 shard_map.119
  41.3 1.0 %shard_map.120 = (f32[64,128]{1,0:T(8,128)S(1)}, bf16[192,2048]{1,0:T(8,128)(2,1)S(1)}) custom-call(f32[64,192]{1,0:T(8,128)S(1)} %get-tuple-element.78.m.mix_ref, f32[64,128]{1,0:T(8,128)S(1)} %get-tuple-element.98.refs_0_, f32[64,128]{1,0:T(8,128)S(1)} %collective-permute-done.14.refs_1_, ...), custom_call_target="tpu_custom_call" | custom-call | tf_op jit(solution)/shard_map/pallas_call | solution.py:20
  42.4 0.4 collective-permute-start.19
  42.7 1.7 %collective-permute-start.16 = (f32[64,128]{1,0:T(8,128)S(1)}, f32[64,128]{1,0:T(8,128)S(1)}, u32[]{:S(2)}, u32[]{:S(2)}) collective-permute-start(f32[64,128]{1,0:T(8,128)S(1)} %add.45.refs_0_), channel_id=1, source_target_pairs={{0,24},{2,26},{4,28},{6,30},{8,16},{10,18},{12,20},{14,22},{16,8},... | collective-permute-start | bytes 98312 | tf_op jit(solution)/shard_map/ppermute | solution.py:318
  44.5 1.1 %collective-permute-start.17 = (f32[64,128]{1,0:T(8,128)S(1)}, f32[64,128]{1,0:T(8,128)S(1)}, u32[]{:S(2)}, u32[]{:S(2)}) collective-permute-start(f32[64,128]{1,0:T(8,128)S(1)} %add.45.refs_0_), channel_id=1, source_target_pairs={{0,16},{2,18},{4,20},{6,22},{8,24},{10,26},{12,28},{14,30},{16,0},... | collective-permute-start | bytes 98312 | tf_op jit(solution)/shard_map/ppermute | solution.py:318
  45.6 1.5 %collective-permute-start.18 = (f32[64,128]{1,0:T(8,128)S(1)}, f32[64,128]{1,0:T(8,128)S(1)}, u32[]{:S(2)}, u32[]{:S(2)}) collective-permute-start(f32[64,128]{1,0:T(8,128)S(1)} %add.45.refs_0_), channel_id=1, source_target_pairs={{0,8},{2,10},{4,12},{6,14},{8,0},{10,2},{12,4},{14,6},{16,24},{18,... | collective-permute-start | bytes 98312 | tf_op jit(solution)/shard_map/ppermute | solution.py:318
  47.1 2.2 %shard_map.121.refs_4_.inverse_ref = f32[64,64]{1,0:T(8,128)S(1)} custom-call(f32[64,128]{1,0:T(8,128)S(1)} %get-tuple-element.105.refs_0_, f32[64,128]{1,0:T(8,128)S(1)} %collective-permute-done.19.refs_1_), custom_call_target="tpu_custom_call" | custom-call | tf_op jit(solution)/shard_map/pallas_call | solution.py:20
  49.3 0.3 collective-permute-done.17.refs_2_
  49.6 0.3 collective-permute-done.18.refs_3_
  50.2 1.5 %collective-permute-start.20 = (bf16[256,128]{1,0:T(8,128)(2,1)S(1)}, bf16[256,128]{1,0:T(8,128)(2,1)S(1)}, u32[]{:S(2)}, u32[]{:S(2)}) collective-permute-start(bf16[256,128]{1,0:T(8,128)(2,1)S(1)} %shard_map.122.refs_0_), channel_id=1, source_target_pairs={{0,6},{2,4},{4,2},{6,0},{8,14},{10,12},{12,10},{14,8},{16,22},{18,... | collective-permute-start | bytes 196616 | tf_op jit(solution)/shard_map/ppermute | solution.py:318
  51.7 0.6 collective-permute-start.21
  52.3 1.5 %collective-permute-start.22 = (bf16[256,128]{1,0:T(8,128)(2,1)S(1)}, bf16[256,128]{1,0:T(8,128)(2,1)S(1)}, u32[]{:S(2)}, u32[]{:S(2)}) collective-permute-start(bf16[256,128]{1,0:T(8,128)(2,1)S(1)} %shard_map.122.refs_0_), channel_id=1, source_target_pairs={{0,2},{2,0},{4,6},{6,4},{8,10},{10,8},{12,14},{14,12},{16,18},{18,... | collective-permute-start | bytes 196616 | tf_op jit(solution)/shard_map/ppermute | solution.py:318
  53.7 0.8 %shard_map.123 = (bf16[128,2048]{1,0:T(8,128)(2,1)S(1)}, f32[64,2048]{1,0:T(8,128)S(1)}, f32[64,128]{1,0:T(8,128)S(1)}) custom-call(f32[64,64]{1,0:T(8,128)S(1)} %shard_map.121.refs_4_.inverse_ref, bf16[192,2048]{1,0:T(8,128)(2,1)S(1)} %get-tuple-element.111.stack_ref, f32[64,192]{1,0:T(8,128)S(1)} %get-tuple-element.78.m.mix_ref, ...), custom_call_target="tpu_custom_call" | custom-call | tf_op jit(solution)/shard_map/pallas_call | solution.py:20
  54.6 1.5 %collective-permute-done.20.refs_1_ = bf16[256,128]{1,0:T(8,128)(2,1)S(1)} collective-permute-done((bf16[256,128]{1,0:T(8,128)(2,1)S(1)}, bf16[256,128]{1,0:T(8,128)(2,1)S(1)}, u32[]{:S(2)}, u32[]{:S(2)}) %collective-permute-start.20) | collective-permute-done | bytes 65568 | tf_op jit(solution)/shard_map/ppermute | solution.py:318
  56.5 0.3 shard_map.124
  57.0 0.4 shard_map.126.refs_2_
  57.3 0.8 %collective-permute-done.23.refs_1_ = f32[64,128]{1,0:T(8,128)S(1)} collective-permute-done((f32[64,128]{1,0:T(8,128)S(1)}, f32[64,128]{1,0:T(8,128)S(1)}, u32[]{:S(2)}, u32[]{:S(2)}) %collective-permute-start.23) | collective-permute-done | bytes 32800 | tf_op jit(solution)/shard_map/ppermute | solution.py:318
  58.2 0.4 shard_map.127
  58.8 1.1 %shard_map.125 = (f32[64,128]{1,0:T(8,128)S(1)}, f32[64,128]{1,0:T(8,128)S(1)}, f32[64,128]{1,0:T(8,128)S(1)}) custom-call(f32[64,192]{1,0:T(8,128)S(1)} %get-tuple-element.77.m, f32[64,128]{1,0:T(8,128)S(1)} %get-tuple-element.115.refs_0_, f32[64,128]{1,0:T(8,128)S(1)} %collective-permute-done.23.refs_1_, ...), custom_call_target="tpu_custom_call" | custom-call | tf_op jit(solution)/shard_map/pallas_call | solution.py:20
  59.9 0.4 collective-permute-start.28
  60.3 0.3 shard_map.128
  60.6 1.8 %collective-permute-start.25 = (f32[64,128]{1,0:T(8,128)S(1)}, f32[64,128]{1,0:T(8,128)S(1)}, u32[]{:S(2)}, u32[]{:S(2)}) collective-permute-start(f32[64,128]{1,0:T(8,128)S(1)} %shard_map.128), channel_id=1, source_target_pairs={{0,24},{2,26},{4,28},{6,30},{8,16},{10,18},{12,20},{14,22},{16,8},... | collective-permute-start | bytes 98312 | tf_op jit(solution)/shard_map/ppermute | solution.py:318
  62.4 0.8 %collective-permute-start.26 = (f32[64,128]{1,0:T(8,128)S(1)}, f32[64,128]{1,0:T(8,128)S(1)}, u32[]{:S(2)}, u32[]{:S(2)}) collective-permute-start(f32[64,128]{1,0:T(8,128)S(1)} %shard_map.128), channel_id=1, source_target_pairs={{0,16},{2,18},{4,20},{6,22},{8,24},{10,26},{12,28},{14,30},{16,0},... | collective-permute-start | bytes 98312 | tf_op jit(solution)/shard_map/ppermute | solution.py:318
  63.3 1.8 %collective-permute-start.27 = (f32[64,128]{1,0:T(8,128)S(1)}, f32[64,128]{1,0:T(8,128)S(1)}, u32[]{:S(2)}, u32[]{:S(2)}) collective-permute-start(f32[64,128]{1,0:T(8,128)S(1)} %shard_map.128), channel_id=1, source_target_pairs={{0,8},{2,10},{4,12},{6,14},{8,0},{10,2},{12,4},{14,6},{16,24},{18,... | collective-permute-start | bytes 98312 | tf_op jit(solution)/shard_map/ppermute | solution.py:318
  65.1 2.2 %shard_map.129 = (f32[64,64]{1,0:T(8,128)S(1)}, f32[64,128]{1,0:T(8,128)S(1)}) custom-call(f32[64,128]{1,0:T(8,128)S(1)} %get-tuple-element.124.refs_0_, f32[64,128]{1,0:T(8,128)S(1)} %collective-permute-done.28.refs_1_), custom_call_target="tpu_custom_call" | custom-call | tf_op jit(solution)/shard_map/pallas_call | solution.py:20
  67.7 1.7 %collective-permute-start.31 = (f32[64,128]{1,0:T(8,128)S(1)}, f32[64,128]{1,0:T(8,128)S(1)}, u32[]{:S(2)}, u32[]{:S(2)}) collective-permute-start(f32[64,128]{1,0:T(8,128)S(1)} %add_add_fusion.1), channel_id=1, source_target_pairs={{0,6},{2,4},{4,2},{6,0},{8,14},{10,12},{12,10},{14,8},{16,22},{18,... | collective-permute-start | bytes 98312 | tf_op jit(solution)/shard_map/ppermute | solution.py:318
  69.4 1.2 %collective-permute-start.29 = (f32[64,128]{1,0:T(8,128)S(1)}, f32[64,128]{1,0:T(8,128)S(1)}, u32[]{:S(2)}, u32[]{:S(2)}) collective-permute-start(f32[64,128]{1,0:T(8,128)S(1)} %add_add_fusion.1), channel_id=1, source_target_pairs={{0,2},{2,0},{4,6},{6,4},{8,10},{10,8},{12,14},{14,12},{16,18},{18,... | collective-permute-start | bytes 98312 | tf_op jit(solution)/shard_map/ppermute | solution.py:318
  70.6 0.6 collective-permute-start.30
  71.2 1.6 %collective-permute-done.31 = f32[64,128]{1,0:T(8,128)S(1)} collective-permute-done((f32[64,128]{1,0:T(8,128)S(1)}, f32[64,128]{1,0:T(8,128)S(1)}, u32[]{:S(2)}, u32[]{:S(2)}) %collective-permute-start.31) | collective-permute-done | bytes 32800 | tf_op jit(solution)/shard_map/ppermute | solution.py:318
  72.8 0.5 collective-permute-done.29
  73.3 1.2 %collective-permute-done.30 = f32[64,128]{1,0:T(8,128)S(1)} collective-permute-done((f32[64,128]{1,0:T(8,128)S(1)}, f32[64,128]{1,0:T(8,128)S(1)}, u32[]{:S(2)}, u32[]{:S(2)}) %collective-permute-start.30) | collective-permute-done | bytes 32800 | tf_op jit(solution)/shard_map/ppermute | solution.py:318
  74.6 0.8 %shard_map.130 = (f32[64,128]{1,0:T(8,128)}, f32[64,128]{1,0:T(8,128)}, f32[64,256]{1,0:T(8,128)S(1)}) custom-call(f32[64,64]{1,0:T(8,128)S(1)} %get-tuple-element.126.inverse_ref.refs_2_, f32[64,128]{1,0:T(8,128)S(1)} %get-tuple-element.127.scale_ref, f32[64,128]{1,0:T(8,128)S(1)} %get-tuple-element.119.rotated_ref, f32[64,128]{1,0:T(8,128)S(1)} %add.46.adj_ref, ...), custom_call_target="tpu_custom_call" | custom-call | tf_op jit(solution)/shard_map/pallas_call | solution.py:20
  75.4 0.4 collective-permute-done.32.refs_1_
  75.8 1.2 %shard_map.131 = (f32[64,128]{1,0:T(8,128)}, f32[64,64]{1,0:T(8,128)}) custom-call(f32[64,128]{1,0:T(8,128)S(1)} %add_add_fusion.refs_0_, f32[64,128]{1,0:T(8,128)S(1)} %collective-permute-done.32.refs_1_, f32[64,64]{1,0:T(8,128)S(1)} %get-tuple-element.126.inverse_ref.refs_2_, f32[64,256]{1,0:T(8,128)S(1)} %get-tuple-element.134.refs_3_), custom_call_target="tpu_custom_call" | custom-call | tf_op jit(solution)/shard_map/pallas_call | solution.py:20
  (43 shorter events, 2.5 us)
Async XLA Ops:
  1.4 7.3 %collective-permute-start.2 = (bf16[1,192,128]{2,1,0:T(8,128)(2,1)S(1)}, bf16[1,192,128]{2,1,0:T(8,128)(2,1)S(1)}, u32[]{:S(2)}, u32[]{:S(2)}) collective-permute-start(bf16[1,192,128]{2,1,0:T(8,128)(2,1)S(1)} %maximum_bitcast_fusion), channel_id=1, source_target_pairs={{0,24},{2,26},{4,28},{6,30},{8,16},{10,18},{12,20},{14,22},{16,8},... | collective-permute-start | bytes 147464 | tf_op jit(solution)/shard_map/ppermute | solution.py:318
  6.4 5.0 %collective-permute-start.1 = (bf16[1,192,128]{2,1,0:T(8,128)(2,1)S(1)}, bf16[1,192,128]{2,1,0:T(8,128)(2,1)S(1)}, u32[]{:S(2)}, u32[]{:S(2)}) collective-permute-start(bf16[1,192,128]{2,1,0:T(8,128)(2,1)S(1)} %maximum_bitcast_fusion), channel_id=1, source_target_pairs={{0,16},{2,18},{4,20},{6,22},{8,24},{10,26},{12,28},{14,30},{16,0},... | collective-permute-start | bytes 147464 | tf_op jit(solution)/shard_map/ppermute | solution.py:318
  6.4 5.0 %collective-permute-start = (bf16[1,192,128]{2,1,0:T(8,128)(2,1)S(1)}, bf16[1,192,128]{2,1,0:T(8,128)(2,1)S(1)}, u32[]{:S(2)}, u32[]{:S(2)}) collective-permute-start(bf16[1,192,128]{2,1,0:T(8,128)(2,1)S(1)} %maximum_bitcast_fusion), channel_id=1, source_target_pairs={{0,8},{2,10},{4,12},{6,14},{8,0},{10,2},{12,4},{14,6},{16,24},{18,... | collective-permute-start | bytes 147464 | tf_op jit(solution)/shard_map/ppermute | solution.py:318
  7.0 8.0 %copy-start.1 = (f32[3,64,192]{2,1,0:T(8,128)S(1)}, f32[3,64,192]{2,1,0:T(8,128)}, u32[]{:S(2)}) copy-start(f32[3,64,192]{2,1,0:T(8,128)} %param.14) | copy-start | bytes 442372
  11.5 3.6 %copy-start.3 = (s32[1,1,2,16]{3,2,1,0:T(2,128)S(1)}, s32[1,1,2,16]{3,2,1,0:T(2,128)}, u32[]{:S(2)}) copy-start(s32[1,1,2,16]{3,2,1,0:T(2,128)} %param.10) | copy-start | bytes 388
  11.5 3.6 %copy-start.4 = (s32[1,1,2]{2,1,0:T(1,128)S(1)}, s32[1,1,2]{2,1,0:T(1,128)}, u32[]{:S(2)}) copy-start(s32[1,1,2]{2,1,0:T(1,128)} %param.9) | copy-start | bytes 28
  11.5 8.5 %collective-permute-start.3 = (bf16[4,192,128]{2,1,0:T(8,128)(2,1)S(1)}, bf16[4,192,128]{2,1,0:T(8,128)(2,1)S(1)}, u32[]{:S(2)}, u32[]{:S(2)}) collective-permute-start(bf16[4,192,128]{2,1,0:T(8,128)(2,1)S(1)} %pad_maximum_fusion.refs_0_), channel_id=1, source_target_pairs={{0,6},{2,4},{4,2},{6,0},{8,14},{10,12},{12,10},{14,8},{16,22},{18,... | collective-permute-start | bytes 589832 | tf_op jit(solution)/shard_map/ppermute | solution.py:318
  14.0 8.4 %collective-permute-start.4 = (bf16[4,192,128]{2,1,0:T(8,128)(2,1)S(1)}, bf16[4,192,128]{2,1,0:T(8,128)(2,1)S(1)}, u32[]{:S(2)}, u32[]{:S(2)}) collective-permute-start(bf16[4,192,128]{2,1,0:T(8,128)(2,1)S(1)} %pad_maximum_fusion.refs_0_), channel_id=1, source_target_pairs={{0,4},{2,6},{4,0},{6,2},{8,12},{10,14},{12,8},{14,10},{16,20},{18,... | collective-permute-start | bytes 589832 | tf_op jit(solution)/shard_map/ppermute | solution.py:318
  14.5 8.0 %collective-permute-start.5 = (bf16[4,192,128]{2,1,0:T(8,128)(2,1)S(1)}, bf16[4,192,128]{2,1,0:T(8,128)(2,1)S(1)}, u32[]{:S(2)}, u32[]{:S(2)}) collective-permute-start(bf16[4,192,128]{2,1,0:T(8,128)(2,1)S(1)} %pad_maximum_fusion.refs_0_), channel_id=1, source_target_pairs={{0,2},{2,0},{4,6},{6,4},{8,10},{10,8},{12,14},{14,12},{16,18},{18,... | collective-permute-start | bytes 589832 | tf_op jit(solution)/shard_map/ppermute | solution.py:318
  15.2 1.2 %copy-start = (bf16[1,1,2,16,128,128]{5,4,3,2,1,0:T(8,128)(2,1)S(1)}, bf16[1,1,2,16,128,128]{5,4,3,2,1,0:T(8,128)(2,1)}, u32[]{:S(2)}) copy-start(bf16[1,1,2,16,128,128]{5,4,3,2,1,0:T(8,128)(2,1)} %param.8) | copy-start | bytes 3145732
  16.4 2.0 %copy-start.2 = (f32[3,64,128]{2,1,0:T(8,128)S(1)}, f32[3,64,128]{2,1,0:T(8,128)}, u32[]{:S(2)}) copy-start(f32[3,64,128]{2,1,0:T(8,128)} %param.15) | copy-start | bytes 294916
  23.1 1.3 %collective-permute-start.6 = (f32[64,128]{1,0:T(8,128)S(1)}, f32[64,128]{1,0:T(8,128)S(1)}, u32[]{:S(2)}, u32[]{:S(2)}) collective-permute-start(f32[64,128]{1,0:T(8,128)S(1)} %get-tuple-element.86), channel_id=1, source_target_pairs={{0,1},{1,0},{2,3},{3,2},{4,5},{5,4},{6,7},{7,6},{8,9},{9,8},{10,11... | collective-permute-start | bytes 98312 | tf_op jit(solution)/shard_map/ppermute | solution.py:318
  24.4 4.6 %collective-permute-start.10 = (f32[64,128]{1,0:T(8,128)S(1)}, f32[64,128]{1,0:T(8,128)S(1)}, u32[]{:S(2)}, u32[]{:S(2)}) collective-permute-start(f32[64,128]{1,0:T(8,128)S(1)} %shard_map.113.refs_0_), channel_id=1, source_target_pairs={{0,1},{1,0},{2,3},{3,2},{4,5},{5,4},{6,7},{7,6},{8,9},{9,8},{10,11... | collective-permute-start | bytes 98312 | tf_op jit(solution)/shard_map/ppermute | solution.py:318
  24.6 6.6 %collective-permute-start.7 = (f32[64,128]{1,0:T(8,128)S(1)}, f32[64,128]{1,0:T(8,128)S(1)}, u32[]{:S(2)}, u32[]{:S(2)}) collective-permute-start(f32[64,128]{1,0:T(8,128)S(1)} %add.44.refs_0_), channel_id=1, source_target_pairs={{0,24},{2,26},{4,28},{6,30},{8,16},{10,18},{12,20},{14,22},{16,8},... | collective-permute-start | bytes 98312 | tf_op jit(solution)/shard_map/ppermute | solution.py:318
  26.2 5.3 %collective-permute-start.8 = (f32[64,128]{1,0:T(8,128)S(1)}, f32[64,128]{1,0:T(8,128)S(1)}, u32[]{:S(2)}, u32[]{:S(2)}) collective-permute-start(f32[64,128]{1,0:T(8,128)S(1)} %add.44.refs_0_), channel_id=1, source_target_pairs={{0,16},{2,18},{4,20},{6,22},{8,24},{10,26},{12,28},{14,30},{16,0},... | collective-permute-start | bytes 98312 | tf_op jit(solution)/shard_map/ppermute | solution.py:318
  26.7 4.7 %collective-permute-start.9 = (f32[64,128]{1,0:T(8,128)S(1)}, f32[64,128]{1,0:T(8,128)S(1)}, u32[]{:S(2)}, u32[]{:S(2)}) collective-permute-start(f32[64,128]{1,0:T(8,128)S(1)} %add.44.refs_0_), channel_id=1, source_target_pairs={{0,8},{2,10},{4,12},{6,14},{8,0},{10,2},{12,4},{14,6},{16,24},{18,... | collective-permute-start | bytes 98312 | tf_op jit(solution)/shard_map/ppermute | solution.py:318
  31.7 5.3 %collective-permute-start.11 = (bf16[256,128]{1,0:T(8,128)(2,1)S(1)}, bf16[256,128]{1,0:T(8,128)(2,1)S(1)}, u32[]{:S(2)}, u32[]{:S(2)}) collective-permute-start(bf16[256,128]{1,0:T(8,128)(2,1)S(1)} %shard_map.115.refs_0_), channel_id=1, source_target_pairs={{0,6},{2,4},{4,2},{6,0},{8,14},{10,12},{12,10},{14,8},{16,22},{18,... | collective-permute-start | bytes 196616 | tf_op jit(solution)/shard_map/ppermute | solution.py:318
  33.5 4.6 %collective-permute-start.12 = (bf16[256,128]{1,0:T(8,128)(2,1)S(1)}, bf16[256,128]{1,0:T(8,128)(2,1)S(1)}, u32[]{:S(2)}, u32[]{:S(2)}) collective-permute-start(bf16[256,128]{1,0:T(8,128)(2,1)S(1)} %shard_map.115.refs_0_), channel_id=1, source_target_pairs={{0,4},{2,6},{4,0},{6,2},{8,12},{10,14},{12,8},{14,10},{16,20},{18,... | collective-permute-start | bytes 196616 | tf_op jit(solution)/shard_map/ppermute | solution.py:318
  34.8 4.3 %collective-permute-start.13 = (bf16[256,128]{1,0:T(8,128)(2,1)S(1)}, bf16[256,128]{1,0:T(8,128)(2,1)S(1)}, u32[]{:S(2)}, u32[]{:S(2)}) collective-permute-start(bf16[256,128]{1,0:T(8,128)(2,1)S(1)} %shard_map.115.refs_0_), channel_id=1, source_target_pairs={{0,2},{2,0},{4,6},{6,4},{8,10},{10,8},{12,14},{14,12},{16,18},{18,... | collective-permute-start | bytes 196616 | tf_op jit(solution)/shard_map/ppermute | solution.py:318
  39.4 1.3 %collective-permute-start.14 = (f32[64,128]{1,0:T(8,128)S(1)}, f32[64,128]{1,0:T(8,128)S(1)}, u32[]{:S(2)}, u32[]{:S(2)}) collective-permute-start(f32[64,128]{1,0:T(8,128)S(1)} %get-tuple-element.98.refs_0_), channel_id=1, source_target_pairs={{0,1},{1,0},{2,3},{3,2},{4,5},{5,4},{6,7},{7,6},{8,9},{9,8},{10,11... | collective-permute-start | bytes 98312 | tf_op jit(solution)/shard_map/ppermute | solution.py:318
  41.1 1.3 %collective-permute-start.15 = (f32[64,128]{1,0:T(8,128)S(1)}, f32[64,128]{1,0:T(8,128)S(1)}, u32[]{:S(2)}, u32[]{:S(2)}) collective-permute-start(f32[64,128]{1,0:T(8,128)S(1)} %get-tuple-element.102), channel_id=1, source_target_pairs={{0,1},{1,0},{2,3},{3,2},{4,5},{5,4},{6,7},{7,6},{8,9},{9,8},{10,11... | collective-permute-start | bytes 98312 | tf_op jit(solution)/shard_map/ppermute | solution.py:318
  42.4 4.8 %collective-permute-start.19 = (f32[64,128]{1,0:T(8,128)S(1)}, f32[64,128]{1,0:T(8,128)S(1)}, u32[]{:S(2)}, u32[]{:S(2)}) collective-permute-start(f32[64,128]{1,0:T(8,128)S(1)} %get-tuple-element.105.refs_0_), channel_id=1, source_target_pairs={{0,1},{1,0},{2,3},{3,2},{4,5},{5,4},{6,7},{7,6},{8,9},{9,8},{10,11... | collective-permute-start | bytes 98312 | tf_op jit(solution)/shard_map/ppermute | solution.py:318
  42.7 6.6 %collective-permute-start.16 = (f32[64,128]{1,0:T(8,128)S(1)}, f32[64,128]{1,0:T(8,128)S(1)}, u32[]{:S(2)}, u32[]{:S(2)}) collective-permute-start(f32[64,128]{1,0:T(8,128)S(1)} %add.45.refs_0_), channel_id=1, source_target_pairs={{0,24},{2,26},{4,28},{6,30},{8,16},{10,18},{12,20},{14,22},{16,8},... | collective-permute-start | bytes 98312 | tf_op jit(solution)/shard_map/ppermute | solution.py:318
  44.5 5.2 %collective-permute-start.17 = (f32[64,128]{1,0:T(8,128)S(1)}, f32[64,128]{1,0:T(8,128)S(1)}, u32[]{:S(2)}, u32[]{:S(2)}) collective-permute-start(f32[64,128]{1,0:T(8,128)S(1)} %add.45.refs_0_), channel_id=1, source_target_pairs={{0,16},{2,18},{4,20},{6,22},{8,24},{10,26},{12,28},{14,30},{16,0},... | collective-permute-start | bytes 98312 | tf_op jit(solution)/shard_map/ppermute | solution.py:318
  45.6 4.3 %collective-permute-start.18 = (f32[64,128]{1,0:T(8,128)S(1)}, f32[64,128]{1,0:T(8,128)S(1)}, u32[]{:S(2)}, u32[]{:S(2)}) collective-permute-start(f32[64,128]{1,0:T(8,128)S(1)} %add.45.refs_0_), channel_id=1, source_target_pairs={{0,8},{2,10},{4,12},{6,14},{8,0},{10,2},{12,4},{14,6},{16,24},{18,... | collective-permute-start | bytes 98312 | tf_op jit(solution)/shard_map/ppermute | solution.py:318
  50.2 5.9 %collective-permute-start.20 = (bf16[256,128]{1,0:T(8,128)(2,1)S(1)}, bf16[256,128]{1,0:T(8,128)(2,1)S(1)}, u32[]{:S(2)}, u32[]{:S(2)}) collective-permute-start(bf16[256,128]{1,0:T(8,128)(2,1)S(1)} %shard_map.122.refs_0_), channel_id=1, source_target_pairs={{0,6},{2,4},{4,2},{6,0},{8,14},{10,12},{12,10},{14,8},{16,22},{18,... | collective-permute-start | bytes 196616 | tf_op jit(solution)/shard_map/ppermute | solution.py:318
  51.7 4.7 %collective-permute-start.21 = (bf16[256,128]{1,0:T(8,128)(2,1)S(1)}, bf16[256,128]{1,0:T(8,128)(2,1)S(1)}, u32[]{:S(2)}, u32[]{:S(2)}) collective-permute-start(bf16[256,128]{1,0:T(8,128)(2,1)S(1)} %shard_map.122.refs_0_), channel_id=1, source_target_pairs={{0,4},{2,6},{4,0},{6,2},{8,12},{10,14},{12,8},{14,10},{16,20},{18,... | collective-permute-start | bytes 196616 | tf_op jit(solution)/shard_map/ppermute | solution.py:318
  52.3 4.3 %collective-permute-start.22 = (bf16[256,128]{1,0:T(8,128)(2,1)S(1)}, bf16[256,128]{1,0:T(8,128)(2,1)S(1)}, u32[]{:S(2)}, u32[]{:S(2)}) collective-permute-start(bf16[256,128]{1,0:T(8,128)(2,1)S(1)} %shard_map.122.refs_0_), channel_id=1, source_target_pairs={{0,2},{2,0},{4,6},{6,4},{8,10},{10,8},{12,14},{14,12},{16,18},{18,... | collective-permute-start | bytes 196616 | tf_op jit(solution)/shard_map/ppermute | solution.py:318
  56.9 1.3 %collective-permute-start.23 = (f32[64,128]{1,0:T(8,128)S(1)}, f32[64,128]{1,0:T(8,128)S(1)}, u32[]{:S(2)}, u32[]{:S(2)}) collective-permute-start(f32[64,128]{1,0:T(8,128)S(1)} %get-tuple-element.115.refs_0_), channel_id=1, source_target_pairs={{0,1},{1,0},{2,3},{3,2},{4,5},{5,4},{6,7},{7,6},{8,9},{9,8},{10,11... | collective-permute-start | bytes 98312 | tf_op jit(solution)/shard_map/ppermute | solution.py:318
  58.6 1.3 %collective-permute-start.24 = (f32[64,128]{1,0:T(8,128)S(1)}, f32[64,128]{1,0:T(8,128)S(1)}, u32[]{:S(2)}, u32[]{:S(2)}) collective-permute-start(f32[64,128]{1,0:T(8,128)S(1)} %get-tuple-element.121), channel_id=1, source_target_pairs={{0,1},{1,0},{2,3},{3,2},{4,5},{5,4},{6,7},{7,6},{8,9},{9,8},{10,11... | collective-permute-start | bytes 98312 | tf_op jit(solution)/shard_map/ppermute | solution.py:318
  59.9 5.2 %collective-permute-start.28 = (f32[64,128]{1,0:T(8,128)S(1)}, f32[64,128]{1,0:T(8,128)S(1)}, u32[]{:S(2)}, u32[]{:S(2)}) collective-permute-start(f32[64,128]{1,0:T(8,128)S(1)} %get-tuple-element.124.refs_0_), channel_id=1, source_target_pairs={{0,1},{1,0},{2,3},{3,2},{4,5},{5,4},{6,7},{7,6},{8,9},{9,8},{10,11... | collective-permute-start | bytes 98312 | tf_op jit(solution)/shard_map/ppermute | solution.py:318
  60.6 6.7 %collective-permute-start.25 = (f32[64,128]{1,0:T(8,128)S(1)}, f32[64,128]{1,0:T(8,128)S(1)}, u32[]{:S(2)}, u32[]{:S(2)}) collective-permute-start(f32[64,128]{1,0:T(8,128)S(1)} %shard_map.128), channel_id=1, source_target_pairs={{0,24},{2,26},{4,28},{6,30},{8,16},{10,18},{12,20},{14,22},{16,8},... | collective-permute-start | bytes 98312 | tf_op jit(solution)/shard_map/ppermute | solution.py:318
  62.4 5.0 %collective-permute-start.26 = (f32[64,128]{1,0:T(8,128)S(1)}, f32[64,128]{1,0:T(8,128)S(1)}, u32[]{:S(2)}, u32[]{:S(2)}) collective-permute-start(f32[64,128]{1,0:T(8,128)S(1)} %shard_map.128), channel_id=1, source_target_pairs={{0,16},{2,18},{4,20},{6,22},{8,24},{10,26},{12,28},{14,30},{16,0},... | collective-permute-start | bytes 98312 | tf_op jit(solution)/shard_map/ppermute | solution.py:318
  63.3 4.4 %collective-permute-start.27 = (f32[64,128]{1,0:T(8,128)S(1)}, f32[64,128]{1,0:T(8,128)S(1)}, u32[]{:S(2)}, u32[]{:S(2)}) collective-permute-start(f32[64,128]{1,0:T(8,128)S(1)} %shard_map.128), channel_id=1, source_target_pairs={{0,8},{2,10},{4,12},{6,14},{8,0},{10,2},{12,4},{14,6},{16,24},{18,... | collective-permute-start | bytes 98312 | tf_op jit(solution)/shard_map/ppermute | solution.py:318
  67.7 5.2 %collective-permute-start.31 = (f32[64,128]{1,0:T(8,128)S(1)}, f32[64,128]{1,0:T(8,128)S(1)}, u32[]{:S(2)}, u32[]{:S(2)}) collective-permute-start(f32[64,128]{1,0:T(8,128)S(1)} %add_add_fusion.1), channel_id=1, source_target_pairs={{0,6},{2,4},{4,2},{6,0},{8,14},{10,12},{12,10},{14,8},{16,22},{18,... | collective-permute-start | bytes 98312 | tf_op jit(solution)/shard_map/ppermute | solution.py:318
  69.4 3.9 %collective-permute-start.29 = (f32[64,128]{1,0:T(8,128)S(1)}, f32[64,128]{1,0:T(8,128)S(1)}, u32[]{:S(2)}, u32[]{:S(2)}) collective-permute-start(f32[64,128]{1,0:T(8,128)S(1)} %add_add_fusion.1), channel_id=1, source_target_pairs={{0,2},{2,0},{4,6},{6,4},{8,10},{10,8},{12,14},{14,12},{16,18},{18,... | collective-permute-start | bytes 98312 | tf_op jit(solution)/shard_map/ppermute | solution.py:318
  70.6 3.9 %collective-permute-start.30 = (f32[64,128]{1,0:T(8,128)S(1)}, f32[64,128]{1,0:T(8,128)S(1)}, u32[]{:S(2)}, u32[]{:S(2)}) collective-permute-start(f32[64,128]{1,0:T(8,128)S(1)} %add_add_fusion.1), channel_id=1, source_target_pairs={{0,4},{2,6},{4,0},{6,2},{8,12},{10,14},{12,8},{14,10},{16,20},{18,... | collective-permute-start | bytes 98312 | tf_op jit(solution)/shard_map/ppermute | solution.py:318
  74.5 1.3 %collective-permute-start.32 = (f32[64,128]{1,0:T(8,128)S(1)}, f32[64,128]{1,0:T(8,128)S(1)}, u32[]{:S(2)}, u32[]{:S(2)}) collective-permute-start(f32[64,128]{1,0:T(8,128)S(1)} %add_add_fusion.refs_0_), channel_id=1, source_target_pairs={{0,1},{1,0},{2,3},{3,2},{4,5},{5,4},{6,7},{7,6},{8,9},{9,8},{10,11... | collective-permute-start | bytes 98312 | tf_op jit(solution)/shard_map/ppermute | solution.py:318
